TPU v7x, 256 devices: a whole 4x4x8 slice. The times are simulated.
256 devices in a mesh: space: 128 (over y, z, x), orb: 2 (over core).
Axes of the slice: x: 4, y: 4, z: 8, core: 2. Of those that a mesh axis runs over, the one named last changes fastest.
Arguments:
- coefficients: float32 [2, 128, 128, 512], P(None, 'space', None, 'orb'), may hold values from -6 to 6
- margin: float32 [128, 16, 128, 128], P('space'), may hold values from -0.125 to 0.125
- step_matrix: float32 [128, 16, 128, 128], P('space'), may hold values from -0.1875 to 0.1875
- neighbours: int32 [128, 16], P('space'), may hold values from 0 to 127, as said below
- pattern: int32 [128, 16], P('space'), may hold values 0 or 1
Outputs:
- propagated: float32 [2, 128, 128, 512], P(None, 'space', None, 'orb')
- projections: float32 [2, 512, 512], P(None, 'space', 'orb')
Inputs may be any that keep to these rules, and one draw needn't show every extreme that they name: neighbours[i, 0] = i; every other entry is an atom block of a spatial domain at most 2 domains away from that of block i (domain = block index); the block of slot 1 lies 2 domains ahead of block i and the block of slot 2 lies 2 domains behind it, each clipped to the first and last domain.
All inputs are finite; a program needn't handle non-finite values. No bound on the sum of `pattern` on one device may be relied on, other than what follows from the above.
Results may differ from a plain program's by a relative error of at most 0.0001.
Values sent between devices are 32-bit elements; how exact they have to be, the bound alone decides.
No kernel may reach another device: no remote copies, remote signals or barrier semaphores. Data moves between devices by JAX's collectives and lax.ppermute only.
A program may use at most 64 MiB of HBM per device.

v0:
```python
import jax
import jax.numpy as jnp
from jax import lax
from jax.sharding import PartitionSpec as P

REACH_DEV = 2
ORDER = 4


def shifted(value, axis, by):
    length = lax.axis_size(axis)
    pairs = [(i, i + by) for i in range(length) if 0 <= i + by < length]
    return lax.ppermute(value, axis, pairs)


def local(coefficients, margin, step_matrix, neighbours, pattern):
    blocks_here = coefficients.shape[1]
    block_width = coefficients.shape[2]
    columns = coefficients.shape[3]
    position = lax.axis_index("space")
    column_ids = jnp.arange(neighbours.shape[1], dtype=jnp.int32)[None, :]
    weights = jnp.where(column_ids == 0, jnp.float32(1.0), pattern.astype(jnp.float32))
    margin_live = margin * weights[:, :, None, None]
    step_live = step_matrix * weights[:, :, None, None]
    local_index = (neighbours - (position - REACH_DEV) * blocks_here).reshape(-1)

    def window_of(state):
        ahead = [shifted(state, "space", -distance) for distance in range(1, REACH_DEV + 1)]
        behind = [shifted(state, "space", distance) for distance in range(1, REACH_DEV + 1)]
        return jnp.concatenate(behind[::-1] + [state] + ahead, axis=0)

    def apply_blocks(matrix, state):
        window = window_of(state)
        picked = jnp.take(window, local_index, axis=0)
        picked = picked.reshape(blocks_here, -1, block_width, state.shape[2])
        return jnp.einsum("rkab,rkbc->rac", matrix, picked, precision=lax.Precision.HIGHEST)

    state = jnp.concatenate([coefficients[0], coefficients[1]], axis=-1)
    moved = state + apply_blocks(margin_live, state)
    total = moved
    term = moved
    for order_index in range(1, ORDER + 1):
        image = apply_blocks(step_live, term)
        term = jnp.concatenate([image[..., columns:], -image[..., :columns]], axis=-1) / order_index
        total = total + term
    propagated = jnp.stack([total[..., :columns], total[..., columns:]])
    reference_all = lax.all_gather(coefficients, "orb", axis=3, tiled=True)
    all_orbitals = reference_all.shape[3]
    old_real = reference_all[0].reshape(-1, all_orbitals)
    old_imag = reference_all[1].reshape(-1, all_orbitals)
    new_real = propagated[0].reshape(-1, columns)
    new_imag = propagated[1].reshape(-1, columns)
    highest = lax.Precision.HIGHEST
    part_real = jnp.einsum("ra,rb->ab", old_real, new_real, precision=highest) + jnp.einsum(
        "ra,rb->ab", old_imag, new_imag, precision=highest
    )
    part_imag = jnp.einsum("ra,rb->ab", old_real, new_imag, precision=highest) - jnp.einsum(
        "ra,rb->ab", old_imag, new_real, precision=highest
    )
    partial_value = jnp.stack([part_real, part_imag])
    rows_total = blocks_here * block_width * lax.axis_size("space")
    summed = lax.psum(partial_value, "space")
    share = all_orbitals // lax.axis_size("space")
    owned = lax.dynamic_slice_in_dim(summed, position * share, share, 1)
    return (propagated, owned / rows_total)


def solution(mesh):
    return jax.shard_map(
        local,
        mesh=mesh,
        in_specs=(
            P(None, "space", None, "orb"),
            P("space", None, None, None),
            P("space", None, None, None),
            P("space", None),
            P("space", None),
        ),
        out_specs=(P(None, "space", None, "orb"), P(None, "space", "orb")),
        check_vma=False,
    )
```

profile of v0, /device:TPU:32, one launch (start us, length us, event | category | flops | bytes accessed | tf_op | source)
XLA Modules:
  0.0 406.9 jit_solution(16764335391815661623)
XLA Ops:
  8.3 4.9 %collective-permute-start = (f32[1,128,512]{2,1,0:T(8,128)S(1)}, f32[1,128,512]{2,1,0:T(8,128)S(1)}, u32[]{:S(2)}, u32[]{:S(2)}) collective-permute-start(f32[1,128,512]{2,1,0:T(8,128)S(1)} %pad_maximum_fusion.1), channel_id=1, source_target_pairs={{0,4},{2,6},{4,8},{6,10},{8,12},{10,14},{12,16},{14,18},{16,20},{1... | collective-permute-start | bytes 786440 | tf_op jit(solution)/shard_map/ppermute | solution.py:13
  13.2 2.5 collective-permute-start.1
  15.7 5.5 %collective-permute-start.2 = (f32[1,128,512]{2,1,0:T(8,128)S(1)}, f32[1,128,512]{2,1,0:T(8,128)S(1)}, u32[]{:S(2)}, u32[]{:S(2)}) collective-permute-start(f32[1,128,512]{2,1,0:T(8,128)S(1)} %pad_maximum_fusion.1), channel_id=1, source_target_pairs={{2,0},{4,2},{6,4},{8,6},{10,8},{12,10},{14,12},{16,14},{18,16},{20... | collective-permute-start | bytes 786440 | tf_op jit(solution)/shard_map/ppermute | solution.py:13
  23.2 4.3 %collective-permute-done.1 = f32[1,128,512]{2,1,0:T(8,128)S(1)} collective-permute-done((f32[1,128,512]{2,1,0:T(8,128)S(1)}, f32[1,128,512]{2,1,0:T(8,128)S(1)}, u32[]{:S(2)}, u32[]{:S(2)}) %collective-permute-start.1) | collective-permute-done | bytes 262176 | tf_op jit(solution)/shard_map/ppermute | solution.py:13
  28.9 3.8 collective-permute-done.3
  32.8 2.8 gather_fusion
  35.5 4.2 %fusion.37 = f32[128,512]{1,0:T(8,128)S(1)} fusion(f32[16,128,512]{2,1,0:T(8,128)} %gather_fusion, pred[16]{0:T(512)(128)(4,1)S(1)} %get-tuple-element.5, f32[1,16,128,128]{3,2,1,0:T(8,128)S(1)} %copy-done.2, f32[16]{0:T(128)S(1)} %fusion.70, f32[128,256]{1,0:T(8,128)S(1)} %get-tuple-element.26, f32[128,256]{1,0:T(8,128)S(1)} %get-tuple-element.23), kind=kOutput, calls=%fused_computation.34 | convolution fusion | flops 1612054528 | bytes 5767248 | tf_op jit(solution)/shard_map/rkab,rkbc->rac/dot_general | solution.py:36
  39.8 7.2 %collective-permute-start.4 = (f32[1,128,512]{2,1,0:T(8,128)S(1)}, f32[1,128,512]{2,1,0:T(8,128)S(1)}, u32[]{:S(2)}, u32[]{:S(2)}) collective-permute-start(f32[1,128,512]{2,1,0:T(8,128)S(1)} %bitcast.91), channel_id=1, source_target_pairs={{0,4},{2,6},{4,8},{6,10},{8,12},{10,14},{12,16},{14,18},{16,20},{1... | collective-permute-start | bytes 786440 | tf_op jit(solution)/shard_map/ppermute | solution.py:13
  49.0 6.0 %collective-permute-start.6 = (f32[1,128,512]{2,1,0:T(8,128)S(1)}, f32[1,128,512]{2,1,0:T(8,128)S(1)}, u32[]{:S(2)}, u32[]{:S(2)}) collective-permute-start(f32[1,128,512]{2,1,0:T(8,128)S(1)} %bitcast.93), channel_id=1, source_target_pairs={{2,0},{4,2},{6,4},{8,6},{10,8},{12,10},{14,12},{16,14},{18,16},{20... | collective-permute-start | bytes 786440 | tf_op jit(solution)/shard_map/ppermute | solution.py:13
  57.5 4.4 %collective-permute-done.6 = f32[1,128,512]{2,1,0:T(8,128)S(1)} collective-permute-done((f32[1,128,512]{2,1,0:T(8,128)S(1)}, f32[1,128,512]{2,1,0:T(8,128)S(1)}, u32[]{:S(2)}, u32[]{:S(2)}) %collective-permute-start.6) | collective-permute-done | bytes 262176 | tf_op jit(solution)/shard_map/ppermute | solution.py:13
  61.9 2.8 collective-permute-done.7
  64.8 2.8 gather_fusion.1
  67.6 4.3 %fusion.25 = f32[1,128,512]{2,1,0:T(8,128)S(1)} fusion(f32[16,128,512]{2,1,0:T(8,128)} %gather_fusion.1, pred[16]{0:T(512)(128)(4,1)S(1)} %get-tuple-element.5, f32[1,16,128,128]{3,2,1,0:T(8,128)S(1)} %copy-done, f32[16]{0:T(128)S(1)} %fusion.70), kind=kOutput, calls=%fused_computation.30 | convolution fusion | flops 1611923456 | bytes 5505104 | tf_op jit(solution)/shard_map/rkab,rkbc->rac/dot_general | solution.py:36
  71.9 7.2 %collective-permute-start.8 = (f32[1,128,512]{2,1,0:T(8,128)S(1)}, f32[1,128,512]{2,1,0:T(8,128)S(1)}, u32[]{:S(2)}, u32[]{:S(2)}) collective-permute-start(f32[1,128,512]{2,1,0:T(8,128)S(1)} %pad_maximum_fusion.2), channel_id=1, source_target_pairs={{0,4},{2,6},{4,8},{6,10},{8,12},{10,14},{12,16},{14,18},{16,20},{1... | collective-permute-start | bytes 786440 | tf_op jit(solution)/shard_map/ppermute | solution.py:13
  81.1 6.0 %collective-permute-start.10 = (f32[1,128,512]{2,1,0:T(8,128)S(1)}, f32[1,128,512]{2,1,0:T(8,128)S(1)}, u32[]{:S(2)}, u32[]{:S(2)}) collective-permute-start(f32[1,128,512]{2,1,0:T(8,128)S(1)} %pad_maximum_fusion.2), channel_id=1, source_target_pairs={{2,0},{4,2},{6,4},{8,6},{10,8},{12,10},{14,12},{16,14},{18,16},{20... | collective-permute-start | bytes 786440 | tf_op jit(solution)/shard_map/ppermute | solution.py:13
  91.2 5.7 %collective-permute-done.11 = f32[1,128,512]{2,1,0:T(8,128)S(1)} collective-permute-done((f32[1,128,512]{2,1,0:T(8,128)S(1)}, f32[1,128,512]{2,1,0:T(8,128)S(1)}, u32[]{:S(2)}, u32[]{:S(2)}) %collective-permute-start.11) | collective-permute-done | bytes 262176 | tf_op jit(solution)/shard_map/ppermute | solution.py:13
  96.9 2.8 gather_fusion.2
  99.7 4.3 %fusion.28 = f32[1,128,512]{2,1,0:T(8,128)S(1)} fusion(f32[16,128,512]{2,1,0:T(8,128)} %gather_fusion.2, pred[16]{0:T(512)(128)(4,1)S(1)} %get-tuple-element.5, f32[1,16,128,128]{3,2,1,0:T(8,128)S(1)} %copy-done, f32[16]{0:T(128)S(1)} %fusion.70), kind=kOutput, calls=%fused_computation.31 | convolution fusion | flops 1611923456 | bytes 5505104 | tf_op jit(solution)/shard_map/rkab,rkbc->rac/dot_general | solution.py:36
  104.7 5.8 %collective-permute-start.12 = (f32[1,128,512]{2,1,0:T(8,128)S(1)}, f32[1,128,512]{2,1,0:T(8,128)S(1)}, u32[]{:S(2)}, u32[]{:S(2)}) collective-permute-start(f32[1,128,512]{2,1,0:T(8,128)S(1)} %maximum_multiply_fusion.1), channel_id=1, source_target_pairs={{0,4},{2,6},{4,8},{6,10},{8,12},{10,14},{12,16},{14,18},{16,20},{1... | collective-permute-start | bytes 786440 | tf_op jit(solution)/shard_map/ppermute | solution.py:13
  113.0 5.5 %collective-permute-start.14 = (f32[1,128,512]{2,1,0:T(8,128)S(1)}, f32[1,128,512]{2,1,0:T(8,128)S(1)}, u32[]{:S(2)}, u32[]{:S(2)}) collective-permute-start(f32[1,128,512]{2,1,0:T(8,128)S(1)} %maximum_multiply_fusion.1), channel_id=1, source_target_pairs={{2,0},{4,2},{6,4},{8,6},{10,8},{12,10},{14,12},{16,14},{18,16},{20... | collective-permute-start | bytes 786440 | tf_op jit(solution)/shard_map/ppermute | solution.py:13
  120.4 2.5 collective-permute-done.13
  123.0 3.6 collective-permute-done.14
  128.3 2.8 gather_fusion.3
  131.0 4.3 %fusion.31 = f32[1,128,512]{2,1,0:T(8,128)S(1)} fusion(f32[16,128,512]{2,1,0:T(8,128)} %gather_fusion.3, pred[16]{0:T(512)(128)(4,1)S(1)} %get-tuple-element.5, f32[1,16,128,128]{3,2,1,0:T(8,128)S(1)} %copy-done, f32[16]{0:T(128)S(1)} %fusion.70), kind=kOutput, calls=%fused_computation.32 | convolution fusion | flops 1611923456 | bytes 5505104 | tf_op jit(solution)/shard_map/rkab,rkbc->rac/dot_general | solution.py:36
  136.1 4.7 %collective-permute-start.16 = (f32[1,128,512]{2,1,0:T(8,128)S(1)}, f32[1,128,512]{2,1,0:T(8,128)S(1)}, u32[]{:S(2)}, u32[]{:S(2)}) collective-permute-start(f32[1,128,512]{2,1,0:T(8,128)S(1)} %maximum_multiply_fusion.3), channel_id=1, source_target_pairs={{0,4},{2,6},{4,8},{6,10},{8,12},{10,14},{12,16},{14,18},{16,20},{1... | collective-permute-start | bytes 786440 | tf_op jit(solution)/shard_map/ppermute | solution.py:13
  140.9 2.5 collective-permute-start.17
  145.5 5.5 %collective-permute-start.18 = (f32[1,128,512]{2,1,0:T(8,128)S(1)}, f32[1,128,512]{2,1,0:T(8,128)S(1)}, u32[]{:S(2)}, u32[]{:S(2)}) collective-permute-start(f32[1,128,512]{2,1,0:T(8,128)S(1)} %maximum_multiply_fusion.3), channel_id=1, source_target_pairs={{2,0},{4,2},{6,4},{8,6},{10,8},{12,10},{14,12},{16,14},{18,16},{20... | collective-permute-start | bytes 786440 | tf_op jit(solution)/shard_map/ppermute | solution.py:13
  153.2 6.3 %collective-permute-done.18 = f32[1,128,512]{2,1,0:T(8,128)S(1)} collective-permute-done((f32[1,128,512]{2,1,0:T(8,128)S(1)}, f32[1,128,512]{2,1,0:T(8,128)S(1)}, u32[]{:S(2)}, u32[]{:S(2)}) %collective-permute-start.18) | collective-permute-done | bytes 262176 | tf_op jit(solution)/shard_map/ppermute | solution.py:13
  159.6 4.8 %collective-permute-done.19 = f32[1,128,512]{2,1,0:T(8,128)S(1)} collective-permute-done((f32[1,128,512]{2,1,0:T(8,128)S(1)}, f32[1,128,512]{2,1,0:T(8,128)S(1)}, u32[]{:S(2)}, u32[]{:S(2)}) %collective-permute-start.19) | collective-permute-done | bytes 262176 | tf_op jit(solution)/shard_map/ppermute | solution.py:13
  164.4 2.8 gather_fusion.4
  167.2 4.3 %fusion.34 = f32[1,128,512]{2,1,0:T(8,128)S(1)} fusion(f32[16,128,512]{2,1,0:T(8,128)} %gather_fusion.4, pred[16]{0:T(512)(128)(4,1)S(1)} %get-tuple-element.5, f32[1,16,128,128]{3,2,1,0:T(8,128)S(1)} %copy-done, f32[16]{0:T(128)S(1)} %fusion.70), kind=kOutput, calls=%fused_computation.33 | convolution fusion | flops 1611923456 | bytes 5505104 | tf_op jit(solution)/shard_map/rkab,rkbc->rac/dot_general | solution.py:36
  176.0 222.3 %all-reduce.2.cloned.1.call-done = f32[2,512,256]{1,2,0:T(8,128)} async-done(((f32[2,512,256]{1,2,0:T(8,128)}), f32[2,512,256]{1,2,0:T(8,128)}) %all-reduce.2.cloned.1.call-update) | async-done | bytes 1048592 | tf_op jit(solution)/shard_map/psum | solution.py:62
  (85 shorter events, 33.1 us)
Async XLA Ops:
  7.2 16.0 %copy-start.6 = (s32[1,16]{1,0:T(1,128)S(1)}, s32[1,16]{1,0:T(1,128)}, u32[]{:S(2)}) copy-start(s32[1,16]{1,0:T(1,128)} %param.10) | copy-start | bytes 196
  7.2 16.0 %copy-start.7 = (s32[1,16]{1,0:T(1,128)S(1)}, s32[1,16]{1,0:T(1,128)}, u32[]{:S(2)}) copy-start(s32[1,16]{1,0:T(1,128)} %param.11) | copy-start | bytes 196
  7.2 391.1 %all-reduce.2.cloned.1.call-start = ((), (), s32[]{:S(2)}) async-start(), calls=%async_computation | async-start | bytes 2097152 | tf_op jit(solution)/shard_map/psum | solution.py:62
  8.3 14.9 %collective-permute-start = (f32[1,128,512]{2,1,0:T(8,128)S(1)}, f32[1,128,512]{2,1,0:T(8,128)S(1)}, u32[]{:S(2)}, u32[]{:S(2)}) collective-permute-start(f32[1,128,512]{2,1,0:T(8,128)S(1)} %pad_maximum_fusion.1), channel_id=1, source_target_pairs={{0,4},{2,6},{4,8},{6,10},{8,12},{10,14},{12,16},{14,18},{16,20},{1... | collective-permute-start | bytes 786440 | tf_op jit(solution)/shard_map/ppermute | solution.py:13
  13.2 14.3 %collective-permute-start.1 = (f32[1,128,512]{2,1,0:T(8,128)S(1)}, f32[1,128,512]{2,1,0:T(8,128)S(1)}, u32[]{:S(2)}, u32[]{:S(2)}) collective-permute-start(f32[1,128,512]{2,1,0:T(8,128)S(1)} %pad_maximum_fusion.1), channel_id=1, source_target_pairs={{0,2},{2,4},{4,6},{6,8},{8,10},{10,12},{12,14},{14,16},{16,18},{18... | collective-permute-start | bytes 786440 | tf_op jit(solution)/shard_map/ppermute | solution.py:13
  15.7 13.1 %collective-permute-start.2 = (f32[1,128,512]{2,1,0:T(8,128)S(1)}, f32[1,128,512]{2,1,0:T(8,128)S(1)}, u32[]{:S(2)}, u32[]{:S(2)}) collective-permute-start(f32[1,128,512]{2,1,0:T(8,128)S(1)} %pad_maximum_fusion.1), channel_id=1, source_target_pairs={{2,0},{4,2},{6,4},{8,6},{10,8},{12,10},{14,12},{16,14},{18,16},{20... | collective-permute-start | bytes 786440 | tf_op jit(solution)/shard_map/ppermute | solution.py:13
  21.2 11.5 %collective-permute-start.3 = (f32[1,128,512]{2,1,0:T(8,128)S(1)}, f32[1,128,512]{2,1,0:T(8,128)S(1)}, u32[]{:S(2)}, u32[]{:S(2)}) collective-permute-start(f32[1,128,512]{2,1,0:T(8,128)S(1)} %pad_maximum_fusion.1), channel_id=1, source_target_pairs={{4,0},{6,2},{8,4},{10,6},{12,8},{14,10},{16,12},{18,14},{20,16},{2... | collective-permute-start | bytes 786440 | tf_op jit(solution)/shard_map/ppermute | solution.py:13
  32.7 2.8 copy-start.2
  39.8 17.2 %collective-permute-start.4 = (f32[1,128,512]{2,1,0:T(8,128)S(1)}, f32[1,128,512]{2,1,0:T(8,128)S(1)}, u32[]{:S(2)}, u32[]{:S(2)}) collective-permute-start(f32[1,128,512]{2,1,0:T(8,128)S(1)} %bitcast.91), channel_id=1, source_target_pairs={{0,4},{2,6},{4,8},{6,10},{8,12},{10,14},{12,16},{14,18},{16,20},{1... | collective-permute-start | bytes 786440 | tf_op jit(solution)/shard_map/ppermute | solution.py:13
  47.0 10.4 %collective-permute-start.5 = (f32[1,128,512]{2,1,0:T(8,128)S(1)}, f32[1,128,512]{2,1,0:T(8,128)S(1)}, u32[]{:S(2)}, u32[]{:S(2)}) collective-permute-start(f32[1,128,512]{2,1,0:T(8,128)S(1)} %bitcast.92), channel_id=1, source_target_pairs={{0,2},{2,4},{4,6},{6,8},{8,10},{10,12},{12,14},{14,16},{16,18},{18... | collective-permute-start | bytes 786440 | tf_op jit(solution)/shard_map/ppermute | solution.py:13
  49.0 13.0 %collective-permute-start.6 = (f32[1,128,512]{2,1,0:T(8,128)S(1)}, f32[1,128,512]{2,1,0:T(8,128)S(1)}, u32[]{:S(2)}, u32[]{:S(2)}) collective-permute-start(f32[1,128,512]{2,1,0:T(8,128)S(1)} %bitcast.93), channel_id=1, source_target_pairs={{2,0},{4,2},{6,4},{8,6},{10,8},{12,10},{14,12},{16,14},{18,16},{20... | collective-permute-start | bytes 786440 | tf_op jit(solution)/shard_map/ppermute | solution.py:13
  55.0 9.8 %collective-permute-start.7 = (f32[1,128,512]{2,1,0:T(8,128)S(1)}, f32[1,128,512]{2,1,0:T(8,128)S(1)}, u32[]{:S(2)}, u32[]{:S(2)}) collective-permute-start(f32[1,128,512]{2,1,0:T(8,128)S(1)} %bitcast.94), channel_id=1, source_target_pairs={{4,0},{6,2},{8,4},{10,6},{12,8},{14,10},{16,12},{18,14},{20,16},{2... | collective-permute-start | bytes 786440 | tf_op jit(solution)/shard_map/ppermute | solution.py:13
  64.8 2.8 copy-start
  71.9 17.1 %collective-permute-start.8 = (f32[1,128,512]{2,1,0:T(8,128)S(1)}, f32[1,128,512]{2,1,0:T(8,128)S(1)}, u32[]{:S(2)}, u32[]{:S(2)}) collective-permute-start(f32[1,128,512]{2,1,0:T(8,128)S(1)} %pad_maximum_fusion.2), channel_id=1, source_target_pairs={{0,4},{2,6},{4,8},{6,10},{8,12},{10,14},{12,16},{14,18},{16,20},{1... | collective-permute-start | bytes 786440 | tf_op jit(solution)/shard_map/ppermute | solution.py:13
  79.1 11.3 %collective-permute-start.9 = (f32[1,128,512]{2,1,0:T(8,128)S(1)}, f32[1,128,512]{2,1,0:T(8,128)S(1)}, u32[]{:S(2)}, u32[]{:S(2)}) collective-permute-start(f32[1,128,512]{2,1,0:T(8,128)S(1)} %pad_maximum_fusion.2), channel_id=1, source_target_pairs={{0,2},{2,4},{4,6},{6,8},{8,10},{10,12},{12,14},{14,16},{16,18},{18... | collective-permute-start | bytes 786440 | tf_op jit(solution)/shard_map/ppermute | solution.py:13
  81.1 10.1 %collective-permute-start.10 = (f32[1,128,512]{2,1,0:T(8,128)S(1)}, f32[1,128,512]{2,1,0:T(8,128)S(1)}, u32[]{:S(2)}, u32[]{:S(2)}) collective-permute-start(f32[1,128,512]{2,1,0:T(8,128)S(1)} %pad_maximum_fusion.2), channel_id=1, source_target_pairs={{2,0},{4,2},{6,4},{8,6},{10,8},{12,10},{14,12},{16,14},{18,16},{20... | collective-permute-start | bytes 786440 | tf_op jit(solution)/shard_map/ppermute | solution.py:13
  87.1 9.8 %collective-permute-start.11 = (f32[1,128,512]{2,1,0:T(8,128)S(1)}, f32[1,128,512]{2,1,0:T(8,128)S(1)}, u32[]{:S(2)}, u32[]{:S(2)}) collective-permute-start(f32[1,128,512]{2,1,0:T(8,128)S(1)} %pad_maximum_fusion.2), channel_id=1, source_target_pairs={{4,0},{6,2},{8,4},{10,6},{12,8},{14,10},{16,12},{18,14},{20,16},{2... | collective-permute-start | bytes 786440 | tf_op jit(solution)/shard_map/ppermute | solution.py:13
  104.7 15.7 %collective-permute-start.12 = (f32[1,128,512]{2,1,0:T(8,128)S(1)}, f32[1,128,512]{2,1,0:T(8,128)S(1)}, u32[]{:S(2)}, u32[]{:S(2)}) collective-permute-start(f32[1,128,512]{2,1,0:T(8,128)S(1)} %maximum_multiply_fusion.1), channel_id=1, source_target_pairs={{0,4},{2,6},{4,8},{6,10},{8,12},{10,14},{12,16},{14,18},{16,20},{1... | collective-permute-start | bytes 786440 | tf_op jit(solution)/shard_map/ppermute | solution.py:13
  110.5 12.5 %collective-permute-start.13 = (f32[1,128,512]{2,1,0:T(8,128)S(1)}, f32[1,128,512]{2,1,0:T(8,128)S(1)}, u32[]{:S(2)}, u32[]{:S(2)}) collective-permute-start(f32[1,128,512]{2,1,0:T(8,128)S(1)} %maximum_multiply_fusion.1), channel_id=1, source_target_pairs={{0,2},{2,4},{4,6},{6,8},{8,10},{10,12},{12,14},{14,16},{16,18},{18... | collective-permute-start | bytes 786440 | tf_op jit(solution)/shard_map/ppermute | solution.py:13
  113.0 13.7 %collective-permute-start.14 = (f32[1,128,512]{2,1,0:T(8,128)S(1)}, f32[1,128,512]{2,1,0:T(8,128)S(1)}, u32[]{:S(2)}, u32[]{:S(2)}) collective-permute-start(f32[1,128,512]{2,1,0:T(8,128)S(1)} %maximum_multiply_fusion.1), channel_id=1, source_target_pairs={{2,0},{4,2},{6,4},{8,6},{10,8},{12,10},{14,12},{16,14},{18,16},{20... | collective-permute-start | bytes 786440 | tf_op jit(solution)/shard_map/ppermute | solution.py:13
  118.5 9.8 %collective-permute-start.15 = (f32[1,128,512]{2,1,0:T(8,128)S(1)}, f32[1,128,512]{2,1,0:T(8,128)S(1)}, u32[]{:S(2)}, u32[]{:S(2)}) collective-permute-start(f32[1,128,512]{2,1,0:T(8,128)S(1)} %maximum_multiply_fusion.1), channel_id=1, source_target_pairs={{4,0},{6,2},{8,4},{10,6},{12,8},{14,10},{16,12},{18,14},{20,16},{2... | collective-permute-start | bytes 786440 | tf_op jit(solution)/shard_map/ppermute | solution.py:13
  135.3 8.0 %copy-start.1 = (f32[2,1,128,256]{3,2,1,0:T(8,128)S(1)}, f32[2,1,128,256]{3,2,1,0:T(8,128)}, u32[]{:S(2)}) copy-start(f32[2,1,128,256]{3,2,1,0:T(8,128)} %param.7) | copy-start | bytes 786436
  136.1 17.0 %collective-permute-start.16 = (f32[1,128,512]{2,1,0:T(8,128)S(1)}, f32[1,128,512]{2,1,0:T(8,128)S(1)}, u32[]{:S(2)}, u32[]{:S(2)}) collective-permute-start(f32[1,128,512]{2,1,0:T(8,128)S(1)} %maximum_multiply_fusion.3), channel_id=1, source_target_pairs={{0,4},{2,6},{4,8},{6,10},{8,12},{10,14},{12,16},{14,18},{16,20},{1... | collective-permute-start | bytes 786440 | tf_op jit(solution)/shard_map/ppermute | solution.py:13
  140.9 12.3 %collective-permute-start.17 = (f32[1,128,512]{2,1,0:T(8,128)S(1)}, f32[1,128,512]{2,1,0:T(8,128)S(1)}, u32[]{:S(2)}, u32[]{:S(2)}) collective-permute-start(f32[1,128,512]{2,1,0:T(8,128)S(1)} %maximum_multiply_fusion.3), channel_id=1, source_target_pairs={{0,2},{2,4},{4,6},{6,8},{8,10},{10,12},{12,14},{14,16},{16,18},{18... | collective-permute-start | bytes 786440 | tf_op jit(solution)/shard_map/ppermute | solution.py:13
  145.5 14.0 %collective-permute-start.18 = (f32[1,128,512]{2,1,0:T(8,128)S(1)}, f32[1,128,512]{2,1,0:T(8,128)S(1)}, u32[]{:S(2)}, u32[]{:S(2)}) collective-permute-start(f32[1,128,512]{2,1,0:T(8,128)S(1)} %maximum_multiply_fusion.3), channel_id=1, source_target_pairs={{2,0},{4,2},{6,4},{8,6},{10,8},{12,10},{14,12},{16,14},{18,16},{20... | collective-permute-start | bytes 786440 | tf_op jit(solution)/shard_map/ppermute | solution.py:13
  151.0 13.4 %collective-permute-start.19 = (f32[1,128,512]{2,1,0:T(8,128)S(1)}, f32[1,128,512]{2,1,0:T(8,128)S(1)}, u32[]{:S(2)}, u32[]{:S(2)}) collective-permute-start(f32[1,128,512]{2,1,0:T(8,128)S(1)} %maximum_multiply_fusion.3), channel_id=1, source_target_pairs={{4,0},{6,2},{8,4},{10,6},{12,8},{14,10},{16,12},{18,14},{20,16},{2... | collective-permute-start | bytes 786440 | tf_op jit(solution)/shard_map/ppermute | solution.py:13
  167.2 4.4 %copy-start.3 = (f32[128,256]{1,0:T(8,128)S(1)}, f32[128,256]{1,0:T(8,128)}, u32[]{:S(2)}) copy-start(f32[128,256]{1,0:T(8,128)} %get-tuple-element.17) | copy-start | bytes 393220
  167.2 4.4 %copy-start.4 = (f32[128,256]{1,0:T(8,128)S(1)}, f32[128,256]{1,0:T(8,128)}, u32[]{:S(2)}) copy-start(f32[128,256]{1,0:T(8,128)} %get-tuple-element.12) | copy-start | bytes 393220
  167.2 4.4 %copy-start.5 = (f32[128,256]{1,0:T(8,128)S(1)}, f32[128,256]{1,0:T(8,128)}, u32[]{:S(2)}) copy-start(f32[128,256]{1,0:T(8,128)} %get-tuple-element.13) | copy-start | bytes 393220
Sparse Core Ops, SparseCore 0:
  175.4 222.8 all-reduce.1
where the time goes:
time: 409 us; the launch traced here: 407 us
  waiting for transfers between devices  266 us (65%)
  starting transfers between devices  79.5 us (19%)
  matrix products  23.8 us (6%)
  local copies, waits for them, and re-layouts  16.1 us (4%)
  between operations  14.6 us (4%)
  other arithmetic  4.6 us (1%)
    psum x1, waiting for transfers between devices, local(): summed = lax.psum(partial_value, 'space')  222 us
    ppermute x20, starting transfers between devices, shifted(): return lax.ppermute(value, axis, pairs)  79.5 us
    ppermute x20, waiting for transfers between devices, shifted(): return lax.ppermute(value, axis, pairs)  43.8 us
    dot_general x5, matrix products, apply_blocks(): jnp.einsum('rkab,rkbc->rac', matrix, picked, precision=lax.Precision.HIGH...  21.3 us
    gather x5, local copies, waits for them, and re-layouts, apply_blocks(): picked = jnp.take(window, local_index, axis=0)  13.9 us
  transfers between devices with their start and end apart: 21, of which 15 were waited for; matrix products, arithmetic and copies ran while one was open for 0% of the time, Pallas kernels for 0%

commit v1 on v0

v1 whole, which is shorter than its diff:
```python
import functools

import jax
import jax.numpy as jnp
from jax import lax
from jax.experimental import pallas as pl
from jax.experimental.pallas import tpu as pltpu
from jax.sharding import PartitionSpec as P

ORDER = 4
ROW = 4
BAND = 5
B = 128
HALF = B // 2
F32 = jnp.float32
BF16 = jnp.bfloat16

SMEM = pl.BlockSpec(memory_space=pltpu.SMEM)
VMEM = pl.BlockSpec(memory_space=pltpu.VMEM)


def cost(flops, moved):
    return pl.CostEstimate(flops=flops, bytes_accessed=moved, transcendentals=0)


def split(value):
    high = value.astype(BF16)
    return high, (value - high.astype(F32)).astype(BF16)


def product(a_high, a_low, b_high, b_low):
    dot = functools.partial(jnp.dot, preferred_element_type=F32)
    return dot(a_high, b_high) + (dot(a_high, b_low) + dot(a_low, b_high))


def turned(value):
    lane = lax.broadcasted_iota(jnp.int32, value.shape, 1)
    rolled = pltpu.roll(value, HALF, axis=1)
    return jnp.where(lane < HALF, rolled, -rolled)


def quarter_kernel(me, coef, out):
    x = (me[0] // 2) % ROW
    for q in range(ROW):
        columns = slice(q * HALF, (q + 1) * HALF)
        out[lax.rem(q - x + ROW, ROW)] = jnp.concatenate([coef[0, 0, :, columns], coef[1, 0, :, columns]], axis=1)


def band_kernel(me, nbr, pat, margin, step, margin_out, step_out):
    position = me[0] // 2
    for source, out in ((margin, margin_out), (step, step_out)):
        for d in range(BAND):
            total = None
            for k in range(16):
                weight = F32(1.0) if k == 0 else pat[0, k].astype(F32)
                here = jnp.where(nbr[0, k] == position + (d - 2), weight, F32(0.0))
                part = source[0, k] * here
                total = part if total is None else total + part
            out[:, d * B : (d + 1) * B] = total


def assemble(me, mine, g1, g2, g3, other, full):
    x = (me[0] // 2) % ROW
    core = me[0] % 2
    for j, ref in enumerate((mine, g1, g2, g3)):
        q = lax.rem(x - j + ROW, ROW)
        full[q, pl.ds(pl.multiple_of(core * HALF, HALF), HALF), :] = ref[...]
        full[q, pl.ds(pl.multiple_of((1 - core) * HALF, HALF), HALF), :] = other[j]


def margin_kernel(me, quarters, r1, r2, r3, h0, h1, h2, h3, mine, g1, g2, g3, other, low, high, v, full):
    x = (me[0] // 2) % ROW

    def put(place, tile):
        v[pl.ds(pl.multiple_of(place * B, B), B), :] = tile

    put(x + 2, quarters[0])
    for j, ref in enumerate((r1, r2, r3)):
        put(lax.rem(x - j - 1 + ROW, ROW) + 2, ref[...])
    for j, ref in enumerate((h0, h1, h2, h3)):
        q = lax.rem(x - j + ROW, ROW)
        put(jnp.where(q >= 2, q - 2, q + 6), ref[...])
    assemble(me, mine, g1, g2, g3, other, full)
    v_high, v_low = split(v[...])
    for q in range(ROW):
        m_high, m_low = split(full[q])
        rows = slice(q * B, (q + BAND) * B)
        value = v[(q + 2) * B : (q + 3) * B, :] + product(m_high, m_low, v_high[rows], v_low[rows])
        out = low if q < 2 else high
        out[(q % 2) * B : (q % 2 + 1) * B, :] = value


def parts_kernel(me, mine, g1, g2, g3, other, out_high, out_low, full):
    assemble(me, mine, g1, g2, g3, other, full)
    out_high[...], out_low[...] = split(full[...])


def images(m_high, m_low, before, low, high, after, scale):
    value = jnp.concatenate([before[...], low[...], high[...], after[...]], axis=0)
    v_high, v_low = split(value)
    for q in range(ROW):
        rows = slice(q * B, (q + BAND) * B)
        yield q, product(m_high[q], m_low[q], v_high[rows], v_low[rows]) * scale


def apply_kernel(scale, m_high, m_low, before, low, high, after, out_low, out_high):
    for q, value in images(m_high, m_low, before, low, high, after, scale):
        out = out_low if q < 2 else out_high
        out[(q % 2) * B : (q % 2 + 1) * B, :] = value


def last_kernel(scale, me, m_high, m_low, before, low, high, after, y0l, y0h, y1l, y1h, y2l, y2h, out):
    x = (me[0] // 2) % ROW
    for q, value in images(m_high, m_low, before, low, high, after, scale):
        rows = slice((q % 2) * B, (q % 2 + 1) * B)
        y0, y1, y2, y3 = ((y0l, y1l, y2l, low) if q < 2 else (y0h, y1h, y2h, high))
        out[lax.rem(q - x + ROW, ROW)] = (y0[rows, :] - y2[rows, :]) + value + turned(y1[rows, :] - y3[rows, :])


def old_kernel(me, coef, c1, c2, c3, other, out_high, out_low):
    x = (me[0] // 2) % ROW
    core = me[0] % 2
    width = coef.shape[3]
    for j, ref in enumerate((coef, c1, c2, c3)):
        q = lax.rem(x - j + ROW, ROW)
        for part in range(2):
            for place, tile in ((core, ref[part, 0]), (1 - core, other[j, part])):
                rows = pl.ds(pl.multiple_of(place * width, width), width)
                columns = pl.ds(pl.multiple_of((part * ROW + q) * B, B), B)
                out_high[rows, columns], out_low[rows, columns] = split(jnp.transpose(tile))


def project_kernel(me, old_high, old_low, new, out):
    x = (me[0] // 2) % ROW
    tiles = [new[lax.rem(q - x + ROW, ROW)] for q in range(ROW)]
    value = jnp.concatenate(tiles + [turned(t) for t in tiles], axis=0)
    v_high, v_low = split(value)
    out[...] = product(old_high[...], old_low[...], v_high, v_low)


def reduce_kernel(scale, parts, out):
    total = jnp.sum(parts[...].reshape(-1, 2 * ROW * 2, B), axis=0) * scale
    share = out.shape[1]
    for q in range(ROW):
        for part in range(2):
            tile = total[q * share : (q + 1) * share, part * HALF : (part + 1) * HALF]
            out[part, :, q * HALF : (q + 1) * HALF] = tile


def back_kernel(me, mine, b1, b2, b3, out, held):
    x = (me[0] // 2) % ROW
    for j, tile in enumerate((mine[0], b1[...], b2[...], b3[...])):
        held[lax.rem(x - j + ROW, ROW)] = tile
    for q in range(ROW):
        for part in range(2):
            out[part, 0, :, q * HALF : (q + 1) * HALF] = held[q, :, part * HALF : (part + 1) * HALF]


def local(domains, coefficients, margin, step_matrix, neighbours, pattern):
    width = coefficients.shape[3]
    rows = domains // ROW
    me = (lax.axis_index("space") * 2 + lax.axis_index("orb")).astype(jnp.int32).reshape(1)
    struct = jax.ShapeDtypeStruct

    def call(kernel, out_shape, in_specs, args, scratch=(), estimate=None, name=None):
        outs = jax.tree.map(lambda _: VMEM, out_shape)
        return pl.pallas_call(
            kernel,
            out_shape=out_shape,
            in_specs=in_specs,
            out_specs=outs,
            scratch_shapes=list(scratch),
            cost_estimate=estimate,
            name=name,
            compiler_params=pltpu.CompilerParams(vmem_limit_bytes=40 * 2**20),
        )(*args)

    def in_row(value, by):
        pairs = [(r * ROW + x, r * ROW + (x + by) % ROW) for r in range(rows) for x in range(ROW)]
        return lax.ppermute(value, "space", pairs)

    def across(value, by):
        pairs = [
            (r * ROW + x, (r + (1 if x >= 2 else -1)) % rows * ROW + (x + by) % ROW)
            for r in range(rows)
            for x in range(ROW)
        ]
        return lax.ppermute(value, "space", pairs)

    def next_row(value, by):
        pairs = [(i, (i + by * ROW) % domains) for i in range(domains)]
        return lax.ppermute(value, "space", pairs)

    def swap(value):
        return lax.ppermute(value, "orb", [(0, 1), (1, 0)])

    block = struct((2 * B, B), F32)
    tile_bytes = 4 * B * B

    quarters = call(
        quarter_kernel, struct((ROW, B, B), F32), [SMEM, VMEM], (me, coefficients), name="quarters",
        estimate=cost(10**6, 8 * tile_bytes),
    )
    own_row = [in_row(quarters[j], j) for j in range(1, ROW)]
    halo = [across(quarters[j], j) for j in range(ROW)]

    half_block = pl.BlockSpec((1, 16, HALF, B), lambda i, where, nbr, pat: (0, 0, lax.rem(where[0], 2), 0))
    whole = pl.BlockSpec((HALF, BAND * B), lambda i, where, nbr, pat: (0, 0))
    margin_half, step_half = pl.pallas_call(
        band_kernel,
        grid_spec=pltpu.PrefetchScalarGridSpec(
            num_scalar_prefetch=3, grid=(1,), in_specs=[half_block, half_block], out_specs=[whole, whole]
        ),
        out_shape=[struct((HALF, BAND * B), F32)] * 2,
        cost_estimate=cost(10**6, 22 * tile_bytes),
        name="bands",
    )(me, neighbours, pattern, margin, step_matrix)

    def gathered(half):
        others = [in_row(half, j) for j in range(1, ROW)]
        stack = jnp.stack([half] + others)
        return [half] + others + [swap(stack)]

    margin_parts = gathered(margin_half)
    step_parts = gathered(step_half)
    full = pltpu.VMEM((ROW, B, BAND * B), F32)
    apply_flops = 2 * 3 * ROW * B * BAND * B * B

    y0 = call(
        margin_kernel, [block, block], [SMEM] + [VMEM] * 13,
        [me, quarters] + own_row + halo + margin_parts,
        scratch=[pltpu.VMEM((2 * ROW * B, B), F32), full], name="margin",
        estimate=cost(apply_flops, 40 * tile_bytes),
    )
    half_type = struct((ROW, B, BAND * B), BF16)
    step_high, step_low = call(
        parts_kernel, [half_type, half_type], [SMEM] + [VMEM] * 5, [me] + step_parts, scratch=[full],
        name="step_parts", estimate=cost(10**6, 60 * tile_bytes),
    )

    old_row = [in_row(coefficients, j) for j in range(1, ROW)]
    old_stack = jnp.stack([coefficients[:, 0]] + [o[:, 0] for o in old_row])
    old_type = struct((2 * width, 2 * ROW * B), BF16)
    old_high, old_low = call(
        old_kernel, [old_type, old_type], [SMEM] + [VMEM] * 5, [me, coefficients] + old_row + [swap(old_stack)],
        name="old_parts", estimate=cost(10**6, 64 * tile_bytes),
    )

    def surrounded(y):
        return [next_row(y[1], 1), y[0], y[1], next_row(y[0], -1)]

    states = [list(y0)]
    for n in range(1, ORDER):
        y = call(
            functools.partial(apply_kernel, 1.0 / n), [block, block], [VMEM] * 6,
            [step_high, step_low] + surrounded(states[-1]), name="apply",
            estimate=cost(apply_flops, 32 * tile_bytes),
        )
        states.append(list(y))
    new = call(
        functools.partial(last_kernel, 1.0 / ORDER), struct((ROW, B, B), F32), [SMEM] + [VMEM] * 12,
        [me, step_high, step_low] + surrounded(states[3]) + states[0] + states[1] + states[2], name="last",
        estimate=cost(apply_flops, 44 * tile_bytes),
    )
    back = [in_row(new[j], j) for j in range(1, ROW)]
    partial_value = call(
        project_kernel, struct((2 * width, B), F32), [SMEM] + [VMEM] * 3, [me, old_high, old_low, new],
        name="project", estimate=cost(2 * 3 * 2 * width * 2 * ROW * B * B, 44 * tile_bytes),
    )
    parts = lax.all_to_all(partial_value, "space", 0, 0, tiled=True)
    share = 2 * width // domains
    owned = call(
        functools.partial(reduce_kernel, 1.0 / (domains * B)), struct((2, share, width), F32), [VMEM], [parts],
        name="reduce", estimate=cost(10**5, 5 * tile_bytes),
    )
    propagated = call(
        back_kernel, struct((2, 1, B, width), F32), [SMEM] + [VMEM] * 4, [me, new] + back,
        scratch=[pltpu.VMEM((ROW, B, B), F32)], name="back", estimate=cost(10**5, 8 * tile_bytes),
    )
    return propagated, owned


def solution(mesh):
    return jax.shard_map(
        functools.partial(local, mesh.shape["space"]),
        mesh=mesh,
        in_specs=(
            P(None, "space", None, "orb"),
            P("space", None, None, None),
            P("space", None, None, None),
            P("space", None),
            P("space", None),
        ),
        out_specs=(P(None, "space", None, "orb"), P(None, "space", "orb")),
        check_vma=False,
    )
```

time: 409 us -> 130 us (0.32)
  waiting for transfers between devices: 266 us -> 39.6 us
  matrix products: 23.8 us -> 0 us
  local copies, waits for them, and re-layouts: 16.1 us -> 0.05 us
  between operations: 14.6 us -> 0.84 us
  Pallas kernels: 0 us -> 11.3 us
  other arithmetic: 4.6 us -> 0.16 us
    psum x1 -> x0, waiting for transfers between devices: 222 us -> none  [local(): summed = lax.psum(partial_value, 'space')]
    dot_general x9 -> x0, matrix products: 23.8 us -> none  [the longest x5 21.3 us: apply_blocks(): jnp.einsum('rkab,rkbc->rac', matrix, picked, precision=lax.Precision.HIGH...]
    ppermute x20 -> x30, starting transfers between devices: 79.5 us -> 62.8 us  [the longest x15 23.9 us: in_row(): return lax.ppermute(value, 'space', pairs)]
    all_to_all x0 -> x1, starting transfers between devices: none -> 14.9 us  [local(): parts = lax.all_to_all(partial_value, 'space', 0, 0, tiled=True)]
    gather x5 -> x0, local copies, waits for them, and re-layouts: 13.9 us -> none  [apply_blocks(): picked = jnp.take(window, local_index, axis=0)]
    pallas_call x0 -> x12, Pallas kernels: none -> 11.3 us  [the longest x11 8.22 us: call(): pl.pallas_call(kernel, out_shape=out_shape, in_specs=in_specs, out_specs=...]
    ppermute x20 -> x30, waiting for transfers between devices: 43.8 us -> 36.4 us  [the longest x15 20.2 us: in_row(): return lax.ppermute(value, 'space', pairs)]
  transfers between devices with their start and end apart: 21 -> 31, of which waited for: 15 -> 20; matrix products, arithmetic and copies ran while one was open for 0% -> 0% of each run, Pallas kernels for 0% -> 4%
where the time goes in v1:
time: 130 us
  starting transfers between devices  77.7 us (60%)
  waiting for transfers between devices  39.6 us (30%)
  Pallas kernels  11.3 us (9%)
    ppermute x15, starting transfers between devices, in_row(): return lax.ppermute(value, 'space', pairs)  23.9 us
    ppermute x8, starting transfers between devices, next_row(): return lax.ppermute(value, 'space', pairs)  20.5 us
    ppermute x15, waiting for transfers between devices, in_row(): return lax.ppermute(value, 'space', pairs)  20.2 us
    ppermute x4, starting transfers between devices, across(): return lax.ppermute(value, 'space', pairs)  18.2 us
    all_to_all x1, starting transfers between devices, local(): parts = lax.all_to_all(partial_value, 'space', 0, 0, tiled=True)  14.9 us
    ppermute x8, waiting for transfers between devices, next_row(): return lax.ppermute(value, 'space', pairs)  10 us
    pallas_call x11, Pallas kernels, call(): pl.pallas_call(kernel, out_shape=out_shape, in_specs=in_specs, out_specs=...  8.22 us
    ppermute x4, waiting for transfers between devices, across(): return lax.ppermute(value, 'space', pairs)  6.16 us
  transfers between devices with their start and end apart: 31, of which 20 were waited for; matrix products, arithmetic and copies ran while one was open for 0% of the time, Pallas kernels for 4%

profile of v1, /device:TPU:32, one launch (start us, length us, event | category | flops | bytes accessed | tf_op | source)
XLA Modules:
  0.0 129.7 jit_solution(6916193087082129591)
XLA Ops:
  0.6 3.1 %bands.1 = (f32[64,640]{1,0:T(8,128)}, f32[64,640]{1,0:T(8,128)}) custom-call(s32[1]{0:T(128)} %bitcast.me, s32[1,16]{1,0:T(1,128)} %nbr.1, s32[1,16]{1,0:T(1,128)} %pat.1, f32[1,16,128,128]{3,2,1,0:T(8,128)} %margin.2, f32[1,16,128,128]{3,2,1,0:T(8,128)} %step.1), custom_call_target="tpu_custom_call" | custom-call | flops 1000000 | bytes 1441792 | tf_op jit(solution)/shard_map/bands/pallas_call | solution.py:209
  3.7 1.5 %collective-permute-start.11 = (f32[64,640]{1,0:T(8,128)}, f32[64,640]{1,0:T(8,128)S(1)}, u32[]{:S(2)}, u32[]{:S(2)}) collective-permute-start(f32[64,640]{1,0:T(8,128)} %get-tuple-element.19.mine), channel_id=1, source_target_pairs={{0,2},{2,4},{4,6},{6,0},{8,10},{10,12},{12,14},{14,8},{16,18},{18,... | collective-permute-start | bytes 491528 | tf_op jit(solution)/shard_map/ppermute | solution.py:180
  5.2 2.7 %collective-permute-start.12 = (f32[64,640]{1,0:T(8,128)}, f32[64,640]{1,0:T(8,128)S(1)}, u32[]{:S(2)}, u32[]{:S(2)}) collective-permute-start(f32[64,640]{1,0:T(8,128)} %get-tuple-element.19.mine), channel_id=1, source_target_pairs={{0,4},{2,6},{4,0},{6,2},{8,12},{10,14},{12,8},{14,10},{16,20},{18,... | collective-permute-start | bytes 491528 | tf_op jit(solution)/shard_map/ppermute | solution.py:180
  11.2 2.5 %collective-permute-start.2 = (f32[64,640]{1,0:T(8,128)}, f32[64,640]{1,0:T(8,128)S(1)}, u32[]{:S(2)}, u32[]{:S(2)}) collective-permute-start(f32[64,640]{1,0:T(8,128)} %get-tuple-element.16.mine), channel_id=1, source_target_pairs={{0,6},{2,0},{4,2},{6,4},{8,14},{10,8},{12,10},{14,12},{16,22},{18,... | collective-permute-start | bytes 491528 | tf_op jit(solution)/shard_map/ppermute | solution.py:180
  13.8 3.0 %collective-permute-done.12.g2 = f32[64,640]{1,0:T(8,128)S(1)} collective-permute-done((f32[64,640]{1,0:T(8,128)}, f32[64,640]{1,0:T(8,128)S(1)}, u32[]{:S(2)}, u32[]{:S(2)}) %collective-permute-start.12) | collective-permute-done | bytes 163872 | tf_op jit(solution)/shard_map/ppermute | solution.py:180
  17.4 2.2 %collective-permute-start.27 = (f32[2,1,128,256]{3,2,0,1:T(8,128)S(1)}, f32[2,1,128,256]{3,2,0,1:T(8,128)S(1)}, u32[]{:S(2)}, u32[]{:S(2)}) collective-permute-start(f32[2,1,128,256]{3,2,0,1:T(8,128)S(1)} %bitcast.34), channel_id=1, source_target_pairs={{0,4},{2,6},{4,0},{6,2},{8,12},{10,14},{12,8},{14,10},{16,20},{18,... | collective-permute-start | bytes 786440 | tf_op jit(solution)/shard_map/ppermute | solution.py:180
  20.2 2.4 %collective-permute-start.28 = (f32[2,1,128,256]{3,2,0,1:T(8,128)S(1)}, f32[2,1,128,256]{3,2,0,1:T(8,128)S(1)}, u32[]{:S(2)}, u32[]{:S(2)}) collective-permute-start(f32[2,1,128,256]{3,2,0,1:T(8,128)S(1)} %bitcast.35), channel_id=1, source_target_pairs={{0,6},{2,0},{4,2},{6,4},{8,14},{10,8},{12,10},{14,12},{16,22},{18,... | collective-permute-start | bytes 786440 | tf_op jit(solution)/shard_map/ppermute | solution.py:180
  23.8 2.4 %collective-permute-done.2.g3 = f32[64,640]{1,0:T(8,128)S(1)} collective-permute-done((f32[64,640]{1,0:T(8,128)}, f32[64,640]{1,0:T(8,128)S(1)}, u32[]{:S(2)}, u32[]{:S(2)}) %collective-permute-start.2) | collective-permute-done | bytes 163872 | tf_op jit(solution)/shard_map/ppermute | solution.py:180
  26.4 2.0 %collective-permute-done.26 = f32[2,1,128,256]{3,2,0,1:T(8,128)S(1)} collective-permute-done((f32[2,1,128,256]{3,2,0,1:T(8,128)S(1)}, f32[2,1,128,256]{3,2,0,1:T(8,128)S(1)}, u32[]{:S(2)}, u32[]{:S(2)}) %collective-permute-start.26) | collective-permute-done | bytes 262176 | tf_op jit(solution)/shard_map/ppermute | solution.py:180
  28.4 5.5 %collective-permute-done.27 = f32[2,1,128,256]{3,2,0,1:T(8,128)S(1)} collective-permute-done((f32[2,1,128,256]{3,2,0,1:T(8,128)S(1)}, f32[2,1,128,256]{3,2,0,1:T(8,128)S(1)}, u32[]{:S(2)}, u32[]{:S(2)}) %collective-permute-start.27) | collective-permute-done | bytes 262176 | tf_op jit(solution)/shard_map/ppermute | solution.py:180
  34.1 1.9 %collective-permute-start.10 = (f32[128,128]{1,0:T(8,128)S(1)}, f32[128,128]{1,0:T(8,128)S(1)}, u32[]{:S(2)}, u32[]{:S(2)}) collective-permute-start(f32[128,128]{1,0:T(8,128)S(1)} %get-tuple-element.34), channel_id=1, source_target_pairs={{0,254},{2,248},{4,10},{6,12},{8,6},{10,0},{12,18},{14,20},{16,14}... | collective-permute-start | bytes 196616 | tf_op jit(solution)/shard_map/ppermute | solution.py:188
  36.0 3.6 %collective-permute-done.10.h3 = f32[128,128]{1,0:T(8,128)S(1)} collective-permute-done((f32[128,128]{1,0:T(8,128)S(1)}, f32[128,128]{1,0:T(8,128)S(1)}, u32[]{:S(2)}, u32[]{:S(2)}) %collective-permute-start.10) | collective-permute-done | bytes 65568 | tf_op jit(solution)/shard_map/ppermute | solution.py:188
  39.6 2.6 %collective-permute-start.5 = (f32[128,128]{1,0:T(8,128)S(1)}, f32[128,128]{1,0:T(8,128)S(1)}, u32[]{:S(2)}, u32[]{:S(2)}) collective-permute-start(f32[128,128]{1,0:T(8,128)S(1)} %get-tuple-element.35), channel_id=1, source_target_pairs={{0,4},{2,6},{4,0},{6,2},{8,12},{10,14},{12,8},{14,10},{16,20},{18,... | collective-permute-start | bytes 196616 | tf_op jit(solution)/shard_map/ppermute | solution.py:180
  43.5 1.8 %collective-permute-done.5.r2 = f32[128,128]{1,0:T(8,128)S(1)} collective-permute-done((f32[128,128]{1,0:T(8,128)S(1)}, f32[128,128]{1,0:T(8,128)S(1)}, u32[]{:S(2)}, u32[]{:S(2)}) %collective-permute-start.5) | collective-permute-done | bytes 65568 | tf_op jit(solution)/shard_map/ppermute | solution.py:180
  45.4 7.6 %collective-permute-start.8 = (f32[128,128]{1,0:T(8,128)S(1)}, f32[128,128]{1,0:T(8,128)S(1)}, u32[]{:S(2)}, u32[]{:S(2)}) collective-permute-start(f32[128,128]{1,0:T(8,128)S(1)} %get-tuple-element.36), channel_id=1, source_target_pairs={{0,250},{2,252},{4,14},{6,8},{8,2},{10,4},{12,22},{14,16},{16,10},... | collective-permute-start | bytes 196616 | tf_op jit(solution)/shard_map/ppermute | solution.py:188
  54.9 7.4 %collective-permute-start.7 = (f32[128,128]{1,0:T(8,128)S(1)}, f32[128,128]{1,0:T(8,128)S(1)}, u32[]{:S(2)}, u32[]{:S(2)}) collective-permute-start(f32[128,128]{1,0:T(8,128)S(1)} %get-tuple-element.33), channel_id=1, source_target_pairs={{0,248},{2,250},{4,12},{6,14},{8,0},{10,2},{12,20},{14,22},{16,8},... | collective-permute-start | bytes 196616 | tf_op jit(solution)/shard_map/ppermute | solution.py:188
  62.4 1.9 %collective-permute-done.7.h0 = f32[128,128]{1,0:T(8,128)S(1)} collective-permute-done((f32[128,128]{1,0:T(8,128)S(1)}, f32[128,128]{1,0:T(8,128)S(1)}, u32[]{:S(2)}, u32[]{:S(2)}) %collective-permute-start.7) | collective-permute-done | bytes 65568 | tf_op jit(solution)/shard_map/ppermute | solution.py:188
  65.2 3.6 %collective-permute-start.16 = (f32[256,128]{1,0:T(8,128)S(1)}, f32[256,128]{1,0:T(8,128)S(1)}, u32[]{:S(2)}, u32[]{:S(2)}) collective-permute-start(f32[256,128]{1,0:T(8,128)S(1)} %get-tuple-element.21.low.y0l), channel_id=1, source_target_pairs={{0,248},{2,250},{4,252},{6,254},{8,0},{10,2},{12,4},{14,6},{16,8},... | collective-permute-start | bytes 393224 | tf_op jit(solution)/shard_map/ppermute | solution.py:192
  69.2 2.4 %collective-permute-done.15.before = f32[256,128]{1,0:T(8,128)S(1)} collective-permute-done((f32[256,128]{1,0:T(8,128)S(1)}, f32[256,128]{1,0:T(8,128)S(1)}, u32[]{:S(2)}, u32[]{:S(2)}) %collective-permute-start.15) | collective-permute-done | bytes 131104 | tf_op jit(solution)/shard_map/ppermute | solution.py:192
  72.4 5.4 %collective-permute-start.18 = (f32[256,128]{1,0:T(8,128)S(1)}, f32[256,128]{1,0:T(8,128)S(1)}, u32[]{:S(2)}, u32[]{:S(2)}) collective-permute-start(f32[256,128]{1,0:T(8,128)S(1)} %get-tuple-element.23.low.y1l), channel_id=1, source_target_pairs={{0,248},{2,250},{4,252},{6,254},{8,0},{10,2},{12,4},{14,6},{16,8},... | collective-permute-start | bytes 393224 | tf_op jit(solution)/shard_map/ppermute | solution.py:192
  77.8 2.9 %collective-permute-done.17.before = f32[256,128]{1,0:T(8,128)S(1)} collective-permute-done((f32[256,128]{1,0:T(8,128)S(1)}, f32[256,128]{1,0:T(8,128)S(1)}, u32[]{:S(2)}, u32[]{:S(2)}) %collective-permute-start.17) | collective-permute-done | bytes 131104 | tf_op jit(solution)/shard_map/ppermute | solution.py:192
  81.5 5.4 %collective-permute-start.20 = (f32[256,128]{1,0:T(8,128)S(1)}, f32[256,128]{1,0:T(8,128)S(1)}, u32[]{:S(2)}, u32[]{:S(2)}) collective-permute-start(f32[256,128]{1,0:T(8,128)S(1)} %get-tuple-element.25.low.y2l), channel_id=1, source_target_pairs={{0,248},{2,250},{4,252},{6,254},{8,0},{10,2},{12,4},{14,6},{16,8},... | collective-permute-start | bytes 393224 | tf_op jit(solution)/shard_map/ppermute | solution.py:192
  86.9 2.9 %collective-permute-done.19.before = f32[256,128]{1,0:T(8,128)S(1)} collective-permute-done((f32[256,128]{1,0:T(8,128)S(1)}, f32[256,128]{1,0:T(8,128)S(1)}, u32[]{:S(2)}, u32[]{:S(2)}) %collective-permute-start.19) | collective-permute-done | bytes 131104 | tf_op jit(solution)/shard_map/ppermute | solution.py:192
  90.5 5.7 %collective-permute-start.22 = (f32[256,128]{1,0:T(8,128)S(1)}, f32[256,128]{1,0:T(8,128)S(1)}, u32[]{:S(2)}, u32[]{:S(2)}) collective-permute-start(f32[256,128]{1,0:T(8,128)S(1)} %get-tuple-element.27.low), channel_id=1, source_target_pairs={{0,248},{2,250},{4,252},{6,254},{8,0},{10,2},{12,4},{14,6},{16,8},... | collective-permute-start | bytes 393224 | tf_op jit(solution)/shard_map/ppermute | solution.py:192
  97.0 1.9 %collective-permute-done.21.before = f32[256,128]{1,0:T(8,128)S(1)} collective-permute-done((f32[256,128]{1,0:T(8,128)S(1)}, f32[256,128]{1,0:T(8,128)S(1)}, u32[]{:S(2)}, u32[]{:S(2)}) %collective-permute-start.21) | collective-permute-done | bytes 131104 | tf_op jit(solution)/shard_map/ppermute | solution.py:192
  99.6 1.8 %project.1 = f32[512,128]{1,0:T(8,128)} custom-call(s32[1]{0:T(128)} %bitcast.me, bf16[512,1024]{1,0:T(8,128)(2,1)S(1)} %get-tuple-element.28.old_high, bf16[512,1024]{1,0:T(8,128)(2,1)S(1)} %get-tuple-element.29.old_low, f32[4,128,128]{2,1,0:T(8,128)S(1)} %last.1.mine.new), custom_call_target="tpu_custom_call" | custom-call | flops 402653184 | bytes 2883584 | tf_op jit(solution)/shard_map/project/pallas_call | solution.py:167
  101.4 14.9 %all-to-all-start = ((f32[128,4,128]{2,1,0:T(4,128)}), f32[128,4,128]{2,1,0:T(4,128)S(1)}, u32[]{:S(2)}, u32[]{:S(2)}) async-start(f32[128,4,128]{2,1,0:T(4,128)} %bitcast.24), calls=%async_computation | async-start | bytes 524288 | tf_op jit(solution)/shard_map/all_to_all | solution.py:270
  116.4 1.5 %collective-permute-start.23 = (f32[128,128]{1,0:T(8,128)S(1)}, f32[128,128]{1,0:T(8,128)S(1)}, u32[]{:S(2)}, u32[]{:S(2)}) collective-permute-start(f32[128,128]{1,0:T(8,128)S(1)} %get-tuple-element.32), channel_id=1, source_target_pairs={{0,2},{2,4},{4,6},{6,0},{8,10},{10,12},{12,14},{14,8},{16,18},{18,... | collective-permute-start | bytes 196616 | tf_op jit(solution)/shard_map/ppermute | solution.py:180
  117.9 2.7 %collective-permute-start.24 = (f32[128,128]{1,0:T(8,128)S(1)}, f32[128,128]{1,0:T(8,128)S(1)}, u32[]{:S(2)}, u32[]{:S(2)}) collective-permute-start(f32[128,128]{1,0:T(8,128)S(1)} %get-tuple-element.31), channel_id=1, source_target_pairs={{0,4},{2,6},{4,0},{6,2},{8,12},{10,14},{12,8},{14,10},{16,20},{18,... | collective-permute-start | bytes 196616 | tf_op jit(solution)/shard_map/ppermute | solution.py:180
  120.6 1.5 %collective-permute-start.25 = (f32[128,128]{1,0:T(8,128)S(1)}, f32[128,128]{1,0:T(8,128)S(1)}, u32[]{:S(2)}, u32[]{:S(2)}) collective-permute-start(f32[128,128]{1,0:T(8,128)S(1)} %get-tuple-element.30), channel_id=1, source_target_pairs={{0,6},{2,0},{4,2},{6,4},{8,14},{10,8},{12,10},{14,12},{16,22},{18,... | collective-permute-start | bytes 196616 | tf_op jit(solution)/shard_map/ppermute | solution.py:180
  122.1 1.9 %collective-permute-done.24.b2 = f32[128,128]{1,0:T(8,128)S(1)} collective-permute-done((f32[128,128]{1,0:T(8,128)S(1)}, f32[128,128]{1,0:T(8,128)S(1)}, u32[]{:S(2)}, u32[]{:S(2)}) %collective-permute-start.24) | collective-permute-done | bytes 65568 | tf_op jit(solution)/shard_map/ppermute | solution.py:180
  125.8 3.2 %all-to-all-done = f32[128,4,128]{2,1,0:T(4,128)S(1)} async-done(((f32[128,4,128]{2,1,0:T(4,128)}), f32[128,4,128]{2,1,0:T(4,128)S(1)}, u32[]{:S(2)}, u32[]{:S(2)}) %all-to-all-start) | async-done | bytes 262176 | tf_op jit(solution)/shard_map/all_to_all | solution.py:270
  (53 shorter events, 16.9 us)
Async XLA Ops:
  0.6 16.1 %copy-start = (f32[2,1,128,256]{3,2,1,0:T(8,128)S(1)}, f32[2,1,128,256]{3,2,1,0:T(8,128)}, u32[]{:S(2)}) copy-start(f32[2,1,128,256]{3,2,1,0:T(8,128)} %coef.3) | copy-start | bytes 786436
  3.7 7.5 %collective-permute-start.11 = (f32[64,640]{1,0:T(8,128)}, f32[64,640]{1,0:T(8,128)S(1)}, u32[]{:S(2)}, u32[]{:S(2)}) collective-permute-start(f32[64,640]{1,0:T(8,128)} %get-tuple-element.19.mine), channel_id=1, source_target_pairs={{0,2},{2,4},{4,6},{6,0},{8,10},{10,12},{12,14},{14,8},{16,18},{18,... | collective-permute-start | bytes 491528 | tf_op jit(solution)/shard_map/ppermute | solution.py:180
  5.2 11.6 %collective-permute-start.12 = (f32[64,640]{1,0:T(8,128)}, f32[64,640]{1,0:T(8,128)S(1)}, u32[]{:S(2)}, u32[]{:S(2)}) collective-permute-start(f32[64,640]{1,0:T(8,128)} %get-tuple-element.19.mine), channel_id=1, source_target_pairs={{0,4},{2,6},{4,0},{6,2},{8,12},{10,14},{12,8},{14,10},{16,20},{18,... | collective-permute-start | bytes 491528 | tf_op jit(solution)/shard_map/ppermute | solution.py:180
  7.9 9.5 %collective-permute-start.13 = (f32[64,640]{1,0:T(8,128)}, f32[64,640]{1,0:T(8,128)S(1)}, u32[]{:S(2)}, u32[]{:S(2)}) collective-permute-start(f32[64,640]{1,0:T(8,128)} %get-tuple-element.19.mine), channel_id=1, source_target_pairs={{0,6},{2,0},{4,2},{6,4},{8,14},{10,8},{12,10},{14,12},{16,22},{18,... | collective-permute-start | bytes 491528 | tf_op jit(solution)/shard_map/ppermute | solution.py:180
  9.4 10.8 %collective-permute-start = (f32[64,640]{1,0:T(8,128)}, f32[64,640]{1,0:T(8,128)S(1)}, u32[]{:S(2)}, u32[]{:S(2)}) collective-permute-start(f32[64,640]{1,0:T(8,128)} %get-tuple-element.16.mine), channel_id=1, source_target_pairs={{0,2},{2,4},{4,6},{6,0},{8,10},{10,12},{12,14},{14,8},{16,18},{18,... | collective-permute-start | bytes 491528 | tf_op jit(solution)/shard_map/ppermute | solution.py:180
  10.0 13.9 %collective-permute-start.1 = (f32[64,640]{1,0:T(8,128)}, f32[64,640]{1,0:T(8,128)S(1)}, u32[]{:S(2)}, u32[]{:S(2)}) collective-permute-start(f32[64,640]{1,0:T(8,128)} %get-tuple-element.16.mine), channel_id=1, source_target_pairs={{0,4},{2,6},{4,0},{6,2},{8,12},{10,14},{12,8},{14,10},{16,20},{18,... | collective-permute-start | bytes 491528 | tf_op jit(solution)/shard_map/ppermute | solution.py:180
  11.2 15.0 %collective-permute-start.2 = (f32[64,640]{1,0:T(8,128)}, f32[64,640]{1,0:T(8,128)S(1)}, u32[]{:S(2)}, u32[]{:S(2)}) collective-permute-start(f32[64,640]{1,0:T(8,128)} %get-tuple-element.16.mine), channel_id=1, source_target_pairs={{0,6},{2,0},{4,2},{6,4},{8,14},{10,8},{12,10},{14,12},{16,22},{18,... | collective-permute-start | bytes 491528 | tf_op jit(solution)/shard_map/ppermute | solution.py:180
  16.8 11.7 %collective-permute-start.26 = (f32[2,1,128,256]{3,2,0,1:T(8,128)S(1)}, f32[2,1,128,256]{3,2,0,1:T(8,128)S(1)}, u32[]{:S(2)}, u32[]{:S(2)}) collective-permute-start(f32[2,1,128,256]{3,2,0,1:T(8,128)S(1)} %bitcast.33), channel_id=1, source_target_pairs={{0,2},{2,4},{4,6},{6,0},{8,10},{10,12},{12,14},{14,8},{16,18},{18,... | collective-permute-start | bytes 786440 | tf_op jit(solution)/shard_map/ppermute | solution.py:180
  17.4 16.5 %collective-permute-start.27 = (f32[2,1,128,256]{3,2,0,1:T(8,128)S(1)}, f32[2,1,128,256]{3,2,0,1:T(8,128)S(1)}, u32[]{:S(2)}, u32[]{:S(2)}) collective-permute-start(f32[2,1,128,256]{3,2,0,1:T(8,128)S(1)} %bitcast.34), channel_id=1, source_target_pairs={{0,4},{2,6},{4,0},{6,2},{8,12},{10,14},{12,8},{14,10},{16,20},{18,... | collective-permute-start | bytes 786440 | tf_op jit(solution)/shard_map/ppermute | solution.py:180
  20.2 13.7 %collective-permute-start.28 = (f32[2,1,128,256]{3,2,0,1:T(8,128)S(1)}, f32[2,1,128,256]{3,2,0,1:T(8,128)S(1)}, u32[]{:S(2)}, u32[]{:S(2)}) collective-permute-start(f32[2,1,128,256]{3,2,0,1:T(8,128)S(1)} %bitcast.35), channel_id=1, source_target_pairs={{0,6},{2,0},{4,2},{6,4},{8,14},{10,8},{12,10},{14,12},{16,22},{18,... | collective-permute-start | bytes 786440 | tf_op jit(solution)/shard_map/ppermute | solution.py:180
  23.8 40.4 %collective-permute-start.14 = (f32[4,64,640]{2,1,0:T(8,128)S(1)}, f32[4,64,640]{2,1,0:T(8,128)S(1)}, u32[]{:S(2)}, u32[]{:S(2)}) collective-permute-start(f32[4,64,640]{2,1,0:T(8,128)S(1)} %pad_maximum_fusion.2), channel_id=1, source_target_pairs={{0,1},{1,0},{2,3},{3,2},{4,5},{5,4},{6,7},{7,6},{8,9},{9,8},{10,11... | collective-permute-start | bytes 1966088 | tf_op jit(solution)/shard_map/ppermute | solution.py:195
  26.3 42.5 %collective-permute-start.3 = (f32[4,64,640]{2,1,0:T(8,128)S(1)}, f32[4,64,640]{2,1,0:T(8,128)S(1)}, u32[]{:S(2)}, u32[]{:S(2)}) collective-permute-start(f32[4,64,640]{2,1,0:T(8,128)S(1)} %pad_maximum_fusion.1), channel_id=1, source_target_pairs={{0,1},{1,0},{2,3},{3,2},{4,5},{5,4},{6,7},{7,6},{8,9},{9,8},{10,11... | collective-permute-start | bytes 1966088 | tf_op jit(solution)/shard_map/ppermute | solution.py:195
  34.0 62.3 %collective-permute-start.29 = (f32[4,2,128,256]{3,2,1,0:T(8,128)S(1)}, f32[4,2,128,256]{3,2,1,0:T(8,128)S(1)}, u32[]{:S(2)}, u32[]{:S(2)}) collective-permute-start(f32[4,2,128,256]{3,2,1,0:T(8,128)S(1)} %pad_maximum_fusion), channel_id=1, source_target_pairs={{0,1},{1,0},{2,3},{3,2},{4,5},{5,4},{6,7},{7,6},{8,9},{9,8},{10,11... | collective-permute-start | bytes 3145736 | tf_op jit(solution)/shard_map/ppermute | solution.py:195
  34.1 5.5 %collective-permute-start.10 = (f32[128,128]{1,0:T(8,128)S(1)}, f32[128,128]{1,0:T(8,128)S(1)}, u32[]{:S(2)}, u32[]{:S(2)}) collective-permute-start(f32[128,128]{1,0:T(8,128)S(1)} %get-tuple-element.34), channel_id=1, source_target_pairs={{0,254},{2,248},{4,10},{6,12},{8,6},{10,0},{12,18},{14,20},{16,14}... | collective-permute-start | bytes 196616 | tf_op jit(solution)/shard_map/ppermute | solution.py:188
  36.0 6.2 %collective-permute-start.4 = (f32[128,128]{1,0:T(8,128)S(1)}, f32[128,128]{1,0:T(8,128)S(1)}, u32[]{:S(2)}, u32[]{:S(2)}) collective-permute-start(f32[128,128]{1,0:T(8,128)S(1)} %get-tuple-element.36), channel_id=1, source_target_pairs={{0,2},{2,4},{4,6},{6,0},{8,10},{10,12},{12,14},{14,8},{16,18},{18,... | collective-permute-start | bytes 196616 | tf_op jit(solution)/shard_map/ppermute | solution.py:180
  39.6 5.8 %collective-permute-start.5 = (f32[128,128]{1,0:T(8,128)S(1)}, f32[128,128]{1,0:T(8,128)S(1)}, u32[]{:S(2)}, u32[]{:S(2)}) collective-permute-start(f32[128,128]{1,0:T(8,128)S(1)} %get-tuple-element.35), channel_id=1, source_target_pairs={{0,4},{2,6},{4,0},{6,2},{8,12},{10,14},{12,8},{14,10},{16,20},{18,... | collective-permute-start | bytes 196616 | tf_op jit(solution)/shard_map/ppermute | solution.py:180
  42.2 10.8 %collective-permute-start.6 = (f32[128,128]{1,0:T(8,128)S(1)}, f32[128,128]{1,0:T(8,128)S(1)}, u32[]{:S(2)}, u32[]{:S(2)}) collective-permute-start(f32[128,128]{1,0:T(8,128)S(1)} %get-tuple-element.34), channel_id=1, source_target_pairs={{0,6},{2,0},{4,2},{6,4},{8,14},{10,8},{12,10},{14,12},{16,22},{18,... | collective-permute-start | bytes 196616 | tf_op jit(solution)/shard_map/ppermute | solution.py:180
  45.4 9.6 %collective-permute-start.8 = (f32[128,128]{1,0:T(8,128)S(1)}, f32[128,128]{1,0:T(8,128)S(1)}, u32[]{:S(2)}, u32[]{:S(2)}) collective-permute-start(f32[128,128]{1,0:T(8,128)S(1)} %get-tuple-element.36), channel_id=1, source_target_pairs={{0,250},{2,252},{4,14},{6,8},{8,2},{10,4},{12,22},{14,16},{16,10},... | collective-permute-start | bytes 196616 | tf_op jit(solution)/shard_map/ppermute | solution.py:188
  53.0 9.4 %collective-permute-start.9 = (f32[128,128]{1,0:T(8,128)S(1)}, f32[128,128]{1,0:T(8,128)S(1)}, u32[]{:S(2)}, u32[]{:S(2)}) collective-permute-start(f32[128,128]{1,0:T(8,128)S(1)} %get-tuple-element.35), channel_id=1, source_target_pairs={{0,252},{2,254},{4,8},{6,10},{8,4},{10,6},{12,16},{14,18},{16,12},... | collective-permute-start | bytes 196616 | tf_op jit(solution)/shard_map/ppermute | solution.py:188
  54.9 9.4 %collective-permute-start.7 = (f32[128,128]{1,0:T(8,128)S(1)}, f32[128,128]{1,0:T(8,128)S(1)}, u32[]{:S(2)}, u32[]{:S(2)}) collective-permute-start(f32[128,128]{1,0:T(8,128)S(1)} %get-tuple-element.33), channel_id=1, source_target_pairs={{0,248},{2,250},{4,12},{6,14},{8,0},{10,2},{12,20},{14,22},{16,8},... | collective-permute-start | bytes 196616 | tf_op jit(solution)/shard_map/ppermute | solution.py:188
  65.1 6.5 %collective-permute-start.15 = (f32[256,128]{1,0:T(8,128)S(1)}, f32[256,128]{1,0:T(8,128)S(1)}, u32[]{:S(2)}, u32[]{:S(2)}) collective-permute-start(f32[256,128]{1,0:T(8,128)S(1)} %get-tuple-element.20.high.y0h), channel_id=1, source_target_pairs={{0,8},{2,10},{4,12},{6,14},{8,16},{10,18},{12,20},{14,22},{16,24},... | collective-permute-start | bytes 393224 | tf_op jit(solution)/shard_map/ppermute | solution.py:192
  65.2 6.4 %collective-permute-start.16 = (f32[256,128]{1,0:T(8,128)S(1)}, f32[256,128]{1,0:T(8,128)S(1)}, u32[]{:S(2)}, u32[]{:S(2)}) collective-permute-start(f32[256,128]{1,0:T(8,128)S(1)} %get-tuple-element.21.low.y0l), channel_id=1, source_target_pairs={{0,248},{2,250},{4,252},{6,254},{8,0},{10,2},{12,4},{14,6},{16,8},... | collective-permute-start | bytes 393224 | tf_op jit(solution)/shard_map/ppermute | solution.py:192
  72.3 8.4 %collective-permute-start.17 = (f32[256,128]{1,0:T(8,128)S(1)}, f32[256,128]{1,0:T(8,128)S(1)}, u32[]{:S(2)}, u32[]{:S(2)}) collective-permute-start(f32[256,128]{1,0:T(8,128)S(1)} %get-tuple-element.22.high.y1h), channel_id=1, source_target_pairs={{0,8},{2,10},{4,12},{6,14},{8,16},{10,18},{12,20},{14,22},{16,24},... | collective-permute-start | bytes 393224 | tf_op jit(solution)/shard_map/ppermute | solution.py:192
  72.4 8.3 %collective-permute-start.18 = (f32[256,128]{1,0:T(8,128)S(1)}, f32[256,128]{1,0:T(8,128)S(1)}, u32[]{:S(2)}, u32[]{:S(2)}) collective-permute-start(f32[256,128]{1,0:T(8,128)S(1)} %get-tuple-element.23.low.y1l), channel_id=1, source_target_pairs={{0,248},{2,250},{4,252},{6,254},{8,0},{10,2},{12,4},{14,6},{16,8},... | collective-permute-start | bytes 393224 | tf_op jit(solution)/shard_map/ppermute | solution.py:192
  81.4 8.4 %collective-permute-start.19 = (f32[256,128]{1,0:T(8,128)S(1)}, f32[256,128]{1,0:T(8,128)S(1)}, u32[]{:S(2)}, u32[]{:S(2)}) collective-permute-start(f32[256,128]{1,0:T(8,128)S(1)} %get-tuple-element.24.high.y2h), channel_id=1, source_target_pairs={{0,8},{2,10},{4,12},{6,14},{8,16},{10,18},{12,20},{14,22},{16,24},... | collective-permute-start | bytes 393224 | tf_op jit(solution)/shard_map/ppermute | solution.py:192
  81.5 8.3 %collective-permute-start.20 = (f32[256,128]{1,0:T(8,128)S(1)}, f32[256,128]{1,0:T(8,128)S(1)}, u32[]{:S(2)}, u32[]{:S(2)}) collective-permute-start(f32[256,128]{1,0:T(8,128)S(1)} %get-tuple-element.25.low.y2l), channel_id=1, source_target_pairs={{0,248},{2,250},{4,252},{6,254},{8,0},{10,2},{12,4},{14,6},{16,8},... | collective-permute-start | bytes 393224 | tf_op jit(solution)/shard_map/ppermute | solution.py:192
  90.4 8.5 %collective-permute-start.21 = (f32[256,128]{1,0:T(8,128)S(1)}, f32[256,128]{1,0:T(8,128)S(1)}, u32[]{:S(2)}, u32[]{:S(2)}) collective-permute-start(f32[256,128]{1,0:T(8,128)S(1)} %get-tuple-element.26.high), channel_id=1, source_target_pairs={{0,8},{2,10},{4,12},{6,14},{8,16},{10,18},{12,20},{14,22},{16,24},... | collective-permute-start | bytes 393224 | tf_op jit(solution)/shard_map/ppermute | solution.py:192
  90.5 8.4 %collective-permute-start.22 = (f32[256,128]{1,0:T(8,128)S(1)}, f32[256,128]{1,0:T(8,128)S(1)}, u32[]{:S(2)}, u32[]{:S(2)}) collective-permute-start(f32[256,128]{1,0:T(8,128)S(1)} %get-tuple-element.27.low), channel_id=1, source_target_pairs={{0,248},{2,250},{4,252},{6,254},{8,0},{10,2},{12,4},{14,6},{16,8},... | collective-permute-start | bytes 393224 | tf_op jit(solution)/shard_map/ppermute | solution.py:192
  101.4 27.6 %all-to-all-start = ((f32[128,4,128]{2,1,0:T(4,128)}), f32[128,4,128]{2,1,0:T(4,128)S(1)}, u32[]{:S(2)}, u32[]{:S(2)}) async-start(f32[128,4,128]{2,1,0:T(4,128)} %bitcast.24), calls=%async_computation | async-start | bytes 524288 | tf_op jit(solution)/shard_map/all_to_all | solution.py:270
  116.4 5.7 %collective-permute-start.23 = (f32[128,128]{1,0:T(8,128)S(1)}, f32[128,128]{1,0:T(8,128)S(1)}, u32[]{:S(2)}, u32[]{:S(2)}) collective-permute-start(f32[128,128]{1,0:T(8,128)S(1)} %get-tuple-element.32), channel_id=1, source_target_pairs={{0,2},{2,4},{4,6},{6,0},{8,10},{10,12},{12,14},{14,8},{16,18},{18,... | collective-permute-start | bytes 196616 | tf_op jit(solution)/shard_map/ppermute | solution.py:180
  117.9 6.1 %collective-permute-start.24 = (f32[128,128]{1,0:T(8,128)S(1)}, f32[128,128]{1,0:T(8,128)S(1)}, u32[]{:S(2)}, u32[]{:S(2)}) collective-permute-start(f32[128,128]{1,0:T(8,128)S(1)} %get-tuple-element.31), channel_id=1, source_target_pairs={{0,4},{2,6},{4,0},{6,2},{8,12},{10,14},{12,8},{14,10},{16,20},{18,... | collective-permute-start | bytes 196616 | tf_op jit(solution)/shard_map/ppermute | solution.py:180
  120.6 4.4 %collective-permute-start.25 = (f32[128,128]{1,0:T(8,128)S(1)}, f32[128,128]{1,0:T(8,128)S(1)}, u32[]{:S(2)}, u32[]{:S(2)}) collective-permute-start(f32[128,128]{1,0:T(8,128)S(1)} %get-tuple-element.30), channel_id=1, source_target_pairs={{0,6},{2,0},{4,2},{6,4},{8,14},{10,8},{12,10},{14,12},{16,22},{18,... | collective-permute-start | bytes 196616 | tf_op jit(solution)/shard_map/ppermute | solution.py:180
  (2 other events, 9.5 us)

commit v2 on v0

v2 whole, which is shorter than its diff:
```python
import functools

import jax
import jax.numpy as jnp
from jax import lax
from jax.experimental import pallas as pl
from jax.experimental.pallas import tpu as pltpu
from jax.sharding import Mesh, PartitionSpec as P

ORDER = 4
ROW = 4
BAND = 5
B = 128
HALF = B // 2
F32 = jnp.float32
BF16 = jnp.bfloat16

SMEM = pl.BlockSpec(memory_space=pltpu.SMEM)
VMEM = pl.BlockSpec(memory_space=pltpu.VMEM)


def cost(flops, moved):
    return pl.CostEstimate(flops=flops, bytes_accessed=moved, transcendentals=0)


def split(value):
    high = value.astype(BF16)
    return high, (value - high.astype(F32)).astype(BF16)


def product(a_high, a_low, b_high, b_low):
    dot = functools.partial(jnp.dot, preferred_element_type=F32)
    return dot(a_high, b_high) + (dot(a_high, b_low) + dot(a_low, b_high))


def turned(value):
    lane = lax.broadcasted_iota(jnp.int32, value.shape, 1)
    rolled = pltpu.roll(value, HALF, axis=1)
    return jnp.where(lane < HALF, rolled, -rolled)


def member(me):
    return lax.rem(lax.div(me[0], 2), ROW), lax.rem(me[0], 2)


def turn_to(q, x):
    return lax.rem(q - x + ROW, ROW)


def pack_kernel(me, nbr, pat, coef, margin, step, out):
    position = lax.div(me[0], 2)
    for i in range(ROW):
        columns = slice(i * HALF, (i + 1) * HALF)
        tile = jnp.concatenate([coef[0, 0, :, columns], coef[1, 0, :, columns]], axis=1)
        for q in range(ROW):
            out[q, i * B : (i + 1) * B, :] = tile
    for i, source in enumerate((margin, step)):
        for d in range(BAND):
            total = None
            for k in range(16):
                weight = F32(1.0) if k == 0 else pat[0, k].astype(F32)
                here = jnp.where(nbr[0, k] == position + (d - 2), weight, F32(0.0))
                part = source[0, k] * here
                total = part if total is None else total + part
            start = ROW * B + (i * BAND + d) * HALF
            for q in range(ROW):
                out[q, start : start + HALF, :] = total


def band_rows(i, q, core, mine, other, put):
    for place, ref in ((core, mine), (1 - core, other)):
        rows = pl.ds(pl.multiple_of(place * HALF, HALF), HALF)
        for d in range(BAND):
            start = ROW * B + (i * BAND + d) * HALF
            put(rows, slice(d * B, (d + 1) * B), ref[q, start : start + HALF, :])


def edge_kernel(me, mine, low, high):
    x, _ = member(me)
    for i, out in enumerate((low, high)):
        for q in range(2):
            out[q * B : (q + 1) * B, :] = mine[2 * i + q, pl.ds(pl.multiple_of(x * B, B), B), :]


def margin_kernel(me, mine, other, before, after, out, full):
    x, core = member(me)
    own = [mine[q, pl.ds(pl.multiple_of(x * B, B), B), :] for q in range(ROW)]
    v_high, v_low = split(jnp.concatenate([before[...]] + own + [after[...]], axis=0))
    for q in range(ROW):

        def put(rows, columns, tile):
            full[q, rows, columns] = tile

        band_rows(0, q, core, mine, other, put)
    for q in range(ROW):
        m_high, m_low = split(full[q])
        rows = slice(q * B, (q + BAND) * B)
        out[q * B : (q + 1) * B, :] = own[q] + product(m_high, m_low, v_high[rows], v_low[rows])


def ghost_kernel(me, mine, other, out):
    _, core = member(me)
    for i in range(2):

        def put(rows, columns, tile):
            out[i, rows, columns] = tile

        band_rows(1, i + 2 - 2 * core, core, mine, other, put)


def parts_kernel(me, mine, other, ghost, ghost_other, out_high, out_low):
    _, core = member(me)
    for q in range(ROW):

        def put(rows, columns, tile):
            out_high[q + 2, rows, columns], out_low[q + 2, rows, columns] = split(tile)

        band_rows(1, q, core, mine, other, put)
    for start, ref in ((core * 6, ghost), ((1 - core) * 6, ghost_other)):
        for i in range(2):
            out_high[start + i], out_low[start + i] = split(ref[i])


def two_steps(n, m_high, m_low, before, own, after):
    value = jnp.concatenate([before[...], own[...], after[...]], axis=0)
    v_high, v_low = split(value)
    firsts = []
    for q in range(2 * ROW):
        rows = slice(q * B, (q + BAND) * B)
        firsts.append(product(m_high[q], m_low[q], v_high[rows], v_low[rows]) * F32(1.0 / n))
    v_high, v_low = split(jnp.concatenate(firsts, axis=0))
    for q in range(ROW):
        rows = slice(q * B, (q + BAND) * B)
        second = product(m_high[q + 2], m_low[q + 2], v_high[rows], v_low[rows]) * F32(1.0 / (n + 1))
        yield q, firsts[q + 2], second


def two_kernel(n, m_high, m_low, before, own, after, first, second):
    for q, a, b in two_steps(n, m_high, m_low, before, own, after):
        first[q * B : (q + 1) * B, :] = a
        second[q * B : (q + 1) * B, :] = b


def last_kernel(n, me, m_high, m_low, before, own, after, y0, y1, out):
    x, _ = member(me)
    for q, y3, y4 in two_steps(n, m_high, m_low, before, own, after):
        rows = slice(q * B, (q + 1) * B)
        out[turn_to(q, x)] = (y0[rows, :] - own[rows, :]) + y4 + turned(y1[rows, :] - y3)


def old_kernel(me, mine, other, out_high, out_low):
    _, core = member(me)
    for q in range(ROW):
        for place, ref in ((core, mine), (1 - core, other)):
            for i in range(ROW):
                high, low = split(jnp.transpose(ref[q, i * B : (i + 1) * B, :]))
                rows = pl.ds(pl.multiple_of((place * ROW + i) * HALF, HALF), HALF)
                for part in range(2):
                    columns = slice((part * ROW + q) * B, (part * ROW + q + 1) * B)
                    out_high[rows, columns] = high[part * HALF : (part + 1) * HALF]
                    out_low[rows, columns] = low[part * HALF : (part + 1) * HALF]


def project_kernel(me, old_high, old_low, new, out):
    x, _ = member(me)
    tiles = [new[turn_to(q, x)] for q in range(ROW)]
    v_high, v_low = split(jnp.concatenate(tiles + [turned(t) for t in tiles], axis=0))
    out[...] = product(old_high[...], old_low[...], v_high, v_low)


def reduce_kernel(scale, parts, out):
    share = out.shape[1]
    total = jnp.sum(parts[...].reshape(-1, ROW * share, B), axis=0) * scale
    for q in range(ROW):
        for part in range(2):
            tile = total[q * share : (q + 1) * share, part * HALF : (part + 1) * HALF]
            out[part, :, q * HALF : (q + 1) * HALF] = tile


def back_kernel(me, mine, b1, b2, b3, out, held):
    x, _ = member(me)
    for j, tile in enumerate((mine[0], b1[...], b2[...], b3[...])):
        held[turn_to(x, j)] = tile
    for q in range(ROW):
        for part in range(2):
            out[part, 0, :, q * HALF : (q + 1) * HALF] = held[q, :, part * HALF : (part + 1) * HALF]


def local(rows, coefficients, margin, step_matrix, neighbours, pattern):
    width = coefficients.shape[3]
    domains = rows * ROW
    me = lax.axis_index(("row", "x", "orb")).astype(jnp.int32).reshape(1)
    struct = jax.ShapeDtypeStruct
    tile_bytes = 4 * B * B
    step_flops = 2 * 3 * B * BAND * B * B

    def call(kernel, out_shape, args, flops, moved, name, scratch=(), scalars=1):
        return pl.pallas_call(
            kernel,
            out_shape=out_shape,
            in_specs=[SMEM] * scalars + [VMEM] * (len(args) - scalars),
            out_specs=jax.tree.map(lambda _: VMEM, out_shape),
            scratch_shapes=list(scratch),
            cost_estimate=cost(flops, moved * tile_bytes),
            name=name,
            compiler_params=pltpu.CompilerParams(vmem_limit_bytes=40 * 2**20),
        )(*args)

    def in_row(value, by):
        return lax.ppermute(value, "x", [(x, (x + by) % ROW) for x in range(ROW)])

    def next_row(value, by):
        return lax.ppermute(value, "row", [(r, (r + by) % rows) for r in range(rows)])

    def swap(value):
        return lax.ppermute(value, "orb", [(0, 1), (1, 0)])

    def apart(value):
        pairs = []
        for r in range(rows):
            for x in range(ROW):
                for core, by in ((0, 1), (1, -1)):
                    pairs.append(((r * ROW + x) * 2 + core, ((r + by) % rows * ROW + x) * 2 + core))
        return lax.ppermute(value, ("row", "x", "orb"), pairs)

    half_block = pl.BlockSpec((1, 16, HALF, B), lambda i, where, nbr, pat: (0, 0, lax.rem(where[0], 2), 0))
    packed_rows = ROW * B + 2 * BAND * HALF
    packed = pl.pallas_call(
        pack_kernel,
        grid_spec=pltpu.PrefetchScalarGridSpec(
            num_scalar_prefetch=3,
            grid=(1,),
            in_specs=[pl.BlockSpec(coefficients.shape, lambda i, *_: (0, 0, 0, 0)), half_block, half_block],
            out_specs=pl.BlockSpec((ROW, packed_rows, B), lambda i, *_: (0, 0, 0)),
        ),
        out_shape=struct((ROW, packed_rows, B), F32),
        cost_estimate=cost(10**6, 44 * tile_bytes),
        name="pack",
    )(me, neighbours, pattern, coefficients, margin, step_matrix)
    mine = lax.all_to_all(packed, "x", 0, 0, tiled=True)
    edge = struct((2 * B, B), F32)
    low, high = call(edge_kernel, [edge, edge], [me, mine], 10**5, 8, "edges")
    high, low, held = lax.optimization_barrier((high, low, mine))
    before = next_row(high, 1)
    after = next_row(low, -1)
    other = swap(held)
    before, kept = lax.optimization_barrier((before, mine))
    state = struct((ROW * B, B), F32)
    y0 = call(
        margin_kernel, state, [me, mine, other, before, after], 10**11, 60, "margin",
        scratch=[pltpu.VMEM((ROW, B, BAND * B), F32)],
    )
    ghost = apart(call(ghost_kernel, struct((2, B, BAND * B), F32), [me, kept, other], 10**5, 20, "ghost"))
    ghost, y0 = lax.optimization_barrier((ghost, y0))
    parts_type = struct((2 * ROW, B, BAND * B), BF16)
    step = call(
        parts_kernel, [parts_type, parts_type], [me, mine, other, ghost, swap(ghost)], 10**6, 80, "step_parts"
    )
    step = list(step)

    old_type = struct((2 * width, 2 * ROW * B), BF16)
    old_high, old_low = call(old_kernel, [old_type, old_type], [me, mine, other], 10**6, 64, "old_parts")

    y1, y2 = call(
        functools.partial(two_kernel, 1), [state, state], step + [next_row(y0, 1), y0, next_row(y0, -1)],
        3 * ROW * step_flops, 64, "two", scalars=0,
    )
    before, old_high = lax.optimization_barrier((next_row(y2, 1), old_high))
    new = call(
        functools.partial(last_kernel, 3), struct((ROW, B, B), F32),
        [me] + step + [before, y2, next_row(y2, -1), y0, y1],
        3 * ROW * step_flops, 72, "last",
    )
    back = [in_row(new[j], j) for j in range(1, ROW)]
    partial_value = call(
        project_kernel, struct((2 * width, B), F32), [me, old_high, old_low, new],
        2 * 3 * 2 * width * 2 * ROW * B * B, 44, "project",
    )
    partial_value, *back = lax.optimization_barrier((partial_value, *back))
    parts = lax.all_to_all(partial_value, ("row", "x"), 0, 0, tiled=True)
    share = 2 * width // domains
    owned = call(
        functools.partial(reduce_kernel, 1.0 / (domains * B)), struct((2, share, width), F32), [parts],
        10**5, 5, "reduce", scalars=0,
    )
    propagated = call(
        back_kernel, struct((2, 1, B, width), F32), [me, new] + back, 10**5, 8, "back",
        scratch=[pltpu.VMEM((ROW, B, B), F32)],
    )
    return propagated, owned


def solution(mesh):
    rows = mesh.shape["space"] // ROW
    grouped = Mesh(mesh.devices.reshape(rows, ROW, mesh.shape["orb"]), ("row", "x", "orb"))
    space = ("row", "x")
    return jax.shard_map(
        functools.partial(local, rows),
        mesh=grouped,
        in_specs=(
            P(None, space, None, "orb"),
            P(space, None, None, None),
            P(space, None, None, None),
            P(space, None),
            P(space, None),
        ),
        out_specs=(P(None, space, None, "orb"), P(None, space, "orb")),
        check_vma=False,
    )
```

time: 409 us -> 121 us (0.30)
  waiting for transfers between devices: 266 us -> 44.8 us
  starting transfers between devices: 79.5 us -> 29.4 us
  blocking collectives: 2.18 us -> 33.4 us
  matrix products: 23.8 us -> 0 us
  local copies, waits for them, and re-layouts: 16.1 us -> 0.02 us
  between operations: 14.6 us -> 0.72 us
  Pallas kernels: 0 us -> 12.5 us
  other arithmetic: 4.6 us -> 0 us
    psum x1 -> x0, waiting for transfers between devices: 222 us -> none  [local(): summed = lax.psum(partial_value, 'space')]
    ppermute x20 -> x12, starting transfers between devices: 79.5 us -> 16.2 us  [the longest x6 11.4 us: next_row(): lax.ppermute(value, 'row', [(r, (r + by) % rows) for r in range(rows)])]
    all_to_all x0 -> x1, blocking collectives: none -> 33.4 us  [local(): mine = lax.all_to_all(packed, 'x', 0, 0, tiled=True)]
    dot_general x9 -> x0, matrix products: 23.8 us -> none  [the longest x5 21.3 us: apply_blocks(): jnp.einsum('rkab,rkbc->rac', matrix, picked, precision=lax.Precision.HIGH...]
    gather x5 -> x0, local copies, waits for them, and re-layouts: 13.9 us -> none  [apply_blocks(): picked = jnp.take(window, local_index, axis=0)]
    all_to_all x0 -> x1, starting transfers between devices: none -> 13.2 us  [local(): parts = lax.all_to_all(partial_value, ('row', 'x'), 0, 0, tiled=True)]
    pallas_call x0 -> x11, Pallas kernels: none -> 12.5 us  [the longest x10 8.69 us: call(): pl.pallas_call(kernel, out_shape=out_shape, in_specs=[SMEM] * scalars + [...]
    all_to_all x0 -> x1, waiting for transfers between devices: none -> 11.8 us  [local(): parts = lax.all_to_all(partial_value, ('row', 'x'), 0, 0, tiled=True)]
  transfers between devices with their start and end apart: 21 -> 13, of which waited for: 15 -> 8; matrix products, arithmetic and copies ran while one was open for 0% -> 0% of each run, Pallas kernels for 0% -> 4%
where the time goes in v2:
time: 121 us
  waiting for transfers between devices  44.8 us (37%)
  blocking collectives  33.4 us (28%)
  starting transfers between devices  29.4 us (24%)
  Pallas kernels  12.5 us (10%)
    all_to_all x1, blocking collectives, local(): mine = lax.all_to_all(packed, 'x', 0, 0, tiled=True)  33.4 us
    ppermute x6, waiting for transfers between devices, next_row(): lax.ppermute(value, 'row', [(r, (r + by) % rows) for r in range(rows)])  16.7 us
    all_to_all x1, starting transfers between devices, local(): parts = lax.all_to_all(partial_value, ('row', 'x'), 0, 0, tiled=True)  13.2 us
    ppermute x1, waiting for transfers between devices, apart(): return lax.ppermute(value, ('row', 'x', 'orb'), pairs)  12.5 us
    all_to_all x1, waiting for transfers between devices, local(): parts = lax.all_to_all(partial_value, ('row', 'x'), 0, 0, tiled=True)  11.8 us
    ppermute x6, starting transfers between devices, next_row(): lax.ppermute(value, 'row', [(r, (r + by) % rows) for r in range(rows)])  11.4 us
    pallas_call x10, Pallas kernels, call(): pl.pallas_call(kernel, out_shape=out_shape, in_specs=[SMEM] * scalars + [...  8.69 us
    pallas_call x1, Pallas kernels, local(): pl.pallas_call(pack_kernel, grid_spec=pltpu.PrefetchScalarGridSpec(num_sc...  3.85 us
  transfers between devices with their start and end apart: 13, of which 8 were waited for; matrix products, arithmetic and copies ran while one was open for 0% of the time, Pallas kernels for 4%

profile of v2, /device:TPU:32, one launch (start us, length us, event | category | flops | bytes accessed | tf_op | source)
XLA Modules:
  0.0 120.9 jit_solution(9753476590110326078)
XLA Ops:
  0.6 3.9 %pack.1 = f32[4,1152,128]{2,1,0:T(8,128)} custom-call(s32[1]{0:T(128)} %bitcast.me, s32[1,16]{1,0:T(1,128)} %nbr.1, s32[1,16]{1,0:T(1,128)} %pat.1, f32[2,1,128,256]{3,2,1,0:T(8,128)} %coef.1, f32[1,16,128,128]{3,2,1,0:T(8,128)} %margin.2, f32[1,16,128,128]{3,2,1,0:T(8,128)} %step.1), custom_call_target="tpu_custom_call" | custom-call | flops 1000000 | bytes 2883584 | tf_op jit(solution)/shard_map/pack/pallas_call | solution.py:228
  4.5 33.4 %all_to_all.16.mine = f32[4,1152,128]{2,1,0:T(8,128)S(1)} all-to-all(f32[4,1152,128]{2,1,0:T(8,128)} %pack.1), channel_id=1, replica_groups=mesh['row'=32,'x'=4,'orb'=2] {'x'}, dimensions={0} | all-to-all | bytes 4718592 | tf_op jit(solution)/shard_map/all_to_all | solution.py:240
  37.9 0.1 collective-permute-start
  38.0 2.0 %collective-permute-start.1 = (f32[256,128]{1,0:T(8,128)S(1)}, f32[256,128]{1,0:T(8,128)S(1)}, u32[]{:S(2)}, u32[]{:S(2)}) collective-permute-start(f32[256,128]{1,0:T(8,128)S(1)} %get-tuple-element.26), channel_id=1, source_target_pairs={{0,8},{8,16},{16,24},{24,32},{32,40},{40,48},{48,56},{56,64},{64,7... | collective-permute-start | bytes 393224 | tf_op jit(solution)/shard_map/ppermute | solution.py:213
  40.0 0.1 collective-permute-start.3
  40.1 3.8 %collective-permute-done.1.before = f32[256,128]{1,0:T(8,128)S(1)} collective-permute-done((f32[256,128]{1,0:T(8,128)S(1)}, f32[256,128]{1,0:T(8,128)S(1)}, u32[]{:S(2)}, u32[]{:S(2)}) %collective-permute-start.1) | collective-permute-done | bytes 131104 | tf_op jit(solution)/shard_map/ppermute | solution.py:213
  44.0 0.0 collective-permute-done.other
  44.0 2.0 %collective-permute-start.2 = (f32[2,128,640]{2,1,0:T(8,128)S(1)}, f32[2,128,640]{2,1,0:T(8,128)S(1)}, u32[]{:S(2)}, u32[]{:S(2)}) collective-permute-start(f32[2,128,640]{2,1,0:T(8,128)S(1)} %ghost.1), channel_id=1, source_target_pairs={{0,8},{1,249},{2,10},{3,251},{4,12},{5,253},{6,14},{7,255},{8,16},... | collective-permute-start | bytes 1966088 | tf_op jit(solution)/shard_map/ppermute | solution.py:224
  46.0 0.0 collective-permute-done.3.after
  46.0 0.8 margin.3.own.y0
  46.8 12.5 %collective-permute-done.2.ghost = f32[2,128,640]{2,1,0:T(8,128)S(1)} collective-permute-done((f32[2,128,640]{2,1,0:T(8,128)S(1)}, f32[2,128,640]{2,1,0:T(8,128)S(1)}, u32[]{:S(2)}, u32[]{:S(2)}) %collective-permute-start.2) | collective-permute-done | bytes 655392 | tf_op jit(solution)/shard_map/ppermute | solution.py:224
  59.3 0.0 collective-permute-start.4
  59.3 5.3 %collective-permute-start.6 = (f32[512,128]{1,0:T(8,128)S(1)}, f32[512,128]{1,0:T(8,128)S(1)}, u32[]{:S(2)}, u32[]{:S(2)}) collective-permute-start(f32[512,128]{1,0:T(8,128)S(1)} %margin.3.own.y0), channel_id=1, source_target_pairs={{0,248},{8,0},{16,8},{24,16},{32,24},{40,32},{48,40},{56,48},{64,5... | collective-permute-start | bytes 786440 | tf_op jit(solution)/shard_map/ppermute | solution.py:213
  64.7 0.0 collective-permute-start.5
  64.7 0.4 step_parts.1
  65.1 5.8 %collective-permute-done.6.after = f32[512,128]{1,0:T(8,128)S(1)} collective-permute-done((f32[512,128]{1,0:T(8,128)S(1)}, f32[512,128]{1,0:T(8,128)S(1)}, u32[]{:S(2)}, u32[]{:S(2)}) %collective-permute-start.6) | collective-permute-done | bytes 262176 | tf_op jit(solution)/shard_map/ppermute | solution.py:213
  70.9 2.2 %collective-permute-done.5.before = f32[512,128]{1,0:T(8,128)S(1)} collective-permute-done((f32[512,128]{1,0:T(8,128)S(1)}, f32[512,128]{1,0:T(8,128)S(1)}, u32[]{:S(2)}, u32[]{:S(2)}) %collective-permute-start.5) | collective-permute-done | bytes 262176 | tf_op jit(solution)/shard_map/ppermute | solution.py:213
  73.1 1.7 %two.1 = (f32[512,128]{1,0:T(8,128)S(1)}, f32[512,128]{1,0:T(8,128)S(1)}) custom-call(bf16[8,128,640]{2,1,0:T(8,128)(2,1)S(1)} %get-tuple-element.31.m_high, bf16[8,128,640]{2,1,0:T(8,128)(2,1)S(1)} %get-tuple-element.32.m_low, f32[512,128]{1,0:T(8,128)S(1)} %collective-permute-done.5.before, f32[512,128]{1,0:T(8,128)S(1)} %margin.3.own.y0, ...), custom_call_target="tpu_custom_call" | custom-call | flops 754974720 | bytes 4194304 | tf_op jit(solution)/shard_map/two/pallas_call | solution.py:198
  74.8 0.4 collective-permute-start.7
  75.2 3.6 %collective-permute-start.8 = (f32[512,128]{1,0:T(8,128)S(1)}, f32[512,128]{1,0:T(8,128)S(1)}, u32[]{:S(2)}, u32[]{:S(2)}) collective-permute-start(f32[512,128]{1,0:T(8,128)S(1)} %get-tuple-element.34.own), channel_id=1, source_target_pairs={{0,248},{8,0},{16,8},{24,16},{32,24},{40,32},{48,40},{56,48},{64,5... | collective-permute-start | bytes 786440 | tf_op jit(solution)/shard_map/ppermute | solution.py:213
  78.8 0.7 old_parts.1
  79.5 4.9 %collective-permute-done.7.before = f32[512,128]{1,0:T(8,128)S(1)} collective-permute-done((f32[512,128]{1,0:T(8,128)S(1)}, f32[512,128]{1,0:T(8,128)S(1)}, u32[]{:S(2)}, u32[]{:S(2)}) %collective-permute-start.7) | collective-permute-done | bytes 262176 | tf_op jit(solution)/shard_map/ppermute | solution.py:213
  84.4 1.7 %last.1.new.mine = f32[4,128,128]{2,1,0:T(8,128)S(1)} custom-call(s32[1]{0:T(128)} %bitcast.me, bf16[8,128,640]{2,1,0:T(8,128)(2,1)S(1)} %get-tuple-element.31.m_high, bf16[8,128,640]{2,1,0:T(8,128)(2,1)S(1)} %get-tuple-element.32.m_low, f32[512,128]{1,0:T(8,128)S(1)} %collective-permute-done.7.before, f32[512,128]{1,0:T(8,128)S(1)} %get-tuple-element.34.own, ...), custom_call_target="tpu_custom_call" | custom-call | flops 754974720 | bytes 4718592 | tf_op jit(solution)/shard_map/last/pallas_call | solution.py:198
  86.1 1.2 %collective-permute-start.11 = (f32[128,128]{1,0:T(8,128)S(1)}, f32[128,128]{1,0:T(8,128)S(1)}, u32[]{:S(2)}, u32[]{:S(2)}) collective-permute-start(f32[128,128]{1,0:T(8,128)S(1)} %get-tuple-element.44), channel_id=1, source_target_pairs={{0,6},{2,0},{4,2},{6,4},{1,7},{3,1},{5,3},{7,5},{8,14},{10,8},{12,... | collective-permute-start | bytes 196616 | tf_op jit(solution)/shard_map/ppermute | solution.py:210
  87.4 1.5 %collective-permute-start.10 = (f32[128,128]{1,0:T(8,128)S(1)}, f32[128,128]{1,0:T(8,128)S(1)}, u32[]{:S(2)}, u32[]{:S(2)}) collective-permute-start(f32[128,128]{1,0:T(8,128)S(1)} %get-tuple-element.45), channel_id=1, source_target_pairs={{0,4},{2,6},{4,0},{6,2},{1,5},{3,7},{5,1},{7,3},{8,12},{10,14},{12... | collective-permute-start | bytes 196616 | tf_op jit(solution)/shard_map/ppermute | solution.py:210
  88.9 1.7 %project.1 = f32[512,128]{1,0:T(8,128)} custom-call(s32[1]{0:T(128)} %bitcast.me, bf16[512,1024]{1,0:T(8,128)(2,1)S(1)} %get-tuple-element.38.old_high, bf16[512,1024]{1,0:T(8,128)(2,1)S(1)} %get-tuple-element.39.old_low, f32[4,128,128]{2,1,0:T(8,128)S(1)} %last.1.new.mine), custom_call_target="tpu_custom_call" | custom-call | flops 402653184 | bytes 2883584 | tf_op jit(solution)/shard_map/project/pallas_call | solution.py:198
  90.6 2.6 %collective-permute-done.10.b2 = f32[128,128]{1,0:T(8,128)S(1)} collective-permute-done((f32[128,128]{1,0:T(8,128)S(1)}, f32[128,128]{1,0:T(8,128)S(1)}, u32[]{:S(2)}, u32[]{:S(2)}) %collective-permute-start.10) | collective-permute-done | bytes 65568 | tf_op jit(solution)/shard_map/ppermute | solution.py:210
  93.2 1.2 collective-permute-done.9.b1
  94.3 13.2 %all-to-all-start.1 = ((f32[128,4,128]{2,1,0:T(4,128)}), f32[128,4,128]{2,1,0:T(4,128)S(1)}, u32[]{:S(2)}, u32[]{:S(2)}) async-start(f32[128,4,128]{2,1,0:T(4,128)} %bitcast.4), calls=%async_computation.1 | async-start | bytes 524288 | tf_op jit(solution)/shard_map/all_to_all | solution.py:280
  107.5 0.9 back.1
  108.4 11.8 %all-to-all-done.1 = f32[128,4,128]{2,1,0:T(4,128)S(1)} async-done(((f32[128,4,128]{2,1,0:T(4,128)}), f32[128,4,128]{2,1,0:T(4,128)S(1)}, u32[]{:S(2)}, u32[]{:S(2)}) %all-to-all-start.1) | async-done | bytes 262176 | tf_op jit(solution)/shard_map/all_to_all | solution.py:280
  120.2 0.7 reduce.1
  (7 shorter events, 0.1 us)
Async XLA Ops:
  37.9 6.0 %collective-permute-start = (f32[4,1152,128]{2,1,0:T(8,128)S(1)}, f32[4,1152,128]{2,1,0:T(8,128)S(1)}, u32[]{:S(2)}, u32[]{:S(2)}) collective-permute-start(f32[4,1152,128]{2,1,0:T(8,128)S(1)} %all_to_all.16.mine), channel_id=1, source_target_pairs={{0,1},{1,0},{2,3},{3,2},{4,5},{5,4},{6,7},{7,6},{8,9},{9,8},{10,11... | collective-permute-start | bytes 7077896 | tf_op jit(solution)/shard_map/ppermute | solution.py:216
  38.0 5.9 %collective-permute-start.1 = (f32[256,128]{1,0:T(8,128)S(1)}, f32[256,128]{1,0:T(8,128)S(1)}, u32[]{:S(2)}, u32[]{:S(2)}) collective-permute-start(f32[256,128]{1,0:T(8,128)S(1)} %get-tuple-element.26), channel_id=1, source_target_pairs={{0,8},{8,16},{16,24},{24,32},{32,40},{40,48},{48,56},{56,64},{64,7... | collective-permute-start | bytes 393224 | tf_op jit(solution)/shard_map/ppermute | solution.py:213
  40.0 6.0 %collective-permute-start.3 = (f32[256,128]{1,0:T(8,128)S(1)}, f32[256,128]{1,0:T(8,128)S(1)}, u32[]{:S(2)}, u32[]{:S(2)}) collective-permute-start(f32[256,128]{1,0:T(8,128)S(1)} %get-tuple-element.29), channel_id=1, source_target_pairs={{0,248},{8,0},{16,8},{24,16},{32,24},{40,32},{48,40},{56,48},{64,5... | collective-permute-start | bytes 393224 | tf_op jit(solution)/shard_map/ppermute | solution.py:213
  44.0 15.3 %collective-permute-start.2 = (f32[2,128,640]{2,1,0:T(8,128)S(1)}, f32[2,128,640]{2,1,0:T(8,128)S(1)}, u32[]{:S(2)}, u32[]{:S(2)}) collective-permute-start(f32[2,128,640]{2,1,0:T(8,128)S(1)} %ghost.1), channel_id=1, source_target_pairs={{0,8},{1,249},{2,10},{3,251},{4,12},{5,253},{6,14},{7,255},{8,16},... | collective-permute-start | bytes 1966088 | tf_op jit(solution)/shard_map/ppermute | solution.py:224
  59.3 5.3 %collective-permute-start.4 = (f32[2,128,640]{2,1,0:T(8,128)S(1)}, f32[2,128,640]{2,1,0:T(8,128)S(1)}, u32[]{:S(2)}, u32[]{:S(2)}) collective-permute-start(f32[2,128,640]{2,1,0:T(8,128)S(1)} %collective-permute-done.2.ghost), channel_id=1, source_target_pairs={{0,1},{1,0},{2,3},{3,2},{4,5},{5,4},{6,7},{7,6},{8,9},{9,8},{10,11... | collective-permute-start | bytes 1966088 | tf_op jit(solution)/shard_map/ppermute | solution.py:216
  59.3 11.6 %collective-permute-start.6 = (f32[512,128]{1,0:T(8,128)S(1)}, f32[512,128]{1,0:T(8,128)S(1)}, u32[]{:S(2)}, u32[]{:S(2)}) collective-permute-start(f32[512,128]{1,0:T(8,128)S(1)} %margin.3.own.y0), channel_id=1, source_target_pairs={{0,248},{8,0},{16,8},{24,16},{32,24},{40,32},{48,40},{56,48},{64,5... | collective-permute-start | bytes 786440 | tf_op jit(solution)/shard_map/ppermute | solution.py:213
  64.7 8.4 %collective-permute-start.5 = (f32[512,128]{1,0:T(8,128)S(1)}, f32[512,128]{1,0:T(8,128)S(1)}, u32[]{:S(2)}, u32[]{:S(2)}) collective-permute-start(f32[512,128]{1,0:T(8,128)S(1)} %margin.3.own.y0), channel_id=1, source_target_pairs={{0,8},{8,16},{16,24},{24,32},{32,40},{40,48},{48,56},{56,64},{64,7... | collective-permute-start | bytes 786440 | tf_op jit(solution)/shard_map/ppermute | solution.py:213
  74.8 9.6 %collective-permute-start.7 = (f32[512,128]{1,0:T(8,128)S(1)}, f32[512,128]{1,0:T(8,128)S(1)}, u32[]{:S(2)}, u32[]{:S(2)}) collective-permute-start(f32[512,128]{1,0:T(8,128)S(1)} %get-tuple-element.34.own), channel_id=1, source_target_pairs={{0,8},{8,16},{16,24},{24,32},{32,40},{40,48},{48,56},{56,64},{64,7... | collective-permute-start | bytes 786440 | tf_op jit(solution)/shard_map/ppermute | solution.py:213
  75.2 9.2 %collective-permute-start.8 = (f32[512,128]{1,0:T(8,128)S(1)}, f32[512,128]{1,0:T(8,128)S(1)}, u32[]{:S(2)}, u32[]{:S(2)}) collective-permute-start(f32[512,128]{1,0:T(8,128)S(1)} %get-tuple-element.34.own), channel_id=1, source_target_pairs={{0,248},{8,0},{16,8},{24,16},{32,24},{40,32},{48,40},{56,48},{64,5... | collective-permute-start | bytes 786440 | tf_op jit(solution)/shard_map/ppermute | solution.py:213
  86.1 4.5 %collective-permute-start.11 = (f32[128,128]{1,0:T(8,128)S(1)}, f32[128,128]{1,0:T(8,128)S(1)}, u32[]{:S(2)}, u32[]{:S(2)}) collective-permute-start(f32[128,128]{1,0:T(8,128)S(1)} %get-tuple-element.44), channel_id=1, source_target_pairs={{0,6},{2,0},{4,2},{6,4},{1,7},{3,1},{5,3},{7,5},{8,14},{10,8},{12,... | collective-permute-start | bytes 196616 | tf_op jit(solution)/shard_map/ppermute | solution.py:210
  87.4 5.8 %collective-permute-start.10 = (f32[128,128]{1,0:T(8,128)S(1)}, f32[128,128]{1,0:T(8,128)S(1)}, u32[]{:S(2)}, u32[]{:S(2)}) collective-permute-start(f32[128,128]{1,0:T(8,128)S(1)} %get-tuple-element.45), channel_id=1, source_target_pairs={{0,4},{2,6},{4,0},{6,2},{1,5},{3,7},{5,1},{7,3},{8,12},{10,14},{12... | collective-permute-start | bytes 196616 | tf_op jit(solution)/shard_map/ppermute | solution.py:210
  88.9 5.5 %collective-permute-start.9 = (f32[128,128]{1,0:T(8,128)S(1)}, f32[128,128]{1,0:T(8,128)S(1)}, u32[]{:S(2)}, u32[]{:S(2)}) collective-permute-start(f32[128,128]{1,0:T(8,128)S(1)} %get-tuple-element.46), channel_id=1, source_target_pairs={{0,2},{2,4},{4,6},{6,0},{1,3},{3,5},{5,7},{7,1},{8,10},{10,12},{12... | collective-permute-start | bytes 196616 | tf_op jit(solution)/shard_map/ppermute | solution.py:210
  94.3 25.8 %all-to-all-start.1 = ((f32[128,4,128]{2,1,0:T(4,128)}), f32[128,4,128]{2,1,0:T(4,128)S(1)}, u32[]{:S(2)}, u32[]{:S(2)}) async-start(f32[128,4,128]{2,1,0:T(4,128)} %bitcast.4), calls=%async_computation.1 | async-start | bytes 524288 | tf_op jit(solution)/shard_map/all_to_all | solution.py:280

commit v3 on v2

v3 whole, which is shorter than its diff:
```python
import functools

import jax
import jax.numpy as jnp
from jax import lax
from jax.experimental import pallas as pl
from jax.experimental.pallas import tpu as pltpu
from jax.sharding import Mesh, PartitionSpec as P

ORDER = 4
ROW = 4
BAND = 5
B = 128
HALF = B // 2
F32 = jnp.float32
BF16 = jnp.bfloat16

SMEM = pl.BlockSpec(memory_space=pltpu.SMEM)
VMEM = pl.BlockSpec(memory_space=pltpu.VMEM)


def cost(flops, moved):
    return pl.CostEstimate(flops=flops, bytes_accessed=moved, transcendentals=0)


def split(value):
    high = value.astype(BF16)
    return high, (value - high.astype(F32)).astype(BF16)


def product(a_high, a_low, b_high, b_low):
    dot = functools.partial(jnp.dot, preferred_element_type=F32)
    return dot(a_high, b_high) + (dot(a_high, b_low) + dot(a_low, b_high))


def turned(value):
    lane = lax.broadcasted_iota(jnp.int32, value.shape, 1)
    rolled = pltpu.roll(value, HALF, axis=1)
    return jnp.where(lane < HALF, rolled, -rolled)


def member(me):
    return lax.rem(lax.div(me[0], 2), ROW), lax.rem(me[0], 2)


def turn_to(q, x):
    return lax.rem(q - x + ROW, ROW)


def parity(me):
    return lax.rem(lax.div(me[0], 2 * ROW), 2)


def pack_kernel(me, nbr, pat, coef, margin, step, out):
    position = lax.div(me[0], 2)
    for q in range(ROW):
        columns = slice(q * HALF, (q + 1) * HALF)
        out[q, :B, :] = jnp.concatenate([coef[0, 0, :, columns], coef[1, 0, :, columns]], axis=1)
    for i, source in enumerate((margin, step)):
        for d in range(BAND):
            total = None
            for k in range(16):
                weight = F32(1.0) if k == 0 else pat[0, k].astype(F32)
                here = jnp.where(nbr[0, k] == position + (d - 2), weight, F32(0.0))
                part = source[0, k] * here
                total = part if total is None else total + part
            start = B + (i * BAND + d) * HALF
            for q in range(ROW):
                out[q, start : start + HALF, :] = total


def band_rows(i, q, core, mine, other, put):
    for place, ref in ((core, mine), (1 - core, other)):
        rows = pl.ds(pl.multiple_of(place * HALF, HALF), HALF)
        for d in range(BAND):
            start = B + (i * BAND + d) * HALF
            put(rows, slice(d * B, (d + 1) * B), ref[q, start : start + HALF, :])


def edge_kernel(me, mine, to_a, to_b):
    odd = parity(me)
    for out, first in ((to_a, 2 - 2 * odd), (to_b, 2 * odd)):
        for q in range(2):
            out[q * B : (q + 1) * B, :] = mine[first + q, :B, :]


def window(odd, from_a, from_b, own, v_high, v_low):
    for start, tile in (
        ((1 - odd) * (ROW + 2) * B, from_a[...]),
        (odd * (ROW + 2) * B, from_b[...]),
        (2 * B, own),
    ):
        rows = pl.ds(pl.multiple_of(start, B), tile.shape[0])
        v_high[rows, :], v_low[rows, :] = split(tile)


def hand_out(odd, y, to_a, to_b):
    to_a[...] = y[pl.ds(pl.multiple_of((2 - 2 * odd) * B, B), 2 * B), :]
    to_b[...] = y[pl.ds(pl.multiple_of(2 * odd * B, B), 2 * B), :]


def margin_kernel(me, mine, other, from_a, from_b, out, to_a, to_b, full, v_high, v_low):
    _, core = member(me)
    odd = parity(me)
    own = [mine[q, :B, :] for q in range(ROW)]
    window(odd, from_a, from_b, jnp.concatenate(own, axis=0), v_high, v_low)
    for q in range(ROW):

        def put(rows, columns, tile):
            full[q, rows, columns] = tile

        band_rows(0, q, core, mine, other, put)
    for q in range(ROW):
        m_high, m_low = split(full[q])
        rows = slice(q * B, (q + BAND) * B)
        out[q * B : (q + 1) * B, :] = own[q] + product(m_high, m_low, v_high[rows], v_low[rows])
    hand_out(odd, out, to_a, to_b)


def parts_kernel(me, mine, other, out_high, out_low):
    _, core = member(me)
    for q in range(ROW):

        def put(rows, columns, tile):
            out_high[q, rows, columns], out_low[q, rows, columns] = split(tile)

        band_rows(1, q, core, mine, other, put)


def images(scale, m_high, m_low, v_high, v_low):
    for q in range(ROW):
        rows = slice(q * B, (q + BAND) * B)
        yield q, product(m_high[q], m_low[q], v_high[rows], v_low[rows]) * F32(scale)


def apply_kernel(scale, me, m_high, m_low, from_a, from_b, own, out, to_a, to_b, v_high, v_low):
    odd = parity(me)
    window(odd, from_a, from_b, own[...], v_high, v_low)
    for q, value in images(scale, m_high, m_low, v_high, v_low):
        out[q * B : (q + 1) * B, :] = value
    hand_out(odd, out, to_a, to_b)


def last_kernel(scale, me, m_high, m_low, from_a, from_b, own, y0, y1, y2, out, v_high, v_low):
    x, _ = member(me)
    window(parity(me), from_a, from_b, own[...], v_high, v_low)
    for q, y4 in images(scale, m_high, m_low, v_high, v_low):
        rows = slice(q * B, (q + 1) * B)
        out[turn_to(q, x)] = (y0[rows, :] - y2[rows, :]) + y4 + turned(y1[rows, :] - own[rows, :])


def old_kernel(me, coef, c1, c2, c3, other, out_high, out_low):
    x, core = member(me)
    width = coef.shape[3]
    for j, ref in enumerate((coef, c1, c2, c3)):
        q = turn_to(x, j)
        for part in range(2):
            for place, tile in ((core, ref[part, 0]), (1 - core, other[j, part])):
                rows = pl.ds(pl.multiple_of(place * width, width), width)
                columns = pl.ds(pl.multiple_of((part * ROW + q) * B, B), B)
                out_high[rows, columns], out_low[rows, columns] = split(jnp.transpose(tile))


def project_kernel(me, old_high, old_low, new, out):
    x, _ = member(me)
    tiles = [new[turn_to(q, x)] for q in range(ROW)]
    v_high, v_low = split(jnp.concatenate(tiles + [turned(t) for t in tiles], axis=0))
    out[...] = product(old_high[...], old_low[...], v_high, v_low)


def reduce_kernel(scale, parts, out):
    share = out.shape[1]
    total = jnp.sum(parts[...].reshape(-1, ROW * share, B), axis=0) * scale
    for q in range(ROW):
        for part in range(2):
            tile = total[q * share : (q + 1) * share, part * HALF : (part + 1) * HALF]
            out[part, :, q * HALF : (q + 1) * HALF] = tile


def back_kernel(me, mine, b1, b2, b3, out, held):
    x, _ = member(me)
    for j, tile in enumerate((mine[0], b1[...], b2[...], b3[...])):
        held[turn_to(x, j)] = tile
    for q in range(ROW):
        for part in range(2):
            out[part, 0, :, q * HALF : (q + 1) * HALF] = held[q, :, part * HALF : (part + 1) * HALF]


def local(rows, coefficients, margin, step_matrix, neighbours, pattern):
    width = coefficients.shape[3]
    domains = rows * ROW
    me = lax.axis_index(("row", "x", "orb")).astype(jnp.int32).reshape(1)
    struct = jax.ShapeDtypeStruct
    tile_bytes = 4 * B * B
    step_flops = 2 * 3 * B * BAND * B * B

    def call(kernel, out_shape, args, flops, moved, name, scratch=(), scalars=1):
        return pl.pallas_call(
            kernel,
            out_shape=out_shape,
            in_specs=[SMEM] * scalars + [VMEM] * (len(args) - scalars),
            out_specs=jax.tree.map(lambda _: VMEM, out_shape),
            scratch_shapes=list(scratch),
            cost_estimate=cost(flops, moved * tile_bytes),
            name=name,
            compiler_params=pltpu.CompilerParams(vmem_limit_bytes=40 * 2**20),
        )(*args)

    def in_row(value, by):
        return lax.ppermute(value, "x", [(x, (x + by) % ROW) for x in range(ROW)])

    def swap(value):
        return lax.ppermute(value, "orb", [(0, 1), (1, 0)])

    def exchange(to_a, to_b):
        def swap_rows(value, first):
            pairs = [(r, r + 1) for r in range(first, rows - 1, 2)]
            return lax.ppermute(value, "row", pairs + [(j, i) for i, j in pairs])

        return [swap_rows(to_a, 0), swap_rows(to_b, 1)]

    half_block = pl.BlockSpec((1, 16, HALF, B), lambda i, where, nbr, pat: (0, 0, lax.rem(where[0], 2), 0))
    packed_rows = B + 2 * BAND * HALF
    packed = pl.pallas_call(
        pack_kernel,
        grid_spec=pltpu.PrefetchScalarGridSpec(
            num_scalar_prefetch=3,
            grid=(1,),
            in_specs=[pl.BlockSpec(coefficients.shape, lambda i, *_: (0, 0, 0, 0)), half_block, half_block],
            out_specs=pl.BlockSpec((ROW, packed_rows, B), lambda i, *_: (0, 0, 0)),
        ),
        out_shape=struct((ROW, packed_rows, B), F32),
        cost_estimate=cost(10**6, 44 * tile_bytes),
        name="pack",
    )(me, neighbours, pattern, coefficients, margin, step_matrix)
    mine = lax.all_to_all(packed, "x", 0, 0, tiled=True)
    state = struct((ROW * B, B), F32)
    edge = struct((2 * B, B), F32)
    parts = [pltpu.VMEM((2 * ROW * B, B), BF16)] * 2
    edges = call(edge_kernel, [edge, edge], [me, mine], 10**5, 8, "edges")
    *edges, held = lax.optimization_barrier((*edges, mine))
    arrived = exchange(*edges)
    other = swap(held)
    arrived[0], held = lax.optimization_barrier((arrived[0], coefficients))
    old = [coefficients, in_row(held, 1)]
    y0, *edges = call(
        margin_kernel, [state, edge, edge], [me, mine, other] + arrived, ROW * step_flops, 60, "margin",
        scratch=[pltpu.VMEM((ROW, B, BAND * B), F32)] + parts,
    )
    parts_type = struct((ROW, B, BAND * B), BF16)
    step = list(call(parts_kernel, [parts_type, parts_type], [me, mine, other], 10**6, 40, "step_parts"))

    states = [y0]
    for n in range(1, ORDER):
        arrived = exchange(*edges)
        *arrived, old[n], held = lax.optimization_barrier((*arrived, old[n], coefficients))
        if n < ROW - 1:
            old.append(in_row(held, n + 1))
        y, *edges = call(
            functools.partial(apply_kernel, 1.0 / n), [state, edge, edge], [me] + step + arrived + [states[-1]],
            ROW * step_flops, 40, "apply", scratch=parts,
        )
        states.append(y)
    arrived = exchange(*edges)
    old_stack = jnp.stack([o[:, 0] for o in old])
    old_type = struct((2 * width, 2 * ROW * B), BF16)
    old_high, old_low = call(
        old_kernel, [old_type, old_type], [me] + old + [swap(old_stack)], 10**6, 64, "old_parts"
    )
    arrived[0], old_high = lax.optimization_barrier((arrived[0], old_high))
    y0, y1, y2, y3 = states
    new = call(
        functools.partial(last_kernel, 1.0 / ORDER), struct((ROW, B, B), F32),
        [me] + step + arrived + [y3, y0, y1, y2], ROW * step_flops, 48, "last", scratch=parts,
    )
    back = [in_row(new[j], j) for j in range(1, ROW)]
    partial_value = call(
        project_kernel, struct((2 * width, B), F32), [me, old_high, old_low, new],
        2 * 3 * 2 * width * 2 * ROW * B * B, 44, "project",
    )
    partial_value, *back = lax.optimization_barrier((partial_value, *back))
    sums = lax.all_to_all(partial_value, ("row", "x"), 0, 0, tiled=True)
    share = 2 * width // domains
    owned = call(
        functools.partial(reduce_kernel, 1.0 / (domains * B)), struct((2, share, width), F32), [sums],
        10**5, 5, "reduce", scalars=0,
    )
    propagated = call(
        back_kernel, struct((2, 1, B, width), F32), [me, new] + back, 10**5, 8, "back",
        scratch=[pltpu.VMEM((ROW, B, B), F32)],
    )
    return propagated, owned


def solution(mesh):
    rows = mesh.shape["space"] // ROW
    grouped = Mesh(mesh.devices.reshape(rows, ROW, mesh.shape["orb"]), ("row", "x", "orb"))
    space = ("row", "x")
    return jax.shard_map(
        functools.partial(local, rows),
        mesh=grouped,
        in_specs=(
            P(None, space, None, "orb"),
            P(space, None, None, None),
            P(space, None, None, None),
            P(space, None),
            P(space, None),
        ),
        out_specs=(P(None, space, None, "orb"), P(None, space, "orb")),
        check_vma=False,
    )
```

time: 121 us -> 119 us (0.983)
  starting transfers between devices: 29.4 us -> 50.2 us
  waiting for transfers between devices: 44.8 us -> 30.7 us
  blocking collectives: 33.4 us -> 25 us
    ppermute x7 -> x10, starting transfers between devices: 13.4 us -> 28.1 us  [swap_rows(): return lax.ppermute(value, 'row', pairs + [(j, i) for i, j in pairs])]
    ppermute x7 -> x10, waiting for transfers between devices: 29.3 us -> 17.2 us  [swap_rows(): return lax.ppermute(value, 'row', pairs + [(j, i) for i, j in pairs])]
    all_to_all x1, blocking collectives: 33.4 us -> 25 us  [local(): mine = lax.all_to_all(packed, 'x', 0, 0, tiled=True)]
    ppermute x3 -> x6, starting transfers between devices: 2.71 us -> 7.54 us  [in_row(): return lax.ppermute(value, 'x', [(x, (x + by) % ROW) for x in range(ROW)])]
    ppermute x3 -> x6, waiting for transfers between devices: 3.72 us -> 1.8 us  [in_row(): return lax.ppermute(value, 'x', [(x, (x + by) % ROW) for x in range(ROW)])]
    pallas_call x10 -> x11, Pallas kernels: 8.69 us -> 7.98 us  [call(): pl.pallas_call(kernel, out_shape=out_shape, in_specs=[SMEM] * scalars + [...]
  transfers between devices with their start and end apart: 13 -> 19, of which waited for: 8 -> 10; matrix products, arithmetic and copies ran while one was open for 0% -> 0% of each run, Pallas kernels for 4% -> 6%
where the time goes in v3:
time: 119 us; the launch traced here: 118 us
  starting transfers between devices  50.2 us (42%)
  waiting for transfers between devices  30.7 us (26%)
  blocking collectives  25 us (21%)
  Pallas kernels  11.6 us (10%)
    ppermute x10, starting transfers between devices, swap_rows(): return lax.ppermute(value, 'row', pairs + [(j, i) for i, j in pairs])  28.1 us
    all_to_all x1, blocking collectives, local(): mine = lax.all_to_all(packed, 'x', 0, 0, tiled=True)  25 us
    ppermute x10, waiting for transfers between devices, swap_rows(): return lax.ppermute(value, 'row', pairs + [(j, i) for i, j in pairs])  17.2 us
    all_to_all x1, starting transfers between devices, local(): sums = lax.all_to_all(partial_value, ('row', 'x'), 0, 0, tiled=True)  14.4 us
    all_to_all x1, waiting for transfers between devices, local(): sums = lax.all_to_all(partial_value, ('row', 'x'), 0, 0, tiled=True)  11.7 us
    pallas_call x11, Pallas kernels, call(): pl.pallas_call(kernel, out_shape=out_shape, in_specs=[SMEM] * scalars + [...  7.98 us
    ppermute x6, starting transfers between devices, in_row(): return lax.ppermute(value, 'x', [(x, (x + by) % ROW) for x in range(ROW)])  7.54 us
    pallas_call x1, Pallas kernels, local(): pl.pallas_call(pack_kernel, grid_spec=pltpu.PrefetchScalarGridSpec(num_sc...  3.59 us
  transfers between devices with their start and end apart: 19, of which 10 were waited for; matrix products, arithmetic and copies ran while one was open for 0% of the time, Pallas kernels for 6%

profile of v3, /device:TPU:32, one launch (start us, length us, event | category | flops | bytes accessed | tf_op | source)
XLA Modules:
  0.0 118.4 jit_solution(797605576128967590)
XLA Ops:
  0.6 3.6 %pack.1 = f32[4,768,128]{2,1,0:T(8,128)} custom-call(s32[1]{0:T(128)} %bitcast.me, s32[1,16]{1,0:T(1,128)} %nbr.1, s32[1,16]{1,0:T(1,128)} %pat.1, f32[2,1,128,256]{3,2,1,0:T(8,128)} %coef.3, f32[1,16,128,128]{3,2,1,0:T(8,128)} %margin.2, f32[1,16,128,128]{3,2,1,0:T(8,128)} %step.1), custom_call_target="tpu_custom_call" | custom-call | flops 1000000 | bytes 2883584 | tf_op jit(solution)/shard_map/pack/pallas_call | solution.py:224
  4.2 25.0 %all_to_all.16.mine = f32[4,768,128]{2,1,0:T(8,128)S(1)} all-to-all(f32[4,768,128]{2,1,0:T(8,128)} %pack.1), channel_id=1, replica_groups=mesh['row'=32,'x'=4,'orb'=2] {'x'}, dimensions={0} | all-to-all | bytes 3145728 | tf_op jit(solution)/shard_map/all_to_all | solution.py:236
  29.6 5.6 %collective-permute-start.2 = (f32[256,128]{1,0:T(8,128)S(1)}, f32[256,128]{1,0:T(8,128)S(1)}, u32[]{:S(2)}, u32[]{:S(2)}) collective-permute-start(f32[256,128]{1,0:T(8,128)S(1)} %get-tuple-element.49), channel_id=1, source_target_pairs={{8,16},{24,32},{40,48},{56,64},{72,80},{88,96},{104,112},{120,128}... | collective-permute-start | bytes 393224 | tf_op jit(solution)/shard_map/ppermute | solution.py:218
  35.3 0.6 collective-permute-start.5
  35.8 3.1 %collective-permute-done.2.from_b = f32[256,128]{1,0:T(8,128)S(1)} collective-permute-done((f32[256,128]{1,0:T(8,128)S(1)}, f32[256,128]{1,0:T(8,128)S(1)}, u32[]{:S(2)}, u32[]{:S(2)}) %collective-permute-start.2) | collective-permute-done | bytes 131104 | tf_op jit(solution)/shard_map/ppermute | solution.py:218
  39.0 0.8 margin.3
  39.9 6.0 %collective-permute-start.4 = (f32[256,128]{1,0:T(8,128)S(1)}, f32[256,128]{1,0:T(8,128)S(1)}, u32[]{:S(2)}, u32[]{:S(2)}) collective-permute-start(f32[256,128]{1,0:T(8,128)S(1)} %get-tuple-element.51), channel_id=1, source_target_pairs={{8,16},{24,32},{40,48},{56,64},{72,80},{88,96},{104,112},{120,128}... | collective-permute-start | bytes 393224 | tf_op jit(solution)/shard_map/ppermute | solution.py:218
  45.9 3.0 %collective-permute-done.4.from_b = f32[256,128]{1,0:T(8,128)S(1)} collective-permute-done((f32[256,128]{1,0:T(8,128)S(1)}, f32[256,128]{1,0:T(8,128)S(1)}, u32[]{:S(2)}, u32[]{:S(2)}) %collective-permute-start.4) | collective-permute-done | bytes 131104 | tf_op jit(solution)/shard_map/ppermute | solution.py:218
  48.9 0.8 collective-permute-start.8
  49.9 0.7 apply.3
  50.8 5.1 %collective-permute-start.7 = (f32[256,128]{1,0:T(8,128)S(1)}, f32[256,128]{1,0:T(8,128)S(1)}, u32[]{:S(2)}, u32[]{:S(2)}) collective-permute-start(f32[256,128]{1,0:T(8,128)S(1)} %get-tuple-element.57), channel_id=1, source_target_pairs={{8,16},{24,32},{40,48},{56,64},{72,80},{88,96},{104,112},{120,128}... | collective-permute-start | bytes 393224 | tf_op jit(solution)/shard_map/ppermute | solution.py:218
  55.9 2.9 %collective-permute-done.7.from_b = f32[256,128]{1,0:T(8,128)S(1)} collective-permute-done((f32[256,128]{1,0:T(8,128)S(1)}, f32[256,128]{1,0:T(8,128)S(1)}, u32[]{:S(2)}, u32[]{:S(2)}) %collective-permute-start.7) | collective-permute-done | bytes 131104 | tf_op jit(solution)/shard_map/ppermute | solution.py:218
  58.9 2.4 %collective-permute-start.11 = (f32[2,1,128,256]{3,2,0,1:T(8,128)S(1)}, f32[2,1,128,256]{3,2,0,1:T(8,128)S(1)}, u32[]{:S(2)}, u32[]{:S(2)}) collective-permute-start(f32[2,1,128,256]{3,2,0,1:T(8,128)S(1)} %bitcast.21), channel_id=1, source_target_pairs={{0,6},{2,0},{4,2},{6,4},{1,7},{3,1},{5,3},{7,5},{8,14},{10,8},{12,... | collective-permute-start | bytes 786440 | tf_op jit(solution)/shard_map/ppermute | solution.py:210
  61.3 0.7 apply.4
  62.0 3.9 %collective-permute-start.10 = (f32[256,128]{1,0:T(8,128)S(1)}, f32[256,128]{1,0:T(8,128)S(1)}, u32[]{:S(2)}, u32[]{:S(2)}) collective-permute-start(f32[256,128]{1,0:T(8,128)S(1)} %get-tuple-element.63), channel_id=1, source_target_pairs={{8,16},{24,32},{40,48},{56,64},{72,80},{88,96},{104,112},{120,128}... | collective-permute-start | bytes 393224 | tf_op jit(solution)/shard_map/ppermute | solution.py:218
  66.1 2.8 %collective-permute-done.10.from_b = f32[256,128]{1,0:T(8,128)S(1)} collective-permute-done((f32[256,128]{1,0:T(8,128)S(1)}, f32[256,128]{1,0:T(8,128)S(1)}, u32[]{:S(2)}, u32[]{:S(2)}) %collective-permute-start.10) | collective-permute-done | bytes 131104 | tf_op jit(solution)/shard_map/ppermute | solution.py:218
  68.9 2.1 %collective-permute-done.9.from_a = f32[256,128]{1,0:T(8,128)S(1)} collective-permute-done((f32[256,128]{1,0:T(8,128)S(1)}, f32[256,128]{1,0:T(8,128)S(1)}, u32[]{:S(2)}, u32[]{:S(2)}) %collective-permute-start.9) | collective-permute-done | bytes 131104 | tf_op jit(solution)/shard_map/ppermute | solution.py:218
  71.2 0.7 apply.5
  72.0 6.8 %collective-permute-start.14 = (f32[256,128]{1,0:T(8,128)S(1)}, f32[256,128]{1,0:T(8,128)S(1)}, u32[]{:S(2)}, u32[]{:S(2)}) collective-permute-start(f32[256,128]{1,0:T(8,128)S(1)} %get-tuple-element.74), channel_id=1, source_target_pairs={{8,16},{24,32},{40,48},{56,64},{72,80},{88,96},{104,112},{120,128}... | collective-permute-start | bytes 393224 | tf_op jit(solution)/shard_map/ppermute | solution.py:218
  78.8 0.7 old_parts.1
  79.6 3.1 %collective-permute-done.14.from_b = f32[256,128]{1,0:T(8,128)S(1)} collective-permute-done((f32[256,128]{1,0:T(8,128)S(1)}, f32[256,128]{1,0:T(8,128)S(1)}, u32[]{:S(2)}, u32[]{:S(2)}) %collective-permute-start.14) | collective-permute-done | bytes 131104 | tf_op jit(solution)/shard_map/ppermute | solution.py:218
  82.7 0.7 last.1.new.mine
  83.4 0.3 collective-permute-start.15
  83.7 2.3 %collective-permute-start.16 = (f32[128,128]{1,0:T(8,128)S(1)}, f32[128,128]{1,0:T(8,128)S(1)}, u32[]{:S(2)}, u32[]{:S(2)}) collective-permute-start(f32[128,128]{1,0:T(8,128)S(1)} %get-tuple-element.83), channel_id=1, source_target_pairs={{0,4},{2,6},{4,0},{6,2},{1,5},{3,7},{5,1},{7,3},{8,12},{10,14},{12... | collective-permute-start | bytes 196616 | tf_op jit(solution)/shard_map/ppermute | solution.py:210
  86.0 1.2 collective-permute-start.17
  87.1 1.8 %project.1 = f32[512,128]{1,0:T(8,128)} custom-call(s32[1]{0:T(128)} %bitcast.me, bf16[512,1024]{1,0:T(8,128)(2,1)S(1)} %get-tuple-element.76.old_high, bf16[512,1024]{1,0:T(8,128)(2,1)S(1)} %get-tuple-element.77.old_low, f32[4,128,128]{2,1,0:T(8,128)S(1)} %last.1.new.mine), custom_call_target="tpu_custom_call" | custom-call | flops 402653184 | bytes 2883584 | tf_op jit(solution)/shard_map/project/pallas_call | solution.py:198
  88.9 1.2 %collective-permute-done.15.b1 = f32[128,128]{1,0:T(8,128)S(1)} collective-permute-done((f32[128,128]{1,0:T(8,128)S(1)}, f32[128,128]{1,0:T(8,128)S(1)}, u32[]{:S(2)}, u32[]{:S(2)}) %collective-permute-start.15) | collective-permute-done | bytes 65568 | tf_op jit(solution)/shard_map/ppermute | solution.py:210
  90.1 0.6 collective-permute-done.17.b3
  90.7 14.4 %all-to-all-start.1 = ((f32[128,4,128]{2,1,0:T(4,128)}), f32[128,4,128]{2,1,0:T(4,128)S(1)}, u32[]{:S(2)}, u32[]{:S(2)}) async-start(f32[128,4,128]{2,1,0:T(4,128)} %bitcast.14), calls=%async_computation.1 | async-start | bytes 524288 | tf_op jit(solution)/shard_map/all_to_all | solution.py:282
  105.1 0.9 back.1
  106.0 11.7 %all-to-all-done.1 = f32[128,4,128]{2,1,0:T(4,128)S(1)} async-done(((f32[128,4,128]{2,1,0:T(4,128)}), f32[128,4,128]{2,1,0:T(4,128)S(1)}, u32[]{:S(2)}, u32[]{:S(2)}) %all-to-all-start.1) | async-done | bytes 262176 | tf_op jit(solution)/shard_map/all_to_all | solution.py:282
  117.7 0.7 reduce.1
  (23 shorter events, 1.2 us)
Async XLA Ops:
  29.2 6.0 %copy-start = (f32[2,1,128,256]{3,2,1,0:T(8,128)S(1)}, f32[2,1,128,256]{3,2,1,0:T(8,128)}, u32[]{:S(2)}) copy-start(f32[2,1,128,256]{3,2,1,0:T(8,128)} %coef.3) | copy-start | bytes 786436
  29.3 9.7 %collective-permute-start = (f32[4,768,128]{2,1,0:T(8,128)S(1)}, f32[4,768,128]{2,1,0:T(8,128)S(1)}, u32[]{:S(2)}, u32[]{:S(2)}) collective-permute-start(f32[4,768,128]{2,1,0:T(8,128)S(1)} %all_to_all.16.mine), channel_id=1, source_target_pairs={{0,1},{1,0},{2,3},{3,2},{4,5},{5,4},{6,7},{7,6},{8,9},{9,8},{10,11... | collective-permute-start | bytes 4718600 | tf_op jit(solution)/shard_map/ppermute | solution.py:213
  29.4 5.9 %collective-permute-start.1 = (f32[256,128]{1,0:T(8,128)S(1)}, f32[256,128]{1,0:T(8,128)S(1)}, u32[]{:S(2)}, u32[]{:S(2)}) collective-permute-start(f32[256,128]{1,0:T(8,128)S(1)} %get-tuple-element.47), channel_id=1, source_target_pairs={{0,8},{16,24},{32,40},{48,56},{64,72},{80,88},{96,104},{112,120},{... | collective-permute-start | bytes 393224 | tf_op jit(solution)/shard_map/ppermute | solution.py:218
  29.6 9.4 %collective-permute-start.2 = (f32[256,128]{1,0:T(8,128)S(1)}, f32[256,128]{1,0:T(8,128)S(1)}, u32[]{:S(2)}, u32[]{:S(2)}) collective-permute-start(f32[256,128]{1,0:T(8,128)S(1)} %get-tuple-element.49), channel_id=1, source_target_pairs={{8,16},{24,32},{40,48},{56,64},{72,80},{88,96},{104,112},{120,128}... | collective-permute-start | bytes 393224 | tf_op jit(solution)/shard_map/ppermute | solution.py:218
  35.3 10.6 %collective-permute-start.5 = (f32[2,1,128,256]{3,2,0,1:T(8,128)S(1)}, f32[2,1,128,256]{3,2,0,1:T(8,128)S(1)}, u32[]{:S(2)}, u32[]{:S(2)}) collective-permute-start(f32[2,1,128,256]{3,2,0,1:T(8,128)S(1)} %bitcast.19), channel_id=1, source_target_pairs={{0,2},{2,4},{4,6},{6,0},{1,3},{3,5},{5,7},{7,1},{8,10},{10,12},{12... | collective-permute-start | bytes 786440 | tf_op jit(solution)/shard_map/ppermute | solution.py:210
  39.8 6.2 %collective-permute-start.3 = (f32[256,128]{1,0:T(8,128)S(1)}, f32[256,128]{1,0:T(8,128)S(1)}, u32[]{:S(2)}, u32[]{:S(2)}) collective-permute-start(f32[256,128]{1,0:T(8,128)S(1)} %get-tuple-element.50), channel_id=1, source_target_pairs={{0,8},{16,24},{32,40},{48,56},{64,72},{80,88},{96,104},{112,120},{... | collective-permute-start | bytes 393224 | tf_op jit(solution)/shard_map/ppermute | solution.py:218
  39.9 9.0 %collective-permute-start.4 = (f32[256,128]{1,0:T(8,128)S(1)}, f32[256,128]{1,0:T(8,128)S(1)}, u32[]{:S(2)}, u32[]{:S(2)}) collective-permute-start(f32[256,128]{1,0:T(8,128)S(1)} %get-tuple-element.51), channel_id=1, source_target_pairs={{8,16},{24,32},{40,48},{56,64},{72,80},{88,96},{104,112},{120,128}... | collective-permute-start | bytes 393224 | tf_op jit(solution)/shard_map/ppermute | solution.py:218
  48.9 10.0 %collective-permute-start.8 = (f32[2,1,128,256]{3,2,0,1:T(8,128)S(1)}, f32[2,1,128,256]{3,2,0,1:T(8,128)S(1)}, u32[]{:S(2)}, u32[]{:S(2)}) collective-permute-start(f32[2,1,128,256]{3,2,0,1:T(8,128)S(1)} %bitcast.20), channel_id=1, source_target_pairs={{0,4},{2,6},{4,0},{6,2},{1,5},{3,7},{5,1},{7,3},{8,12},{10,14},{12... | collective-permute-start | bytes 786440 | tf_op jit(solution)/shard_map/ppermute | solution.py:210
  50.7 5.3 %collective-permute-start.6 = (f32[256,128]{1,0:T(8,128)S(1)}, f32[256,128]{1,0:T(8,128)S(1)}, u32[]{:S(2)}, u32[]{:S(2)}) collective-permute-start(f32[256,128]{1,0:T(8,128)S(1)} %get-tuple-element.56), channel_id=1, source_target_pairs={{0,8},{16,24},{32,40},{48,56},{64,72},{80,88},{96,104},{112,120},{... | collective-permute-start | bytes 393224 | tf_op jit(solution)/shard_map/ppermute | solution.py:218
  50.8 8.1 %collective-permute-start.7 = (f32[256,128]{1,0:T(8,128)S(1)}, f32[256,128]{1,0:T(8,128)S(1)}, u32[]{:S(2)}, u32[]{:S(2)}) collective-permute-start(f32[256,128]{1,0:T(8,128)S(1)} %get-tuple-element.57), channel_id=1, source_target_pairs={{8,16},{24,32},{40,48},{56,64},{72,80},{88,96},{104,112},{120,128}... | collective-permute-start | bytes 393224 | tf_op jit(solution)/shard_map/ppermute | solution.py:218
  58.9 12.1 %collective-permute-start.11 = (f32[2,1,128,256]{3,2,0,1:T(8,128)S(1)}, f32[2,1,128,256]{3,2,0,1:T(8,128)S(1)}, u32[]{:S(2)}, u32[]{:S(2)}) collective-permute-start(f32[2,1,128,256]{3,2,0,1:T(8,128)S(1)} %bitcast.21), channel_id=1, source_target_pairs={{0,6},{2,0},{4,2},{6,4},{1,7},{3,1},{5,3},{7,5},{8,14},{10,8},{12,... | collective-permute-start | bytes 786440 | tf_op jit(solution)/shard_map/ppermute | solution.py:210
  62.0 6.9 %collective-permute-start.10 = (f32[256,128]{1,0:T(8,128)S(1)}, f32[256,128]{1,0:T(8,128)S(1)}, u32[]{:S(2)}, u32[]{:S(2)}) collective-permute-start(f32[256,128]{1,0:T(8,128)S(1)} %get-tuple-element.63), channel_id=1, source_target_pairs={{8,16},{24,32},{40,48},{56,64},{72,80},{88,96},{104,112},{120,128}... | collective-permute-start | bytes 393224 | tf_op jit(solution)/shard_map/ppermute | solution.py:218
  66.0 5.1 %collective-permute-start.9 = (f32[256,128]{1,0:T(8,128)S(1)}, f32[256,128]{1,0:T(8,128)S(1)}, u32[]{:S(2)}, u32[]{:S(2)}) collective-permute-start(f32[256,128]{1,0:T(8,128)S(1)} %get-tuple-element.62), channel_id=1, source_target_pairs={{0,8},{16,24},{32,40},{48,56},{64,72},{80,88},{96,104},{112,120},{... | collective-permute-start | bytes 393224 | tf_op jit(solution)/shard_map/ppermute | solution.py:218
  71.1 7.7 %collective-permute-start.13 = (f32[4,2,128,256]{3,2,1,0:T(8,128)S(1)}, f32[4,2,128,256]{3,2,1,0:T(8,128)S(1)}, u32[]{:S(2)}, u32[]{:S(2)}) collective-permute-start(f32[4,2,128,256]{3,2,1,0:T(8,128)S(1)} %pad_maximum_fusion), channel_id=1, source_target_pairs={{0,1},{1,0},{2,3},{3,2},{4,5},{5,4},{6,7},{7,6},{8,9},{9,8},{10,11... | collective-permute-start | bytes 3145736 | tf_op jit(solution)/shard_map/ppermute | solution.py:213
  71.9 7.6 %collective-permute-start.12 = (f32[256,128]{1,0:T(8,128)S(1)}, f32[256,128]{1,0:T(8,128)S(1)}, u32[]{:S(2)}, u32[]{:S(2)}) collective-permute-start(f32[256,128]{1,0:T(8,128)S(1)} %get-tuple-element.68), channel_id=1, source_target_pairs={{0,8},{16,24},{32,40},{48,56},{64,72},{80,88},{96,104},{112,120},{... | collective-permute-start | bytes 393224 | tf_op jit(solution)/shard_map/ppermute | solution.py:218
  72.0 10.6 %collective-permute-start.14 = (f32[256,128]{1,0:T(8,128)S(1)}, f32[256,128]{1,0:T(8,128)S(1)}, u32[]{:S(2)}, u32[]{:S(2)}) collective-permute-start(f32[256,128]{1,0:T(8,128)S(1)} %get-tuple-element.74), channel_id=1, source_target_pairs={{8,16},{24,32},{40,48},{56,64},{72,80},{88,96},{104,112},{120,128}... | collective-permute-start | bytes 393224 | tf_op jit(solution)/shard_map/ppermute | solution.py:218
  83.4 6.7 %collective-permute-start.15 = (f32[128,128]{1,0:T(8,128)S(1)}, f32[128,128]{1,0:T(8,128)S(1)}, u32[]{:S(2)}, u32[]{:S(2)}) collective-permute-start(f32[128,128]{1,0:T(8,128)S(1)} %get-tuple-element.84), channel_id=1, source_target_pairs={{0,2},{2,4},{4,6},{6,0},{1,3},{3,5},{5,7},{7,1},{8,10},{10,12},{12... | collective-permute-start | bytes 196616 | tf_op jit(solution)/shard_map/ppermute | solution.py:210
  83.7 6.4 %collective-permute-start.16 = (f32[128,128]{1,0:T(8,128)S(1)}, f32[128,128]{1,0:T(8,128)S(1)}, u32[]{:S(2)}, u32[]{:S(2)}) collective-permute-start(f32[128,128]{1,0:T(8,128)S(1)} %get-tuple-element.83), channel_id=1, source_target_pairs={{0,4},{2,6},{4,0},{6,2},{1,5},{3,7},{5,1},{7,3},{8,12},{10,14},{12... | collective-permute-start | bytes 196616 | tf_op jit(solution)/shard_map/ppermute | solution.py:210
  86.0 4.7 %collective-permute-start.17 = (f32[128,128]{1,0:T(8,128)S(1)}, f32[128,128]{1,0:T(8,128)S(1)}, u32[]{:S(2)}, u32[]{:S(2)}) collective-permute-start(f32[128,128]{1,0:T(8,128)S(1)} %get-tuple-element.82), channel_id=1, source_target_pairs={{0,6},{2,0},{4,2},{6,4},{1,7},{3,1},{5,3},{7,5},{8,14},{10,8},{12,... | collective-permute-start | bytes 196616 | tf_op jit(solution)/shard_map/ppermute | solution.py:210
  90.7 27.0 %all-to-all-start.1 = ((f32[128,4,128]{2,1,0:T(4,128)}), f32[128,4,128]{2,1,0:T(4,128)S(1)}, u32[]{:S(2)}, u32[]{:S(2)}) async-start(f32[128,4,128]{2,1,0:T(4,128)} %bitcast.14), calls=%async_computation.1 | async-start | bytes 524288 | tf_op jit(solution)/shard_map/all_to_all | solution.py:282

commit v4 on v3

--- a/solution.py
+++ b/solution.py
@@ -51,29 +51,43 @@
     return lax.rem(lax.div(me[0], 2 * ROW), 2)
 
 
-def pack_kernel(me, nbr, pat, coef, margin, step, out):
+def bands(me, nbr, pat, source):
     position = lax.div(me[0], 2)
+    for d in range(BAND):
+        total = None
+        for k in range(source.shape[1]):
+            weight = F32(1.0) if k == 0 else pat[0, k].astype(F32)
+            here = jnp.where(nbr[0, k] == position + (d - 2), weight, F32(0.0))
+            part = source[0, k] * here
+            total = part if total is None else total + part
+        yield d * HALF, total
+
+
+def pack_kernel(me, nbr, pat, coef, margin, out):
     for q in range(ROW):
         columns = slice(q * HALF, (q + 1) * HALF)
         out[q, :B, :] = jnp.concatenate([coef[0, 0, :, columns], coef[1, 0, :, columns]], axis=1)
-    for i, source in enumerate((margin, step)):
-        for d in range(BAND):
-            total = None
-            for k in range(16):
-                weight = F32(1.0) if k == 0 else pat[0, k].astype(F32)
-                here = jnp.where(nbr[0, k] == position + (d - 2), weight, F32(0.0))
-                part = source[0, k] * here
-                total = part if total is None else total + part
-            start = B + (i * BAND + d) * HALF
-            for q in range(ROW):
-                out[q, start : start + HALF, :] = total
-
-
-def band_rows(i, q, core, mine, other, put):
+    for start, total in bands(me, nbr, pat, margin):
+        for q in range(ROW):
+            out[q, B + start : B + start + HALF, :] = total
+
+
+def step_kernel(me, nbr, pat, step, out):
+    for start, total in bands(me, nbr, pat, step):
+        out[start : start + HALF, :] = total
+
+
+def gather_kernel(me, mine, s1, s2, s3, out):
+    x, _ = member(me)
+    for j, ref in enumerate((mine, s1, s2, s3)):
+        out[turn_to(x, j)] = ref[...]
+
+
+def band_rows(first, q, core, mine, other, put):
     for place, ref in ((core, mine), (1 - core, other)):
         rows = pl.ds(pl.multiple_of(place * HALF, HALF), HALF)
         for d in range(BAND):
-            start = B + (i * BAND + d) * HALF
+            start = first + d * HALF
             put(rows, slice(d * B, (d + 1) * B), ref[q, start : start + HALF, :])
 
 
@@ -109,7 +123,7 @@
         def put(rows, columns, tile):
             full[q, rows, columns] = tile
 
-        band_rows(0, q, core, mine, other, put)
+        band_rows(B, q, core, mine, other, put)
     for q in range(ROW):
         m_high, m_low = split(full[q])
         rows = slice(q * B, (q + BAND) * B)
@@ -124,7 +138,7 @@
         def put(rows, columns, tile):
             out_high[q, rows, columns], out_low[q, rows, columns] = split(tile)
 
-        band_rows(1, q, core, mine, other, put)
+        band_rows(0, q, core, mine, other, put)
 
 
 def images(scale, m_high, m_low, v_high, v_low):
@@ -168,22 +182,30 @@
     out[...] = product(old_high[...], old_low[...], v_high, v_low)
 
 
-def reduce_kernel(scale, parts, out):
-    share = out.shape[1]
-    total = jnp.sum(parts[...].reshape(-1, ROW * share, B), axis=0) * scale
-    for q in range(ROW):
+def tail_kernel(scale, me, sums, new, *outs):
+    x, _ = member(me)
+    share = 4
+    total = jnp.sum(sums[...].reshape(-1, ROW * share, B), axis=0) * scale
+    for j, out in enumerate(outs):
+        out[:B, :] = new[j]
+        for q in range(ROW):
+
+            @pl.when(q == lax.rem(x + j, ROW))
+            def _():
+                out[B : B + share, :] = total[q * share : (q + 1) * share, :]
+
+
+def finish_kernel(me, mine, b1, b2, b3, propagated, owned, held):
+    x, _ = member(me)
+    share = owned.shape[1]
+    for j, ref in enumerate((mine, b1, b2, b3)):
+        held[turn_to(x, j)] = ref[...]
+    for q in range(ROW):
+        columns = slice(q * HALF, (q + 1) * HALF)
         for part in range(2):
-            tile = total[q * share : (q + 1) * share, part * HALF : (part + 1) * HALF]
-            out[part, :, q * HALF : (q + 1) * HALF] = tile
-
-
-def back_kernel(me, mine, b1, b2, b3, out, held):
-    x, _ = member(me)
-    for j, tile in enumerate((mine[0], b1[...], b2[...], b3[...])):
-        held[turn_to(x, j)] = tile
-    for q in range(ROW):
-        for part in range(2):
-            out[part, 0, :, q * HALF : (q + 1) * HALF] = held[q, :, part * HALF : (part + 1) * HALF]
+            lanes = slice(part * HALF, (part + 1) * HALF)
+            propagated[part, 0, :, columns] = held[q, :B, lanes]
+            owned[part, :, columns] = held[q, B : B + share, lanes]
 
 
 def local(rows, coefficients, margin, step_matrix, neighbours, pattern):
@@ -219,20 +241,23 @@
 
         return [swap_rows(to_a, 0), swap_rows(to_b, 1)]
 
+    def prefetched(kernel, arrays, specs, out_shape, moved, name):
+        zeros = (0,) * len(out_shape)
+        return pl.pallas_call(
+            kernel,
+            grid_spec=pltpu.PrefetchScalarGridSpec(
+                num_scalar_prefetch=3, grid=(1,), in_specs=specs, out_specs=pl.BlockSpec(out_shape, lambda i, *_: zeros)
+            ),
+            out_shape=struct(out_shape, F32),
+            cost_estimate=cost(10**6, moved * tile_bytes),
+            name=name,
+        )(me, neighbours, pattern, *arrays)
+
     half_block = pl.BlockSpec((1, 16, HALF, B), lambda i, where, nbr, pat: (0, 0, lax.rem(where[0], 2), 0))
-    packed_rows = B + 2 * BAND * HALF
-    packed = pl.pallas_call(
-        pack_kernel,
-        grid_spec=pltpu.PrefetchScalarGridSpec(
-            num_scalar_prefetch=3,
-            grid=(1,),
-            in_specs=[pl.BlockSpec(coefficients.shape, lambda i, *_: (0, 0, 0, 0)), half_block, half_block],
-            out_specs=pl.BlockSpec((ROW, packed_rows, B), lambda i, *_: (0, 0, 0)),
-        ),
-        out_shape=struct((ROW, packed_rows, B), F32),
-        cost_estimate=cost(10**6, 44 * tile_bytes),
-        name="pack",
-    )(me, neighbours, pattern, coefficients, margin, step_matrix)
+    whole = pl.BlockSpec(coefficients.shape, lambda i, *_: (0, 0, 0, 0))
+    packed = prefetched(
+        pack_kernel, (coefficients, margin), [whole, half_block], (ROW, B + BAND * HALF, B), 26, "pack"
+    )
     mine = lax.all_to_all(packed, "x", 0, 0, tiled=True)
     state = struct((ROW * B, B), F32)
     edge = struct((2 * B, B), F32)
@@ -241,21 +266,27 @@
     *edges, held = lax.optimization_barrier((*edges, mine))
     arrived = exchange(*edges)
     other = swap(held)
-    arrived[0], held = lax.optimization_barrier((arrived[0], coefficients))
-    old = [coefficients, in_row(held, 1)]
+    edges[0], held = lax.optimization_barrier((edges[0], step_matrix))
+    step_half = prefetched(step_kernel, (held,), [half_block], (BAND * HALF, B), 10, "step")
+    step_row = [step_half] + [in_row(step_half, j) for j in range(1, ROW)]
     y0, *edges = call(
         margin_kernel, [state, edge, edge], [me, mine, other] + arrived, ROW * step_flops, 60, "margin",
         scratch=[pltpu.VMEM((ROW, B, BAND * B), F32)] + parts,
     )
     parts_type = struct((ROW, B, BAND * B), BF16)
-    step = list(call(parts_kernel, [parts_type, parts_type], [me, mine, other], 10**6, 40, "step_parts"))
+    _, *step_row = lax.optimization_barrier((y0, *step_row))
+    step_mine = call(gather_kernel, struct((ROW, BAND * HALF, B), F32), [me] + step_row, 10**5, 20, "step_row")
+    step = list(
+        call(parts_kernel, [parts_type, parts_type], [me, step_mine, swap(step_mine)], 10**6, 40, "step_parts")
+    )
 
     states = [y0]
+    old = [coefficients]
     for n in range(1, ORDER):
         arrived = exchange(*edges)
-        *arrived, old[n], held = lax.optimization_barrier((*arrived, old[n], coefficients))
-        if n < ROW - 1:
-            old.append(in_row(held, n + 1))
+        *arrived, old[-1], held = lax.optimization_barrier((*arrived, old[-1], coefficients))
+        for j in ((), (1,), (2, 3), ())[n]:
+            old.append(in_row(held, j))
         y, *edges = call(
             functools.partial(apply_kernel, 1.0 / n), [state, edge, edge], [me] + step + arrived + [states[-1]],
             ROW * step_flops, 40, "apply", scratch=parts,
@@ -273,23 +304,21 @@
         functools.partial(last_kernel, 1.0 / ORDER), struct((ROW, B, B), F32),
         [me] + step + arrived + [y3, y0, y1, y2], ROW * step_flops, 48, "last", scratch=parts,
     )
-    back = [in_row(new[j], j) for j in range(1, ROW)]
     partial_value = call(
         project_kernel, struct((2 * width, B), F32), [me, old_high, old_low, new],
         2 * 3 * 2 * width * 2 * ROW * B * B, 44, "project",
     )
-    partial_value, *back = lax.optimization_barrier((partial_value, *back))
-    sums = lax.all_to_all(partial_value, ("row", "x"), 0, 0, tiled=True)
+    sums = lax.all_to_all(partial_value, "row", 0, 0, tiled=True)
     share = 2 * width // domains
-    owned = call(
-        functools.partial(reduce_kernel, 1.0 / (domains * B)), struct((2, share, width), F32), [sums],
-        10**5, 5, "reduce", scalars=0,
-    )
-    propagated = call(
-        back_kernel, struct((2, 1, B, width), F32), [me, new] + back, 10**5, 8, "back",
-        scratch=[pltpu.VMEM((ROW, B, B), F32)],
-    )
-    return propagated, owned
+    sent = struct((B + 2 * share, B), F32)
+    tail = call(
+        functools.partial(tail_kernel, 1.0 / (domains * B)), [sent] * ROW, [me, sums, new], 10**5, 12, "tail"
+    )
+    tail = [tail[0]] + [in_row(tail[j], j) for j in range(1, ROW)]
+    return call(
+        finish_kernel, (struct((2, 1, B, width), F32), struct((2, share, width), F32)), [me] + tail, 10**5, 8,
+        "finish", scratch=[pltpu.VMEM((ROW, B + 2 * share, B), F32)],
+    )
 
 
 def solution(mesh):

time: 119 us -> 117 us (0.983)
  blocking collectives: 25 us -> 41.9 us
  waiting for transfers between devices: 30.7 us -> 20.8 us
  starting transfers between devices: 50.2 us -> 40.9 us
    all_to_all x0 -> x1, blocking collectives: none -> 23.9 us  [local(): sums = lax.all_to_all(partial_value, 'row', 0, 0, tiled=True)]
    all_to_all x1 -> x0, starting transfers between devices: 14.4 us -> none  [local(): sums = lax.all_to_all(partial_value, ('row', 'x'), 0, 0, tiled=True)]
    all_to_all x1 -> x0, waiting for transfers between devices: 11.7 us -> none  [local(): sums = lax.all_to_all(partial_value, ('row', 'x'), 0, 0, tiled=True)]
    all_to_all x1, blocking collectives: 25 us -> 18 us  [local(): mine = lax.all_to_all(packed, 'x', 0, 0, tiled=True)]
    ppermute x6 -> x9, starting transfers between devices: 7.54 us -> 12.8 us  [in_row(): return lax.ppermute(value, 'x', [(x, (x + by) % ROW) for x in range(ROW)])]
    ppermute x6 -> x9, waiting for transfers between devices: 1.8 us -> 6.18 us  [in_row(): return lax.ppermute(value, 'x', [(x, (x + by) % ROW) for x in range(ROW)])]
    ppermute x10, waiting for transfers between devices: 17.2 us -> 14.6 us  [swap_rows(): return lax.ppermute(value, 'row', pairs + [(j, i) for i, j in pairs])]
    pallas_call x1 -> x2, Pallas kernels: 3.59 us -> 5.58 us  [prefetched(): pl.pallas_call(kernel, grid_spec=pltpu.PrefetchScalarGridSpec(num_scalar_...]
  transfers between devices with their start and end apart: 19 -> 22, of which waited for: 10 -> 9; matrix products, arithmetic and copies ran while one was open for 0% -> 0% of each run, Pallas kernels for 6% -> 6%
where the time goes in v4:
time: 117 us
  blocking collectives  41.9 us (36%)
  starting transfers between devices  40.9 us (35%)
  waiting for transfers between devices  20.8 us (18%)
  Pallas kernels  12.3 us (11%)
    ppermute x10, starting transfers between devices, swap_rows(): return lax.ppermute(value, 'row', pairs + [(j, i) for i, j in pairs])  27.6 us
    all_to_all x1, blocking collectives, local(): sums = lax.all_to_all(partial_value, 'row', 0, 0, tiled=True)  23.9 us
    all_to_all x1, blocking collectives, local(): mine = lax.all_to_all(packed, 'x', 0, 0, tiled=True)  18 us
    ppermute x10, waiting for transfers between devices, swap_rows(): return lax.ppermute(value, 'row', pairs + [(j, i) for i, j in pairs])  14.6 us
    ppermute x9, starting transfers between devices, in_row(): return lax.ppermute(value, 'x', [(x, (x + by) % ROW) for x in range(ROW)])  12.8 us
    pallas_call x12, Pallas kernels, call(): pl.pallas_call(kernel, out_shape=out_shape, in_specs=[SMEM] * scalars + [...  6.77 us
    ppermute x9, waiting for transfers between devices, in_row(): return lax.ppermute(value, 'x', [(x, (x + by) % ROW) for x in range(ROW)])  6.18 us
    pallas_call x2, Pallas kernels, prefetched(): pl.pallas_call(kernel, grid_spec=pltpu.PrefetchScalarGridSpec(num_scalar_...  5.58 us
  transfers between devices with their start and end apart: 22, of which 9 were waited for; matrix products, arithmetic and copies ran while one was open for 0% of the time, Pallas kernels for 6%

profile of v4, /device:TPU:32, one launch (start us, length us, event | category | flops | bytes accessed | tf_op | source)
XLA Modules:
  0.0 116.8 jit_solution(5784854130302670302)
XLA Ops:
  0.6 3.0 %pack.1 = f32[4,448,128]{2,1,0:T(8,128)} custom-call(s32[1]{0:T(128)} %bitcast.me, s32[1,16]{1,0:T(1,128)} %nbr.3, s32[1,16]{1,0:T(1,128)} %pat.3, f32[2,1,128,256]{3,2,1,0:T(8,128)} %coef.2, f32[1,16,128,128]{3,2,1,0:T(8,128)} %margin.2), custom_call_target="tpu_custom_call" | custom-call | flops 1000000 | bytes 1703936 | tf_op jit(solution)/shard_map/pack/pallas_call | solution.py:246
  3.6 18.0 %all_to_all.16.mine = f32[4,448,128]{2,1,0:T(8,128)S(1)} all-to-all(f32[4,448,128]{2,1,0:T(8,128)} %pack.1), channel_id=1, replica_groups=mesh['row'=32,'x'=4,'orb'=2] {'x'}, dimensions={0} | all-to-all | bytes 1835008 | tf_op jit(solution)/shard_map/all_to_all | solution.py:261
  21.9 2.6 %step.1.mine = f32[320,128]{1,0:T(8,128)} custom-call(s32[1]{0:T(128)} %bitcast.me, s32[1,16]{1,0:T(1,128)} %nbr.3, s32[1,16]{1,0:T(1,128)} %pat.3, f32[1,16,128,128]{3,2,1,0:T(8,128)} %step.2), custom_call_target="tpu_custom_call" | custom-call | flops 1000000 | bytes 655360 | tf_op jit(solution)/shard_map/step/pallas_call | solution.py:246
  25.1 2.1 %collective-permute-start.4 = (f32[320,128]{1,0:T(8,128)}, f32[320,128]{1,0:T(8,128)S(1)}, u32[]{:S(2)}, u32[]{:S(2)}) collective-permute-start(f32[320,128]{1,0:T(8,128)} %step.1.mine), channel_id=1, source_target_pairs={{0,4},{2,6},{4,0},{6,2},{1,5},{3,7},{5,1},{7,3},{8,12},{10,14},{12... | collective-permute-start | bytes 491528 | tf_op jit(solution)/shard_map/ppermute | solution.py:232
  27.2 0.8 collective-permute-start.5
  28.0 5.6 %collective-permute-start.2 = (f32[256,128]{1,0:T(8,128)S(1)}, f32[256,128]{1,0:T(8,128)S(1)}, u32[]{:S(2)}, u32[]{:S(2)}) collective-permute-start(f32[256,128]{1,0:T(8,128)S(1)} %get-tuple-element.49), channel_id=1, source_target_pairs={{8,16},{24,32},{40,48},{56,64},{72,80},{88,96},{104,112},{120,128}... | collective-permute-start | bytes 393224 | tf_op jit(solution)/shard_map/ppermute | solution.py:240
  33.6 3.0 %collective-permute-done.2.from_b = f32[256,128]{1,0:T(8,128)S(1)} collective-permute-done((f32[256,128]{1,0:T(8,128)S(1)}, f32[256,128]{1,0:T(8,128)S(1)}, u32[]{:S(2)}, u32[]{:S(2)}) %collective-permute-start.2) | collective-permute-done | bytes 131104 | tf_op jit(solution)/shard_map/ppermute | solution.py:240
  36.6 0.8 margin.3
  37.6 0.9 collective-permute-start.7
  38.5 5.3 %collective-permute-start.8 = (f32[256,128]{1,0:T(8,128)S(1)}, f32[256,128]{1,0:T(8,128)S(1)}, u32[]{:S(2)}, u32[]{:S(2)}) collective-permute-start(f32[256,128]{1,0:T(8,128)S(1)} %get-tuple-element.59), channel_id=1, source_target_pairs={{8,16},{24,32},{40,48},{56,64},{72,80},{88,96},{104,112},{120,128}... | collective-permute-start | bytes 393224 | tf_op jit(solution)/shard_map/ppermute | solution.py:240
  43.8 3.8 %collective-permute-done.8.from_b = f32[256,128]{1,0:T(8,128)S(1)} collective-permute-done((f32[256,128]{1,0:T(8,128)S(1)}, f32[256,128]{1,0:T(8,128)S(1)}, u32[]{:S(2)}, u32[]{:S(2)}) %collective-permute-start.8) | collective-permute-done | bytes 131104 | tf_op jit(solution)/shard_map/ppermute | solution.py:240
  47.6 1.1 collective-permute-start.11
  48.9 0.7 apply.3
  49.7 3.7 %collective-permute-start.10 = (f32[256,128]{1,0:T(8,128)S(1)}, f32[256,128]{1,0:T(8,128)S(1)}, u32[]{:S(2)}, u32[]{:S(2)}) collective-permute-start(f32[256,128]{1,0:T(8,128)S(1)} %get-tuple-element.63), channel_id=1, source_target_pairs={{8,16},{24,32},{40,48},{56,64},{72,80},{88,96},{104,112},{120,128}... | collective-permute-start | bytes 393224 | tf_op jit(solution)/shard_map/ppermute | solution.py:240
  53.4 3.2 %collective-permute-done.11 = f32[2,1,128,256]{3,2,0,1:T(8,128)S(1)} collective-permute-done((f32[2,1,128,256]{3,2,0,1:T(8,128)S(1)}, f32[2,1,128,256]{3,2,0,1:T(8,128)S(1)}, u32[]{:S(2)}, u32[]{:S(2)}) %collective-permute-start.11) | collective-permute-done | bytes 262176 | tf_op jit(solution)/shard_map/ppermute | solution.py:232
  56.6 1.7 %collective-permute-done.9.from_a = f32[256,128]{1,0:T(8,128)S(1)} collective-permute-done((f32[256,128]{1,0:T(8,128)S(1)}, f32[256,128]{1,0:T(8,128)S(1)}, u32[]{:S(2)}, u32[]{:S(2)}) %collective-permute-start.9) | collective-permute-done | bytes 131104 | tf_op jit(solution)/shard_map/ppermute | solution.py:240
  58.4 2.1 %collective-permute-start.14 = (f32[2,1,128,256]{3,2,0,1:T(8,128)S(1)}, f32[2,1,128,256]{3,2,0,1:T(8,128)S(1)}, u32[]{:S(2)}, u32[]{:S(2)}) collective-permute-start(f32[2,1,128,256]{3,2,0,1:T(8,128)S(1)} %bitcast.13), channel_id=1, source_target_pairs={{0,6},{2,0},{4,2},{6,4},{1,7},{3,1},{5,3},{7,5},{8,14},{10,8},{12,... | collective-permute-start | bytes 786440 | tf_op jit(solution)/shard_map/ppermute | solution.py:232
  60.5 1.4 %collective-permute-start.16 = (f32[2,1,128,256]{3,2,0,1:T(8,128)S(1)}, f32[2,1,128,256]{3,2,0,1:T(8,128)S(1)}, u32[]{:S(2)}, u32[]{:S(2)}) collective-permute-start(f32[2,1,128,256]{3,2,0,1:T(8,128)S(1)} %bitcast.14), channel_id=1, source_target_pairs={{0,4},{2,6},{4,0},{6,2},{1,5},{3,7},{5,1},{7,3},{8,12},{10,14},{12... | collective-permute-start | bytes 786440 | tf_op jit(solution)/shard_map/ppermute | solution.py:232
  61.9 0.7 apply.4
  62.8 6.6 %collective-permute-start.13 = (f32[256,128]{1,0:T(8,128)S(1)}, f32[256,128]{1,0:T(8,128)S(1)}, u32[]{:S(2)}, u32[]{:S(2)}) collective-permute-start(f32[256,128]{1,0:T(8,128)S(1)} %get-tuple-element.69), channel_id=1, source_target_pairs={{8,16},{24,32},{40,48},{56,64},{72,80},{88,96},{104,112},{120,128}... | collective-permute-start | bytes 393224 | tf_op jit(solution)/shard_map/ppermute | solution.py:240
  69.3 2.9 %collective-permute-done.13.from_b = f32[256,128]{1,0:T(8,128)S(1)} collective-permute-done((f32[256,128]{1,0:T(8,128)S(1)}, f32[256,128]{1,0:T(8,128)S(1)}, u32[]{:S(2)}, u32[]{:S(2)}) %collective-permute-start.13) | collective-permute-done | bytes 131104 | tf_op jit(solution)/shard_map/ppermute | solution.py:240
  73.5 5.1 %collective-permute-start.18 = (f32[256,128]{1,0:T(8,128)S(1)}, f32[256,128]{1,0:T(8,128)S(1)}, u32[]{:S(2)}, u32[]{:S(2)}) collective-permute-start(f32[256,128]{1,0:T(8,128)S(1)} %get-tuple-element.82), channel_id=1, source_target_pairs={{8,16},{24,32},{40,48},{56,64},{72,80},{88,96},{104,112},{120,128}... | collective-permute-start | bytes 393224 | tf_op jit(solution)/shard_map/ppermute | solution.py:240
  78.6 0.7 old_parts.1
  79.4 3.1 %collective-permute-done.18.from_b = f32[256,128]{1,0:T(8,128)S(1)} collective-permute-done((f32[256,128]{1,0:T(8,128)S(1)}, f32[256,128]{1,0:T(8,128)S(1)}, u32[]{:S(2)}, u32[]{:S(2)}) %collective-permute-start.18) | collective-permute-done | bytes 131104 | tf_op jit(solution)/shard_map/ppermute | solution.py:240
  83.2 1.0 project.1
  84.2 23.9 %all_to_all.17 = f32[32,16,128]{2,1,0:T(8,128)S(1)} all-to-all(f32[32,16,128]{2,1,0:T(8,128)S(1)} %bitcast.23), channel_id=1, replica_groups=mesh['row'=32,'x'=4,'orb'=2] {'row'}, dimensions={0} | all-to-all | bytes 524288 | tf_op jit(solution)/shard_map/all_to_all | solution.py:311
  108.4 3.2 %collective-permute-start.20 = (f32[136,128]{1,0:T(8,128)S(1)}, f32[136,128]{1,0:T(8,128)S(1)}, u32[]{:S(2)}, u32[]{:S(2)}) collective-permute-start(f32[136,128]{1,0:T(8,128)S(1)} %get-tuple-element.86), channel_id=1, source_target_pairs={{0,4},{2,6},{4,0},{6,2},{1,5},{3,7},{5,1},{7,3},{8,12},{10,14},{12... | collective-permute-start | bytes 208904 | tf_op jit(solution)/shard_map/ppermute | solution.py:232
  111.6 1.3 %collective-permute-start.21 = (f32[136,128]{1,0:T(8,128)S(1)}, f32[136,128]{1,0:T(8,128)S(1)}, u32[]{:S(2)}, u32[]{:S(2)}) collective-permute-start(f32[136,128]{1,0:T(8,128)S(1)} %get-tuple-element.87), channel_id=1, source_target_pairs={{0,6},{2,0},{4,2},{6,4},{1,7},{3,1},{5,3},{7,5},{8,14},{10,8},{12,... | collective-permute-start | bytes 208904 | tf_op jit(solution)/shard_map/ppermute | solution.py:232
  113.0 0.9 collective-permute-done.19.b1
  113.8 0.8 collective-permute-done.20.b2
  114.6 1.3 %collective-permute-done.21.b3 = f32[136,128]{1,0:T(8,128)S(1)} collective-permute-done((f32[136,128]{1,0:T(8,128)S(1)}, f32[136,128]{1,0:T(8,128)S(1)}, u32[]{:S(2)}, u32[]{:S(2)}) %collective-permute-start.21) | collective-permute-done | bytes 69664 | tf_op jit(solution)/shard_map/ppermute | solution.py:232
  115.9 0.9 finish.1
  (33 shorter events, 3.6 us)
Async XLA Ops:
  21.6 15.0 %collective-permute-start = (f32[4,448,128]{2,1,0:T(8,128)S(1)}, f32[4,448,128]{2,1,0:T(8,128)S(1)}, u32[]{:S(2)}, u32[]{:S(2)}) collective-permute-start(f32[4,448,128]{2,1,0:T(8,128)S(1)} %all_to_all.16.mine), channel_id=1, source_target_pairs={{0,1},{1,0},{2,3},{3,2},{4,5},{5,4},{6,7},{7,6},{8,9},{9,8},{10,11... | collective-permute-start | bytes 2752520 | tf_op jit(solution)/shard_map/ppermute | solution.py:235
  21.7 6.2 %collective-permute-start.1 = (f32[256,128]{1,0:T(8,128)S(1)}, f32[256,128]{1,0:T(8,128)S(1)}, u32[]{:S(2)}, u32[]{:S(2)}) collective-permute-start(f32[256,128]{1,0:T(8,128)S(1)} %get-tuple-element.48), channel_id=1, source_target_pairs={{0,8},{16,24},{32,40},{48,56},{64,72},{80,88},{96,104},{112,120},{... | collective-permute-start | bytes 393224 | tf_op jit(solution)/shard_map/ppermute | solution.py:240
  24.5 12.9 %copy-start.1 = (f32[320,128]{1,0:T(8,128)S(1)}, f32[320,128]{1,0:T(8,128)}, u32[]{:S(2)}) copy-start(f32[320,128]{1,0:T(8,128)} %step.1.mine) | copy-start | bytes 491524
  24.5 12.9 %collective-permute-start.3 = (f32[320,128]{1,0:T(8,128)}, f32[320,128]{1,0:T(8,128)S(1)}, u32[]{:S(2)}, u32[]{:S(2)}) collective-permute-start(f32[320,128]{1,0:T(8,128)} %step.1.mine), channel_id=1, source_target_pairs={{0,2},{2,4},{4,6},{6,0},{1,3},{3,5},{5,7},{7,1},{8,10},{10,12},{12... | collective-permute-start | bytes 491528 | tf_op jit(solution)/shard_map/ppermute | solution.py:232
  25.1 12.3 %collective-permute-start.4 = (f32[320,128]{1,0:T(8,128)}, f32[320,128]{1,0:T(8,128)S(1)}, u32[]{:S(2)}, u32[]{:S(2)}) collective-permute-start(f32[320,128]{1,0:T(8,128)} %step.1.mine), channel_id=1, source_target_pairs={{0,4},{2,6},{4,0},{6,2},{1,5},{3,7},{5,1},{7,3},{8,12},{10,14},{12... | collective-permute-start | bytes 491528 | tf_op jit(solution)/shard_map/ppermute | solution.py:232
  27.2 10.3 %collective-permute-start.5 = (f32[320,128]{1,0:T(8,128)}, f32[320,128]{1,0:T(8,128)S(1)}, u32[]{:S(2)}, u32[]{:S(2)}) collective-permute-start(f32[320,128]{1,0:T(8,128)} %step.1.mine), channel_id=1, source_target_pairs={{0,6},{2,0},{4,2},{6,4},{1,7},{3,1},{5,3},{7,5},{8,14},{10,8},{12,... | collective-permute-start | bytes 491528 | tf_op jit(solution)/shard_map/ppermute | solution.py:232
  28.0 8.7 %collective-permute-start.2 = (f32[256,128]{1,0:T(8,128)S(1)}, f32[256,128]{1,0:T(8,128)S(1)}, u32[]{:S(2)}, u32[]{:S(2)}) collective-permute-start(f32[256,128]{1,0:T(8,128)S(1)} %get-tuple-element.49), channel_id=1, source_target_pairs={{8,16},{24,32},{40,48},{56,64},{72,80},{88,96},{104,112},{120,128}... | collective-permute-start | bytes 393224 | tf_op jit(solution)/shard_map/ppermute | solution.py:240
  37.5 10.1 %copy-start = (f32[2,1,128,256]{3,2,1,0:T(8,128)S(1)}, f32[2,1,128,256]{3,2,1,0:T(8,128)}, u32[]{:S(2)}) copy-start(f32[2,1,128,256]{3,2,1,0:T(8,128)} %coef.2) | copy-start | bytes 786436
  37.5 11.2 %collective-permute-start.6 = (f32[4,320,128]{2,1,0:T(8,128)S(1)}, f32[4,320,128]{2,1,0:T(8,128)S(1)}, u32[]{:S(2)}, u32[]{:S(2)}) collective-permute-start(f32[4,320,128]{2,1,0:T(8,128)S(1)} %step_row.1.mine), channel_id=1, source_target_pairs={{0,1},{1,0},{2,3},{3,2},{4,5},{5,4},{6,7},{7,6},{8,9},{9,8},{10,11... | collective-permute-start | bytes 1966088 | tf_op jit(solution)/shard_map/ppermute | solution.py:235
  37.6 6.1 %collective-permute-start.7 = (f32[256,128]{1,0:T(8,128)S(1)}, f32[256,128]{1,0:T(8,128)S(1)}, u32[]{:S(2)}, u32[]{:S(2)}) collective-permute-start(f32[256,128]{1,0:T(8,128)S(1)} %get-tuple-element.58), channel_id=1, source_target_pairs={{0,8},{16,24},{32,40},{48,56},{64,72},{80,88},{96,104},{112,120},{... | collective-permute-start | bytes 393224 | tf_op jit(solution)/shard_map/ppermute | solution.py:240
  38.5 9.1 %collective-permute-start.8 = (f32[256,128]{1,0:T(8,128)S(1)}, f32[256,128]{1,0:T(8,128)S(1)}, u32[]{:S(2)}, u32[]{:S(2)}) collective-permute-start(f32[256,128]{1,0:T(8,128)S(1)} %get-tuple-element.59), channel_id=1, source_target_pairs={{8,16},{24,32},{40,48},{56,64},{72,80},{88,96},{104,112},{120,128}... | collective-permute-start | bytes 393224 | tf_op jit(solution)/shard_map/ppermute | solution.py:240
  47.6 9.1 %collective-permute-start.11 = (f32[2,1,128,256]{3,2,0,1:T(8,128)S(1)}, f32[2,1,128,256]{3,2,0,1:T(8,128)S(1)}, u32[]{:S(2)}, u32[]{:S(2)}) collective-permute-start(f32[2,1,128,256]{3,2,0,1:T(8,128)S(1)} %bitcast.12), channel_id=1, source_target_pairs={{0,2},{2,4},{4,6},{6,0},{1,3},{3,5},{5,7},{7,1},{8,10},{10,12},{12... | collective-permute-start | bytes 786440 | tf_op jit(solution)/shard_map/ppermute | solution.py:232
  49.7 7.0 %collective-permute-start.10 = (f32[256,128]{1,0:T(8,128)S(1)}, f32[256,128]{1,0:T(8,128)S(1)}, u32[]{:S(2)}, u32[]{:S(2)}) collective-permute-start(f32[256,128]{1,0:T(8,128)S(1)} %get-tuple-element.63), channel_id=1, source_target_pairs={{8,16},{24,32},{40,48},{56,64},{72,80},{88,96},{104,112},{120,128}... | collective-permute-start | bytes 393224 | tf_op jit(solution)/shard_map/ppermute | solution.py:240
  53.3 5.1 %collective-permute-start.9 = (f32[256,128]{1,0:T(8,128)S(1)}, f32[256,128]{1,0:T(8,128)S(1)}, u32[]{:S(2)}, u32[]{:S(2)}) collective-permute-start(f32[256,128]{1,0:T(8,128)S(1)} %get-tuple-element.62), channel_id=1, source_target_pairs={{0,8},{16,24},{32,40},{48,56},{64,72},{80,88},{96,104},{112,120},{... | collective-permute-start | bytes 393224 | tf_op jit(solution)/shard_map/ppermute | solution.py:240
  58.4 13.9 %collective-permute-start.14 = (f32[2,1,128,256]{3,2,0,1:T(8,128)S(1)}, f32[2,1,128,256]{3,2,0,1:T(8,128)S(1)}, u32[]{:S(2)}, u32[]{:S(2)}) collective-permute-start(f32[2,1,128,256]{3,2,0,1:T(8,128)S(1)} %bitcast.13), channel_id=1, source_target_pairs={{0,6},{2,0},{4,2},{6,4},{1,7},{3,1},{5,3},{7,5},{8,14},{10,8},{12,... | collective-permute-start | bytes 786440 | tf_op jit(solution)/shard_map/ppermute | solution.py:232
  60.5 11.8 %collective-permute-start.16 = (f32[2,1,128,256]{3,2,0,1:T(8,128)S(1)}, f32[2,1,128,256]{3,2,0,1:T(8,128)S(1)}, u32[]{:S(2)}, u32[]{:S(2)}) collective-permute-start(f32[2,1,128,256]{3,2,0,1:T(8,128)S(1)} %bitcast.14), channel_id=1, source_target_pairs={{0,4},{2,6},{4,0},{6,2},{1,5},{3,7},{5,1},{7,3},{8,12},{10,14},{12... | collective-permute-start | bytes 786440 | tf_op jit(solution)/shard_map/ppermute | solution.py:232
  62.7 6.7 %collective-permute-start.12 = (f32[256,128]{1,0:T(8,128)S(1)}, f32[256,128]{1,0:T(8,128)S(1)}, u32[]{:S(2)}, u32[]{:S(2)}) collective-permute-start(f32[256,128]{1,0:T(8,128)S(1)} %get-tuple-element.68), channel_id=1, source_target_pairs={{0,8},{16,24},{32,40},{48,56},{64,72},{80,88},{96,104},{112,120},{... | collective-permute-start | bytes 393224 | tf_op jit(solution)/shard_map/ppermute | solution.py:240
  62.8 9.5 %collective-permute-start.13 = (f32[256,128]{1,0:T(8,128)S(1)}, f32[256,128]{1,0:T(8,128)S(1)}, u32[]{:S(2)}, u32[]{:S(2)}) collective-permute-start(f32[256,128]{1,0:T(8,128)S(1)} %get-tuple-element.69), channel_id=1, source_target_pairs={{8,16},{24,32},{40,48},{56,64},{72,80},{88,96},{104,112},{120,128}... | collective-permute-start | bytes 393224 | tf_op jit(solution)/shard_map/ppermute | solution.py:240
  72.3 6.3 %collective-permute-start.17 = (f32[4,2,128,256]{3,2,1,0:T(8,128)S(1)}, f32[4,2,128,256]{3,2,1,0:T(8,128)S(1)}, u32[]{:S(2)}, u32[]{:S(2)}) collective-permute-start(f32[4,2,128,256]{3,2,1,0:T(8,128)S(1)} %pad_maximum_fusion), channel_id=1, source_target_pairs={{0,1},{1,0},{2,3},{3,2},{4,5},{5,4},{6,7},{7,6},{8,9},{9,8},{10,11... | collective-permute-start | bytes 3145736 | tf_op jit(solution)/shard_map/ppermute | solution.py:235
  73.4 6.0 %collective-permute-start.15 = (f32[256,128]{1,0:T(8,128)S(1)}, f32[256,128]{1,0:T(8,128)S(1)}, u32[]{:S(2)}, u32[]{:S(2)}) collective-permute-start(f32[256,128]{1,0:T(8,128)S(1)} %get-tuple-element.74), channel_id=1, source_target_pairs={{0,8},{16,24},{32,40},{48,56},{64,72},{80,88},{96,104},{112,120},{... | collective-permute-start | bytes 393224 | tf_op jit(solution)/shard_map/ppermute | solution.py:240
  73.5 9.0 %collective-permute-start.18 = (f32[256,128]{1,0:T(8,128)S(1)}, f32[256,128]{1,0:T(8,128)S(1)}, u32[]{:S(2)}, u32[]{:S(2)}) collective-permute-start(f32[256,128]{1,0:T(8,128)S(1)} %get-tuple-element.82), channel_id=1, source_target_pairs={{8,16},{24,32},{40,48},{56,64},{72,80},{88,96},{104,112},{120,128}... | collective-permute-start | bytes 393224 | tf_op jit(solution)/shard_map/ppermute | solution.py:240
  108.2 5.6 %collective-permute-start.19 = (f32[136,128]{1,0:T(8,128)S(1)}, f32[136,128]{1,0:T(8,128)S(1)}, u32[]{:S(2)}, u32[]{:S(2)}) collective-permute-start(f32[136,128]{1,0:T(8,128)S(1)} %get-tuple-element.85), channel_id=1, source_target_pairs={{0,2},{2,4},{4,6},{6,0},{1,3},{3,5},{5,7},{7,1},{8,10},{10,12},{12... | collective-permute-start | bytes 208904 | tf_op jit(solution)/shard_map/ppermute | solution.py:232
  108.4 6.3 %collective-permute-start.20 = (f32[136,128]{1,0:T(8,128)S(1)}, f32[136,128]{1,0:T(8,128)S(1)}, u32[]{:S(2)}, u32[]{:S(2)}) collective-permute-start(f32[136,128]{1,0:T(8,128)S(1)} %get-tuple-element.86), channel_id=1, source_target_pairs={{0,4},{2,6},{4,0},{6,2},{1,5},{3,7},{5,1},{7,3},{8,12},{10,14},{12... | collective-permute-start | bytes 208904 | tf_op jit(solution)/shard_map/ppermute | solution.py:232
  111.6 4.3 %collective-permute-start.21 = (f32[136,128]{1,0:T(8,128)S(1)}, f32[136,128]{1,0:T(8,128)S(1)}, u32[]{:S(2)}, u32[]{:S(2)}) collective-permute-start(f32[136,128]{1,0:T(8,128)S(1)} %get-tuple-element.87), channel_id=1, source_target_pairs={{0,6},{2,0},{4,2},{6,4},{1,7},{3,1},{5,3},{7,5},{8,14},{10,8},{12,... | collective-permute-start | bytes 208904 | tf_op jit(solution)/shard_map/ppermute | solution.py:232

commit v5 on v4

v5 whole, which is shorter than its diff:
```python
import functools

import jax
import jax.numpy as jnp
from jax import lax
from jax.experimental import pallas as pl
from jax.experimental.pallas import tpu as pltpu
from jax.sharding import Mesh, PartitionSpec as P

ORDER = 4
ROW = 4
BAND = 5
B = 128
HALF = B // 2
F32 = jnp.float32
BF16 = jnp.bfloat16

SMEM = pl.BlockSpec(memory_space=pltpu.SMEM)
VMEM = pl.BlockSpec(memory_space=pltpu.VMEM)


def cost(flops, moved):
    return pl.CostEstimate(flops=flops, bytes_accessed=moved, transcendentals=0)


def split(value):
    high = value.astype(BF16)
    return high, (value - high.astype(F32)).astype(BF16)


def product(a_high, a_low, b_high, b_low):
    dot = functools.partial(jnp.dot, preferred_element_type=F32)
    return dot(a_high, b_high) + (dot(a_high, b_low) + dot(a_low, b_high))


def turned(value):
    lane = lax.broadcasted_iota(jnp.int32, value.shape, 1)
    rolled = pltpu.roll(value, HALF, axis=1)
    return jnp.where(lane < HALF, rolled, -rolled)


def member(me):
    return lax.rem(lax.div(me[0], 2), ROW), lax.rem(me[0], 2)


def turn_to(q, x):
    return lax.rem(q - x + ROW, ROW)


def parity(me):
    return lax.rem(lax.div(me[0], 2 * ROW), 2)


def pack_kernel(me, nbr, pat, coef, margin, step, out):
    chunk = pl.program_id(0)

    @pl.when(chunk == 0)
    def _():
        for q in range(ROW):
            columns = slice(q * HALF, (q + 1) * HALF)
            out[q, :B, :] = jnp.concatenate([coef[0, 0, :, columns], coef[1, 0, :, columns]], axis=1)

    first = lax.div(me[0], 2) - 2
    size = margin.shape[2]
    for i, source in enumerate((margin, step)):
        totals = [jnp.zeros((size, B), F32)] * BAND
        for k in range(source.shape[1]):
            block = source[0, k]
            weight = F32(1.0) if k == 0 else pat[0, k].astype(F32)
            for d in range(BAND):
                totals[d] = totals[d] + block * jnp.where(nbr[0, k] == first + d, weight, F32(0.0))
        for d in range(BAND):
            start = pl.multiple_of(B + (i * BAND + d) * HALF + chunk * size, size)
            for q in range(ROW):
                out[q, pl.ds(start, size), :] = totals[d]


def place_half(out, q, place, source, first):
    rows = pl.ds(pl.multiple_of(place * HALF, HALF), HALF)
    for d in range(BAND):
        start = first + d * HALF
        yield q, rows, slice(d * B, (d + 1) * B), source(slice(start, start + HALF))


def edge_kernel(me, mine, to_a, to_b):
    odd = parity(me)
    for out, first in ((to_a, 2 - 2 * odd), (to_b, 2 * odd)):
        for q in range(2):
            out[q * B : (q + 1) * B, :] = mine[first + q, :B, :]
            start = 2 * B + q * BAND * HALF
            out[start : start + BAND * HALF, :] = mine[first + q, B + BAND * HALF :, :]


def window(odd, from_a, from_b, own, v_high, v_low):
    reach, size = from_a.shape[0], own.shape[0]
    v_high[reach : reach + size, :], v_low[reach : reach + size, :] = split(own)
    for start, tile in (((1 - odd) * (reach + size), from_a), (odd * (reach + size), from_b)):
        rows = pl.ds(pl.multiple_of(start, B), reach)
        v_high[rows, :], v_low[rows, :] = split(tile)


def margin_kernel(me, mine, other, from_a, from_b, out, full, v_high, v_low):
    _, core = member(me)
    own = [mine[q, :B, :] for q in range(ROW)]
    window(parity(me), from_a[: 2 * B, :], from_b[: 2 * B, :], jnp.concatenate(own, axis=0), v_high, v_low)
    for q in range(ROW):
        for place, ref in ((core, mine), (1 - core, other)):
            for _, rows, columns, tile in place_half(full, q, place, lambda at: ref[q, at, :], B):
                full[q, rows, columns] = tile
    for q in range(ROW):
        m_high, m_low = split(full[q])
        rows = slice(q * B, (q + BAND) * B)
        out[q * B : (q + 1) * B, :] = own[q] + product(m_high, m_low, v_high[rows], v_low[rows])


def parts_kernel(me, mine, other, from_a, from_b, other_a, other_b, out_high, out_low):
    _, core = member(me)
    odd = parity(me)
    for q in range(ROW):
        for place, ref in ((core, mine), (1 - core, other)):
            for to, rows, columns, tile in place_half(out_high, q + 2, place, lambda at: ref[q, at, :], B + BAND * HALF):
                out_high[to, rows, columns], out_low[to, rows, columns] = split(tile)
    for start, own, across in (((1 - odd) * 6, from_a, other_a), (odd * 6, from_b, other_b)):
        for q in range(2):
            for place, ref in ((core, own), (1 - core, across)):
                first = 2 * B + q * BAND * HALF
                for to, rows, columns, tile in place_half(out_high, start + q, place, lambda at: ref[at, :], first):
                    out_high[to, rows, columns], out_low[to, rows, columns] = split(tile)


def two_steps(n, me, m_high, m_low, from_a, from_b, own, v_high, v_low, w_high, w_low):
    window(parity(me), from_a[...], from_b[...], own[...], v_high, v_low)
    firsts = []
    for q in range(2 * ROW):
        rows = slice(q * B, (q + BAND) * B)
        value = product(m_high[q], m_low[q], v_high[rows], v_low[rows]) * F32(1.0 / n)
        w_high[q * B : (q + 1) * B, :], w_low[q * B : (q + 1) * B, :] = split(value)
        firsts.append(value)
    for q in range(ROW):
        rows = slice(q * B, (q + BAND) * B)
        second = product(m_high[q + 2], m_low[q + 2], w_high[rows], w_low[rows]) * F32(1.0 / (n + 1))
        yield q, firsts[q + 2], second


def two_kernel(n, me, m_high, m_low, from_a, from_b, own, first, second, *scratch):
    for q, a, b in two_steps(n, me, m_high, m_low, from_a, from_b, own, *scratch):
        first[q * B : (q + 1) * B, :] = a
        second[q * B : (q + 1) * B, :] = b


def last_kernel(n, me, m_high, m_low, from_a, from_b, own, y0, y1, out, *scratch):
    x, _ = member(me)
    for q, y3, y4 in two_steps(n, me, m_high, m_low, from_a, from_b, own, *scratch):
        rows = slice(q * B, (q + 1) * B)
        out[turn_to(q, x)] = (y0[rows, :] - own[rows, :]) + y4 + turned(y1[rows, :] - y3)


def old_kernel(me, coef, c1, c2, c3, other, out_high, out_low):
    x, core = member(me)
    width = coef.shape[3]
    for j, ref in enumerate((coef, c1, c2, c3)):
        q = turn_to(x, j)
        for part in range(2):
            for place, tile in ((core, ref[part, 0]), (1 - core, other[j, part])):
                rows = pl.ds(pl.multiple_of(place * width, width), width)
                columns = pl.ds(pl.multiple_of((part * ROW + q) * B, B), B)
                out_high[rows, columns], out_low[rows, columns] = split(jnp.transpose(tile))


def project_kernel(me, old_high, old_low, new, out):
    x, _ = member(me)
    tiles = [new[turn_to(q, x)] for q in range(ROW)]
    v_high, v_low = split(jnp.concatenate(tiles + [turned(t) for t in tiles], axis=0))
    out[...] = product(old_high[...], old_low[...], v_high, v_low)


def tail_kernel(scale, me, sums, new, *outs):
    x, _ = member(me)
    share = 4
    total = jnp.sum(sums[...].reshape(-1, ROW * share, B), axis=0) * scale
    for j, out in enumerate(outs):
        out[:B, :] = new[j]
        for q in range(ROW):

            @pl.when(q == lax.rem(x + j, ROW))
            def _():
                out[B : B + share, :] = total[q * share : (q + 1) * share, :]


def finish_kernel(me, mine, b1, b2, b3, propagated, owned, held):
    x, _ = member(me)
    share = owned.shape[1]
    for j, ref in enumerate((mine, b1, b2, b3)):
        held[turn_to(x, j)] = ref[...]
    for q in range(ROW):
        columns = slice(q * HALF, (q + 1) * HALF)
        for part in range(2):
            lanes = slice(part * HALF, (part + 1) * HALF)
            propagated[part, 0, :, columns] = held[q, :B, lanes]
            owned[part, :, columns] = held[q, B : B + share, lanes]


def local(rows, coefficients, margin, step_matrix, neighbours, pattern):
    width = coefficients.shape[3]
    domains = rows * ROW
    me = lax.axis_index(("row", "x", "orb")).astype(jnp.int32).reshape(1)
    struct = jax.ShapeDtypeStruct
    tile_bytes = 4 * B * B
    step_flops = 2 * 3 * B * BAND * B * B

    def call(kernel, out_shape, args, flops, moved, name, scratch=(), scalars=1):
        return pl.pallas_call(
            kernel,
            out_shape=out_shape,
            in_specs=[SMEM] * scalars + [VMEM] * (len(args) - scalars),
            out_specs=jax.tree.map(lambda _: VMEM, out_shape),
            scratch_shapes=list(scratch),
            cost_estimate=cost(flops, moved * tile_bytes),
            name=name,
            compiler_params=pltpu.CompilerParams(vmem_limit_bytes=40 * 2**20),
        )(*args)

    def in_row(value, by):
        return lax.ppermute(value, "x", [(x, (x + by) % ROW) for x in range(ROW)])

    def swap(value):
        return lax.ppermute(value, "orb", [(0, 1), (1, 0)])

    def exchange(to_a, to_b):
        def swap_rows(value, first):
            pairs = [(r, r + 1) for r in range(first, rows - 1, 2)]
            return lax.ppermute(value, "row", pairs + [(j, i) for i, j in pairs])

        return [swap_rows(to_a, 0), swap_rows(to_b, 1)]

    chunks = 4
    slots = neighbours.shape[1]
    half_block = pl.BlockSpec(
        (1, slots, HALF // chunks, B), lambda i, where, nbr, pat: (0, 0, lax.rem(where[0], 2) * chunks + i, 0)
    )
    packed_shape = (ROW, B + 2 * BAND * HALF, B)
    packed = pl.pallas_call(
        pack_kernel,
        grid_spec=pltpu.PrefetchScalarGridSpec(
            num_scalar_prefetch=3,
            grid=(chunks,),
            in_specs=[pl.BlockSpec(coefficients.shape, lambda i, *_: (0, 0, 0, 0)), half_block, half_block],
            out_specs=pl.BlockSpec(packed_shape, lambda i, *_: (0, 0, 0)),
        ),
        out_shape=struct(packed_shape, F32),
        cost_estimate=cost(10**6, 44 * tile_bytes),
        name="pack",
    )(me, neighbours, pattern, coefficients, margin, step_matrix)
    mine = lax.all_to_all(packed, "x", 0, 0, tiled=True)

    state = struct((ROW * B, B), F32)
    edge = struct((2 * B + 2 * BAND * HALF, B), F32)
    edges = call(edge_kernel, [edge, edge], [me, mine], 10**5, 28, "edges")
    *edges, held = lax.optimization_barrier((*edges, mine))
    other = swap(held)
    from_a, from_b = exchange(*edges)
    y0 = call(
        margin_kernel, state, [me, mine, other, from_a, from_b], ROW * step_flops, 60, "margin",
        scratch=[pltpu.VMEM((ROW, B, BAND * B), F32)] + [pltpu.VMEM((2 * ROW * B, B), BF16)] * 2,
    )
    parts_type = struct((2 * ROW, B, BAND * B), BF16)
    step = list(
        call(
            parts_kernel, [parts_type, parts_type], [me, mine, other, from_a, from_b, swap(from_a), swap(from_b)],
            10**6, 80, "step_parts",
        )
    )
    scratch = [pltpu.VMEM((3 * ROW * B, B), BF16)] * 2 + [pltpu.VMEM((2 * ROW * B, B), BF16)] * 2
    arrived = exchange(y0, y0)

    _, held = lax.optimization_barrier((step[0], coefficients))
    old = [coefficients] + [in_row(held, j) for j in range(1, ROW)]
    y1, y2 = call(
        functools.partial(two_kernel, 1), [state, state], [me] + step + arrived + [y0], 3 * ROW * step_flops, 64,
        "two", scratch=scratch,
    )
    _, *old = lax.optimization_barrier((y2, *old))
    arrived = exchange(y2, y2)
    old_stack = jnp.stack([o[:, 0] for o in old])
    old_type = struct((2 * width, 2 * ROW * B), BF16)
    old_high, old_low = call(
        old_kernel, [old_type, old_type], [me] + old + [swap(old_stack)], 10**6, 64, "old_parts"
    )
    arrived[0], old_high = lax.optimization_barrier((arrived[0], old_high))
    new = call(
        functools.partial(last_kernel, 3), struct((ROW, B, B), F32), [me] + step + arrived + [y2, y0, y1],
        3 * ROW * step_flops, 72, "last", scratch=scratch,
    )
    partial_value = call(
        project_kernel, struct((2 * width, B), F32), [me, old_high, old_low, new],
        2 * 3 * 2 * width * 2 * ROW * B * B, 44, "project",
    )
    sums = lax.all_to_all(partial_value, "row", 0, 0, tiled=True)
    share = 2 * width // domains
    sent = struct((B + 2 * share, B), F32)
    tail = call(
        functools.partial(tail_kernel, 1.0 / (domains * B)), [sent] * ROW, [me, sums, new], 10**5, 12, "tail"
    )
    tail = [tail[0]] + [in_row(tail[j], j) for j in range(1, ROW)]
    return call(
        finish_kernel, (struct((2, 1, B, width), F32), struct((2, share, width), F32)), [me] + tail, 10**5, 8,
        "finish", scratch=[pltpu.VMEM((ROW, B + 2 * share, B), F32)],
    )


def solution(mesh):
    rows = mesh.shape["space"] // ROW
    grouped = Mesh(mesh.devices.reshape(rows, ROW, mesh.shape["orb"]), ("row", "x", "orb"))
    space = ("row", "x")
    return jax.shard_map(
        functools.partial(local, rows),
        mesh=grouped,
        in_specs=(
            P(None, space, None, "orb"),
            P(space, None, None, None),
            P(space, None, None, None),
            P(space, None),
            P(space, None),
        ),
        out_specs=(P(None, space, None, "orb"), P(None, space, "orb")),
        check_vma=False,
    )
```

time: 117 us -> 117 us (level)
  starting transfers between devices: 40.9 us -> 25 us
  waiting for transfers between devices: 20.8 us -> 31.2 us
  blocking collectives: 41.9 us -> 47.6 us
    ppermute x10 -> x6, starting transfers between devices: 27.6 us -> 17.3 us  [swap_rows(): return lax.ppermute(value, 'row', pairs + [(j, i) for i, j in pairs])]
    all_to_all x1, blocking collectives: 18 us -> 25 us  [local(): mine = lax.all_to_all(packed, 'x', 0, 0, tiled=True)]
    ppermute x9 -> x6, waiting for transfers between devices: 6.18 us -> 12 us  [in_row(): return lax.ppermute(value, 'x', [(x, (x + by) % ROW) for x in range(ROW)])]
    ppermute x9 -> x6, starting transfers between devices: 12.8 us -> 7.5 us  [in_row(): return lax.ppermute(value, 'x', [(x, (x + by) % ROW) for x in range(ROW)])]
    ppermute x10 -> x6, waiting for transfers between devices: 14.6 us -> 19.2 us  [swap_rows(): return lax.ppermute(value, 'row', pairs + [(j, i) for i, j in pairs])]
    all_to_all x1, blocking collectives: 23.9 us -> 22.6 us  [local(): sums = lax.all_to_all(partial_value, 'row', 0, 0, tiled=True)]
    pallas_call x12 -> x9, Pallas kernels: 6.77 us -> 7.59 us  [call(): pl.pallas_call(kernel, out_shape=out_shape, in_specs=[SMEM] * scalars + [...]
    pallas_call x2 -> x1, Pallas kernels: 5.58 us -> 4.77 us  [local(): pl.pallas_call(pack_kernel, grid_spec=pltpu.PrefetchScalarGridSpec(num_sc...]
  transfers between devices with their start and end apart: 22 -> 16, of which waited for: 9 -> 10; matrix products, arithmetic and copies ran while one was open for 0% -> 0% of each run, Pallas kernels for 6% -> 3%
where the time goes in v5:
time: 117 us
  blocking collectives  47.6 us (41%)
  waiting for transfers between devices  31.2 us (27%)
  starting transfers between devices  25 us (21%)
  Pallas kernels  12.4 us (11%)
    all_to_all x1, blocking collectives, local(): mine = lax.all_to_all(packed, 'x', 0, 0, tiled=True)  25 us
    all_to_all x1, blocking collectives, local(): sums = lax.all_to_all(partial_value, 'row', 0, 0, tiled=True)  22.6 us
    ppermute x6, waiting for transfers between devices, swap_rows(): return lax.ppermute(value, 'row', pairs + [(j, i) for i, j in pairs])  19.2 us
    ppermute x6, starting transfers between devices, swap_rows(): return lax.ppermute(value, 'row', pairs + [(j, i) for i, j in pairs])  17.3 us
    ppermute x6, waiting for transfers between devices, in_row(): return lax.ppermute(value, 'x', [(x, (x + by) % ROW) for x in range(ROW)])  12 us
    pallas_call x9, Pallas kernels, call(): pl.pallas_call(kernel, out_shape=out_shape, in_specs=[SMEM] * scalars + [...  7.59 us
    ppermute x6, starting transfers between devices, in_row(): return lax.ppermute(value, 'x', [(x, (x + by) % ROW) for x in range(ROW)])  7.5 us
    pallas_call x1, Pallas kernels, local(): pl.pallas_call(pack_kernel, grid_spec=pltpu.PrefetchScalarGridSpec(num_sc...  4.77 us
  transfers between devices with their start and end apart: 16, of which 10 were waited for; matrix products, arithmetic and copies ran while one was open for 0% of the time, Pallas kernels for 3%

profile of v5, /device:TPU:32, one launch (start us, length us, event | category | flops | bytes accessed | tf_op | source)
XLA Modules:
  0.0 117.0 jit_solution(16071807989565701543)
XLA Ops:
  0.6 4.8 %pack.1 = f32[4,768,128]{2,1,0:T(8,128)} custom-call(s32[1]{0:T(128)} %bitcast.me, s32[1,16]{1,0:T(1,128)} %nbr.1, s32[1,16]{1,0:T(1,128)} %pat.1, f32[2,1,128,256]{3,2,1,0:T(8,128)} %coef.2, f32[1,16,128,128]{3,2,1,0:T(8,128)} %margin.2, f32[1,16,128,128]{3,2,1,0:T(8,128)} %step.1), custom_call_target="tpu_custom_call" | custom-call | flops 1000000 | bytes 2883584 | tf_op jit(solution)/shard_map/pack/pallas_call | solution.py:242
  5.4 25.0 %all_to_all.16.mine = f32[4,768,128]{2,1,0:T(8,128)S(1)} all-to-all(f32[4,768,128]{2,1,0:T(8,128)} %pack.1), channel_id=1, replica_groups=mesh['row'=32,'x'=4,'orb'=2] {'x'}, dimensions={0} | all-to-all | bytes 3145728 | tf_op jit(solution)/shard_map/all_to_all | solution.py:254
  30.6 0.2 collective-permute-start.1
  30.8 5.6 %collective-permute-start.2 = (f32[896,128]{1,0:T(8,128)S(1)}, f32[896,128]{1,0:T(8,128)S(1)}, u32[]{:S(2)}, u32[]{:S(2)}) collective-permute-start(f32[896,128]{1,0:T(8,128)S(1)} %get-tuple-element.28), channel_id=1, source_target_pairs={{8,16},{24,32},{40,48},{56,64},{72,80},{88,96},{104,112},{120,128}... | collective-permute-start | bytes 1376264 | tf_op jit(solution)/shard_map/ppermute | solution.py:232
  36.4 7.1 %collective-permute-done.1.from_a = f32[896,128]{1,0:T(8,128)S(1)} collective-permute-done((f32[896,128]{1,0:T(8,128)S(1)}, f32[896,128]{1,0:T(8,128)S(1)}, u32[]{:S(2)}, u32[]{:S(2)}) %collective-permute-start.1) | collective-permute-done | bytes 458784 | tf_op jit(solution)/shard_map/ppermute | solution.py:232
  43.5 3.7 %collective-permute-done.2.from_b = f32[896,128]{1,0:T(8,128)S(1)} collective-permute-done((f32[896,128]{1,0:T(8,128)S(1)}, f32[896,128]{1,0:T(8,128)S(1)}, u32[]{:S(2)}, u32[]{:S(2)}) %collective-permute-start.2) | collective-permute-done | bytes 458784 | tf_op jit(solution)/shard_map/ppermute | solution.py:232
  47.2 0.8 margin.3.own.y0
  48.0 0.1 collective-permute-start.5
  48.1 6.0 %collective-permute-start.6 = (f32[512,128]{1,0:T(8,128)S(1)}, f32[512,128]{1,0:T(8,128)S(1)}, u32[]{:S(2)}, u32[]{:S(2)}) collective-permute-start(f32[512,128]{1,0:T(8,128)S(1)} %margin.3.own.y0), channel_id=1, source_target_pairs={{8,16},{24,32},{40,48},{56,64},{72,80},{88,96},{104,112},{120,128}... | collective-permute-start | bytes 786440 | tf_op jit(solution)/shard_map/ppermute | solution.py:232
  54.2 0.4 step_parts.1
  54.6 0.6 collective-permute-start.8
  55.3 2.1 %collective-permute-start.9 = (f32[2,1,128,256]{3,2,0,1:T(8,128)S(1)}, f32[2,1,128,256]{3,2,0,1:T(8,128)S(1)}, u32[]{:S(2)}, u32[]{:S(2)}) collective-permute-start(f32[2,1,128,256]{3,2,0,1:T(8,128)S(1)} %bitcast.12), channel_id=1, source_target_pairs={{0,4},{2,6},{4,0},{6,2},{1,5},{3,7},{5,1},{7,3},{8,12},{10,14},{12... | collective-permute-start | bytes 786440 | tf_op jit(solution)/shard_map/ppermute | solution.py:224
  57.3 0.8 collective-permute-start.10
  58.2 2.7 %collective-permute-done.6.from_b = f32[512,128]{1,0:T(8,128)S(1)} collective-permute-done((f32[512,128]{1,0:T(8,128)S(1)}, f32[512,128]{1,0:T(8,128)S(1)}, u32[]{:S(2)}, u32[]{:S(2)}) %collective-permute-start.6) | collective-permute-done | bytes 262176 | tf_op jit(solution)/shard_map/ppermute | solution.py:232
  60.8 1.8 %two.1 = (f32[512,128]{1,0:T(8,128)S(1)}, f32[512,128]{1,0:T(8,128)S(1)}) custom-call(s32[1]{0:T(128)} %bitcast.me, bf16[8,128,640]{2,1,0:T(8,128)(2,1)S(1)} %get-tuple-element.29.m_high, bf16[8,128,640]{2,1,0:T(8,128)(2,1)S(1)} %get-tuple-element.30.m_low, f32[512,128]{1,0:T(8,128)S(1)} %collective-permute-done.5.from_a, ...), custom_call_target="tpu_custom_call" | custom-call | flops 754974720 | bytes 4194304 | tf_op jit(solution)/shard_map/two/pallas_call | solution.py:212
  62.6 7.1 %collective-permute-done.8 = f32[2,1,128,256]{3,2,0,1:T(8,128)S(1)} collective-permute-done((f32[2,1,128,256]{3,2,0,1:T(8,128)S(1)}, f32[2,1,128,256]{3,2,0,1:T(8,128)S(1)}, u32[]{:S(2)}, u32[]{:S(2)}) %collective-permute-start.8) | collective-permute-done | bytes 262176 | tf_op jit(solution)/shard_map/ppermute | solution.py:224
  69.7 0.6 collective-permute-done.10
  70.5 0.1 collective-permute-start.7
  70.6 5.3 %collective-permute-start.12 = (f32[512,128]{1,0:T(8,128)S(1)}, f32[512,128]{1,0:T(8,128)S(1)}, u32[]{:S(2)}, u32[]{:S(2)}) collective-permute-start(f32[512,128]{1,0:T(8,128)S(1)} %get-tuple-element.31.own), channel_id=1, source_target_pairs={{8,16},{24,32},{40,48},{56,64},{72,80},{88,96},{104,112},{120,128}... | collective-permute-start | bytes 786440 | tf_op jit(solution)/shard_map/ppermute | solution.py:232
  75.9 0.7 old_parts.1
  76.7 2.5 %collective-permute-done.7.from_a = f32[512,128]{1,0:T(8,128)S(1)} collective-permute-done((f32[512,128]{1,0:T(8,128)S(1)}, f32[512,128]{1,0:T(8,128)S(1)}, u32[]{:S(2)}, u32[]{:S(2)}) %collective-permute-start.7) | collective-permute-done | bytes 262176 | tf_op jit(solution)/shard_map/ppermute | solution.py:232
  79.2 3.1 %collective-permute-done.12.from_b = f32[512,128]{1,0:T(8,128)S(1)} collective-permute-done((f32[512,128]{1,0:T(8,128)S(1)}, f32[512,128]{1,0:T(8,128)S(1)}, u32[]{:S(2)}, u32[]{:S(2)}) %collective-permute-start.12) | collective-permute-done | bytes 262176 | tf_op jit(solution)/shard_map/ppermute | solution.py:232
  82.3 1.8 %last.1.new = f32[4,128,128]{2,1,0:T(8,128)S(1)} custom-call(s32[1]{0:T(128)} %bitcast.me, bf16[8,128,640]{2,1,0:T(8,128)(2,1)S(1)} %get-tuple-element.29.m_high, bf16[8,128,640]{2,1,0:T(8,128)(2,1)S(1)} %get-tuple-element.30.m_low, f32[512,128]{1,0:T(8,128)S(1)} %collective-permute-done.7.from_a, f32[512,128]{1,0:T(8,128)S(1)} %collective-permute-done.12.from_b, ...), custom_call_target="tpu_custom_call" | custom-call | flops 754974720 | bytes 4718592 | tf_op jit(solution)/shard_map/last/pallas_call | solution.py:212
  84.1 1.0 project.1
  85.2 22.6 %all_to_all.17 = f32[32,16,128]{2,1,0:T(8,128)S(1)} all-to-all(f32[32,16,128]{2,1,0:T(8,128)S(1)} %bitcast.22), channel_id=1, replica_groups=mesh['row'=32,'x'=4,'orb'=2] {'row'}, dimensions={0} | all-to-all | bytes 524288 | tf_op jit(solution)/shard_map/all_to_all | solution.py:298
  107.8 0.1 tail.1
  107.9 0.4 collective-permute-start.13
  108.3 3.6 %collective-permute-start.14 = (f32[136,128]{1,0:T(8,128)S(1)}, f32[136,128]{1,0:T(8,128)S(1)}, u32[]{:S(2)}, u32[]{:S(2)}) collective-permute-start(f32[136,128]{1,0:T(8,128)S(1)} %get-tuple-element.44), channel_id=1, source_target_pairs={{0,4},{2,6},{4,0},{6,2},{1,5},{3,7},{5,1},{7,3},{8,12},{10,14},{12... | collective-permute-start | bytes 208904 | tf_op jit(solution)/shard_map/ppermute | solution.py:224
  111.8 1.6 %collective-permute-done.13.b1 = f32[136,128]{1,0:T(8,128)S(1)} collective-permute-done((f32[136,128]{1,0:T(8,128)S(1)}, f32[136,128]{1,0:T(8,128)S(1)}, u32[]{:S(2)}, u32[]{:S(2)}) %collective-permute-start.13) | collective-permute-done | bytes 69664 | tf_op jit(solution)/shard_map/ppermute | solution.py:224
  113.5 1.4 %collective-permute-done.14.b2 = f32[136,128]{1,0:T(8,128)S(1)} collective-permute-done((f32[136,128]{1,0:T(8,128)S(1)}, f32[136,128]{1,0:T(8,128)S(1)}, u32[]{:S(2)}, u32[]{:S(2)}) %collective-permute-start.14) | collective-permute-done | bytes 69664 | tf_op jit(solution)/shard_map/ppermute | solution.py:224
  114.9 1.3 %collective-permute-done.15.b3 = f32[136,128]{1,0:T(8,128)S(1)} collective-permute-done((f32[136,128]{1,0:T(8,128)S(1)}, f32[136,128]{1,0:T(8,128)S(1)}, u32[]{:S(2)}, u32[]{:S(2)}) %collective-permute-start.15) | collective-permute-done | bytes 69664 | tf_op jit(solution)/shard_map/ppermute | solution.py:224
  116.2 0.9 finish.1
  (15 shorter events, 0.3 us)
Async XLA Ops:
  30.5 16.7 %collective-permute-start = (f32[4,768,128]{2,1,0:T(8,128)S(1)}, f32[4,768,128]{2,1,0:T(8,128)S(1)}, u32[]{:S(2)}, u32[]{:S(2)}) collective-permute-start(f32[4,768,128]{2,1,0:T(8,128)S(1)} %all_to_all.16.mine), channel_id=1, source_target_pairs={{0,1},{1,0},{2,3},{3,2},{4,5},{5,4},{6,7},{7,6},{8,9},{9,8},{10,11... | collective-permute-start | bytes 4718600 | tf_op jit(solution)/shard_map/ppermute | solution.py:227
  30.6 12.9 %collective-permute-start.1 = (f32[896,128]{1,0:T(8,128)S(1)}, f32[896,128]{1,0:T(8,128)S(1)}, u32[]{:S(2)}, u32[]{:S(2)}) collective-permute-start(f32[896,128]{1,0:T(8,128)S(1)} %get-tuple-element.27), channel_id=1, source_target_pairs={{0,8},{16,24},{32,40},{48,56},{64,72},{80,88},{96,104},{112,120},{... | collective-permute-start | bytes 1376264 | tf_op jit(solution)/shard_map/ppermute | solution.py:232
  30.8 16.4 %collective-permute-start.2 = (f32[896,128]{1,0:T(8,128)S(1)}, f32[896,128]{1,0:T(8,128)S(1)}, u32[]{:S(2)}, u32[]{:S(2)}) collective-permute-start(f32[896,128]{1,0:T(8,128)S(1)} %get-tuple-element.28), channel_id=1, source_target_pairs={{8,16},{24,32},{40,48},{56,64},{72,80},{88,96},{104,112},{120,128}... | collective-permute-start | bytes 1376264 | tf_op jit(solution)/shard_map/ppermute | solution.py:232
  43.5 10.6 %collective-permute-start.3 = (f32[896,128]{1,0:T(8,128)S(1)}, f32[896,128]{1,0:T(8,128)S(1)}, u32[]{:S(2)}, u32[]{:S(2)}) collective-permute-start(f32[896,128]{1,0:T(8,128)S(1)} %collective-permute-done.1.from_a), channel_id=1, source_target_pairs={{0,1},{1,0},{2,3},{3,2},{4,5},{5,4},{6,7},{7,6},{8,9},{9,8},{10,11... | collective-permute-start | bytes 1376264 | tf_op jit(solution)/shard_map/ppermute | solution.py:227
  47.2 6.9 %collective-permute-start.4 = (f32[896,128]{1,0:T(8,128)S(1)}, f32[896,128]{1,0:T(8,128)S(1)}, u32[]{:S(2)}, u32[]{:S(2)}) collective-permute-start(f32[896,128]{1,0:T(8,128)S(1)} %collective-permute-done.2.from_b), channel_id=1, source_target_pairs={{0,1},{1,0},{2,3},{3,2},{4,5},{5,4},{6,7},{7,6},{8,9},{9,8},{10,11... | collective-permute-start | bytes 1376264 | tf_op jit(solution)/shard_map/ppermute | solution.py:227
  48.0 6.6 %copy-start = (f32[2,1,128,256]{3,2,1,0:T(8,128)S(1)}, f32[2,1,128,256]{3,2,1,0:T(8,128)}, u32[]{:S(2)}) copy-start(f32[2,1,128,256]{3,2,1,0:T(8,128)} %coef.2) | copy-start | bytes 786436
  48.0 10.1 %collective-permute-start.5 = (f32[512,128]{1,0:T(8,128)S(1)}, f32[512,128]{1,0:T(8,128)S(1)}, u32[]{:S(2)}, u32[]{:S(2)}) collective-permute-start(f32[512,128]{1,0:T(8,128)S(1)} %margin.3.own.y0), channel_id=1, source_target_pairs={{0,8},{16,24},{32,40},{48,56},{64,72},{80,88},{96,104},{112,120},{... | collective-permute-start | bytes 786440 | tf_op jit(solution)/shard_map/ppermute | solution.py:232
  48.1 12.7 %collective-permute-start.6 = (f32[512,128]{1,0:T(8,128)S(1)}, f32[512,128]{1,0:T(8,128)S(1)}, u32[]{:S(2)}, u32[]{:S(2)}) collective-permute-start(f32[512,128]{1,0:T(8,128)S(1)} %margin.3.own.y0), channel_id=1, source_target_pairs={{8,16},{24,32},{40,48},{56,64},{72,80},{88,96},{104,112},{120,128}... | collective-permute-start | bytes 786440 | tf_op jit(solution)/shard_map/ppermute | solution.py:232
  54.6 15.1 %collective-permute-start.8 = (f32[2,1,128,256]{3,2,0,1:T(8,128)S(1)}, f32[2,1,128,256]{3,2,0,1:T(8,128)S(1)}, u32[]{:S(2)}, u32[]{:S(2)}) collective-permute-start(f32[2,1,128,256]{3,2,0,1:T(8,128)S(1)} %bitcast.11), channel_id=1, source_target_pairs={{0,2},{2,4},{4,6},{6,0},{1,3},{3,5},{5,7},{7,1},{8,10},{10,12},{12... | collective-permute-start | bytes 786440 | tf_op jit(solution)/shard_map/ppermute | solution.py:224
  55.3 14.4 %collective-permute-start.9 = (f32[2,1,128,256]{3,2,0,1:T(8,128)S(1)}, f32[2,1,128,256]{3,2,0,1:T(8,128)S(1)}, u32[]{:S(2)}, u32[]{:S(2)}) collective-permute-start(f32[2,1,128,256]{3,2,0,1:T(8,128)S(1)} %bitcast.12), channel_id=1, source_target_pairs={{0,4},{2,6},{4,0},{6,2},{1,5},{3,7},{5,1},{7,3},{8,12},{10,14},{12... | collective-permute-start | bytes 786440 | tf_op jit(solution)/shard_map/ppermute | solution.py:224
  57.3 13.0 %collective-permute-start.10 = (f32[2,1,128,256]{3,2,0,1:T(8,128)S(1)}, f32[2,1,128,256]{3,2,0,1:T(8,128)S(1)}, u32[]{:S(2)}, u32[]{:S(2)}) collective-permute-start(f32[2,1,128,256]{3,2,0,1:T(8,128)S(1)} %bitcast.13), channel_id=1, source_target_pairs={{0,6},{2,0},{4,2},{6,4},{1,7},{3,1},{5,3},{7,5},{8,14},{10,8},{12,... | collective-permute-start | bytes 786440 | tf_op jit(solution)/shard_map/ppermute | solution.py:224
  70.4 5.5 %collective-permute-start.11 = (f32[4,2,128,256]{3,2,1,0:T(8,128)S(1)}, f32[4,2,128,256]{3,2,1,0:T(8,128)S(1)}, u32[]{:S(2)}, u32[]{:S(2)}) collective-permute-start(f32[4,2,128,256]{3,2,1,0:T(8,128)S(1)} %pad_maximum_fusion), channel_id=1, source_target_pairs={{0,1},{1,0},{2,3},{3,2},{4,5},{5,4},{6,7},{7,6},{8,9},{9,8},{10,11... | collective-permute-start | bytes 3145736 | tf_op jit(solution)/shard_map/ppermute | solution.py:227
  70.5 8.7 %collective-permute-start.7 = (f32[512,128]{1,0:T(8,128)S(1)}, f32[512,128]{1,0:T(8,128)S(1)}, u32[]{:S(2)}, u32[]{:S(2)}) collective-permute-start(f32[512,128]{1,0:T(8,128)S(1)} %get-tuple-element.31.own), channel_id=1, source_target_pairs={{0,8},{16,24},{32,40},{48,56},{64,72},{80,88},{96,104},{112,120},{... | collective-permute-start | bytes 786440 | tf_op jit(solution)/shard_map/ppermute | solution.py:232
  70.6 11.7 %collective-permute-start.12 = (f32[512,128]{1,0:T(8,128)S(1)}, f32[512,128]{1,0:T(8,128)S(1)}, u32[]{:S(2)}, u32[]{:S(2)}) collective-permute-start(f32[512,128]{1,0:T(8,128)S(1)} %get-tuple-element.31.own), channel_id=1, source_target_pairs={{8,16},{24,32},{40,48},{56,64},{72,80},{88,96},{104,112},{120,128}... | collective-permute-start | bytes 786440 | tf_op jit(solution)/shard_map/ppermute | solution.py:232
  107.9 5.6 %collective-permute-start.13 = (f32[136,128]{1,0:T(8,128)S(1)}, f32[136,128]{1,0:T(8,128)S(1)}, u32[]{:S(2)}, u32[]{:S(2)}) collective-permute-start(f32[136,128]{1,0:T(8,128)S(1)} %get-tuple-element.43), channel_id=1, source_target_pairs={{0,2},{2,4},{4,6},{6,0},{1,3},{3,5},{5,7},{7,1},{8,10},{10,12},{12... | collective-permute-start | bytes 208904 | tf_op jit(solution)/shard_map/ppermute | solution.py:224
  108.3 6.6 %collective-permute-start.14 = (f32[136,128]{1,0:T(8,128)S(1)}, f32[136,128]{1,0:T(8,128)S(1)}, u32[]{:S(2)}, u32[]{:S(2)}) collective-permute-start(f32[136,128]{1,0:T(8,128)S(1)} %get-tuple-element.44), channel_id=1, source_target_pairs={{0,4},{2,6},{4,0},{6,2},{1,5},{3,7},{5,1},{7,3},{8,12},{10,14},{12... | collective-permute-start | bytes 208904 | tf_op jit(solution)/shard_map/ppermute | solution.py:224
  111.8 4.3 %collective-permute-start.15 = (f32[136,128]{1,0:T(8,128)S(1)}, f32[136,128]{1,0:T(8,128)S(1)}, u32[]{:S(2)}, u32[]{:S(2)}) collective-permute-start(f32[136,128]{1,0:T(8,128)S(1)} %get-tuple-element.45), channel_id=1, source_target_pairs={{0,6},{2,0},{4,2},{6,4},{1,7},{3,1},{5,3},{7,5},{8,14},{10,8},{12,... | collective-permute-start | bytes 208904 | tf_op jit(solution)/shard_map/ppermute | solution.py:224

commit v6 on v5

--- a/solution.py
+++ b/solution.py
@@ -155,13 +155,13 @@
         out[turn_to(q, x)] = (y0[rows, :] - own[rows, :]) + y4 + turned(y1[rows, :] - y3)
 
 
-def old_kernel(me, coef, c1, c2, c3, other, out_high, out_low):
+def old_kernel(me, c0, c1, c2, c3, o0, o1, o2, o3, out_high, out_low):
     x, core = member(me)
-    width = coef.shape[3]
-    for j, ref in enumerate((coef, c1, c2, c3)):
+    width = c0.shape[3]
+    for j, (ref, other) in enumerate(((c0, o0), (c1, o1), (c2, o2), (c3, o3))):
         q = turn_to(x, j)
         for part in range(2):
-            for place, tile in ((core, ref[part, 0]), (1 - core, other[j, part])):
+            for place, tile in ((core, ref[part, 0]), (1 - core, other[part, 0])):
                 rows = pl.ds(pl.multiple_of(place * width, width), width)
                 columns = pl.ds(pl.multiple_of((part * ROW + q) * B, B), B)
                 out_high[rows, columns], out_low[rows, columns] = split(jnp.transpose(tile))
@@ -233,7 +233,7 @@
 
         return [swap_rows(to_a, 0), swap_rows(to_b, 1)]
 
-    chunks = 4
+    chunks = 1
     slots = neighbours.shape[1]
     half_block = pl.BlockSpec(
         (1, slots, HALF // chunks, B), lambda i, where, nbr, pat: (0, 0, lax.rem(where[0], 2) * chunks + i, 0)
@@ -259,6 +259,12 @@
     *edges, held = lax.optimization_barrier((*edges, mine))
     other = swap(held)
     from_a, from_b = exchange(*edges)
+
+    _, held = lax.optimization_barrier((edges[0], coefficients))
+    old = [coefficients, in_row(held, 1), None, in_row(held, ROW - 1)]
+    _, held = lax.optimization_barrier((other, coefficients))
+    old[2] = in_row(held, 2)
+    from_b, old[1], old[3] = lax.optimization_barrier((from_b, old[1], old[3]))
     y0 = call(
         margin_kernel, state, [me, mine, other, from_a, from_b], ROW * step_flops, 60, "margin",
         scratch=[pltpu.VMEM((ROW, B, BAND * B), F32)] + [pltpu.VMEM((2 * ROW * B, B), BF16)] * 2,
@@ -272,19 +278,15 @@
     )
     scratch = [pltpu.VMEM((3 * ROW * B, B), BF16)] * 2 + [pltpu.VMEM((2 * ROW * B, B), BF16)] * 2
     arrived = exchange(y0, y0)
-
-    _, held = lax.optimization_barrier((step[0], coefficients))
-    old = [coefficients] + [in_row(held, j) for j in range(1, ROW)]
+    arrived[0], old[2] = lax.optimization_barrier((arrived[0], old[2]))
     y1, y2 = call(
         functools.partial(two_kernel, 1), [state, state], [me] + step + arrived + [y0], 3 * ROW * step_flops, 64,
         "two", scratch=scratch,
     )
-    _, *old = lax.optimization_barrier((y2, *old))
     arrived = exchange(y2, y2)
-    old_stack = jnp.stack([o[:, 0] for o in old])
     old_type = struct((2 * width, 2 * ROW * B), BF16)
     old_high, old_low = call(
-        old_kernel, [old_type, old_type], [me] + old + [swap(old_stack)], 10**6, 64, "old_parts"
+        old_kernel, [old_type, old_type], [me] + old + [swap(o) for o in old], 10**6, 64, "old_parts"
     )
     arrived[0], old_high = lax.optimization_barrier((arrived[0], old_high))
     new = call(

time: 117 us -> 108 us (0.923)
  waiting for transfers between devices: 31.2 us -> 20.3 us
  starting transfers between devices: 25 us -> 27.7 us
  Pallas kernels: 12.4 us -> 11.2 us
    ppermute x6, waiting for transfers between devices: 19.2 us -> 13.6 us  [swap_rows(): return lax.ppermute(value, 'row', pairs + [(j, i) for i, j in pairs])]
    ppermute x6, waiting for transfers between devices: 12 us -> 6.68 us  [in_row(): return lax.ppermute(value, 'x', [(x, (x + by) % ROW) for x in range(ROW)])]
    ppermute x6, starting transfers between devices: 7.5 us -> 9.65 us  [in_row(): return lax.ppermute(value, 'x', [(x, (x + by) % ROW) for x in range(ROW)])]
    pallas_call x1, Pallas kernels: 4.77 us -> 3.58 us  [local(): pl.pallas_call(pack_kernel, grid_spec=pltpu.PrefetchScalarGridSpec(num_sc...]
  transfers between devices with their start and end apart: 16 -> 19, of which waited for: 10 -> 11; matrix products, arithmetic and copies ran while one was open for 0% -> 0% of each run, Pallas kernels for 3% -> 3%
where the time goes in v6:
time: 108 us
  blocking collectives  47.9 us (44%)
  starting transfers between devices  27.7 us (26%)
  waiting for transfers between devices  20.3 us (19%)
  Pallas kernels  11.2 us (10%)
    all_to_all x1, blocking collectives, local(): mine = lax.all_to_all(packed, 'x', 0, 0, tiled=True)  25 us
    all_to_all x1, blocking collectives, local(): sums = lax.all_to_all(partial_value, 'row', 0, 0, tiled=True)  22.9 us
    ppermute x6, starting transfers between devices, swap_rows(): return lax.ppermute(value, 'row', pairs + [(j, i) for i, j in pairs])  17.3 us
    ppermute x6, waiting for transfers between devices, swap_rows(): return lax.ppermute(value, 'row', pairs + [(j, i) for i, j in pairs])  13.6 us
    ppermute x6, starting transfers between devices, in_row(): return lax.ppermute(value, 'x', [(x, (x + by) % ROW) for x in range(ROW)])  9.65 us
    pallas_call x9, Pallas kernels, call(): pl.pallas_call(kernel, out_shape=out_shape, in_specs=[SMEM] * scalars + [...  7.59 us
    ppermute x6, waiting for transfers between devices, in_row(): return lax.ppermute(value, 'x', [(x, (x + by) % ROW) for x in range(ROW)])  6.68 us
    pallas_call x1, Pallas kernels, local(): pl.pallas_call(pack_kernel, grid_spec=pltpu.PrefetchScalarGridSpec(num_sc...  3.58 us
  transfers between devices with their start and end apart: 19, of which 11 were waited for; matrix products, arithmetic and copies ran while one was open for 0% of the time, Pallas kernels for 3%

profile of v6, /device:TPU:32, one launch (start us, length us, event | category | flops | bytes accessed | tf_op | source)
XLA Modules:
  0.0 107.9 jit_solution(579414835190038894)
XLA Ops:
  0.6 3.6 %pack.1 = f32[4,768,128]{2,1,0:T(8,128)} custom-call(s32[1]{0:T(128)} %bitcast.me, s32[1,16]{1,0:T(1,128)} %nbr.1, s32[1,16]{1,0:T(1,128)} %pat.1, f32[2,1,128,256]{3,2,1,0:T(8,128)} %c0.1, f32[1,16,128,128]{3,2,1,0:T(8,128)} %margin.2, f32[1,16,128,128]{3,2,1,0:T(8,128)} %step.1), custom_call_target="tpu_custom_call" | custom-call | flops 1000000 | bytes 2883584 | tf_op jit(solution)/shard_map/pack/pallas_call | solution.py:242
  4.2 25.0 %all_to_all.16.mine = f32[4,768,128]{2,1,0:T(8,128)S(1)} all-to-all(f32[4,768,128]{2,1,0:T(8,128)} %pack.1), channel_id=1, replica_groups=mesh['row'=32,'x'=4,'orb'=2] {'x'}, dimensions={0} | all-to-all | bytes 3145728 | tf_op jit(solution)/shard_map/all_to_all | solution.py:254
  29.4 0.2 collective-permute-start.1
  29.6 5.6 %collective-permute-start.2 = (f32[896,128]{1,0:T(8,128)S(1)}, f32[896,128]{1,0:T(8,128)S(1)}, u32[]{:S(2)}, u32[]{:S(2)}) collective-permute-start(f32[896,128]{1,0:T(8,128)S(1)} %get-tuple-element.30), channel_id=1, source_target_pairs={{8,16},{24,32},{40,48},{56,64},{72,80},{88,96},{104,112},{120,128}... | collective-permute-start | bytes 1376264 | tf_op jit(solution)/shard_map/ppermute | solution.py:232
  35.2 0.6 collective-permute-start.3
  35.9 2.7 %collective-permute-start.4 = (f32[2,1,128,256]{3,2,1,0:T(8,128)S(1)}, f32[2,1,128,256]{3,2,1,0:T(8,128)S(1)}, u32[]{:S(2)}, u32[]{:S(2)}) collective-permute-start(f32[2,1,128,256]{3,2,1,0:T(8,128)S(1)} %copy-done), channel_id=1, source_target_pairs={{0,6},{2,0},{4,2},{6,4},{1,7},{3,1},{5,3},{7,5},{8,14},{10,8},{12,... | collective-permute-start | bytes 786440 | tf_op jit(solution)/shard_map/ppermute | solution.py:224
  38.5 3.8 %collective-permute-done.1.from_a = f32[896,128]{1,0:T(8,128)S(1)} collective-permute-done((f32[896,128]{1,0:T(8,128)S(1)}, f32[896,128]{1,0:T(8,128)S(1)}, u32[]{:S(2)}, u32[]{:S(2)}) %collective-permute-start.1) | collective-permute-done | bytes 458784 | tf_op jit(solution)/shard_map/ppermute | solution.py:232
  42.3 2.3 %collective-permute-done.3.c1 = f32[2,1,128,256]{3,2,1,0:T(8,128)S(1)} collective-permute-done((f32[2,1,128,256]{3,2,1,0:T(8,128)S(1)}, f32[2,1,128,256]{3,2,1,0:T(8,128)S(1)}, u32[]{:S(2)}, u32[]{:S(2)}) %collective-permute-start.3) | collective-permute-done | bytes 262176 | tf_op jit(solution)/shard_map/ppermute | solution.py:224
  44.6 1.4 %collective-permute-done.2.from_b = f32[896,128]{1,0:T(8,128)S(1)} collective-permute-done((f32[896,128]{1,0:T(8,128)S(1)}, f32[896,128]{1,0:T(8,128)S(1)}, u32[]{:S(2)}, u32[]{:S(2)}) %collective-permute-start.2) | collective-permute-done | bytes 458784 | tf_op jit(solution)/shard_map/ppermute | solution.py:232
  46.0 0.8 margin.3.own.y0
  46.9 0.9 collective-permute-start.8
  47.8 5.9 %collective-permute-start.9 = (f32[512,128]{1,0:T(8,128)S(1)}, f32[512,128]{1,0:T(8,128)S(1)}, u32[]{:S(2)}, u32[]{:S(2)}) collective-permute-start(f32[512,128]{1,0:T(8,128)S(1)} %margin.3.own.y0), channel_id=1, source_target_pairs={{8,16},{24,32},{40,48},{56,64},{72,80},{88,96},{104,112},{120,128}... | collective-permute-start | bytes 786440 | tf_op jit(solution)/shard_map/ppermute | solution.py:232
  53.9 0.5 collective-permute-start.12
  54.4 0.4 step_parts.1
  54.8 0.8 collective-permute-done.7.from_a
  55.6 1.6 %collective-permute-done.8.c2 = f32[2,1,128,256]{3,2,1,0:T(8,128)S(1)} collective-permute-done((f32[2,1,128,256]{3,2,1,0:T(8,128)S(1)}, f32[2,1,128,256]{3,2,1,0:T(8,128)S(1)}, u32[]{:S(2)}, u32[]{:S(2)}) %collective-permute-start.8) | collective-permute-done | bytes 262176 | tf_op jit(solution)/shard_map/ppermute | solution.py:224
  57.2 2.9 %collective-permute-done.9.from_b = f32[512,128]{1,0:T(8,128)S(1)} collective-permute-done((f32[512,128]{1,0:T(8,128)S(1)}, f32[512,128]{1,0:T(8,128)S(1)}, u32[]{:S(2)}, u32[]{:S(2)}) %collective-permute-start.9) | collective-permute-done | bytes 262176 | tf_op jit(solution)/shard_map/ppermute | solution.py:232
  60.2 1.8 %two.1 = (f32[512,128]{1,0:T(8,128)S(1)}, f32[512,128]{1,0:T(8,128)S(1)}) custom-call(s32[1]{0:T(128)} %bitcast.me, bf16[8,128,640]{2,1,0:T(8,128)(2,1)S(1)} %get-tuple-element.33.m_high, bf16[8,128,640]{2,1,0:T(8,128)(2,1)S(1)} %get-tuple-element.34.m_low, f32[512,128]{1,0:T(8,128)S(1)} %collective-permute-done.7.from_a, ...), custom_call_target="tpu_custom_call" | custom-call | flops 754974720 | bytes 4194304 | tf_op jit(solution)/shard_map/two/pallas_call | solution.py:212
  62.1 5.4 %collective-permute-start.15 = (f32[512,128]{1,0:T(8,128)S(1)}, f32[512,128]{1,0:T(8,128)S(1)}, u32[]{:S(2)}, u32[]{:S(2)}) collective-permute-start(f32[512,128]{1,0:T(8,128)S(1)} %get-tuple-element.37.own), channel_id=1, source_target_pairs={{8,16},{24,32},{40,48},{56,64},{72,80},{88,96},{104,112},{120,128}... | collective-permute-start | bytes 786440 | tf_op jit(solution)/shard_map/ppermute | solution.py:232
  67.5 0.7 old_parts.1
  68.2 1.4 %collective-permute-done.10.from_a = f32[512,128]{1,0:T(8,128)S(1)} collective-permute-done((f32[512,128]{1,0:T(8,128)S(1)}, f32[512,128]{1,0:T(8,128)S(1)}, u32[]{:S(2)}, u32[]{:S(2)}) %collective-permute-start.10) | collective-permute-done | bytes 262176 | tf_op jit(solution)/shard_map/ppermute | solution.py:232
  69.7 3.2 %collective-permute-done.15.from_b = f32[512,128]{1,0:T(8,128)S(1)} collective-permute-done((f32[512,128]{1,0:T(8,128)S(1)}, f32[512,128]{1,0:T(8,128)S(1)}, u32[]{:S(2)}, u32[]{:S(2)}) %collective-permute-start.15) | collective-permute-done | bytes 262176 | tf_op jit(solution)/shard_map/ppermute | solution.py:232
  72.9 1.8 %last.1.new = f32[4,128,128]{2,1,0:T(8,128)S(1)} custom-call(s32[1]{0:T(128)} %bitcast.me, bf16[8,128,640]{2,1,0:T(8,128)(2,1)S(1)} %get-tuple-element.33.m_high, bf16[8,128,640]{2,1,0:T(8,128)(2,1)S(1)} %get-tuple-element.34.m_low, f32[512,128]{1,0:T(8,128)S(1)} %collective-permute-done.10.from_a, f32[512,128]{1,0:T(8,128)S(1)} %collective-permute-done.15.from_b, ...), custom_call_target="tpu_custom_call" | custom-call | flops 754974720 | bytes 4718592 | tf_op jit(solution)/shard_map/last/pallas_call | solution.py:212
  74.7 1.0 project.1
  75.7 22.9 %all_to_all.17 = f32[32,16,128]{2,1,0:T(8,128)S(1)} all-to-all(f32[32,16,128]{2,1,0:T(8,128)S(1)} %bitcast.4), channel_id=1, replica_groups=mesh['row'=32,'x'=4,'orb'=2] {'row'}, dimensions={0} | all-to-all | bytes 524288 | tf_op jit(solution)/shard_map/all_to_all | solution.py:300
  98.7 1.3 %collective-permute-start.16 = (f32[136,128]{1,0:T(8,128)S(1)}, f32[136,128]{1,0:T(8,128)S(1)}, u32[]{:S(2)}, u32[]{:S(2)}) collective-permute-start(f32[136,128]{1,0:T(8,128)S(1)} %get-tuple-element.47), channel_id=1, source_target_pairs={{0,2},{2,4},{4,6},{6,0},{1,3},{3,5},{5,7},{7,1},{8,10},{10,12},{12... | collective-permute-start | bytes 208904 | tf_op jit(solution)/shard_map/ppermute | solution.py:224
  100.0 2.7 %collective-permute-start.17 = (f32[136,128]{1,0:T(8,128)S(1)}, f32[136,128]{1,0:T(8,128)S(1)}, u32[]{:S(2)}, u32[]{:S(2)}) collective-permute-start(f32[136,128]{1,0:T(8,128)S(1)} %get-tuple-element.48), channel_id=1, source_target_pairs={{0,4},{2,6},{4,0},{6,2},{1,5},{3,7},{5,1},{7,3},{8,12},{10,14},{12... | collective-permute-start | bytes 208904 | tf_op jit(solution)/shard_map/ppermute | solution.py:224
  102.7 1.5 %collective-permute-start.18 = (f32[136,128]{1,0:T(8,128)S(1)}, f32[136,128]{1,0:T(8,128)S(1)}, u32[]{:S(2)}, u32[]{:S(2)}) collective-permute-start(f32[136,128]{1,0:T(8,128)S(1)} %get-tuple-element.49), channel_id=1, source_target_pairs={{0,6},{2,0},{4,2},{6,4},{1,7},{3,1},{5,3},{7,5},{8,14},{10,8},{12,... | collective-permute-start | bytes 208904 | tf_op jit(solution)/shard_map/ppermute | solution.py:224
  104.2 0.2 collective-permute-done.16.b1
  104.3 1.5 %collective-permute-done.17.b2 = f32[136,128]{1,0:T(8,128)S(1)} collective-permute-done((f32[136,128]{1,0:T(8,128)S(1)}, f32[136,128]{1,0:T(8,128)S(1)}, u32[]{:S(2)}, u32[]{:S(2)}) %collective-permute-start.17) | collective-permute-done | bytes 69664 | tf_op jit(solution)/shard_map/ppermute | solution.py:224
  105.8 1.2 %collective-permute-done.18.b3 = f32[136,128]{1,0:T(8,128)S(1)} collective-permute-done((f32[136,128]{1,0:T(8,128)S(1)}, f32[136,128]{1,0:T(8,128)S(1)}, u32[]{:S(2)}, u32[]{:S(2)}) %collective-permute-start.18) | collective-permute-done | bytes 69664 | tf_op jit(solution)/shard_map/ppermute | solution.py:224
  107.0 0.9 finish.1
  (20 shorter events, 0.6 us)
Async XLA Ops:
  29.2 6.0 %copy-start = (f32[2,1,128,256]{3,2,1,0:T(8,128)S(1)}, f32[2,1,128,256]{3,2,1,0:T(8,128)}, u32[]{:S(2)}) copy-start(f32[2,1,128,256]{3,2,1,0:T(8,128)} %c0.1) | copy-start | bytes 786436
  29.3 16.7 %collective-permute-start = (f32[4,768,128]{2,1,0:T(8,128)S(1)}, f32[4,768,128]{2,1,0:T(8,128)S(1)}, u32[]{:S(2)}, u32[]{:S(2)}) collective-permute-start(f32[4,768,128]{2,1,0:T(8,128)S(1)} %all_to_all.16.mine), channel_id=1, source_target_pairs={{0,1},{1,0},{2,3},{3,2},{4,5},{5,4},{6,7},{7,6},{8,9},{9,8},{10,11... | collective-permute-start | bytes 4718600 | tf_op jit(solution)/shard_map/ppermute | solution.py:227
  29.4 12.9 %collective-permute-start.1 = (f32[896,128]{1,0:T(8,128)S(1)}, f32[896,128]{1,0:T(8,128)S(1)}, u32[]{:S(2)}, u32[]{:S(2)}) collective-permute-start(f32[896,128]{1,0:T(8,128)S(1)} %get-tuple-element.29), channel_id=1, source_target_pairs={{0,8},{16,24},{32,40},{48,56},{64,72},{80,88},{96,104},{112,120},{... | collective-permute-start | bytes 1376264 | tf_op jit(solution)/shard_map/ppermute | solution.py:232
  29.6 16.4 %collective-permute-start.2 = (f32[896,128]{1,0:T(8,128)S(1)}, f32[896,128]{1,0:T(8,128)S(1)}, u32[]{:S(2)}, u32[]{:S(2)}) collective-permute-start(f32[896,128]{1,0:T(8,128)S(1)} %get-tuple-element.30), channel_id=1, source_target_pairs={{8,16},{24,32},{40,48},{56,64},{72,80},{88,96},{104,112},{120,128}... | collective-permute-start | bytes 1376264 | tf_op jit(solution)/shard_map/ppermute | solution.py:232
  35.2 9.4 %collective-permute-start.3 = (f32[2,1,128,256]{3,2,1,0:T(8,128)S(1)}, f32[2,1,128,256]{3,2,1,0:T(8,128)S(1)}, u32[]{:S(2)}, u32[]{:S(2)}) collective-permute-start(f32[2,1,128,256]{3,2,1,0:T(8,128)S(1)} %copy-done), channel_id=1, source_target_pairs={{0,2},{2,4},{4,6},{6,0},{1,3},{3,5},{5,7},{7,1},{8,10},{10,12},{12... | collective-permute-start | bytes 786440 | tf_op jit(solution)/shard_map/ppermute | solution.py:224
  35.9 8.7 %collective-permute-start.4 = (f32[2,1,128,256]{3,2,1,0:T(8,128)S(1)}, f32[2,1,128,256]{3,2,1,0:T(8,128)S(1)}, u32[]{:S(2)}, u32[]{:S(2)}) collective-permute-start(f32[2,1,128,256]{3,2,1,0:T(8,128)S(1)} %copy-done), channel_id=1, source_target_pairs={{0,6},{2,0},{4,2},{6,4},{1,7},{3,1},{5,3},{7,5},{8,14},{10,8},{12,... | collective-permute-start | bytes 786440 | tf_op jit(solution)/shard_map/ppermute | solution.py:224
  42.3 11.4 %collective-permute-start.5 = (f32[896,128]{1,0:T(8,128)S(1)}, f32[896,128]{1,0:T(8,128)S(1)}, u32[]{:S(2)}, u32[]{:S(2)}) collective-permute-start(f32[896,128]{1,0:T(8,128)S(1)} %collective-permute-done.1.from_a), channel_id=1, source_target_pairs={{0,1},{1,0},{2,3},{3,2},{4,5},{5,4},{6,7},{7,6},{8,9},{9,8},{10,11... | collective-permute-start | bytes 1376264 | tf_op jit(solution)/shard_map/ppermute | solution.py:227
  46.0 7.8 %collective-permute-start.6 = (f32[896,128]{1,0:T(8,128)S(1)}, f32[896,128]{1,0:T(8,128)S(1)}, u32[]{:S(2)}, u32[]{:S(2)}) collective-permute-start(f32[896,128]{1,0:T(8,128)S(1)} %collective-permute-done.2.from_b), channel_id=1, source_target_pairs={{0,1},{1,0},{2,3},{3,2},{4,5},{5,4},{6,7},{7,6},{8,9},{9,8},{10,11... | collective-permute-start | bytes 1376264 | tf_op jit(solution)/shard_map/ppermute | solution.py:227
  46.8 8.8 %collective-permute-start.7 = (f32[512,128]{1,0:T(8,128)S(1)}, f32[512,128]{1,0:T(8,128)S(1)}, u32[]{:S(2)}, u32[]{:S(2)}) collective-permute-start(f32[512,128]{1,0:T(8,128)S(1)} %margin.3.own.y0), channel_id=1, source_target_pairs={{0,8},{16,24},{32,40},{48,56},{64,72},{80,88},{96,104},{112,120},{... | collective-permute-start | bytes 786440 | tf_op jit(solution)/shard_map/ppermute | solution.py:232
  46.9 10.3 %collective-permute-start.8 = (f32[2,1,128,256]{3,2,1,0:T(8,128)S(1)}, f32[2,1,128,256]{3,2,1,0:T(8,128)S(1)}, u32[]{:S(2)}, u32[]{:S(2)}) collective-permute-start(f32[2,1,128,256]{3,2,1,0:T(8,128)S(1)} %copy-done), channel_id=1, source_target_pairs={{0,4},{2,6},{4,0},{6,2},{1,5},{3,7},{5,1},{7,3},{8,12},{10,14},{12... | collective-permute-start | bytes 786440 | tf_op jit(solution)/shard_map/ppermute | solution.py:224
  47.8 12.4 %collective-permute-start.9 = (f32[512,128]{1,0:T(8,128)S(1)}, f32[512,128]{1,0:T(8,128)S(1)}, u32[]{:S(2)}, u32[]{:S(2)}) collective-permute-start(f32[512,128]{1,0:T(8,128)S(1)} %margin.3.own.y0), channel_id=1, source_target_pairs={{8,16},{24,32},{40,48},{56,64},{72,80},{88,96},{104,112},{120,128}... | collective-permute-start | bytes 786440 | tf_op jit(solution)/shard_map/ppermute | solution.py:232
  53.8 8.3 %collective-permute-start.11 = (f32[2,1,128,256]{3,2,1,0:T(8,128)S(1)}, f32[2,1,128,256]{3,2,1,0:T(8,128)S(1)}, u32[]{:S(2)}, u32[]{:S(2)}) collective-permute-start(f32[2,1,128,256]{3,2,1,0:T(8,128)S(1)} %copy-done), channel_id=1, source_target_pairs={{0,1},{1,0},{2,3},{3,2},{4,5},{5,4},{6,7},{7,6},{8,9},{9,8},{10,11... | collective-permute-start | bytes 786440 | tf_op jit(solution)/shard_map/ppermute | solution.py:227
  53.9 13.6 %collective-permute-start.12 = (f32[2,1,128,256]{3,2,1,0:T(8,128)S(1)}, f32[2,1,128,256]{3,2,1,0:T(8,128)S(1)}, u32[]{:S(2)}, u32[]{:S(2)}) collective-permute-start(f32[2,1,128,256]{3,2,1,0:T(8,128)S(1)} %collective-permute-done.3.c1), channel_id=1, source_target_pairs={{0,1},{1,0},{2,3},{3,2},{4,5},{5,4},{6,7},{7,6},{8,9},{9,8},{10,11... | collective-permute-start | bytes 786440 | tf_op jit(solution)/shard_map/ppermute | solution.py:227
  55.6 11.9 %collective-permute-start.14 = (f32[2,1,128,256]{3,2,1,0:T(8,128)S(1)}, f32[2,1,128,256]{3,2,1,0:T(8,128)S(1)}, u32[]{:S(2)}, u32[]{:S(2)}) collective-permute-start(f32[2,1,128,256]{3,2,1,0:T(8,128)S(1)} %collective-permute-done.4.c3), channel_id=1, source_target_pairs={{0,1},{1,0},{2,3},{3,2},{4,5},{5,4},{6,7},{7,6},{8,9},{9,8},{10,11... | collective-permute-start | bytes 786440 | tf_op jit(solution)/shard_map/ppermute | solution.py:227
  57.2 10.3 %collective-permute-start.13 = (f32[2,1,128,256]{3,2,1,0:T(8,128)S(1)}, f32[2,1,128,256]{3,2,1,0:T(8,128)S(1)}, u32[]{:S(2)}, u32[]{:S(2)}) collective-permute-start(f32[2,1,128,256]{3,2,1,0:T(8,128)S(1)} %collective-permute-done.8.c2), channel_id=1, source_target_pairs={{0,1},{1,0},{2,3},{3,2},{4,5},{5,4},{6,7},{7,6},{8,9},{9,8},{10,11... | collective-permute-start | bytes 786440 | tf_op jit(solution)/shard_map/ppermute | solution.py:227
  62.0 7.7 %collective-permute-start.10 = (f32[512,128]{1,0:T(8,128)S(1)}, f32[512,128]{1,0:T(8,128)S(1)}, u32[]{:S(2)}, u32[]{:S(2)}) collective-permute-start(f32[512,128]{1,0:T(8,128)S(1)} %get-tuple-element.37.own), channel_id=1, source_target_pairs={{0,8},{16,24},{32,40},{48,56},{64,72},{80,88},{96,104},{112,120},{... | collective-permute-start | bytes 786440 | tf_op jit(solution)/shard_map/ppermute | solution.py:232
  62.1 10.8 %collective-permute-start.15 = (f32[512,128]{1,0:T(8,128)S(1)}, f32[512,128]{1,0:T(8,128)S(1)}, u32[]{:S(2)}, u32[]{:S(2)}) collective-permute-start(f32[512,128]{1,0:T(8,128)S(1)} %get-tuple-element.37.own), channel_id=1, source_target_pairs={{8,16},{24,32},{40,48},{56,64},{72,80},{88,96},{104,112},{120,128}... | collective-permute-start | bytes 786440 | tf_op jit(solution)/shard_map/ppermute | solution.py:232
  98.7 5.6 %collective-permute-start.16 = (f32[136,128]{1,0:T(8,128)S(1)}, f32[136,128]{1,0:T(8,128)S(1)}, u32[]{:S(2)}, u32[]{:S(2)}) collective-permute-start(f32[136,128]{1,0:T(8,128)S(1)} %get-tuple-element.47), channel_id=1, source_target_pairs={{0,2},{2,4},{4,6},{6,0},{1,3},{3,5},{5,7},{7,1},{8,10},{10,12},{12... | collective-permute-start | bytes 208904 | tf_op jit(solution)/shard_map/ppermute | solution.py:224
  100.0 5.8 %collective-permute-start.17 = (f32[136,128]{1,0:T(8,128)S(1)}, f32[136,128]{1,0:T(8,128)S(1)}, u32[]{:S(2)}, u32[]{:S(2)}) collective-permute-start(f32[136,128]{1,0:T(8,128)S(1)} %get-tuple-element.48), channel_id=1, source_target_pairs={{0,4},{2,6},{4,0},{6,2},{1,5},{3,7},{5,1},{7,3},{8,12},{10,14},{12... | collective-permute-start | bytes 208904 | tf_op jit(solution)/shard_map/ppermute | solution.py:224
  102.7 4.3 %collective-permute-start.18 = (f32[136,128]{1,0:T(8,128)S(1)}, f32[136,128]{1,0:T(8,128)S(1)}, u32[]{:S(2)}, u32[]{:S(2)}) collective-permute-start(f32[136,128]{1,0:T(8,128)S(1)} %get-tuple-element.49), channel_id=1, source_target_pairs={{0,6},{2,0},{4,2},{6,4},{1,7},{3,1},{5,3},{7,5},{8,14},{10,8},{12,... | collective-permute-start | bytes 208904 | tf_op jit(solution)/shard_map/ppermute | solution.py:224

commit v7 on v6

--- a/solution.py
+++ b/solution.py
@@ -48,7 +48,7 @@
 
 
 def parity(me):
-    return lax.rem(lax.div(me[0], 2 * ROW), 2)
+    return 1 - lax.rem(lax.div(me[0], 2 * ROW), 2)
 
 
 def pack_kernel(me, nbr, pat, coef, margin, step, out):
@@ -217,7 +217,7 @@
             scratch_shapes=list(scratch),
             cost_estimate=cost(flops, moved * tile_bytes),
             name=name,
-            compiler_params=pltpu.CompilerParams(vmem_limit_bytes=40 * 2**20),
+            compiler_params=pltpu.CompilerParams(vmem_limit_bytes=16 * 2**20),
         )(*args)
 
     def in_row(value, by):
@@ -231,7 +231,7 @@
             pairs = [(r, r + 1) for r in range(first, rows - 1, 2)]
             return lax.ppermute(value, "row", pairs + [(j, i) for i, j in pairs])
 
-        return [swap_rows(to_a, 0), swap_rows(to_b, 1)]
+        return [swap_rows(to_a, 1), swap_rows(to_b, 0)]
 
     chunks = 1
     slots = neighbours.shape[1]
@@ -250,6 +250,7 @@
         out_shape=struct(packed_shape, F32),
         cost_estimate=cost(10**6, 44 * tile_bytes),
         name="pack",
+        compiler_params=pltpu.CompilerParams(vmem_limit_bytes=16 * 2**20),
     )(me, neighbours, pattern, coefficients, margin, step_matrix)
     mine = lax.all_to_all(packed, "x", 0, 0, tiled=True)
 

time: 108 us -> 111 us (1.028)
  waiting for transfers between devices: 20.3 us -> 28.7 us
  starting transfers between devices: 27.7 us -> 20.1 us
  local copies, waits for them, and re-layouts: 0.01 us -> 4.7 us
  Pallas kernels: 11.2 us -> 8.84 us
    ppermute x6, waiting for transfers between devices: 13.6 us -> 21.8 us  [swap_rows(): return lax.ppermute(value, 'row', pairs + [(j, i) for i, j in pairs])]
    ppermute x6, starting transfers between devices: 17.3 us -> 11.8 us  [swap_rows(): return lax.ppermute(value, 'row', pairs + [(j, i) for i, j in pairs])]
    unnamed x2 -> x12, local copies, waits for them, and re-layouts: 0.01 us -> 4.7 us
    pallas_call x1, Pallas kernels: 3.58 us -> 1.02 us  [local(): pl.pallas_call(pack_kernel, grid_spec=pltpu.PrefetchScalarGridSpec(num_sc...]
    ppermute x6, starting transfers between devices: 9.65 us -> 7.63 us  [in_row(): return lax.ppermute(value, 'x', [(x, (x + by) % ROW) for x in range(ROW)])]
  transfers between devices with their start and end apart: 19 -> 19, of which waited for: 11 -> 9; matrix products, arithmetic and copies ran while one was open for 0% -> 0% of each run, Pallas kernels for 3% -> 3%
where the time goes in v7:
time: 111 us
  blocking collectives  47.6 us (43%)
  waiting for transfers between devices  28.7 us (26%)
  starting transfers between devices  20.1 us (18%)
  Pallas kernels  8.84 us (8%)
  local copies, waits for them, and re-layouts  4.7 us (4%)
    all_to_all x1, blocking collectives, local(): mine = lax.all_to_all(packed, 'x', 0, 0, tiled=True)  24.8 us
    all_to_all x1, blocking collectives, local(): sums = lax.all_to_all(partial_value, 'row', 0, 0, tiled=True)  22.7 us
    ppermute x6, waiting for transfers between devices, swap_rows(): return lax.ppermute(value, 'row', pairs + [(j, i) for i, j in pairs])  21.8 us
    ppermute x6, starting transfers between devices, swap_rows(): return lax.ppermute(value, 'row', pairs + [(j, i) for i, j in pairs])  11.8 us
    pallas_call x9, Pallas kernels, call(): pl.pallas_call(kernel, out_shape=out_shape, in_specs=[SMEM] * scalars + [...  7.82 us
    ppermute x6, starting transfers between devices, in_row(): return lax.ppermute(value, 'x', [(x, (x + by) % ROW) for x in range(ROW)])  7.63 us
    ppermute x6, waiting for transfers between devices, in_row(): return lax.ppermute(value, 'x', [(x, (x + by) % ROW) for x in range(ROW)])  6.86 us
    unnamed x12, local copies, waits for them, and re-layouts  4.7 us
  transfers between devices with their start and end apart: 19, of which 9 were waited for; matrix products, arithmetic and copies ran while one was open for 0% of the time, Pallas kernels for 3%

profile of v7, /device:TPU:32, one launch (start us, length us, event | category | flops | bytes accessed | tf_op | source)
XLA Modules:
  0.0 110.7 jit_solution(2894380552405012580)
XLA Ops:
  0.6 1.2 %copy-done = f32[1,16,128,128]{3,2,1,0:T(8,128)S(1)} copy-done((f32[1,16,128,128]{3,2,1,0:T(8,128)S(1)}, f32[1,16,128,128]{3,2,1,0:T(8,128)}, u32[]{:S(2)}) %copy-start) | copy-done | bytes 1048600
  1.9 1.2 %copy-done.1 = f32[1,16,128,128]{3,2,1,0:T(8,128)S(1)} copy-done((f32[1,16,128,128]{3,2,1,0:T(8,128)S(1)}, f32[1,16,128,128]{3,2,1,0:T(8,128)}, u32[]{:S(2)}) %copy-start.1) | copy-done | bytes 1048600
  3.1 0.9 copy-done.2
  4.0 0.7 copy-done.4
  4.7 0.7 copy-done.5
  5.4 1.0 pack.1
  6.4 24.8 %all_to_all.16.mine = f32[4,768,128]{2,1,0:T(8,128)S(1)} all-to-all(f32[4,768,128]{2,1,0:T(8,128)S(1)} %pack.1), channel_id=1, replica_groups=mesh['row'=32,'x'=4,'orb'=2] {'x'}, dimensions={0} | all-to-all | bytes 3145728 | tf_op jit(solution)/shard_map/all_to_all | solution.py:255
  31.3 3.8 %collective-permute-start.1 = (f32[896,128]{1,0:T(8,128)S(1)}, f32[896,128]{1,0:T(8,128)S(1)}, u32[]{:S(2)}, u32[]{:S(2)}) collective-permute-start(f32[896,128]{1,0:T(8,128)S(1)} %get-tuple-element.29), channel_id=1, source_target_pairs={{8,16},{24,32},{40,48},{56,64},{72,80},{88,96},{104,112},{120,128}... | collective-permute-start | bytes 1376264 | tf_op jit(solution)/shard_map/ppermute | solution.py:232
  35.3 0.6 collective-permute-start.3
  35.9 2.7 %collective-permute-start.4 = (f32[2,1,128,256]{3,2,1,0:T(8,128)S(1)}, f32[2,1,128,256]{3,2,1,0:T(8,128)S(1)}, u32[]{:S(2)}, u32[]{:S(2)}) collective-permute-start(f32[2,1,128,256]{3,2,1,0:T(8,128)S(1)} %copy-done.3), channel_id=1, source_target_pairs={{0,6},{2,0},{4,2},{6,4},{1,7},{3,1},{5,3},{7,5},{8,14},{10,8},{12,... | collective-permute-start | bytes 786440 | tf_op jit(solution)/shard_map/ppermute | solution.py:224
  38.6 7.7 %collective-permute-done.1.from_a = f32[896,128]{1,0:T(8,128)S(1)} collective-permute-done((f32[896,128]{1,0:T(8,128)S(1)}, f32[896,128]{1,0:T(8,128)S(1)}, u32[]{:S(2)}, u32[]{:S(2)}) %collective-permute-start.1) | collective-permute-done | bytes 458784 | tf_op jit(solution)/shard_map/ppermute | solution.py:232
  46.3 1.6 %collective-permute-done.2.from_b = f32[896,128]{1,0:T(8,128)S(1)} collective-permute-done((f32[896,128]{1,0:T(8,128)S(1)}, f32[896,128]{1,0:T(8,128)S(1)}, u32[]{:S(2)}, u32[]{:S(2)}) %collective-permute-start.2) | collective-permute-done | bytes 458784 | tf_op jit(solution)/shard_map/ppermute | solution.py:232
  47.9 0.8 margin.3.own.y0
  48.7 5.2 %collective-permute-start.7 = (f32[512,128]{1,0:T(8,128)S(1)}, f32[512,128]{1,0:T(8,128)S(1)}, u32[]{:S(2)}, u32[]{:S(2)}) collective-permute-start(f32[512,128]{1,0:T(8,128)S(1)} %margin.3.own.y0), channel_id=1, source_target_pairs={{8,16},{24,32},{40,48},{56,64},{72,80},{88,96},{104,112},{120,128}... | collective-permute-start | bytes 786440 | tf_op jit(solution)/shard_map/ppermute | solution.py:232
  53.9 0.9 collective-permute-start.8
  54.8 0.5 collective-permute-start.12
  55.8 5.1 %collective-permute-done.7.from_a = f32[512,128]{1,0:T(8,128)S(1)} collective-permute-done((f32[512,128]{1,0:T(8,128)S(1)}, f32[512,128]{1,0:T(8,128)S(1)}, u32[]{:S(2)}, u32[]{:S(2)}) %collective-permute-start.7) | collective-permute-done | bytes 262176 | tf_op jit(solution)/shard_map/ppermute | solution.py:232
  60.9 3.1 %collective-permute-done.8.c2 = f32[2,1,128,256]{3,2,1,0:T(8,128)S(1)} collective-permute-done((f32[2,1,128,256]{3,2,1,0:T(8,128)S(1)}, f32[2,1,128,256]{3,2,1,0:T(8,128)S(1)}, u32[]{:S(2)}, u32[]{:S(2)}) %collective-permute-start.8) | collective-permute-done | bytes 262176 | tf_op jit(solution)/shard_map/ppermute | solution.py:224
  64.0 1.9 %two.1 = (f32[512,128]{1,0:T(8,128)S(1)}, f32[512,128]{1,0:T(8,128)S(1)}) custom-call(s32[1]{0:T(128)} %bitcast.me, bf16[8,128,640]{2,1,0:T(8,128)(2,1)S(1)} %get-tuple-element.33.m_high, bf16[8,128,640]{2,1,0:T(8,128)(2,1)S(1)} %get-tuple-element.34.m_low, f32[512,128]{1,0:T(8,128)S(1)} %collective-permute-done.7.from_a, ...), custom_call_target="tpu_custom_call" | custom-call | flops 754974720 | bytes 4194304 | tf_op jit(solution)/shard_map/two/pallas_call | solution.py:212
  65.8 2.4 %collective-permute-start.10 = (f32[512,128]{1,0:T(8,128)S(1)}, f32[512,128]{1,0:T(8,128)S(1)}, u32[]{:S(2)}, u32[]{:S(2)}) collective-permute-start(f32[512,128]{1,0:T(8,128)S(1)} %get-tuple-element.37.own), channel_id=1, source_target_pairs={{8,16},{24,32},{40,48},{56,64},{72,80},{88,96},{104,112},{120,128}... | collective-permute-start | bytes 786440 | tf_op jit(solution)/shard_map/ppermute | solution.py:232
  68.6 0.7 old_parts.1
  69.3 7.1 %collective-permute-done.10.from_a = f32[512,128]{1,0:T(8,128)S(1)} collective-permute-done((f32[512,128]{1,0:T(8,128)S(1)}, f32[512,128]{1,0:T(8,128)S(1)}, u32[]{:S(2)}, u32[]{:S(2)}) %collective-permute-start.10) | collective-permute-done | bytes 262176 | tf_op jit(solution)/shard_map/ppermute | solution.py:232
  76.8 1.9 %last.1.new = f32[4,128,128]{2,1,0:T(8,128)S(1)} custom-call(s32[1]{0:T(128)} %bitcast.me, bf16[8,128,640]{2,1,0:T(8,128)(2,1)S(1)} %get-tuple-element.33.m_high, bf16[8,128,640]{2,1,0:T(8,128)(2,1)S(1)} %get-tuple-element.34.m_low, f32[512,128]{1,0:T(8,128)S(1)} %collective-permute-done.10.from_a, f32[512,128]{1,0:T(8,128)S(1)} %collective-permute-done.15.from_b, ...), custom_call_target="tpu_custom_call" | custom-call | flops 754974720 | bytes 4718592 | tf_op jit(solution)/shard_map/last/pallas_call | solution.py:212
  78.7 1.0 project.1
  79.7 22.7 %all_to_all.17 = f32[32,16,128]{2,1,0:T(8,128)S(1)} all-to-all(f32[32,16,128]{2,1,0:T(8,128)S(1)} %bitcast.4), channel_id=1, replica_groups=mesh['row'=32,'x'=4,'orb'=2] {'row'}, dimensions={0} | all-to-all | bytes 524288 | tf_op jit(solution)/shard_map/all_to_all | solution.py:301
  102.6 0.6 collective-permute-start.16
  103.2 1.7 %collective-permute-start.17 = (f32[136,128]{1,0:T(8,128)S(1)}, f32[136,128]{1,0:T(8,128)S(1)}, u32[]{:S(2)}, u32[]{:S(2)}) collective-permute-start(f32[136,128]{1,0:T(8,128)S(1)} %get-tuple-element.48), channel_id=1, source_target_pairs={{0,4},{2,6},{4,0},{6,2},{1,5},{3,7},{5,1},{7,3},{8,12},{10,14},{12... | collective-permute-start | bytes 208904 | tf_op jit(solution)/shard_map/ppermute | solution.py:224
  105.0 1.0 collective-permute-start.18
  106.0 2.2 %collective-permute-done.16.b1 = f32[136,128]{1,0:T(8,128)S(1)} collective-permute-done((f32[136,128]{1,0:T(8,128)S(1)}, f32[136,128]{1,0:T(8,128)S(1)}, u32[]{:S(2)}, u32[]{:S(2)}) %collective-permute-start.16) | collective-permute-done | bytes 69664 | tf_op jit(solution)/shard_map/ppermute | solution.py:224
  108.2 0.9 collective-permute-done.17.b2
  109.0 0.7 collective-permute-done.18.b3
  109.8 0.9 finish.1
  (30 shorter events, 1.4 us)
Async XLA Ops:
  0.6 1.2 %copy-start = (f32[1,16,128,128]{3,2,1,0:T(8,128)S(1)}, f32[1,16,128,128]{3,2,1,0:T(8,128)}, u32[]{:S(2)}) copy-start(f32[1,16,128,128]{3,2,1,0:T(8,128)} %margin.2) | copy-start | bytes 3145732
  1.9 1.2 %copy-start.1 = (f32[1,16,128,128]{3,2,1,0:T(8,128)S(1)}, f32[1,16,128,128]{3,2,1,0:T(8,128)}, u32[]{:S(2)}) copy-start(f32[1,16,128,128]{3,2,1,0:T(8,128)} %step.1) | copy-start | bytes 3145732
  3.1 0.9 copy-start.2
  4.0 0.7 copy-start.4
  4.7 0.7 copy-start.5
  31.2 4.1 %copy-start.3 = (f32[2,1,128,256]{3,2,1,0:T(8,128)S(1)}, f32[2,1,128,256]{3,2,1,0:T(8,128)}, u32[]{:S(2)}) copy-start(f32[2,1,128,256]{3,2,1,0:T(8,128)} %c0.1) | copy-start | bytes 786436
  31.2 16.7 %collective-permute-start = (f32[4,768,128]{2,1,0:T(8,128)S(1)}, f32[4,768,128]{2,1,0:T(8,128)S(1)}, u32[]{:S(2)}, u32[]{:S(2)}) collective-permute-start(f32[4,768,128]{2,1,0:T(8,128)S(1)} %all_to_all.16.mine), channel_id=1, source_target_pairs={{0,1},{1,0},{2,3},{3,2},{4,5},{5,4},{6,7},{7,6},{8,9},{9,8},{10,11... | collective-permute-start | bytes 4718600 | tf_op jit(solution)/shard_map/ppermute | solution.py:227
  31.3 15.0 %collective-permute-start.1 = (f32[896,128]{1,0:T(8,128)S(1)}, f32[896,128]{1,0:T(8,128)S(1)}, u32[]{:S(2)}, u32[]{:S(2)}) collective-permute-start(f32[896,128]{1,0:T(8,128)S(1)} %get-tuple-element.29), channel_id=1, source_target_pairs={{8,16},{24,32},{40,48},{56,64},{72,80},{88,96},{104,112},{120,128}... | collective-permute-start | bytes 1376264 | tf_op jit(solution)/shard_map/ppermute | solution.py:232
  35.2 12.7 %collective-permute-start.2 = (f32[896,128]{1,0:T(8,128)S(1)}, f32[896,128]{1,0:T(8,128)S(1)}, u32[]{:S(2)}, u32[]{:S(2)}) collective-permute-start(f32[896,128]{1,0:T(8,128)S(1)} %get-tuple-element.30), channel_id=1, source_target_pairs={{0,8},{16,24},{32,40},{48,56},{64,72},{80,88},{96,104},{112,120},{... | collective-permute-start | bytes 1376264 | tf_op jit(solution)/shard_map/ppermute | solution.py:232
  35.3 11.0 %collective-permute-start.3 = (f32[2,1,128,256]{3,2,1,0:T(8,128)S(1)}, f32[2,1,128,256]{3,2,1,0:T(8,128)S(1)}, u32[]{:S(2)}, u32[]{:S(2)}) collective-permute-start(f32[2,1,128,256]{3,2,1,0:T(8,128)S(1)} %copy-done.3), channel_id=1, source_target_pairs={{0,2},{2,4},{4,6},{6,0},{1,3},{3,5},{5,7},{7,1},{8,10},{10,12},{12... | collective-permute-start | bytes 786440 | tf_op jit(solution)/shard_map/ppermute | solution.py:224
  35.9 10.4 %collective-permute-start.4 = (f32[2,1,128,256]{3,2,1,0:T(8,128)S(1)}, f32[2,1,128,256]{3,2,1,0:T(8,128)S(1)}, u32[]{:S(2)}, u32[]{:S(2)}) collective-permute-start(f32[2,1,128,256]{3,2,1,0:T(8,128)S(1)} %copy-done.3), channel_id=1, source_target_pairs={{0,6},{2,0},{4,2},{6,4},{1,7},{3,1},{5,3},{7,5},{8,14},{10,8},{12,... | collective-permute-start | bytes 786440 | tf_op jit(solution)/shard_map/ppermute | solution.py:224
  46.3 8.5 %collective-permute-start.5 = (f32[896,128]{1,0:T(8,128)S(1)}, f32[896,128]{1,0:T(8,128)S(1)}, u32[]{:S(2)}, u32[]{:S(2)}) collective-permute-start(f32[896,128]{1,0:T(8,128)S(1)} %collective-permute-done.1.from_a), channel_id=1, source_target_pairs={{0,1},{1,0},{2,3},{3,2},{4,5},{5,4},{6,7},{7,6},{8,9},{9,8},{10,11... | collective-permute-start | bytes 1376264 | tf_op jit(solution)/shard_map/ppermute | solution.py:227
  47.9 6.9 %collective-permute-start.6 = (f32[896,128]{1,0:T(8,128)S(1)}, f32[896,128]{1,0:T(8,128)S(1)}, u32[]{:S(2)}, u32[]{:S(2)}) collective-permute-start(f32[896,128]{1,0:T(8,128)S(1)} %collective-permute-done.2.from_b), channel_id=1, source_target_pairs={{0,1},{1,0},{2,3},{3,2},{4,5},{5,4},{6,7},{7,6},{8,9},{9,8},{10,11... | collective-permute-start | bytes 1376264 | tf_op jit(solution)/shard_map/ppermute | solution.py:227
  48.7 12.2 %collective-permute-start.7 = (f32[512,128]{1,0:T(8,128)S(1)}, f32[512,128]{1,0:T(8,128)S(1)}, u32[]{:S(2)}, u32[]{:S(2)}) collective-permute-start(f32[512,128]{1,0:T(8,128)S(1)} %margin.3.own.y0), channel_id=1, source_target_pairs={{8,16},{24,32},{40,48},{56,64},{72,80},{88,96},{104,112},{120,128}... | collective-permute-start | bytes 786440 | tf_op jit(solution)/shard_map/ppermute | solution.py:232
  53.9 10.0 %collective-permute-start.8 = (f32[2,1,128,256]{3,2,1,0:T(8,128)S(1)}, f32[2,1,128,256]{3,2,1,0:T(8,128)S(1)}, u32[]{:S(2)}, u32[]{:S(2)}) collective-permute-start(f32[2,1,128,256]{3,2,1,0:T(8,128)S(1)} %copy-done.3), channel_id=1, source_target_pairs={{0,4},{2,6},{4,0},{6,2},{1,5},{3,7},{5,1},{7,3},{8,12},{10,14},{12... | collective-permute-start | bytes 786440 | tf_op jit(solution)/shard_map/ppermute | solution.py:224
  54.8 9.1 %collective-permute-start.9 = (f32[512,128]{1,0:T(8,128)S(1)}, f32[512,128]{1,0:T(8,128)S(1)}, u32[]{:S(2)}, u32[]{:S(2)}) collective-permute-start(f32[512,128]{1,0:T(8,128)S(1)} %margin.3.own.y0), channel_id=1, source_target_pairs={{0,8},{16,24},{32,40},{48,56},{64,72},{80,88},{96,104},{112,120},{... | collective-permute-start | bytes 786440 | tf_op jit(solution)/shard_map/ppermute | solution.py:232
  54.8 13.5 %collective-permute-start.11 = (f32[2,1,128,256]{3,2,1,0:T(8,128)S(1)}, f32[2,1,128,256]{3,2,1,0:T(8,128)S(1)}, u32[]{:S(2)}, u32[]{:S(2)}) collective-permute-start(f32[2,1,128,256]{3,2,1,0:T(8,128)S(1)} %copy-done.3), channel_id=1, source_target_pairs={{0,1},{1,0},{2,3},{3,2},{4,5},{5,4},{6,7},{7,6},{8,9},{9,8},{10,11... | collective-permute-start | bytes 786440 | tf_op jit(solution)/shard_map/ppermute | solution.py:227
  54.8 13.7 %collective-permute-start.12 = (f32[2,1,128,256]{3,2,1,0:T(8,128)S(1)}, f32[2,1,128,256]{3,2,1,0:T(8,128)S(1)}, u32[]{:S(2)}, u32[]{:S(2)}) collective-permute-start(f32[2,1,128,256]{3,2,1,0:T(8,128)S(1)} %collective-permute-done.3.c1), channel_id=1, source_target_pairs={{0,1},{1,0},{2,3},{3,2},{4,5},{5,4},{6,7},{7,6},{8,9},{9,8},{10,11... | collective-permute-start | bytes 786440 | tf_op jit(solution)/shard_map/ppermute | solution.py:227
  60.9 7.7 %collective-permute-start.14 = (f32[2,1,128,256]{3,2,1,0:T(8,128)S(1)}, f32[2,1,128,256]{3,2,1,0:T(8,128)S(1)}, u32[]{:S(2)}, u32[]{:S(2)}) collective-permute-start(f32[2,1,128,256]{3,2,1,0:T(8,128)S(1)} %collective-permute-done.4.c3), channel_id=1, source_target_pairs={{0,1},{1,0},{2,3},{3,2},{4,5},{5,4},{6,7},{7,6},{8,9},{9,8},{10,11... | collective-permute-start | bytes 786440 | tf_op jit(solution)/shard_map/ppermute | solution.py:227
  63.9 4.6 %collective-permute-start.13 = (f32[2,1,128,256]{3,2,1,0:T(8,128)S(1)}, f32[2,1,128,256]{3,2,1,0:T(8,128)S(1)}, u32[]{:S(2)}, u32[]{:S(2)}) collective-permute-start(f32[2,1,128,256]{3,2,1,0:T(8,128)S(1)} %collective-permute-done.8.c2), channel_id=1, source_target_pairs={{0,1},{1,0},{2,3},{3,2},{4,5},{5,4},{6,7},{7,6},{8,9},{9,8},{10,11... | collective-permute-start | bytes 786440 | tf_op jit(solution)/shard_map/ppermute | solution.py:227
  65.8 10.6 %collective-permute-start.10 = (f32[512,128]{1,0:T(8,128)S(1)}, f32[512,128]{1,0:T(8,128)S(1)}, u32[]{:S(2)}, u32[]{:S(2)}) collective-permute-start(f32[512,128]{1,0:T(8,128)S(1)} %get-tuple-element.37.own), channel_id=1, source_target_pairs={{8,16},{24,32},{40,48},{56,64},{72,80},{88,96},{104,112},{120,128}... | collective-permute-start | bytes 786440 | tf_op jit(solution)/shard_map/ppermute | solution.py:232
  68.3 8.5 %collective-permute-start.15 = (f32[512,128]{1,0:T(8,128)S(1)}, f32[512,128]{1,0:T(8,128)S(1)}, u32[]{:S(2)}, u32[]{:S(2)}) collective-permute-start(f32[512,128]{1,0:T(8,128)S(1)} %get-tuple-element.37.own), channel_id=1, source_target_pairs={{0,8},{16,24},{32,40},{48,56},{64,72},{80,88},{96,104},{112,120},{... | collective-permute-start | bytes 786440 | tf_op jit(solution)/shard_map/ppermute | solution.py:232
  102.6 5.6 %collective-permute-start.16 = (f32[136,128]{1,0:T(8,128)S(1)}, f32[136,128]{1,0:T(8,128)S(1)}, u32[]{:S(2)}, u32[]{:S(2)}) collective-permute-start(f32[136,128]{1,0:T(8,128)S(1)} %get-tuple-element.47), channel_id=1, source_target_pairs={{0,2},{2,4},{4,6},{6,0},{1,3},{3,5},{5,7},{7,1},{8,10},{10,12},{12... | collective-permute-start | bytes 208904 | tf_op jit(solution)/shard_map/ppermute | solution.py:224
  103.2 5.8 %collective-permute-start.17 = (f32[136,128]{1,0:T(8,128)S(1)}, f32[136,128]{1,0:T(8,128)S(1)}, u32[]{:S(2)}, u32[]{:S(2)}) collective-permute-start(f32[136,128]{1,0:T(8,128)S(1)} %get-tuple-element.48), channel_id=1, source_target_pairs={{0,4},{2,6},{4,0},{6,2},{1,5},{3,7},{5,1},{7,3},{8,12},{10,14},{12... | collective-permute-start | bytes 208904 | tf_op jit(solution)/shard_map/ppermute | solution.py:224
  105.0 4.8 %collective-permute-start.18 = (f32[136,128]{1,0:T(8,128)S(1)}, f32[136,128]{1,0:T(8,128)S(1)}, u32[]{:S(2)}, u32[]{:S(2)}) collective-permute-start(f32[136,128]{1,0:T(8,128)S(1)} %get-tuple-element.49), channel_id=1, source_target_pairs={{0,6},{2,0},{4,2},{6,4},{1,7},{3,1},{5,3},{7,5},{8,14},{10,8},{12,... | collective-permute-start | bytes 208904 | tf_op jit(solution)/shard_map/ppermute | solution.py:224

commit v8 on v6

--- a/solution.py
+++ b/solution.py
@@ -51,28 +51,33 @@
     return lax.rem(lax.div(me[0], 2 * ROW), 2)
 
 
-def pack_kernel(me, nbr, pat, coef, margin, step, out):
-    chunk = pl.program_id(0)
-
-    @pl.when(chunk == 0)
-    def _():
-        for q in range(ROW):
-            columns = slice(q * HALF, (q + 1) * HALF)
-            out[q, :B, :] = jnp.concatenate([coef[0, 0, :, columns], coef[1, 0, :, columns]], axis=1)
-
+def pack_kernel(me, nbr, pat, coef_hbm, margin_hbm, step_hbm, out, coef, margin, step, done):
+    core = lax.rem(me[0], 2)
+    rows = pl.ds(pl.multiple_of(core * HALF, HALF), HALF)
+    copies = [
+        pltpu.make_async_copy(margin_hbm.at[0, :, rows, :], margin, done.at[0]),
+        pltpu.make_async_copy(step_hbm.at[0, :, rows, :], step, done.at[1]),
+        pltpu.make_async_copy(coef_hbm, coef, done.at[2]),
+    ]
+    for copy in copies:
+        copy.start()
     first = lax.div(me[0], 2) - 2
-    size = margin.shape[2]
+    slots = margin.shape[0]
     for i, source in enumerate((margin, step)):
-        totals = [jnp.zeros((size, B), F32)] * BAND
-        for k in range(source.shape[1]):
-            block = source[0, k]
-            weight = F32(1.0) if k == 0 else pat[0, k].astype(F32)
-            for d in range(BAND):
-                totals[d] = totals[d] + block * jnp.where(nbr[0, k] == first + d, weight, F32(0.0))
+        copies[i].wait()
         for d in range(BAND):
-            start = pl.multiple_of(B + (i * BAND + d) * HALF + chunk * size, size)
+            total = None
+            for k in range(slots):
+                weight = F32(1.0) if k == 0 else pat[0, k].astype(F32)
+                part = source[k] * jnp.where(nbr[0, k] == first + d, weight, F32(0.0))
+                total = part if total is None else total + part
+            start = B + (i * BAND + d) * HALF
             for q in range(ROW):
-                out[q, pl.ds(start, size), :] = totals[d]
+                out[q, start : start + HALF, :] = total
+    copies[2].wait()
+    for q in range(ROW):
+        columns = slice(q * HALF, (q + 1) * HALF)
+        out[q, :B, :] = jnp.concatenate([coef[0, 0, :, columns], coef[1, 0, :, columns]], axis=1)
 
 
 def place_half(out, q, place, source, first):
@@ -87,8 +92,15 @@
     for out, first in ((to_a, 2 - 2 * odd), (to_b, 2 * odd)):
         for q in range(2):
             out[q * B : (q + 1) * B, :] = mine[first + q, :B, :]
-            start = 2 * B + q * BAND * HALF
-            out[start : start + BAND * HALF, :] = mine[first + q, B + BAND * HALF :, :]
+
+
+def step_edge_kernel(me, mine, other, out):
+    _, core = member(me)
+    first = 2 * lax.rem(parity(me) + core + 1, 2)
+    for q in range(2):
+        for place, ref in ((core, mine), (1 - core, other)):
+            for to, rows, columns, tile in place_half(out, q, place, lambda at: ref[first + q, at, :], B + BAND * HALF):
+                out[to, rows, columns] = tile
 
 
 def window(odd, from_a, from_b, own, v_high, v_low):
@@ -102,7 +114,7 @@
 def margin_kernel(me, mine, other, from_a, from_b, out, full, v_high, v_low):
     _, core = member(me)
     own = [mine[q, :B, :] for q in range(ROW)]
-    window(parity(me), from_a[: 2 * B, :], from_b[: 2 * B, :], jnp.concatenate(own, axis=0), v_high, v_low)
+    window(parity(me), from_a[...], from_b[...], jnp.concatenate(own, axis=0), v_high, v_low)
     for q in range(ROW):
         for place, ref in ((core, mine), (1 - core, other)):
             for _, rows, columns, tile in place_half(full, q, place, lambda at: ref[q, at, :], B):
@@ -113,19 +125,17 @@
         out[q * B : (q + 1) * B, :] = own[q] + product(m_high, m_low, v_high[rows], v_low[rows])
 
 
-def parts_kernel(me, mine, other, from_a, from_b, other_a, other_b, out_high, out_low):
+def parts_kernel(me, mine, other, edge, edge_other, out_high, out_low):
     _, core = member(me)
     odd = parity(me)
     for q in range(ROW):
         for place, ref in ((core, mine), (1 - core, other)):
             for to, rows, columns, tile in place_half(out_high, q + 2, place, lambda at: ref[q, at, :], B + BAND * HALF):
                 out_high[to, rows, columns], out_low[to, rows, columns] = split(tile)
-    for start, own, across in (((1 - odd) * 6, from_a, other_a), (odd * 6, from_b, other_b)):
+    ahead = lax.rem(odd + core + 1, 2)
+    for start, ref in ((ahead * 6, edge), ((1 - ahead) * 6, edge_other)):
         for q in range(2):
-            for place, ref in ((core, own), (1 - core, across)):
-                first = 2 * B + q * BAND * HALF
-                for to, rows, columns, tile in place_half(out_high, start + q, place, lambda at: ref[at, :], first):
-                    out_high[to, rows, columns], out_low[to, rows, columns] = split(tile)
+            out_high[start + q], out_low[start + q] = split(ref[q])
 
 
 def two_steps(n, me, m_high, m_low, from_a, from_b, own, v_high, v_low, w_high, w_low):
@@ -217,7 +227,7 @@
             scratch_shapes=list(scratch),
             cost_estimate=cost(flops, moved * tile_bytes),
             name=name,
-            compiler_params=pltpu.CompilerParams(vmem_limit_bytes=40 * 2**20),
+            compiler_params=pltpu.CompilerParams(vmem_limit_bytes=32 * 2**20),
         )(*args)
 
     def in_row(value, by):
@@ -233,52 +243,59 @@
 
         return [swap_rows(to_a, 0), swap_rows(to_b, 1)]
 
-    chunks = 1
+    def apart(value):
+        pairs = []
+        for core in range(2):
+            for r in range(core, rows - 1, 2):
+                for x in range(ROW):
+                    ends = [((r + i) * ROW + x) * 2 + core for i in range(2)]
+                    pairs += [tuple(ends), tuple(ends[::-1])]
+        return lax.ppermute(value, ("row", "x", "orb"), pairs)
+
     slots = neighbours.shape[1]
-    half_block = pl.BlockSpec(
-        (1, slots, HALF // chunks, B), lambda i, where, nbr, pat: (0, 0, lax.rem(where[0], 2) * chunks + i, 0)
-    )
-    packed_shape = (ROW, B + 2 * BAND * HALF, B)
+    hbm = pl.BlockSpec(memory_space=pltpu.HBM)
+    half_blocks = pltpu.VMEM((slots, HALF, B), F32)
     packed = pl.pallas_call(
         pack_kernel,
-        grid_spec=pltpu.PrefetchScalarGridSpec(
-            num_scalar_prefetch=3,
-            grid=(chunks,),
-            in_specs=[pl.BlockSpec(coefficients.shape, lambda i, *_: (0, 0, 0, 0)), half_block, half_block],
-            out_specs=pl.BlockSpec(packed_shape, lambda i, *_: (0, 0, 0)),
-        ),
-        out_shape=struct(packed_shape, F32),
+        in_specs=[SMEM] * 3 + [hbm] * 3,
+        out_specs=VMEM,
+        out_shape=struct((ROW, B + 2 * BAND * HALF, B), F32),
+        scratch_shapes=[
+            pltpu.VMEM(coefficients.shape, F32), half_blocks, half_blocks, pltpu.SemaphoreType.DMA((3,))
+        ],
         cost_estimate=cost(10**6, 44 * tile_bytes),
         name="pack",
+        compiler_params=pltpu.CompilerParams(vmem_limit_bytes=60 * 2**20),
     )(me, neighbours, pattern, coefficients, margin, step_matrix)
     mine = lax.all_to_all(packed, "x", 0, 0, tiled=True)
 
     state = struct((ROW * B, B), F32)
-    edge = struct((2 * B + 2 * BAND * HALF, B), F32)
+    edge = struct((2 * B, B), F32)
     edges = call(edge_kernel, [edge, edge], [me, mine], 10**5, 28, "edges")
     *edges, held = lax.optimization_barrier((*edges, mine))
     other = swap(held)
     from_a, from_b = exchange(*edges)
-
-    _, held = lax.optimization_barrier((edges[0], coefficients))
-    old = [coefficients, in_row(held, 1), None, in_row(held, ROW - 1)]
+    step_edge = call(step_edge_kernel, struct((2, B, BAND * B), F32), [me, mine, other], 10**5, 20, "step_edges")
+    step_edge = apart(step_edge)
+
     _, held = lax.optimization_barrier((other, coefficients))
-    old[2] = in_row(held, 2)
-    from_b, old[1], old[3] = lax.optimization_barrier((from_b, old[1], old[3]))
+    old = [coefficients, in_row(held, 1), in_row(held, 2), None]
     y0 = call(
-        margin_kernel, state, [me, mine, other, from_a, from_b], ROW * step_flops, 60, "margin",
+        margin_kernel, state, [me, mine, other, from_a, from_b], 10**10, 60, "margin",
         scratch=[pltpu.VMEM((ROW, B, BAND * B), F32)] + [pltpu.VMEM((2 * ROW * B, B), BF16)] * 2,
     )
+    arrived = exchange(y0, y0)
+    _, held = lax.optimization_barrier((old[2], coefficients))
+    old[3] = in_row(held, 3)
+    *arrived, step_edge, old[1], old[2], old[3] = lax.optimization_barrier((*arrived, step_edge, *old[1:]))
     parts_type = struct((2 * ROW, B, BAND * B), BF16)
     step = list(
         call(
-            parts_kernel, [parts_type, parts_type], [me, mine, other, from_a, from_b, swap(from_a), swap(from_b)],
+            parts_kernel, [parts_type, parts_type], [me, mine, other, step_edge, swap(step_edge)],
             10**6, 80, "step_parts",
         )
     )
     scratch = [pltpu.VMEM((3 * ROW * B, B), BF16)] * 2 + [pltpu.VMEM((2 * ROW * B, B), BF16)] * 2
-    arrived = exchange(y0, y0)
-    arrived[0], old[2] = lax.optimization_barrier((arrived[0], old[2]))
     y1, y2 = call(
         functools.partial(two_kernel, 1), [state, state], [me] + step + arrived + [y0], 3 * ROW * step_flops, 64,
         "two", scratch=scratch,

time: 108 us -> 106 us (0.981)
  waiting for transfers between devices: 20.3 us -> 17.2 us
  starting transfers between devices: 27.7 us -> 29.4 us
    ppermute x6, waiting for transfers between devices: 13.6 us -> 10.4 us  [swap_rows(): return lax.ppermute(value, 'row', pairs + [(j, i) for i, j in pairs])]
    ppermute x0 -> x1, starting transfers between devices: none -> 1.92 us  [apart(): return lax.ppermute(value, ('row', 'x', 'orb'), pairs)]
    ppermute x6, starting transfers between devices: 9.65 us -> 7.76 us  [in_row(): return lax.ppermute(value, 'x', [(x, (x + by) % ROW) for x in range(ROW)])]
    ppermute x6, starting transfers between devices: 17.3 us -> 18.5 us  [swap_rows(): return lax.ppermute(value, 'row', pairs + [(j, i) for i, j in pairs])]
    pallas_call x9 -> x10, Pallas kernels: 7.59 us -> 7.63 us  [call(): pl.pallas_call(kernel, out_shape=out_shape, in_specs=[SMEM] * scalars + [...]
  transfers between devices with their start and end apart: 19 -> 19, of which waited for: 11 -> 10; matrix products, arithmetic and copies ran while one was open for 0% -> 0% of each run, Pallas kernels for 3% -> 4%
where the time goes in v8:
time: 106 us
  blocking collectives  47.4 us (45%)
  starting transfers between devices  29.4 us (28%)
  waiting for transfers between devices  17.2 us (16%)
  Pallas kernels  11.1 us (10%)
    all_to_all x1, blocking collectives, local(): mine = lax.all_to_all(packed, 'x', 0, 0, tiled=True)  25 us
    all_to_all x1, blocking collectives, local(): sums = lax.all_to_all(partial_value, 'row', 0, 0, tiled=True)  22.4 us
    ppermute x6, starting transfers between devices, swap_rows(): return lax.ppermute(value, 'row', pairs + [(j, i) for i, j in pairs])  18.5 us
    ppermute x6, waiting for transfers between devices, swap_rows(): return lax.ppermute(value, 'row', pairs + [(j, i) for i, j in pairs])  10.4 us
    ppermute x6, starting transfers between devices, in_row(): return lax.ppermute(value, 'x', [(x, (x + by) % ROW) for x in range(ROW)])  7.76 us
    pallas_call x10, Pallas kernels, call(): pl.pallas_call(kernel, out_shape=out_shape, in_specs=[SMEM] * scalars + [...  7.63 us
    ppermute x6, waiting for transfers between devices, in_row(): return lax.ppermute(value, 'x', [(x, (x + by) % ROW) for x in range(ROW)])  5.76 us
    pallas_call x1, Pallas kernels, local(): pl.pallas_call(pack_kernel, in_specs=[SMEM] * 3 + [hbm] * 3, out_specs=VM...  3.43 us
  transfers between devices with their start and end apart: 19, of which 10 were waited for; matrix products, arithmetic and copies ran while one was open for 0% of the time, Pallas kernels for 4%

profile of v8, /device:TPU:32, one launch (start us, length us, event | category | flops | bytes accessed | tf_op | source)
XLA Modules:
  0.0 105.9 jit_solution(6338211350050748659)
XLA Ops:
  0.6 3.4 %pack.1 = f32[4,768,128]{2,1,0:T(8,128)} custom-call(s32[1]{0:T(128)} %bitcast.me, s32[1,16]{1,0:T(1,128)} %nbr.1, s32[1,16]{1,0:T(1,128)} %pat.1, f32[2,1,128,256]{3,2,1,0:T(8,128)} %c0.1, f32[1,16,128,128]{3,2,1,0:T(8,128)} %margin_hbm.1, f32[1,16,128,128]{3,2,1,0:T(8,128)} %step_hbm.1), custom_call_target="tpu_custom_call" | custom-call | flops 1000000 | bytes 2883584 | tf_op jit(solution)/shard_map/pack/pallas_call | solution.py:258
  4.1 25.0 %all_to_all.16.mine = f32[4,768,128]{2,1,0:T(8,128)S(1)} all-to-all(f32[4,768,128]{2,1,0:T(8,128)} %pack.1), channel_id=1, replica_groups=mesh['row'=32,'x'=4,'orb'=2] {'x'}, dimensions={0} | all-to-all | bytes 3145728 | tf_op jit(solution)/shard_map/all_to_all | solution.py:270
  29.4 5.6 %collective-permute-start.2 = (f32[256,128]{1,0:T(8,128)S(1)}, f32[256,128]{1,0:T(8,128)S(1)}, u32[]{:S(2)}, u32[]{:S(2)}) collective-permute-start(f32[256,128]{1,0:T(8,128)S(1)} %get-tuple-element.31), channel_id=1, source_target_pairs={{8,16},{24,32},{40,48},{56,64},{72,80},{88,96},{104,112},{120,128}... | collective-permute-start | bytes 393224 | tf_op jit(solution)/shard_map/ppermute | solution.py:242
  35.1 1.9 %collective-permute-start.5 = (f32[2,128,640]{2,1,0:T(8,128)S(1)}, f32[2,128,640]{2,1,0:T(8,128)S(1)}, u32[]{:S(2)}, u32[]{:S(2)}) collective-permute-start(f32[2,128,640]{2,1,0:T(8,128)S(1)} %step_edges.1), channel_id=1, source_target_pairs={{0,8},{8,0},{2,10},{10,2},{4,12},{12,4},{6,14},{14,6},{16,24},{24,... | collective-permute-start | bytes 1966088 | tf_op jit(solution)/shard_map/ppermute | solution.py:253
  37.1 0.9 collective-permute-start.7
  38.0 0.9 collective-permute-done.2.from_b
  38.9 0.8 margin.1.own.y0
  39.7 1.2 %collective-permute-start.3 = (f32[512,128]{1,0:T(8,128)S(1)}, f32[512,128]{1,0:T(8,128)S(1)}, u32[]{:S(2)}, u32[]{:S(2)}) collective-permute-start(f32[512,128]{1,0:T(8,128)S(1)} %margin.1.own.y0), channel_id=1, source_target_pairs={{0,8},{16,24},{32,40},{48,56},{64,72},{80,88},{96,104},{112,120},{... | collective-permute-start | bytes 786440 | tf_op jit(solution)/shard_map/ppermute | solution.py:242
  40.9 4.9 %collective-permute-start.4 = (f32[512,128]{1,0:T(8,128)S(1)}, f32[512,128]{1,0:T(8,128)S(1)}, u32[]{:S(2)}, u32[]{:S(2)}) collective-permute-start(f32[512,128]{1,0:T(8,128)S(1)} %margin.1.own.y0), channel_id=1, source_target_pairs={{8,16},{24,32},{40,48},{56,64},{72,80},{88,96},{104,112},{120,128}... | collective-permute-start | bytes 786440 | tf_op jit(solution)/shard_map/ppermute | solution.py:242
  45.8 0.6 collective-permute-start.6
  46.7 2.3 %collective-permute-start.8 = (f32[2,1,128,256]{3,2,1,0:T(8,128)S(1)}, f32[2,1,128,256]{3,2,1,0:T(8,128)S(1)}, u32[]{:S(2)}, u32[]{:S(2)}) collective-permute-start(f32[2,1,128,256]{3,2,1,0:T(8,128)S(1)} %copy-done), channel_id=1, source_target_pairs={{0,6},{2,0},{4,2},{6,4},{1,7},{3,1},{5,3},{7,5},{8,14},{10,8},{12,... | collective-permute-start | bytes 786440 | tf_op jit(solution)/shard_map/ppermute | solution.py:234
  49.1 4.2 %collective-permute-done.3.from_a = f32[512,128]{1,0:T(8,128)S(1)} collective-permute-done((f32[512,128]{1,0:T(8,128)S(1)}, f32[512,128]{1,0:T(8,128)S(1)}, u32[]{:S(2)}, u32[]{:S(2)}) %collective-permute-start.3) | collective-permute-done | bytes 262176 | tf_op jit(solution)/shard_map/ppermute | solution.py:242
  53.2 1.1 %collective-permute-done.6.c1 = f32[2,1,128,256]{3,2,1,0:T(8,128)S(1)} collective-permute-done((f32[2,1,128,256]{3,2,1,0:T(8,128)S(1)}, f32[2,1,128,256]{3,2,1,0:T(8,128)S(1)}, u32[]{:S(2)}, u32[]{:S(2)}) %collective-permute-start.6) | collective-permute-done | bytes 262176 | tf_op jit(solution)/shard_map/ppermute | solution.py:234
  54.4 0.5 collective-permute-start.11
  55.0 0.4 collective-permute-start.13
  55.5 1.0 collective-permute-done.9.edge_other
  56.4 0.4 step_parts.1
  56.9 1.8 %two.1 = (f32[512,128]{1,0:T(8,128)S(1)}, f32[512,128]{1,0:T(8,128)S(1)}) custom-call(s32[1]{0:T(128)} %bitcast.me, bf16[8,128,640]{2,1,0:T(8,128)(2,1)S(1)} %get-tuple-element.35.m_high, bf16[8,128,640]{2,1,0:T(8,128)(2,1)S(1)} %get-tuple-element.36.m_low, f32[512,128]{1,0:T(8,128)S(1)} %collective-permute-done.3.from_a, ...), custom_call_target="tpu_custom_call" | custom-call | flops 754974720 | bytes 4194304 | tf_op jit(solution)/shard_map/two/pallas_call | solution.py:222
  58.7 0.8 collective-permute-start.10
  59.5 5.8 %collective-permute-start.15 = (f32[512,128]{1,0:T(8,128)S(1)}, f32[512,128]{1,0:T(8,128)S(1)}, u32[]{:S(2)}, u32[]{:S(2)}) collective-permute-start(f32[512,128]{1,0:T(8,128)S(1)} %get-tuple-element.39.own), channel_id=1, source_target_pairs={{8,16},{24,32},{40,48},{56,64},{72,80},{88,96},{104,112},{120,128}... | collective-permute-start | bytes 786440 | tf_op jit(solution)/shard_map/ppermute | solution.py:242
  65.4 0.7 old_parts.1
  66.1 1.0 collective-permute-done.10.from_a
  67.1 4.4 %collective-permute-done.15.from_b = f32[512,128]{1,0:T(8,128)S(1)} collective-permute-done((f32[512,128]{1,0:T(8,128)S(1)}, f32[512,128]{1,0:T(8,128)S(1)}, u32[]{:S(2)}, u32[]{:S(2)}) %collective-permute-start.15) | collective-permute-done | bytes 262176 | tf_op jit(solution)/shard_map/ppermute | solution.py:242
  71.5 1.8 %last.1.new = f32[4,128,128]{2,1,0:T(8,128)S(1)} custom-call(s32[1]{0:T(128)} %bitcast.me, bf16[8,128,640]{2,1,0:T(8,128)(2,1)S(1)} %get-tuple-element.35.m_high, bf16[8,128,640]{2,1,0:T(8,128)(2,1)S(1)} %get-tuple-element.36.m_low, f32[512,128]{1,0:T(8,128)S(1)} %collective-permute-done.10.from_a, f32[512,128]{1,0:T(8,128)S(1)} %collective-permute-done.15.from_b, ...), custom_call_target="tpu_custom_call" | custom-call | flops 754974720 | bytes 4718592 | tf_op jit(solution)/shard_map/last/pallas_call | solution.py:222
  73.3 1.0 project.1
  74.3 22.4 %all_to_all.17 = f32[32,16,128]{2,1,0:T(8,128)S(1)} all-to-all(f32[32,16,128]{2,1,0:T(8,128)S(1)} %bitcast.4), channel_id=1, replica_groups=mesh['row'=32,'x'=4,'orb'=2] {'row'}, dimensions={0} | all-to-all | bytes 524288 | tf_op jit(solution)/shard_map/all_to_all | solution.py:317
  96.8 0.6 collective-permute-start.16
  97.5 3.2 %collective-permute-start.17 = (f32[136,128]{1,0:T(8,128)S(1)}, f32[136,128]{1,0:T(8,128)S(1)}, u32[]{:S(2)}, u32[]{:S(2)}) collective-permute-start(f32[136,128]{1,0:T(8,128)S(1)} %get-tuple-element.50), channel_id=1, source_target_pairs={{0,4},{2,6},{4,0},{6,2},{1,5},{3,7},{5,1},{7,3},{8,12},{10,14},{12... | collective-permute-start | bytes 208904 | tf_op jit(solution)/shard_map/ppermute | solution.py:234
  100.7 1.7 %collective-permute-done.16.b1 = f32[136,128]{1,0:T(8,128)S(1)} collective-permute-done((f32[136,128]{1,0:T(8,128)S(1)}, f32[136,128]{1,0:T(8,128)S(1)}, u32[]{:S(2)}, u32[]{:S(2)}) %collective-permute-start.16) | collective-permute-done | bytes 69664 | tf_op jit(solution)/shard_map/ppermute | solution.py:234
  102.4 1.3 %collective-permute-done.17.b2 = f32[136,128]{1,0:T(8,128)S(1)} collective-permute-done((f32[136,128]{1,0:T(8,128)S(1)}, f32[136,128]{1,0:T(8,128)S(1)}, u32[]{:S(2)}, u32[]{:S(2)}) %collective-permute-start.17) | collective-permute-done | bytes 69664 | tf_op jit(solution)/shard_map/ppermute | solution.py:234
  103.7 1.3 %collective-permute-done.18.b3 = f32[136,128]{1,0:T(8,128)S(1)} collective-permute-done((f32[136,128]{1,0:T(8,128)S(1)}, f32[136,128]{1,0:T(8,128)S(1)}, u32[]{:S(2)}, u32[]{:S(2)}) %collective-permute-start.18) | collective-permute-done | bytes 69664 | tf_op jit(solution)/shard_map/ppermute | solution.py:234
  105.0 0.9 finish.1
  (21 shorter events, 1.0 us)
Async XLA Ops:
  29.1 7.9 %copy-start = (f32[2,1,128,256]{3,2,1,0:T(8,128)S(1)}, f32[2,1,128,256]{3,2,1,0:T(8,128)}, u32[]{:S(2)}) copy-start(f32[2,1,128,256]{3,2,1,0:T(8,128)} %c0.1) | copy-start | bytes 786436
  29.1 5.9 %collective-permute-start = (f32[4,768,128]{2,1,0:T(8,128)S(1)}, f32[4,768,128]{2,1,0:T(8,128)S(1)}, u32[]{:S(2)}, u32[]{:S(2)}) collective-permute-start(f32[4,768,128]{2,1,0:T(8,128)S(1)} %all_to_all.16.mine), channel_id=1, source_target_pairs={{0,1},{1,0},{2,3},{3,2},{4,5},{5,4},{6,7},{7,6},{8,9},{9,8},{10,11... | collective-permute-start | bytes 4718600 | tf_op jit(solution)/shard_map/ppermute | solution.py:237
  29.2 8.7 %collective-permute-start.1 = (f32[256,128]{1,0:T(8,128)S(1)}, f32[256,128]{1,0:T(8,128)S(1)}, u32[]{:S(2)}, u32[]{:S(2)}) collective-permute-start(f32[256,128]{1,0:T(8,128)S(1)} %get-tuple-element.30), channel_id=1, source_target_pairs={{0,8},{16,24},{32,40},{48,56},{64,72},{80,88},{96,104},{112,120},{... | collective-permute-start | bytes 393224 | tf_op jit(solution)/shard_map/ppermute | solution.py:242
  29.4 9.5 %collective-permute-start.2 = (f32[256,128]{1,0:T(8,128)S(1)}, f32[256,128]{1,0:T(8,128)S(1)}, u32[]{:S(2)}, u32[]{:S(2)}) collective-permute-start(f32[256,128]{1,0:T(8,128)S(1)} %get-tuple-element.31), channel_id=1, source_target_pairs={{8,16},{24,32},{40,48},{56,64},{72,80},{88,96},{104,112},{120,128}... | collective-permute-start | bytes 393224 | tf_op jit(solution)/shard_map/ppermute | solution.py:242
  35.1 19.2 %collective-permute-start.5 = (f32[2,128,640]{2,1,0:T(8,128)S(1)}, f32[2,128,640]{2,1,0:T(8,128)S(1)}, u32[]{:S(2)}, u32[]{:S(2)}) collective-permute-start(f32[2,128,640]{2,1,0:T(8,128)S(1)} %step_edges.1), channel_id=1, source_target_pairs={{0,8},{8,0},{2,10},{10,2},{4,12},{12,4},{6,14},{14,6},{16,24},{24,... | collective-permute-start | bytes 1966088 | tf_op jit(solution)/shard_map/ppermute | solution.py:253
  37.1 9.7 %collective-permute-start.7 = (f32[2,1,128,256]{3,2,1,0:T(8,128)S(1)}, f32[2,1,128,256]{3,2,1,0:T(8,128)S(1)}, u32[]{:S(2)}, u32[]{:S(2)}) collective-permute-start(f32[2,1,128,256]{3,2,1,0:T(8,128)S(1)} %copy-done), channel_id=1, source_target_pairs={{0,4},{2,6},{4,0},{6,2},{1,5},{3,7},{5,1},{7,3},{8,12},{10,14},{12... | collective-permute-start | bytes 786440 | tf_op jit(solution)/shard_map/ppermute | solution.py:234
  39.7 13.6 %collective-permute-start.3 = (f32[512,128]{1,0:T(8,128)S(1)}, f32[512,128]{1,0:T(8,128)S(1)}, u32[]{:S(2)}, u32[]{:S(2)}) collective-permute-start(f32[512,128]{1,0:T(8,128)S(1)} %margin.1.own.y0), channel_id=1, source_target_pairs={{0,8},{16,24},{32,40},{48,56},{64,72},{80,88},{96,104},{112,120},{... | collective-permute-start | bytes 786440 | tf_op jit(solution)/shard_map/ppermute | solution.py:242
  40.9 12.4 %collective-permute-start.4 = (f32[512,128]{1,0:T(8,128)S(1)}, f32[512,128]{1,0:T(8,128)S(1)}, u32[]{:S(2)}, u32[]{:S(2)}) collective-permute-start(f32[512,128]{1,0:T(8,128)S(1)} %margin.1.own.y0), channel_id=1, source_target_pairs={{8,16},{24,32},{40,48},{56,64},{72,80},{88,96},{104,112},{120,128}... | collective-permute-start | bytes 786440 | tf_op jit(solution)/shard_map/ppermute | solution.py:242
  45.8 8.6 %collective-permute-start.6 = (f32[2,1,128,256]{3,2,1,0:T(8,128)S(1)}, f32[2,1,128,256]{3,2,1,0:T(8,128)S(1)}, u32[]{:S(2)}, u32[]{:S(2)}) collective-permute-start(f32[2,1,128,256]{3,2,1,0:T(8,128)S(1)} %copy-done), channel_id=1, source_target_pairs={{0,2},{2,4},{4,6},{6,0},{1,3},{3,5},{5,7},{7,1},{8,10},{10,12},{12... | collective-permute-start | bytes 786440 | tf_op jit(solution)/shard_map/ppermute | solution.py:234
  46.7 7.6 %collective-permute-start.8 = (f32[2,1,128,256]{3,2,1,0:T(8,128)S(1)}, f32[2,1,128,256]{3,2,1,0:T(8,128)S(1)}, u32[]{:S(2)}, u32[]{:S(2)}) collective-permute-start(f32[2,1,128,256]{3,2,1,0:T(8,128)S(1)} %copy-done), channel_id=1, source_target_pairs={{0,6},{2,0},{4,2},{6,4},{1,7},{3,1},{5,3},{7,5},{8,14},{10,8},{12,... | collective-permute-start | bytes 786440 | tf_op jit(solution)/shard_map/ppermute | solution.py:234
  54.3 2.1 %collective-permute-start.9 = (f32[2,128,640]{2,1,0:T(8,128)S(1)}, f32[2,128,640]{2,1,0:T(8,128)S(1)}, u32[]{:S(2)}, u32[]{:S(2)}) collective-permute-start(f32[2,128,640]{2,1,0:T(8,128)S(1)} %collective-permute-done.5.edge), channel_id=1, source_target_pairs={{0,1},{1,0},{2,3},{3,2},{4,5},{5,4},{6,7},{7,6},{8,9},{9,8},{10,11... | collective-permute-start | bytes 1966088 | tf_op jit(solution)/shard_map/ppermute | solution.py:237
  54.4 5.2 %collective-permute-start.11 = (f32[2,1,128,256]{3,2,1,0:T(8,128)S(1)}, f32[2,1,128,256]{3,2,1,0:T(8,128)S(1)}, u32[]{:S(2)}, u32[]{:S(2)}) collective-permute-start(f32[2,1,128,256]{3,2,1,0:T(8,128)S(1)} %copy-done), channel_id=1, source_target_pairs={{0,1},{1,0},{2,3},{3,2},{4,5},{5,4},{6,7},{7,6},{8,9},{9,8},{10,11... | collective-permute-start | bytes 786440 | tf_op jit(solution)/shard_map/ppermute | solution.py:237
  54.9 10.5 %collective-permute-start.12 = (f32[2,1,128,256]{3,2,1,0:T(8,128)S(1)}, f32[2,1,128,256]{3,2,1,0:T(8,128)S(1)}, u32[]{:S(2)}, u32[]{:S(2)}) collective-permute-start(f32[2,1,128,256]{3,2,1,0:T(8,128)S(1)} %collective-permute-done.6.c1), channel_id=1, source_target_pairs={{0,1},{1,0},{2,3},{3,2},{4,5},{5,4},{6,7},{7,6},{8,9},{9,8},{10,11... | collective-permute-start | bytes 786440 | tf_op jit(solution)/shard_map/ppermute | solution.py:237
  55.0 10.4 %collective-permute-start.13 = (f32[2,1,128,256]{3,2,1,0:T(8,128)S(1)}, f32[2,1,128,256]{3,2,1,0:T(8,128)S(1)}, u32[]{:S(2)}, u32[]{:S(2)}) collective-permute-start(f32[2,1,128,256]{3,2,1,0:T(8,128)S(1)} %collective-permute-done.7.c2), channel_id=1, source_target_pairs={{0,1},{1,0},{2,3},{3,2},{4,5},{5,4},{6,7},{7,6},{8,9},{9,8},{10,11... | collective-permute-start | bytes 786440 | tf_op jit(solution)/shard_map/ppermute | solution.py:237
  55.4 10.0 %collective-permute-start.14 = (f32[2,1,128,256]{3,2,1,0:T(8,128)S(1)}, f32[2,1,128,256]{3,2,1,0:T(8,128)S(1)}, u32[]{:S(2)}, u32[]{:S(2)}) collective-permute-start(f32[2,1,128,256]{3,2,1,0:T(8,128)S(1)} %collective-permute-done.8.c3), channel_id=1, source_target_pairs={{0,1},{1,0},{2,3},{3,2},{4,5},{5,4},{6,7},{7,6},{8,9},{9,8},{10,11... | collective-permute-start | bytes 786440 | tf_op jit(solution)/shard_map/ppermute | solution.py:237
  58.7 8.4 %collective-permute-start.10 = (f32[512,128]{1,0:T(8,128)S(1)}, f32[512,128]{1,0:T(8,128)S(1)}, u32[]{:S(2)}, u32[]{:S(2)}) collective-permute-start(f32[512,128]{1,0:T(8,128)S(1)} %get-tuple-element.39.own), channel_id=1, source_target_pairs={{0,8},{16,24},{32,40},{48,56},{64,72},{80,88},{96,104},{112,120},{... | collective-permute-start | bytes 786440 | tf_op jit(solution)/shard_map/ppermute | solution.py:242
  59.5 12.0 %collective-permute-start.15 = (f32[512,128]{1,0:T(8,128)S(1)}, f32[512,128]{1,0:T(8,128)S(1)}, u32[]{:S(2)}, u32[]{:S(2)}) collective-permute-start(f32[512,128]{1,0:T(8,128)S(1)} %get-tuple-element.39.own), channel_id=1, source_target_pairs={{8,16},{24,32},{40,48},{56,64},{72,80},{88,96},{104,112},{120,128}... | collective-permute-start | bytes 786440 | tf_op jit(solution)/shard_map/ppermute | solution.py:242
  96.8 5.6 %collective-permute-start.16 = (f32[136,128]{1,0:T(8,128)S(1)}, f32[136,128]{1,0:T(8,128)S(1)}, u32[]{:S(2)}, u32[]{:S(2)}) collective-permute-start(f32[136,128]{1,0:T(8,128)S(1)} %get-tuple-element.49), channel_id=1, source_target_pairs={{0,2},{2,4},{4,6},{6,0},{1,3},{3,5},{5,7},{7,1},{8,10},{10,12},{12... | collective-permute-start | bytes 208904 | tf_op jit(solution)/shard_map/ppermute | solution.py:234
  97.5 6.3 %collective-permute-start.17 = (f32[136,128]{1,0:T(8,128)S(1)}, f32[136,128]{1,0:T(8,128)S(1)}, u32[]{:S(2)}, u32[]{:S(2)}) collective-permute-start(f32[136,128]{1,0:T(8,128)S(1)} %get-tuple-element.50), channel_id=1, source_target_pairs={{0,4},{2,6},{4,0},{6,2},{1,5},{3,7},{5,1},{7,3},{8,12},{10,14},{12... | collective-permute-start | bytes 208904 | tf_op jit(solution)/shard_map/ppermute | solution.py:234
  100.7 4.3 %collective-permute-start.18 = (f32[136,128]{1,0:T(8,128)S(1)}, f32[136,128]{1,0:T(8,128)S(1)}, u32[]{:S(2)}, u32[]{:S(2)}) collective-permute-start(f32[136,128]{1,0:T(8,128)S(1)} %get-tuple-element.51), channel_id=1, source_target_pairs={{0,6},{2,0},{4,2},{6,4},{1,7},{3,1},{5,3},{7,5},{8,14},{10,8},{12,... | collective-permute-start | bytes 208904 | tf_op jit(solution)/shard_map/ppermute | solution.py:234

commit v9 on v8

--- a/solution.py
+++ b/solution.py
@@ -28,9 +28,14 @@
     return high, (value - high.astype(F32)).astype(BF16)
 
 
-def product(a_high, a_low, b_high, b_low):
+def product(a_high, a_low, b):
     dot = functools.partial(jnp.dot, preferred_element_type=F32)
-    return dot(a_high, b_high) + (dot(a_high, b_low) + dot(a_low, b_high))
+    both = dot(a_high, b)
+    return both[:, :B] + (both[:, B:] + dot(a_low, b[:, :B]))
+
+
+def put_parts(out, rows, value):
+    out[rows, :B], out[rows, B:] = split(value)
 
 
 def turned(value):
@@ -103,18 +108,17 @@
                 out[to, rows, columns] = tile
 
 
-def window(odd, from_a, from_b, own, v_high, v_low):
+def window(odd, from_a, from_b, own, v):
     reach, size = from_a.shape[0], own.shape[0]
-    v_high[reach : reach + size, :], v_low[reach : reach + size, :] = split(own)
+    put_parts(v, slice(reach, reach + size), own)
     for start, tile in (((1 - odd) * (reach + size), from_a), (odd * (reach + size), from_b)):
-        rows = pl.ds(pl.multiple_of(start, B), reach)
-        v_high[rows, :], v_low[rows, :] = split(tile)
-
-
-def margin_kernel(me, mine, other, from_a, from_b, out, full, v_high, v_low):
+        put_parts(v, pl.ds(pl.multiple_of(start, B), reach), tile)
+
+
+def margin_kernel(me, mine, other, from_a, from_b, out, full, v):
     _, core = member(me)
     own = [mine[q, :B, :] for q in range(ROW)]
-    window(parity(me), from_a[...], from_b[...], jnp.concatenate(own, axis=0), v_high, v_low)
+    window(parity(me), from_a[...], from_b[...], jnp.concatenate(own, axis=0), v)
     for q in range(ROW):
         for place, ref in ((core, mine), (1 - core, other)):
             for _, rows, columns, tile in place_half(full, q, place, lambda at: ref[q, at, :], B):
@@ -122,7 +126,7 @@
     for q in range(ROW):
         m_high, m_low = split(full[q])
         rows = slice(q * B, (q + BAND) * B)
-        out[q * B : (q + 1) * B, :] = own[q] + product(m_high, m_low, v_high[rows], v_low[rows])
+        out[q * B : (q + 1) * B, :] = own[q] + product(m_high, m_low, v[rows, :])
 
 
 def parts_kernel(me, mine, other, edge, edge_other, out_high, out_low):
@@ -138,17 +142,17 @@
             out_high[start + q], out_low[start + q] = split(ref[q])
 
 
-def two_steps(n, me, m_high, m_low, from_a, from_b, own, v_high, v_low, w_high, w_low):
-    window(parity(me), from_a[...], from_b[...], own[...], v_high, v_low)
+def two_steps(n, me, m_high, m_low, from_a, from_b, own, v, w):
+    window(parity(me), from_a[...], from_b[...], own[...], v)
     firsts = []
     for q in range(2 * ROW):
         rows = slice(q * B, (q + BAND) * B)
-        value = product(m_high[q], m_low[q], v_high[rows], v_low[rows]) * F32(1.0 / n)
-        w_high[q * B : (q + 1) * B, :], w_low[q * B : (q + 1) * B, :] = split(value)
+        value = product(m_high[q], m_low[q], v[rows, :]) * F32(1.0 / n)
+        put_parts(w, slice(q * B, (q + 1) * B), value)
         firsts.append(value)
     for q in range(ROW):
         rows = slice(q * B, (q + BAND) * B)
-        second = product(m_high[q + 2], m_low[q + 2], w_high[rows], w_low[rows]) * F32(1.0 / (n + 1))
+        second = product(m_high[q + 2], m_low[q + 2], w[rows, :]) * F32(1.0 / (n + 1))
         yield q, firsts[q + 2], second
 
 
@@ -180,8 +184,8 @@
 def project_kernel(me, old_high, old_low, new, out):
     x, _ = member(me)
     tiles = [new[turn_to(q, x)] for q in range(ROW)]
-    v_high, v_low = split(jnp.concatenate(tiles + [turned(t) for t in tiles], axis=0))
-    out[...] = product(old_high[...], old_low[...], v_high, v_low)
+    parts = split(jnp.concatenate(tiles + [turned(t) for t in tiles], axis=0))
+    out[...] = product(old_high[...], old_low[...], jnp.concatenate(parts, axis=1))
 
 
 def tail_kernel(scale, me, sums, new, *outs):
@@ -282,7 +286,7 @@
     old = [coefficients, in_row(held, 1), in_row(held, 2), None]
     y0 = call(
         margin_kernel, state, [me, mine, other, from_a, from_b], 10**10, 60, "margin",
-        scratch=[pltpu.VMEM((ROW, B, BAND * B), F32)] + [pltpu.VMEM((2 * ROW * B, B), BF16)] * 2,
+        scratch=[pltpu.VMEM((ROW, B, BAND * B), F32)] + [pltpu.VMEM((2 * ROW * B, 2 * B), BF16)],
     )
     arrived = exchange(y0, y0)
     _, held = lax.optimization_barrier((old[2], coefficients))
@@ -295,7 +299,7 @@
             10**6, 80, "step_parts",
         )
     )
-    scratch = [pltpu.VMEM((3 * ROW * B, B), BF16)] * 2 + [pltpu.VMEM((2 * ROW * B, B), BF16)] * 2
+    scratch = [pltpu.VMEM((3 * ROW * B, 2 * B), BF16), pltpu.VMEM((2 * ROW * B, 2 * B), BF16)]
     y1, y2 = call(
         functools.partial(two_kernel, 1), [state, state], [me] + step + arrived + [y0], 3 * ROW * step_flops, 64,
         "two", scratch=scratch,

time: 106 us -> 105 us (level)
  transfers between devices with their start and end apart: 19 -> 19, of which waited for: 10 -> 10; matrix products, arithmetic and copies ran while one was open for 0% -> 0% of each run, Pallas kernels for 4% -> 3%
where the time goes in v9:
time: 105 us
  blocking collectives  47.4 us (45%)
  starting transfers between devices  29.5 us (28%)
  waiting for transfers between devices  17.2 us (16%)
  Pallas kernels  10.2 us (10%)
    all_to_all x1, blocking collectives, local(): mine = lax.all_to_all(packed, 'x', 0, 0, tiled=True)  25 us
    all_to_all x1, blocking collectives, local(): sums = lax.all_to_all(partial_value, 'row', 0, 0, tiled=True)  22.4 us
    ppermute x6, starting transfers between devices, swap_rows(): return lax.ppermute(value, 'row', pairs + [(j, i) for i, j in pairs])  18.6 us
    ppermute x6, waiting for transfers between devices, swap_rows(): return lax.ppermute(value, 'row', pairs + [(j, i) for i, j in pairs])  10.5 us
    ppermute x6, starting transfers between devices, in_row(): return lax.ppermute(value, 'x', [(x, (x + by) % ROW) for x in range(ROW)])  7.75 us
    pallas_call x10, Pallas kernels, call(): pl.pallas_call(kernel, out_shape=out_shape, in_specs=[SMEM] * scalars + [...  6.74 us
    ppermute x6, waiting for transfers between devices, in_row(): return lax.ppermute(value, 'x', [(x, (x + by) % ROW) for x in range(ROW)])  5.75 us
    pallas_call x1, Pallas kernels, local(): pl.pallas_call(pack_kernel, in_specs=[SMEM] * 3 + [hbm] * 3, out_specs=VM...  3.43 us
  transfers between devices with their start and end apart: 19, of which 10 were waited for; matrix products, arithmetic and copies ran while one was open for 0% of the time, Pallas kernels for 3%

profile of v9, /device:TPU:32, one launch (start us, length us, event | category | flops | bytes accessed | tf_op | source)
XLA Modules:
  0.0 105.1 jit_solution(6940422284700064887)
XLA Ops:
  0.6 3.4 %pack.1 = f32[4,768,128]{2,1,0:T(8,128)} custom-call(s32[1]{0:T(128)} %bitcast.me, s32[1,16]{1,0:T(1,128)} %nbr.1, s32[1,16]{1,0:T(1,128)} %pat.1, f32[2,1,128,256]{3,2,1,0:T(8,128)} %c0.1, f32[1,16,128,128]{3,2,1,0:T(8,128)} %margin_hbm.1, f32[1,16,128,128]{3,2,1,0:T(8,128)} %step_hbm.1), custom_call_target="tpu_custom_call" | custom-call | flops 1000000 | bytes 2883584 | tf_op jit(solution)/shard_map/pack/pallas_call | solution.py:262
  4.1 25.0 %all_to_all.16.mine = f32[4,768,128]{2,1,0:T(8,128)S(1)} all-to-all(f32[4,768,128]{2,1,0:T(8,128)} %pack.1), channel_id=1, replica_groups=mesh['row'=32,'x'=4,'orb'=2] {'x'}, dimensions={0} | all-to-all | bytes 3145728 | tf_op jit(solution)/shard_map/all_to_all | solution.py:274
  29.4 5.6 %collective-permute-start.2 = (f32[256,128]{1,0:T(8,128)S(1)}, f32[256,128]{1,0:T(8,128)S(1)}, u32[]{:S(2)}, u32[]{:S(2)}) collective-permute-start(f32[256,128]{1,0:T(8,128)S(1)} %get-tuple-element.31), channel_id=1, source_target_pairs={{8,16},{24,32},{40,48},{56,64},{72,80},{88,96},{104,112},{120,128}... | collective-permute-start | bytes 393224 | tf_op jit(solution)/shard_map/ppermute | solution.py:246
  35.1 1.9 %collective-permute-start.5 = (f32[2,128,640]{2,1,0:T(8,128)S(1)}, f32[2,128,640]{2,1,0:T(8,128)S(1)}, u32[]{:S(2)}, u32[]{:S(2)}) collective-permute-start(f32[2,128,640]{2,1,0:T(8,128)S(1)} %step_edges.1), channel_id=1, source_target_pairs={{0,8},{8,0},{2,10},{10,2},{4,12},{12,4},{6,14},{14,6},{16,24},{24,... | collective-permute-start | bytes 1966088 | tf_op jit(solution)/shard_map/ppermute | solution.py:257
  37.1 0.9 collective-permute-start.7
  38.0 0.9 collective-permute-done.2.from_b
  38.9 0.7 margin.1.own.y0
  39.6 1.2 %collective-permute-start.3 = (f32[512,128]{1,0:T(8,128)S(1)}, f32[512,128]{1,0:T(8,128)S(1)}, u32[]{:S(2)}, u32[]{:S(2)}) collective-permute-start(f32[512,128]{1,0:T(8,128)S(1)} %margin.1.own.y0), channel_id=1, source_target_pairs={{0,8},{16,24},{32,40},{48,56},{64,72},{80,88},{96,104},{112,120},{... | collective-permute-start | bytes 786440 | tf_op jit(solution)/shard_map/ppermute | solution.py:246
  40.8 4.9 %collective-permute-start.4 = (f32[512,128]{1,0:T(8,128)S(1)}, f32[512,128]{1,0:T(8,128)S(1)}, u32[]{:S(2)}, u32[]{:S(2)}) collective-permute-start(f32[512,128]{1,0:T(8,128)S(1)} %margin.1.own.y0), channel_id=1, source_target_pairs={{8,16},{24,32},{40,48},{56,64},{72,80},{88,96},{104,112},{120,128}... | collective-permute-start | bytes 786440 | tf_op jit(solution)/shard_map/ppermute | solution.py:246
  45.7 0.6 collective-permute-start.6
  46.7 2.3 %collective-permute-start.8 = (f32[2,1,128,256]{3,2,1,0:T(8,128)S(1)}, f32[2,1,128,256]{3,2,1,0:T(8,128)S(1)}, u32[]{:S(2)}, u32[]{:S(2)}) collective-permute-start(f32[2,1,128,256]{3,2,1,0:T(8,128)S(1)} %copy-done), channel_id=1, source_target_pairs={{0,6},{2,0},{4,2},{6,4},{1,7},{3,1},{5,3},{7,5},{8,14},{10,8},{12,... | collective-permute-start | bytes 786440 | tf_op jit(solution)/shard_map/ppermute | solution.py:238
  49.0 4.2 %collective-permute-done.3.from_a = f32[512,128]{1,0:T(8,128)S(1)} collective-permute-done((f32[512,128]{1,0:T(8,128)S(1)}, f32[512,128]{1,0:T(8,128)S(1)}, u32[]{:S(2)}, u32[]{:S(2)}) %collective-permute-start.3) | collective-permute-done | bytes 262176 | tf_op jit(solution)/shard_map/ppermute | solution.py:246
  53.2 1.1 %collective-permute-done.6.c1 = f32[2,1,128,256]{3,2,1,0:T(8,128)S(1)} collective-permute-done((f32[2,1,128,256]{3,2,1,0:T(8,128)S(1)}, f32[2,1,128,256]{3,2,1,0:T(8,128)S(1)}, u32[]{:S(2)}, u32[]{:S(2)}) %collective-permute-start.6) | collective-permute-done | bytes 262176 | tf_op jit(solution)/shard_map/ppermute | solution.py:238
  54.3 0.5 collective-permute-start.11
  54.9 0.4 collective-permute-start.13
  55.4 1.0 collective-permute-done.9.edge_other
  56.4 0.4 step_parts.1
  56.9 1.5 %two.1 = (f32[512,128]{1,0:T(8,128)S(1)}, f32[512,128]{1,0:T(8,128)S(1)}) custom-call(s32[1]{0:T(128)} %bitcast.me, bf16[8,128,640]{2,1,0:T(8,128)(2,1)S(1)} %get-tuple-element.35.m_high, bf16[8,128,640]{2,1,0:T(8,128)(2,1)S(1)} %get-tuple-element.36.m_low, f32[512,128]{1,0:T(8,128)S(1)} %collective-permute-done.3.from_a, ...), custom_call_target="tpu_custom_call" | custom-call | flops 754974720 | bytes 4194304 | tf_op jit(solution)/shard_map/two/pallas_call | solution.py:226
  58.4 0.9 collective-permute-start.10
  59.3 5.8 %collective-permute-start.15 = (f32[512,128]{1,0:T(8,128)S(1)}, f32[512,128]{1,0:T(8,128)S(1)}, u32[]{:S(2)}, u32[]{:S(2)}) collective-permute-start(f32[512,128]{1,0:T(8,128)S(1)} %get-tuple-element.39.own), channel_id=1, source_target_pairs={{8,16},{24,32},{40,48},{56,64},{72,80},{88,96},{104,112},{120,128}... | collective-permute-start | bytes 786440 | tf_op jit(solution)/shard_map/ppermute | solution.py:246
  65.1 0.7 old_parts.1
  65.9 1.0 collective-permute-done.10.from_a
  66.8 4.4 %collective-permute-done.15.from_b = f32[512,128]{1,0:T(8,128)S(1)} collective-permute-done((f32[512,128]{1,0:T(8,128)S(1)}, f32[512,128]{1,0:T(8,128)S(1)}, u32[]{:S(2)}, u32[]{:S(2)}) %collective-permute-start.15) | collective-permute-done | bytes 262176 | tf_op jit(solution)/shard_map/ppermute | solution.py:246
  71.2 1.5 %last.1.new = f32[4,128,128]{2,1,0:T(8,128)S(1)} custom-call(s32[1]{0:T(128)} %bitcast.me, bf16[8,128,640]{2,1,0:T(8,128)(2,1)S(1)} %get-tuple-element.35.m_high, bf16[8,128,640]{2,1,0:T(8,128)(2,1)S(1)} %get-tuple-element.36.m_low, f32[512,128]{1,0:T(8,128)S(1)} %collective-permute-done.10.from_a, f32[512,128]{1,0:T(8,128)S(1)} %collective-permute-done.15.from_b, ...), custom_call_target="tpu_custom_call" | custom-call | flops 754974720 | bytes 4718592 | tf_op jit(solution)/shard_map/last/pallas_call | solution.py:226
  72.7 0.7 project.1
  73.5 22.4 %all_to_all.17 = f32[32,16,128]{2,1,0:T(8,128)S(1)} all-to-all(f32[32,16,128]{2,1,0:T(8,128)S(1)} %bitcast.4), channel_id=1, replica_groups=mesh['row'=32,'x'=4,'orb'=2] {'row'}, dimensions={0} | all-to-all | bytes 524288 | tf_op jit(solution)/shard_map/all_to_all | solution.py:321
  96.0 0.6 collective-permute-start.16
  96.6 3.3 %collective-permute-start.17 = (f32[136,128]{1,0:T(8,128)S(1)}, f32[136,128]{1,0:T(8,128)S(1)}, u32[]{:S(2)}, u32[]{:S(2)}) collective-permute-start(f32[136,128]{1,0:T(8,128)S(1)} %get-tuple-element.50), channel_id=1, source_target_pairs={{0,4},{2,6},{4,0},{6,2},{1,5},{3,7},{5,1},{7,3},{8,12},{10,14},{12... | collective-permute-start | bytes 208904 | tf_op jit(solution)/shard_map/ppermute | solution.py:238
  99.9 1.7 %collective-permute-done.16.b1 = f32[136,128]{1,0:T(8,128)S(1)} collective-permute-done((f32[136,128]{1,0:T(8,128)S(1)}, f32[136,128]{1,0:T(8,128)S(1)}, u32[]{:S(2)}, u32[]{:S(2)}) %collective-permute-start.16) | collective-permute-done | bytes 69664 | tf_op jit(solution)/shard_map/ppermute | solution.py:238
  101.6 1.3 %collective-permute-done.17.b2 = f32[136,128]{1,0:T(8,128)S(1)} collective-permute-done((f32[136,128]{1,0:T(8,128)S(1)}, f32[136,128]{1,0:T(8,128)S(1)}, u32[]{:S(2)}, u32[]{:S(2)}) %collective-permute-start.17) | collective-permute-done | bytes 69664 | tf_op jit(solution)/shard_map/ppermute | solution.py:238
  102.9 1.3 %collective-permute-done.18.b3 = f32[136,128]{1,0:T(8,128)S(1)} collective-permute-done((f32[136,128]{1,0:T(8,128)S(1)}, f32[136,128]{1,0:T(8,128)S(1)}, u32[]{:S(2)}, u32[]{:S(2)}) %collective-permute-start.18) | collective-permute-done | bytes 69664 | tf_op jit(solution)/shard_map/ppermute | solution.py:238
  104.2 0.9 finish.1
  (21 shorter events, 1.1 us)
Async XLA Ops:
  29.1 7.9 %copy-start = (f32[2,1,128,256]{3,2,1,0:T(8,128)S(1)}, f32[2,1,128,256]{3,2,1,0:T(8,128)}, u32[]{:S(2)}) copy-start(f32[2,1,128,256]{3,2,1,0:T(8,128)} %c0.1) | copy-start | bytes 786436
  29.1 5.9 %collective-permute-start = (f32[4,768,128]{2,1,0:T(8,128)S(1)}, f32[4,768,128]{2,1,0:T(8,128)S(1)}, u32[]{:S(2)}, u32[]{:S(2)}) collective-permute-start(f32[4,768,128]{2,1,0:T(8,128)S(1)} %all_to_all.16.mine), channel_id=1, source_target_pairs={{0,1},{1,0},{2,3},{3,2},{4,5},{5,4},{6,7},{7,6},{8,9},{9,8},{10,11... | collective-permute-start | bytes 4718600 | tf_op jit(solution)/shard_map/ppermute | solution.py:241
  29.2 8.7 %collective-permute-start.1 = (f32[256,128]{1,0:T(8,128)S(1)}, f32[256,128]{1,0:T(8,128)S(1)}, u32[]{:S(2)}, u32[]{:S(2)}) collective-permute-start(f32[256,128]{1,0:T(8,128)S(1)} %get-tuple-element.30), channel_id=1, source_target_pairs={{0,8},{16,24},{32,40},{48,56},{64,72},{80,88},{96,104},{112,120},{... | collective-permute-start | bytes 393224 | tf_op jit(solution)/shard_map/ppermute | solution.py:246
  29.4 9.5 %collective-permute-start.2 = (f32[256,128]{1,0:T(8,128)S(1)}, f32[256,128]{1,0:T(8,128)S(1)}, u32[]{:S(2)}, u32[]{:S(2)}) collective-permute-start(f32[256,128]{1,0:T(8,128)S(1)} %get-tuple-element.31), channel_id=1, source_target_pairs={{8,16},{24,32},{40,48},{56,64},{72,80},{88,96},{104,112},{120,128}... | collective-permute-start | bytes 393224 | tf_op jit(solution)/shard_map/ppermute | solution.py:246
  35.1 19.2 %collective-permute-start.5 = (f32[2,128,640]{2,1,0:T(8,128)S(1)}, f32[2,128,640]{2,1,0:T(8,128)S(1)}, u32[]{:S(2)}, u32[]{:S(2)}) collective-permute-start(f32[2,128,640]{2,1,0:T(8,128)S(1)} %step_edges.1), channel_id=1, source_target_pairs={{0,8},{8,0},{2,10},{10,2},{4,12},{12,4},{6,14},{14,6},{16,24},{24,... | collective-permute-start | bytes 1966088 | tf_op jit(solution)/shard_map/ppermute | solution.py:257
  37.1 9.7 %collective-permute-start.7 = (f32[2,1,128,256]{3,2,1,0:T(8,128)S(1)}, f32[2,1,128,256]{3,2,1,0:T(8,128)S(1)}, u32[]{:S(2)}, u32[]{:S(2)}) collective-permute-start(f32[2,1,128,256]{3,2,1,0:T(8,128)S(1)} %copy-done), channel_id=1, source_target_pairs={{0,4},{2,6},{4,0},{6,2},{1,5},{3,7},{5,1},{7,3},{8,12},{10,14},{12... | collective-permute-start | bytes 786440 | tf_op jit(solution)/shard_map/ppermute | solution.py:238
  39.6 13.6 %collective-permute-start.3 = (f32[512,128]{1,0:T(8,128)S(1)}, f32[512,128]{1,0:T(8,128)S(1)}, u32[]{:S(2)}, u32[]{:S(2)}) collective-permute-start(f32[512,128]{1,0:T(8,128)S(1)} %margin.1.own.y0), channel_id=1, source_target_pairs={{0,8},{16,24},{32,40},{48,56},{64,72},{80,88},{96,104},{112,120},{... | collective-permute-start | bytes 786440 | tf_op jit(solution)/shard_map/ppermute | solution.py:246
  40.8 12.4 %collective-permute-start.4 = (f32[512,128]{1,0:T(8,128)S(1)}, f32[512,128]{1,0:T(8,128)S(1)}, u32[]{:S(2)}, u32[]{:S(2)}) collective-permute-start(f32[512,128]{1,0:T(8,128)S(1)} %margin.1.own.y0), channel_id=1, source_target_pairs={{8,16},{24,32},{40,48},{56,64},{72,80},{88,96},{104,112},{120,128}... | collective-permute-start | bytes 786440 | tf_op jit(solution)/shard_map/ppermute | solution.py:246
  45.7 8.6 %collective-permute-start.6 = (f32[2,1,128,256]{3,2,1,0:T(8,128)S(1)}, f32[2,1,128,256]{3,2,1,0:T(8,128)S(1)}, u32[]{:S(2)}, u32[]{:S(2)}) collective-permute-start(f32[2,1,128,256]{3,2,1,0:T(8,128)S(1)} %copy-done), channel_id=1, source_target_pairs={{0,2},{2,4},{4,6},{6,0},{1,3},{3,5},{5,7},{7,1},{8,10},{10,12},{12... | collective-permute-start | bytes 786440 | tf_op jit(solution)/shard_map/ppermute | solution.py:238
  46.7 7.6 %collective-permute-start.8 = (f32[2,1,128,256]{3,2,1,0:T(8,128)S(1)}, f32[2,1,128,256]{3,2,1,0:T(8,128)S(1)}, u32[]{:S(2)}, u32[]{:S(2)}) collective-permute-start(f32[2,1,128,256]{3,2,1,0:T(8,128)S(1)} %copy-done), channel_id=1, source_target_pairs={{0,6},{2,0},{4,2},{6,4},{1,7},{3,1},{5,3},{7,5},{8,14},{10,8},{12,... | collective-permute-start | bytes 786440 | tf_op jit(solution)/shard_map/ppermute | solution.py:238
  54.3 2.1 %collective-permute-start.9 = (f32[2,128,640]{2,1,0:T(8,128)S(1)}, f32[2,128,640]{2,1,0:T(8,128)S(1)}, u32[]{:S(2)}, u32[]{:S(2)}) collective-permute-start(f32[2,128,640]{2,1,0:T(8,128)S(1)} %collective-permute-done.5.edge), channel_id=1, source_target_pairs={{0,1},{1,0},{2,3},{3,2},{4,5},{5,4},{6,7},{7,6},{8,9},{9,8},{10,11... | collective-permute-start | bytes 1966088 | tf_op jit(solution)/shard_map/ppermute | solution.py:241
  54.3 5.0 %collective-permute-start.11 = (f32[2,1,128,256]{3,2,1,0:T(8,128)S(1)}, f32[2,1,128,256]{3,2,1,0:T(8,128)S(1)}, u32[]{:S(2)}, u32[]{:S(2)}) collective-permute-start(f32[2,1,128,256]{3,2,1,0:T(8,128)S(1)} %copy-done), channel_id=1, source_target_pairs={{0,1},{1,0},{2,3},{3,2},{4,5},{5,4},{6,7},{7,6},{8,9},{9,8},{10,11... | collective-permute-start | bytes 786440 | tf_op jit(solution)/shard_map/ppermute | solution.py:241
  54.8 10.2 %collective-permute-start.12 = (f32[2,1,128,256]{3,2,1,0:T(8,128)S(1)}, f32[2,1,128,256]{3,2,1,0:T(8,128)S(1)}, u32[]{:S(2)}, u32[]{:S(2)}) collective-permute-start(f32[2,1,128,256]{3,2,1,0:T(8,128)S(1)} %collective-permute-done.6.c1), channel_id=1, source_target_pairs={{0,1},{1,0},{2,3},{3,2},{4,5},{5,4},{6,7},{7,6},{8,9},{9,8},{10,11... | collective-permute-start | bytes 786440 | tf_op jit(solution)/shard_map/ppermute | solution.py:241
  54.9 10.2 %collective-permute-start.13 = (f32[2,1,128,256]{3,2,1,0:T(8,128)S(1)}, f32[2,1,128,256]{3,2,1,0:T(8,128)S(1)}, u32[]{:S(2)}, u32[]{:S(2)}) collective-permute-start(f32[2,1,128,256]{3,2,1,0:T(8,128)S(1)} %collective-permute-done.7.c2), channel_id=1, source_target_pairs={{0,1},{1,0},{2,3},{3,2},{4,5},{5,4},{6,7},{7,6},{8,9},{9,8},{10,11... | collective-permute-start | bytes 786440 | tf_op jit(solution)/shard_map/ppermute | solution.py:241
  55.3 9.8 %collective-permute-start.14 = (f32[2,1,128,256]{3,2,1,0:T(8,128)S(1)}, f32[2,1,128,256]{3,2,1,0:T(8,128)S(1)}, u32[]{:S(2)}, u32[]{:S(2)}) collective-permute-start(f32[2,1,128,256]{3,2,1,0:T(8,128)S(1)} %collective-permute-done.8.c3), channel_id=1, source_target_pairs={{0,1},{1,0},{2,3},{3,2},{4,5},{5,4},{6,7},{7,6},{8,9},{9,8},{10,11... | collective-permute-start | bytes 786440 | tf_op jit(solution)/shard_map/ppermute | solution.py:241
  58.4 8.4 %collective-permute-start.10 = (f32[512,128]{1,0:T(8,128)S(1)}, f32[512,128]{1,0:T(8,128)S(1)}, u32[]{:S(2)}, u32[]{:S(2)}) collective-permute-start(f32[512,128]{1,0:T(8,128)S(1)} %get-tuple-element.39.own), channel_id=1, source_target_pairs={{0,8},{16,24},{32,40},{48,56},{64,72},{80,88},{96,104},{112,120},{... | collective-permute-start | bytes 786440 | tf_op jit(solution)/shard_map/ppermute | solution.py:246
  59.3 11.9 %collective-permute-start.15 = (f32[512,128]{1,0:T(8,128)S(1)}, f32[512,128]{1,0:T(8,128)S(1)}, u32[]{:S(2)}, u32[]{:S(2)}) collective-permute-start(f32[512,128]{1,0:T(8,128)S(1)} %get-tuple-element.39.own), channel_id=1, source_target_pairs={{8,16},{24,32},{40,48},{56,64},{72,80},{88,96},{104,112},{120,128}... | collective-permute-start | bytes 786440 | tf_op jit(solution)/shard_map/ppermute | solution.py:246
  96.0 5.6 %collective-permute-start.16 = (f32[136,128]{1,0:T(8,128)S(1)}, f32[136,128]{1,0:T(8,128)S(1)}, u32[]{:S(2)}, u32[]{:S(2)}) collective-permute-start(f32[136,128]{1,0:T(8,128)S(1)} %get-tuple-element.49), channel_id=1, source_target_pairs={{0,2},{2,4},{4,6},{6,0},{1,3},{3,5},{5,7},{7,1},{8,10},{10,12},{12... | collective-permute-start | bytes 208904 | tf_op jit(solution)/shard_map/ppermute | solution.py:238
  96.6 6.3 %collective-permute-start.17 = (f32[136,128]{1,0:T(8,128)S(1)}, f32[136,128]{1,0:T(8,128)S(1)}, u32[]{:S(2)}, u32[]{:S(2)}) collective-permute-start(f32[136,128]{1,0:T(8,128)S(1)} %get-tuple-element.50), channel_id=1, source_target_pairs={{0,4},{2,6},{4,0},{6,2},{1,5},{3,7},{5,1},{7,3},{8,12},{10,14},{12... | collective-permute-start | bytes 208904 | tf_op jit(solution)/shard_map/ppermute | solution.py:238
  99.9 4.3 %collective-permute-start.18 = (f32[136,128]{1,0:T(8,128)S(1)}, f32[136,128]{1,0:T(8,128)S(1)}, u32[]{:S(2)}, u32[]{:S(2)}) collective-permute-start(f32[136,128]{1,0:T(8,128)S(1)} %get-tuple-element.51), channel_id=1, source_target_pairs={{0,6},{2,0},{4,2},{6,4},{1,7},{3,1},{5,3},{7,5},{8,14},{10,8},{12,... | collective-permute-start | bytes 208904 | tf_op jit(solution)/shard_map/ppermute | solution.py:238

commit v10 on v9

--- a/solution.py
+++ b/solution.py
@@ -56,16 +56,20 @@
     return lax.rem(lax.div(me[0], 2 * ROW), 2)
 
 
-def pack_kernel(me, nbr, pat, coef_hbm, margin_hbm, step_hbm, out, coef, margin, step, done):
+def pack_kernel(me, nbr_hbm, pat_hbm, coef_hbm, margin_hbm, step_hbm, out, nbr, pat, coef, margin, step, done):
     core = lax.rem(me[0], 2)
     rows = pl.ds(pl.multiple_of(core * HALF, HALF), HALF)
     copies = [
         pltpu.make_async_copy(margin_hbm.at[0, :, rows, :], margin, done.at[0]),
         pltpu.make_async_copy(step_hbm.at[0, :, rows, :], step, done.at[1]),
         pltpu.make_async_copy(coef_hbm, coef, done.at[2]),
+        pltpu.make_async_copy(nbr_hbm, nbr, done.at[3]),
+        pltpu.make_async_copy(pat_hbm, pat, done.at[4]),
     ]
-    for copy in copies:
+    for copy in copies[::-1]:
         copy.start()
+    copies[3].wait()
+    copies[4].wait()
     first = lax.div(me[0], 2) - 2
     slots = margin.shape[0]
     for i, source in enumerate((margin, step)):
@@ -261,16 +265,17 @@
     half_blocks = pltpu.VMEM((slots, HALF, B), F32)
     packed = pl.pallas_call(
         pack_kernel,
-        in_specs=[SMEM] * 3 + [hbm] * 3,
+        in_specs=[SMEM] + [hbm] * 5,
         out_specs=VMEM,
         out_shape=struct((ROW, B + 2 * BAND * HALF, B), F32),
         scratch_shapes=[
-            pltpu.VMEM(coefficients.shape, F32), half_blocks, half_blocks, pltpu.SemaphoreType.DMA((3,))
+            pltpu.SMEM(neighbours.shape, jnp.int32), pltpu.SMEM(pattern.shape, jnp.int32),
+            pltpu.VMEM(coefficients.shape, F32), half_blocks, half_blocks, pltpu.SemaphoreType.DMA((5,)),
         ],
         cost_estimate=cost(10**6, 44 * tile_bytes),
         name="pack",
-        compiler_params=pltpu.CompilerParams(vmem_limit_bytes=60 * 2**20),
-    )(me, neighbours, pattern, coefficients, margin, step_matrix)
+        compiler_params=pltpu.CompilerParams(vmem_limit_bytes=28 * 2**20),
+    )(me, *(pltpu.with_memory_space_constraint(a, pltpu.HBM) for a in (neighbours, pattern, coefficients, margin, step_matrix)))
     mine = lax.all_to_all(packed, "x", 0, 0, tiled=True)
 
     state = struct((ROW * B, B), F32)

time: 105 us -> 104 us (level)
  Pallas kernels: 10.2 us -> 8.77 us
    pallas_call x1, Pallas kernels: 3.43 us -> 1.89 us  [local(): pl.pallas_call(pack_kernel, in_specs=[SMEM] + [hbm] * 5, out_specs=VMEM,...]
where the time goes in v10:
time: 104 us; the launch traced here: 103 us
  blocking collectives  47.2 us (45%)
  starting transfers between devices  29.5 us (28%)
  waiting for transfers between devices  17.2 us (17%)
  Pallas kernels  8.77 us (8%)
    all_to_all x1, blocking collectives, local(): mine = lax.all_to_all(packed, 'x', 0, 0, tiled=True)  24.8 us
    all_to_all x1, blocking collectives, local(): sums = lax.all_to_all(partial_value, 'row', 0, 0, tiled=True)  22.4 us
    ppermute x6, starting transfers between devices, swap_rows(): return lax.ppermute(value, 'row', pairs + [(j, i) for i, j in pairs])  18.6 us
    ppermute x6, waiting for transfers between devices, swap_rows(): return lax.ppermute(value, 'row', pairs + [(j, i) for i, j in pairs])  10.4 us
    ppermute x6, starting transfers between devices, in_row(): return lax.ppermute(value, 'x', [(x, (x + by) % ROW) for x in range(ROW)])  7.77 us
    pallas_call x10, Pallas kernels, call(): pl.pallas_call(kernel, out_shape=out_shape, in_specs=[SMEM] * scalars + [...  6.87 us
    ppermute x6, waiting for transfers between devices, in_row(): return lax.ppermute(value, 'x', [(x, (x + by) % ROW) for x in range(ROW)])  5.75 us
  transfers between devices with their start and end apart: 19, of which 10 were waited for; matrix products, arithmetic and copies ran while one was open for 0% of the time, Pallas kernels for 3%

profile of v10, /device:TPU:32, one launch (start us, length us, event | category | flops | bytes accessed | tf_op | source)
XLA Modules:
  0.0 103.4 jit_solution(7602892976917685996)
XLA Ops:
  0.6 1.9 %pack.1 = f32[4,768,128]{2,1,0:T(8,128)S(1)} custom-call(s32[1]{0:T(128)} %bitcast.me, s32[1,16]{1,0:T(1,128)} %nbr_hbm.1, s32[1,16]{1,0:T(1,128)} %pat_hbm.1, f32[2,1,128,256]{3,2,1,0:T(8,128)} %c0.1, f32[1,16,128,128]{3,2,1,0:T(8,128)} %margin_hbm.1, f32[1,16,128,128]{3,2,1,0:T(8,128)} %step_hbm.1), custom_call_target="tpu_custom_call" | custom-call | flops 1000000 | bytes 2883584 | tf_op jit(solution)/shard_map/pack/pallas_call | solution.py:266
  2.5 24.8 %all_to_all.16.mine = f32[4,768,128]{2,1,0:T(8,128)S(1)} all-to-all(f32[4,768,128]{2,1,0:T(8,128)S(1)} %pack.1), channel_id=1, replica_groups=mesh['row'=32,'x'=4,'orb'=2] {'x'}, dimensions={0} | all-to-all | bytes 3145728 | tf_op jit(solution)/shard_map/all_to_all | solution.py:279
  27.7 5.6 %collective-permute-start.2 = (f32[256,128]{1,0:T(8,128)S(1)}, f32[256,128]{1,0:T(8,128)S(1)}, u32[]{:S(2)}, u32[]{:S(2)}) collective-permute-start(f32[256,128]{1,0:T(8,128)S(1)} %get-tuple-element.31), channel_id=1, source_target_pairs={{8,16},{24,32},{40,48},{56,64},{72,80},{88,96},{104,112},{120,128}... | collective-permute-start | bytes 393224 | tf_op jit(solution)/shard_map/ppermute | solution.py:250
  33.4 1.9 %collective-permute-start.5 = (f32[2,128,640]{2,1,0:T(8,128)S(1)}, f32[2,128,640]{2,1,0:T(8,128)S(1)}, u32[]{:S(2)}, u32[]{:S(2)}) collective-permute-start(f32[2,128,640]{2,1,0:T(8,128)S(1)} %step_edges.1), channel_id=1, source_target_pairs={{0,8},{8,0},{2,10},{10,2},{4,12},{12,4},{6,14},{14,6},{16,24},{24,... | collective-permute-start | bytes 1966088 | tf_op jit(solution)/shard_map/ppermute | solution.py:261
  35.3 0.9 collective-permute-start.7
  36.2 0.9 collective-permute-done.2.from_b
  37.1 0.7 margin.1.own.y0
  37.9 1.2 %collective-permute-start.3 = (f32[512,128]{1,0:T(8,128)S(1)}, f32[512,128]{1,0:T(8,128)S(1)}, u32[]{:S(2)}, u32[]{:S(2)}) collective-permute-start(f32[512,128]{1,0:T(8,128)S(1)} %margin.1.own.y0), channel_id=1, source_target_pairs={{0,8},{16,24},{32,40},{48,56},{64,72},{80,88},{96,104},{112,120},{... | collective-permute-start | bytes 786440 | tf_op jit(solution)/shard_map/ppermute | solution.py:250
  39.1 4.9 %collective-permute-start.4 = (f32[512,128]{1,0:T(8,128)S(1)}, f32[512,128]{1,0:T(8,128)S(1)}, u32[]{:S(2)}, u32[]{:S(2)}) collective-permute-start(f32[512,128]{1,0:T(8,128)S(1)} %margin.1.own.y0), channel_id=1, source_target_pairs={{8,16},{24,32},{40,48},{56,64},{72,80},{88,96},{104,112},{120,128}... | collective-permute-start | bytes 786440 | tf_op jit(solution)/shard_map/ppermute | solution.py:250
  44.0 0.6 collective-permute-start.6
  45.0 2.3 %collective-permute-start.8 = (f32[2,1,128,256]{3,2,1,0:T(8,128)S(1)}, f32[2,1,128,256]{3,2,1,0:T(8,128)S(1)}, u32[]{:S(2)}, u32[]{:S(2)}) collective-permute-start(f32[2,1,128,256]{3,2,1,0:T(8,128)S(1)} %copy-done), channel_id=1, source_target_pairs={{0,6},{2,0},{4,2},{6,4},{1,7},{3,1},{5,3},{7,5},{8,14},{10,8},{12,... | collective-permute-start | bytes 786440 | tf_op jit(solution)/shard_map/ppermute | solution.py:242
  47.3 4.2 %collective-permute-done.3.from_a = f32[512,128]{1,0:T(8,128)S(1)} collective-permute-done((f32[512,128]{1,0:T(8,128)S(1)}, f32[512,128]{1,0:T(8,128)S(1)}, u32[]{:S(2)}, u32[]{:S(2)}) %collective-permute-start.3) | collective-permute-done | bytes 262176 | tf_op jit(solution)/shard_map/ppermute | solution.py:250
  51.5 1.1 %collective-permute-done.6.c1 = f32[2,1,128,256]{3,2,1,0:T(8,128)S(1)} collective-permute-done((f32[2,1,128,256]{3,2,1,0:T(8,128)S(1)}, f32[2,1,128,256]{3,2,1,0:T(8,128)S(1)}, u32[]{:S(2)}, u32[]{:S(2)}) %collective-permute-start.6) | collective-permute-done | bytes 262176 | tf_op jit(solution)/shard_map/ppermute | solution.py:242
  52.6 0.5 collective-permute-start.11
  53.2 0.4 collective-permute-start.13
  53.7 1.0 collective-permute-done.9.edge_other
  54.7 0.4 step_parts.1
  55.1 1.6 %two.1 = (f32[512,128]{1,0:T(8,128)S(1)}, f32[512,128]{1,0:T(8,128)S(1)}) custom-call(s32[1]{0:T(128)} %bitcast.me, bf16[8,128,640]{2,1,0:T(8,128)(2,1)S(1)} %get-tuple-element.35.m_high, bf16[8,128,640]{2,1,0:T(8,128)(2,1)S(1)} %get-tuple-element.36.m_low, f32[512,128]{1,0:T(8,128)S(1)} %collective-permute-done.3.from_a, ...), custom_call_target="tpu_custom_call" | custom-call | flops 754974720 | bytes 4194304 | tf_op jit(solution)/shard_map/two/pallas_call | solution.py:230
  56.7 0.9 collective-permute-start.10
  57.6 5.8 %collective-permute-start.15 = (f32[512,128]{1,0:T(8,128)S(1)}, f32[512,128]{1,0:T(8,128)S(1)}, u32[]{:S(2)}, u32[]{:S(2)}) collective-permute-start(f32[512,128]{1,0:T(8,128)S(1)} %get-tuple-element.39.own), channel_id=1, source_target_pairs={{8,16},{24,32},{40,48},{56,64},{72,80},{88,96},{104,112},{120,128}... | collective-permute-start | bytes 786440 | tf_op jit(solution)/shard_map/ppermute | solution.py:250
  63.4 0.7 old_parts.1
  64.2 1.0 collective-permute-done.10.from_a
  65.1 4.4 %collective-permute-done.15.from_b = f32[512,128]{1,0:T(8,128)S(1)} collective-permute-done((f32[512,128]{1,0:T(8,128)S(1)}, f32[512,128]{1,0:T(8,128)S(1)}, u32[]{:S(2)}, u32[]{:S(2)}) %collective-permute-start.15) | collective-permute-done | bytes 262176 | tf_op jit(solution)/shard_map/ppermute | solution.py:250
  69.5 1.6 %last.1.new = f32[4,128,128]{2,1,0:T(8,128)S(1)} custom-call(s32[1]{0:T(128)} %bitcast.me, bf16[8,128,640]{2,1,0:T(8,128)(2,1)S(1)} %get-tuple-element.35.m_high, bf16[8,128,640]{2,1,0:T(8,128)(2,1)S(1)} %get-tuple-element.36.m_low, f32[512,128]{1,0:T(8,128)S(1)} %collective-permute-done.10.from_a, f32[512,128]{1,0:T(8,128)S(1)} %collective-permute-done.15.from_b, ...), custom_call_target="tpu_custom_call" | custom-call | flops 754974720 | bytes 4718592 | tf_op jit(solution)/shard_map/last/pallas_call | solution.py:230
  71.1 0.7 project.1
  71.8 22.4 %all_to_all.17 = f32[32,16,128]{2,1,0:T(8,128)S(1)} all-to-all(f32[32,16,128]{2,1,0:T(8,128)S(1)} %bitcast.4), channel_id=1, replica_groups=mesh['row'=32,'x'=4,'orb'=2] {'row'}, dimensions={0} | all-to-all | bytes 524288 | tf_op jit(solution)/shard_map/all_to_all | solution.py:326
  94.3 0.6 collective-permute-start.16
  95.0 3.3 %collective-permute-start.17 = (f32[136,128]{1,0:T(8,128)S(1)}, f32[136,128]{1,0:T(8,128)S(1)}, u32[]{:S(2)}, u32[]{:S(2)}) collective-permute-start(f32[136,128]{1,0:T(8,128)S(1)} %get-tuple-element.50), channel_id=1, source_target_pairs={{0,4},{2,6},{4,0},{6,2},{1,5},{3,7},{5,1},{7,3},{8,12},{10,14},{12... | collective-permute-start | bytes 208904 | tf_op jit(solution)/shard_map/ppermute | solution.py:242
  98.3 1.7 %collective-permute-done.16.b1 = f32[136,128]{1,0:T(8,128)S(1)} collective-permute-done((f32[136,128]{1,0:T(8,128)S(1)}, f32[136,128]{1,0:T(8,128)S(1)}, u32[]{:S(2)}, u32[]{:S(2)}) %collective-permute-start.16) | collective-permute-done | bytes 69664 | tf_op jit(solution)/shard_map/ppermute | solution.py:242
  99.9 1.3 %collective-permute-done.17.b2 = f32[136,128]{1,0:T(8,128)S(1)} collective-permute-done((f32[136,128]{1,0:T(8,128)S(1)}, f32[136,128]{1,0:T(8,128)S(1)}, u32[]{:S(2)}, u32[]{:S(2)}) %collective-permute-start.17) | collective-permute-done | bytes 69664 | tf_op jit(solution)/shard_map/ppermute | solution.py:242
  101.3 1.3 %collective-permute-done.18.b3 = f32[136,128]{1,0:T(8,128)S(1)} collective-permute-done((f32[136,128]{1,0:T(8,128)S(1)}, f32[136,128]{1,0:T(8,128)S(1)}, u32[]{:S(2)}, u32[]{:S(2)}) %collective-permute-start.18) | collective-permute-done | bytes 69664 | tf_op jit(solution)/shard_map/ppermute | solution.py:242
  102.6 0.9 finish.1
  (21 shorter events, 1.0 us)
Async XLA Ops:
  27.4 7.9 %copy-start = (f32[2,1,128,256]{3,2,1,0:T(8,128)S(1)}, f32[2,1,128,256]{3,2,1,0:T(8,128)}, u32[]{:S(2)}) copy-start(f32[2,1,128,256]{3,2,1,0:T(8,128)} %c0.1) | copy-start | bytes 786436
  27.4 5.9 %collective-permute-start = (f32[4,768,128]{2,1,0:T(8,128)S(1)}, f32[4,768,128]{2,1,0:T(8,128)S(1)}, u32[]{:S(2)}, u32[]{:S(2)}) collective-permute-start(f32[4,768,128]{2,1,0:T(8,128)S(1)} %all_to_all.16.mine), channel_id=1, source_target_pairs={{0,1},{1,0},{2,3},{3,2},{4,5},{5,4},{6,7},{7,6},{8,9},{9,8},{10,11... | collective-permute-start | bytes 4718600 | tf_op jit(solution)/shard_map/ppermute | solution.py:245
  27.5 8.7 %collective-permute-start.1 = (f32[256,128]{1,0:T(8,128)S(1)}, f32[256,128]{1,0:T(8,128)S(1)}, u32[]{:S(2)}, u32[]{:S(2)}) collective-permute-start(f32[256,128]{1,0:T(8,128)S(1)} %get-tuple-element.30), channel_id=1, source_target_pairs={{0,8},{16,24},{32,40},{48,56},{64,72},{80,88},{96,104},{112,120},{... | collective-permute-start | bytes 393224 | tf_op jit(solution)/shard_map/ppermute | solution.py:250
  27.7 9.5 %collective-permute-start.2 = (f32[256,128]{1,0:T(8,128)S(1)}, f32[256,128]{1,0:T(8,128)S(1)}, u32[]{:S(2)}, u32[]{:S(2)}) collective-permute-start(f32[256,128]{1,0:T(8,128)S(1)} %get-tuple-element.31), channel_id=1, source_target_pairs={{8,16},{24,32},{40,48},{56,64},{72,80},{88,96},{104,112},{120,128}... | collective-permute-start | bytes 393224 | tf_op jit(solution)/shard_map/ppermute | solution.py:250
  33.4 19.2 %collective-permute-start.5 = (f32[2,128,640]{2,1,0:T(8,128)S(1)}, f32[2,128,640]{2,1,0:T(8,128)S(1)}, u32[]{:S(2)}, u32[]{:S(2)}) collective-permute-start(f32[2,128,640]{2,1,0:T(8,128)S(1)} %step_edges.1), channel_id=1, source_target_pairs={{0,8},{8,0},{2,10},{10,2},{4,12},{12,4},{6,14},{14,6},{16,24},{24,... | collective-permute-start | bytes 1966088 | tf_op jit(solution)/shard_map/ppermute | solution.py:261
  35.3 9.7 %collective-permute-start.7 = (f32[2,1,128,256]{3,2,1,0:T(8,128)S(1)}, f32[2,1,128,256]{3,2,1,0:T(8,128)S(1)}, u32[]{:S(2)}, u32[]{:S(2)}) collective-permute-start(f32[2,1,128,256]{3,2,1,0:T(8,128)S(1)} %copy-done), channel_id=1, source_target_pairs={{0,4},{2,6},{4,0},{6,2},{1,5},{3,7},{5,1},{7,3},{8,12},{10,14},{12... | collective-permute-start | bytes 786440 | tf_op jit(solution)/shard_map/ppermute | solution.py:242
  37.9 13.6 %collective-permute-start.3 = (f32[512,128]{1,0:T(8,128)S(1)}, f32[512,128]{1,0:T(8,128)S(1)}, u32[]{:S(2)}, u32[]{:S(2)}) collective-permute-start(f32[512,128]{1,0:T(8,128)S(1)} %margin.1.own.y0), channel_id=1, source_target_pairs={{0,8},{16,24},{32,40},{48,56},{64,72},{80,88},{96,104},{112,120},{... | collective-permute-start | bytes 786440 | tf_op jit(solution)/shard_map/ppermute | solution.py:250
  39.1 12.4 %collective-permute-start.4 = (f32[512,128]{1,0:T(8,128)S(1)}, f32[512,128]{1,0:T(8,128)S(1)}, u32[]{:S(2)}, u32[]{:S(2)}) collective-permute-start(f32[512,128]{1,0:T(8,128)S(1)} %margin.1.own.y0), channel_id=1, source_target_pairs={{8,16},{24,32},{40,48},{56,64},{72,80},{88,96},{104,112},{120,128}... | collective-permute-start | bytes 786440 | tf_op jit(solution)/shard_map/ppermute | solution.py:250
  44.0 8.6 %collective-permute-start.6 = (f32[2,1,128,256]{3,2,1,0:T(8,128)S(1)}, f32[2,1,128,256]{3,2,1,0:T(8,128)S(1)}, u32[]{:S(2)}, u32[]{:S(2)}) collective-permute-start(f32[2,1,128,256]{3,2,1,0:T(8,128)S(1)} %copy-done), channel_id=1, source_target_pairs={{0,2},{2,4},{4,6},{6,0},{1,3},{3,5},{5,7},{7,1},{8,10},{10,12},{12... | collective-permute-start | bytes 786440 | tf_op jit(solution)/shard_map/ppermute | solution.py:242
  45.0 7.6 %collective-permute-start.8 = (f32[2,1,128,256]{3,2,1,0:T(8,128)S(1)}, f32[2,1,128,256]{3,2,1,0:T(8,128)S(1)}, u32[]{:S(2)}, u32[]{:S(2)}) collective-permute-start(f32[2,1,128,256]{3,2,1,0:T(8,128)S(1)} %copy-done), channel_id=1, source_target_pairs={{0,6},{2,0},{4,2},{6,4},{1,7},{3,1},{5,3},{7,5},{8,14},{10,8},{12,... | collective-permute-start | bytes 786440 | tf_op jit(solution)/shard_map/ppermute | solution.py:242
  52.6 2.1 %collective-permute-start.9 = (f32[2,128,640]{2,1,0:T(8,128)S(1)}, f32[2,128,640]{2,1,0:T(8,128)S(1)}, u32[]{:S(2)}, u32[]{:S(2)}) collective-permute-start(f32[2,128,640]{2,1,0:T(8,128)S(1)} %collective-permute-done.5.edge), channel_id=1, source_target_pairs={{0,1},{1,0},{2,3},{3,2},{4,5},{5,4},{6,7},{7,6},{8,9},{9,8},{10,11... | collective-permute-start | bytes 1966088 | tf_op jit(solution)/shard_map/ppermute | solution.py:245
  52.6 5.0 %collective-permute-start.11 = (f32[2,1,128,256]{3,2,1,0:T(8,128)S(1)}, f32[2,1,128,256]{3,2,1,0:T(8,128)S(1)}, u32[]{:S(2)}, u32[]{:S(2)}) collective-permute-start(f32[2,1,128,256]{3,2,1,0:T(8,128)S(1)} %copy-done), channel_id=1, source_target_pairs={{0,1},{1,0},{2,3},{3,2},{4,5},{5,4},{6,7},{7,6},{8,9},{9,8},{10,11... | collective-permute-start | bytes 786440 | tf_op jit(solution)/shard_map/ppermute | solution.py:245
  53.1 10.3 %collective-permute-start.12 = (f32[2,1,128,256]{3,2,1,0:T(8,128)S(1)}, f32[2,1,128,256]{3,2,1,0:T(8,128)S(1)}, u32[]{:S(2)}, u32[]{:S(2)}) collective-permute-start(f32[2,1,128,256]{3,2,1,0:T(8,128)S(1)} %collective-permute-done.6.c1), channel_id=1, source_target_pairs={{0,1},{1,0},{2,3},{3,2},{4,5},{5,4},{6,7},{7,6},{8,9},{9,8},{10,11... | collective-permute-start | bytes 786440 | tf_op jit(solution)/shard_map/ppermute | solution.py:245
  53.2 10.2 %collective-permute-start.13 = (f32[2,1,128,256]{3,2,1,0:T(8,128)S(1)}, f32[2,1,128,256]{3,2,1,0:T(8,128)S(1)}, u32[]{:S(2)}, u32[]{:S(2)}) collective-permute-start(f32[2,1,128,256]{3,2,1,0:T(8,128)S(1)} %collective-permute-done.7.c2), channel_id=1, source_target_pairs={{0,1},{1,0},{2,3},{3,2},{4,5},{5,4},{6,7},{7,6},{8,9},{9,8},{10,11... | collective-permute-start | bytes 786440 | tf_op jit(solution)/shard_map/ppermute | solution.py:245
  53.6 9.8 %collective-permute-start.14 = (f32[2,1,128,256]{3,2,1,0:T(8,128)S(1)}, f32[2,1,128,256]{3,2,1,0:T(8,128)S(1)}, u32[]{:S(2)}, u32[]{:S(2)}) collective-permute-start(f32[2,1,128,256]{3,2,1,0:T(8,128)S(1)} %collective-permute-done.8.c3), channel_id=1, source_target_pairs={{0,1},{1,0},{2,3},{3,2},{4,5},{5,4},{6,7},{7,6},{8,9},{9,8},{10,11... | collective-permute-start | bytes 786440 | tf_op jit(solution)/shard_map/ppermute | solution.py:245
  56.7 8.4 %collective-permute-start.10 = (f32[512,128]{1,0:T(8,128)S(1)}, f32[512,128]{1,0:T(8,128)S(1)}, u32[]{:S(2)}, u32[]{:S(2)}) collective-permute-start(f32[512,128]{1,0:T(8,128)S(1)} %get-tuple-element.39.own), channel_id=1, source_target_pairs={{0,8},{16,24},{32,40},{48,56},{64,72},{80,88},{96,104},{112,120},{... | collective-permute-start | bytes 786440 | tf_op jit(solution)/shard_map/ppermute | solution.py:250
  57.6 11.9 %collective-permute-start.15 = (f32[512,128]{1,0:T(8,128)S(1)}, f32[512,128]{1,0:T(8,128)S(1)}, u32[]{:S(2)}, u32[]{:S(2)}) collective-permute-start(f32[512,128]{1,0:T(8,128)S(1)} %get-tuple-element.39.own), channel_id=1, source_target_pairs={{8,16},{24,32},{40,48},{56,64},{72,80},{88,96},{104,112},{120,128}... | collective-permute-start | bytes 786440 | tf_op jit(solution)/shard_map/ppermute | solution.py:250
  94.3 5.6 %collective-permute-start.16 = (f32[136,128]{1,0:T(8,128)S(1)}, f32[136,128]{1,0:T(8,128)S(1)}, u32[]{:S(2)}, u32[]{:S(2)}) collective-permute-start(f32[136,128]{1,0:T(8,128)S(1)} %get-tuple-element.49), channel_id=1, source_target_pairs={{0,2},{2,4},{4,6},{6,0},{1,3},{3,5},{5,7},{7,1},{8,10},{10,12},{12... | collective-permute-start | bytes 208904 | tf_op jit(solution)/shard_map/ppermute | solution.py:242
  95.0 6.3 %collective-permute-start.17 = (f32[136,128]{1,0:T(8,128)S(1)}, f32[136,128]{1,0:T(8,128)S(1)}, u32[]{:S(2)}, u32[]{:S(2)}) collective-permute-start(f32[136,128]{1,0:T(8,128)S(1)} %get-tuple-element.50), channel_id=1, source_target_pairs={{0,4},{2,6},{4,0},{6,2},{1,5},{3,7},{5,1},{7,3},{8,12},{10,14},{12... | collective-permute-start | bytes 208904 | tf_op jit(solution)/shard_map/ppermute | solution.py:242
  98.2 4.3 %collective-permute-start.18 = (f32[136,128]{1,0:T(8,128)S(1)}, f32[136,128]{1,0:T(8,128)S(1)}, u32[]{:S(2)}, u32[]{:S(2)}) collective-permute-start(f32[136,128]{1,0:T(8,128)S(1)} %get-tuple-element.51), channel_id=1, source_target_pairs={{0,6},{2,0},{4,2},{6,4},{1,7},{3,1},{5,3},{7,5},{8,14},{10,8},{12,... | collective-permute-start | bytes 208904 | tf_op jit(solution)/shard_map/ppermute | solution.py:242

commit v11 on v10

--- a/solution.py
+++ b/solution.py
@@ -56,20 +56,29 @@
     return lax.rem(lax.div(me[0], 2 * ROW), 2)
 
 
-def pack_kernel(me, nbr_hbm, pat_hbm, coef_hbm, margin_hbm, step_hbm, out, nbr, pat, coef, margin, step, done):
+def tile_kernel(me, coef, *refs):
+    *outs, held = refs
+    x, _ = member(me)
+    for q in range(ROW):
+        columns = slice(q * HALF, (q + 1) * HALF)
+        held[turn_to(q, x)] = jnp.concatenate([coef[0, 0, :, columns], coef[1, 0, :, columns]], axis=1)
+    for j, out in enumerate(outs):
+        out[...] = held[j]
+
+
+def pack_kernel(me, nbr_hbm, pat_hbm, margin_hbm, step_hbm, out, nbr, pat, margin, step, done):
     core = lax.rem(me[0], 2)
     rows = pl.ds(pl.multiple_of(core * HALF, HALF), HALF)
     copies = [
         pltpu.make_async_copy(margin_hbm.at[0, :, rows, :], margin, done.at[0]),
         pltpu.make_async_copy(step_hbm.at[0, :, rows, :], step, done.at[1]),
-        pltpu.make_async_copy(coef_hbm, coef, done.at[2]),
-        pltpu.make_async_copy(nbr_hbm, nbr, done.at[3]),
-        pltpu.make_async_copy(pat_hbm, pat, done.at[4]),
+        pltpu.make_async_copy(nbr_hbm, nbr, done.at[2]),
+        pltpu.make_async_copy(pat_hbm, pat, done.at[3]),
     ]
     for copy in copies[::-1]:
         copy.start()
+    copies[2].wait()
     copies[3].wait()
-    copies[4].wait()
     first = lax.div(me[0], 2) - 2
     slots = margin.shape[0]
     for i, source in enumerate((margin, step)):
@@ -80,13 +89,14 @@
                 weight = F32(1.0) if k == 0 else pat[0, k].astype(F32)
                 part = source[k] * jnp.where(nbr[0, k] == first + d, weight, F32(0.0))
                 total = part if total is None else total + part
-            start = B + (i * BAND + d) * HALF
-            for q in range(ROW):
-                out[q, start : start + HALF, :] = total
-    copies[2].wait()
-    for q in range(ROW):
-        columns = slice(q * HALF, (q + 1) * HALF)
-        out[q, :B, :] = jnp.concatenate([coef[0, 0, :, columns], coef[1, 0, :, columns]], axis=1)
+            start = (i * BAND + d) * HALF
+            out[start : start + HALF, :] = total
+
+
+def gather_kernel(me, mine, g1, g2, g3, out):
+    x, _ = member(me)
+    for j, ref in enumerate((mine, g1, g2, g3)):
+        out[turn_to(x, j)] = ref[...]
 
 
 def place_half(out, q, place, source, first):
@@ -96,11 +106,13 @@
         yield q, rows, slice(d * B, (d + 1) * B), source(slice(start, start + HALF))
 
 
-def edge_kernel(me, mine, to_a, to_b):
+def edge_kernel(me, t0, t1, t2, t3, own, to_a, to_b):
+    x, _ = member(me)
     odd = parity(me)
+    for j, ref in enumerate((t0, t1, t2, t3)):
+        own[pl.ds(pl.multiple_of(turn_to(x, j) * B, B), B), :] = ref[...]
     for out, first in ((to_a, 2 - 2 * odd), (to_b, 2 * odd)):
-        for q in range(2):
-            out[q * B : (q + 1) * B, :] = mine[first + q, :B, :]
+        out[...] = own[pl.ds(pl.multiple_of(first * B, B), 2 * B), :]
 
 
 def step_edge_kernel(me, mine, other, out):
@@ -108,7 +120,7 @@
     first = 2 * lax.rem(parity(me) + core + 1, 2)
     for q in range(2):
         for place, ref in ((core, mine), (1 - core, other)):
-            for to, rows, columns, tile in place_half(out, q, place, lambda at: ref[first + q, at, :], B + BAND * HALF):
+            for to, rows, columns, tile in place_half(out, q, place, lambda at: ref[first + q, at, :], BAND * HALF):
                 out[to, rows, columns] = tile
 
 
@@ -119,18 +131,17 @@
         put_parts(v, pl.ds(pl.multiple_of(start, B), reach), tile)
 
 
-def margin_kernel(me, mine, other, from_a, from_b, out, full, v):
+def margin_kernel(me, own, mine, other, from_a, from_b, out, full, v):
     _, core = member(me)
-    own = [mine[q, :B, :] for q in range(ROW)]
-    window(parity(me), from_a[...], from_b[...], jnp.concatenate(own, axis=0), v)
+    window(parity(me), from_a[...], from_b[...], own[...], v)
     for q in range(ROW):
         for place, ref in ((core, mine), (1 - core, other)):
-            for _, rows, columns, tile in place_half(full, q, place, lambda at: ref[q, at, :], B):
+            for _, rows, columns, tile in place_half(full, q, place, lambda at: ref[q, at, :], 0):
                 full[q, rows, columns] = tile
     for q in range(ROW):
         m_high, m_low = split(full[q])
         rows = slice(q * B, (q + BAND) * B)
-        out[q * B : (q + 1) * B, :] = own[q] + product(m_high, m_low, v[rows, :])
+        out[q * B : (q + 1) * B, :] = own[q * B : (q + 1) * B, :] + product(m_high, m_low, v[rows, :])
 
 
 def parts_kernel(me, mine, other, edge, edge_other, out_high, out_low):
@@ -138,7 +149,7 @@
     odd = parity(me)
     for q in range(ROW):
         for place, ref in ((core, mine), (1 - core, other)):
-            for to, rows, columns, tile in place_half(out_high, q + 2, place, lambda at: ref[q, at, :], B + BAND * HALF):
+            for to, rows, columns, tile in place_half(out_high, q + 2, place, lambda at: ref[q, at, :], BAND * HALF):
                 out_high[to, rows, columns], out_low[to, rows, columns] = split(tile)
     ahead = lax.rem(odd + core + 1, 2)
     for start, ref in ((ahead * 6, edge), ((1 - ahead) * 6, edge_other)):
@@ -261,36 +272,40 @@
         return lax.ppermute(value, ("row", "x", "orb"), pairs)
 
     slots = neighbours.shape[1]
+    tile = struct((B, B), F32)
+    tiles = call(tile_kernel, [tile] * ROW, [me, coefficients], 10**5, 8, "tiles", scratch=[pltpu.VMEM((ROW, B, B), F32)])
+    tiles = [tiles[0]] + [in_row(tiles[j], j) for j in range(1, ROW)]
     hbm = pl.BlockSpec(memory_space=pltpu.HBM)
     half_blocks = pltpu.VMEM((slots, HALF, B), F32)
     packed = pl.pallas_call(
         pack_kernel,
-        in_specs=[SMEM] + [hbm] * 5,
+        in_specs=[SMEM] + [hbm] * 4,
         out_specs=VMEM,
-        out_shape=struct((ROW, B + 2 * BAND * HALF, B), F32),
+        out_shape=struct((2 * BAND * HALF, B), F32),
         scratch_shapes=[
             pltpu.SMEM(neighbours.shape, jnp.int32), pltpu.SMEM(pattern.shape, jnp.int32),
-            pltpu.VMEM(coefficients.shape, F32), half_blocks, half_blocks, pltpu.SemaphoreType.DMA((5,)),
+            half_blocks, half_blocks, pltpu.SemaphoreType.DMA((4,)),
         ],
         cost_estimate=cost(10**6, 44 * tile_bytes),
         name="pack",
         compiler_params=pltpu.CompilerParams(vmem_limit_bytes=28 * 2**20),
-    )(me, *(pltpu.with_memory_space_constraint(a, pltpu.HBM) for a in (neighbours, pattern, coefficients, margin, step_matrix)))
-    mine = lax.all_to_all(packed, "x", 0, 0, tiled=True)
+    )(me, *(pltpu.with_memory_space_constraint(a, pltpu.HBM) for a in (neighbours, pattern, margin, step_matrix)))
+    bands = [in_row(packed, j) for j in range(1, ROW)]
 
     state = struct((ROW * B, B), F32)
     edge = struct((2 * B, B), F32)
-    edges = call(edge_kernel, [edge, edge], [me, mine], 10**5, 28, "edges")
-    *edges, held = lax.optimization_barrier((*edges, mine))
-    other = swap(held)
+    own, *edges = call(edge_kernel, [state, edge, edge], [me] + tiles, 10**5, 12, "edges")
     from_a, from_b = exchange(*edges)
+    from_a, from_b, *bands = lax.optimization_barrier((from_a, from_b, *bands))
+    mine = call(gather_kernel, struct((ROW, 2 * BAND * HALF, B), F32), [me, packed] + bands, 10**5, 80, "gather")
+    other = swap(mine)
     step_edge = call(step_edge_kernel, struct((2, B, BAND * B), F32), [me, mine, other], 10**5, 20, "step_edges")
     step_edge = apart(step_edge)
 
     _, held = lax.optimization_barrier((other, coefficients))
     old = [coefficients, in_row(held, 1), in_row(held, 2), None]
     y0 = call(
-        margin_kernel, state, [me, mine, other, from_a, from_b], 10**10, 60, "margin",
+        margin_kernel, state, [me, own, mine, other, from_a, from_b], 10**10, 60, "margin",
         scratch=[pltpu.VMEM((ROW, B, BAND * B), F32)] + [pltpu.VMEM((2 * ROW * B, 2 * B), BF16)],
     )
     arrived = exchange(y0, y0)

time: 104 us -> 111 us (1.067)
  blocking collectives: 47.2 us -> 21.7 us
  waiting for transfers between devices: 17.2 us -> 35.8 us
  starting transfers between devices: 29.5 us -> 43.5 us
    all_to_all x1 -> x0, blocking collectives: 24.8 us -> none  [local(): mine = lax.all_to_all(packed, 'x', 0, 0, tiled=True)]
    ppermute x6 -> x12, waiting for transfers between devices: 5.75 us -> 20.9 us  [in_row(): return lax.ppermute(value, 'x', [(x, (x + by) % ROW) for x in range(ROW)])]
    ppermute x6 -> x12, starting transfers between devices: 7.77 us -> 22 us  [in_row(): return lax.ppermute(value, 'x', [(x, (x + by) % ROW) for x in range(ROW)])]
    ppermute x6, waiting for transfers between devices: 0.99 us -> 3.73 us  [swap(): return lax.ppermute(value, 'orb', [(0, 1), (1, 0)])]
    pallas_call x10 -> x12, Pallas kernels: 6.87 us -> 7.13 us  [call(): pl.pallas_call(kernel, out_shape=out_shape, in_specs=[SMEM] * scalars + [...]
  transfers between devices with their start and end apart: 19 -> 25, of which waited for: 10 -> 14; matrix products, arithmetic and copies ran while one was open for 0% -> 0% of each run, Pallas kernels for 3% -> 3%
where the time goes in v11:
time: 111 us
  starting transfers between devices  43.5 us (39%)
  waiting for transfers between devices  35.8 us (32%)
  blocking collectives  21.7 us (20%)
  Pallas kernels  8.81 us (8%)
    ppermute x12, starting transfers between devices, in_row(): return lax.ppermute(value, 'x', [(x, (x + by) % ROW) for x in range(ROW)])  22 us
    all_to_all x1, blocking collectives, local(): sums = lax.all_to_all(partial_value, 'row', 0, 0, tiled=True)  21.7 us
    ppermute x12, waiting for transfers between devices, in_row(): return lax.ppermute(value, 'x', [(x, (x + by) % ROW) for x in range(ROW)])  20.9 us
    ppermute x6, starting transfers between devices, swap_rows(): return lax.ppermute(value, 'row', pairs + [(j, i) for i, j in pairs])  17.8 us
    ppermute x6, waiting for transfers between devices, swap_rows(): return lax.ppermute(value, 'row', pairs + [(j, i) for i, j in pairs])  11.1 us
    pallas_call x12, Pallas kernels, call(): pl.pallas_call(kernel, out_shape=out_shape, in_specs=[SMEM] * scalars + [...  7.13 us
    ppermute x6, waiting for transfers between devices, swap(): return lax.ppermute(value, 'orb', [(0, 1), (1, 0)])  3.73 us
  transfers between devices with their start and end apart: 25, of which 14 were waited for; matrix products, arithmetic and copies ran while one was open for 0% of the time, Pallas kernels for 3%

profile of v11, /device:TPU:32, one launch (start us, length us, event | category | flops | bytes accessed | tf_op | source)
XLA Modules:
  0.0 110.6 jit_solution(11563052831885728473)
XLA Ops:
  0.6 1.7 %pack.1.mine = f32[640,128]{1,0:T(8,128)S(1)} custom-call(s32[1]{0:T(128)} %bitcast.me, s32[1,16]{1,0:T(1,128)} %nbr_hbm.1, s32[1,16]{1,0:T(1,128)} %pat_hbm.1, f32[1,16,128,128]{3,2,1,0:T(8,128)} %margin_hbm.1, f32[1,16,128,128]{3,2,1,0:T(8,128)} %step_hbm.1), custom_call_target="tpu_custom_call" | custom-call | flops 1000000 | bytes 2883584 | tf_op jit(solution)/shard_map/pack/pallas_call | solution.py:280
  2.3 1.6 %collective-permute-start.5 = (f32[640,128]{1,0:T(8,128)S(1)}, f32[640,128]{1,0:T(8,128)S(1)}, u32[]{:S(2)}, u32[]{:S(2)}) collective-permute-start(f32[640,128]{1,0:T(8,128)S(1)} %pack.1.mine), channel_id=1, source_target_pairs={{0,2},{2,4},{4,6},{6,0},{1,3},{3,5},{5,7},{7,1},{8,10},{10,12},{12... | collective-permute-start | bytes 983048 | tf_op jit(solution)/shard_map/ppermute | solution.py:253
  3.9 2.7 %collective-permute-start.6 = (f32[640,128]{1,0:T(8,128)S(1)}, f32[640,128]{1,0:T(8,128)S(1)}, u32[]{:S(2)}, u32[]{:S(2)}) collective-permute-start(f32[640,128]{1,0:T(8,128)S(1)} %pack.1.mine), channel_id=1, source_target_pairs={{0,4},{2,6},{4,0},{6,2},{1,5},{3,7},{5,1},{7,3},{8,12},{10,14},{12... | collective-permute-start | bytes 983048 | tf_op jit(solution)/shard_map/ppermute | solution.py:253
  6.6 1.4 %collective-permute-start.7 = (f32[640,128]{1,0:T(8,128)S(1)}, f32[640,128]{1,0:T(8,128)S(1)}, u32[]{:S(2)}, u32[]{:S(2)}) collective-permute-start(f32[640,128]{1,0:T(8,128)S(1)} %pack.1.mine), channel_id=1, source_target_pairs={{0,6},{2,0},{4,2},{6,4},{1,7},{3,1},{5,3},{7,5},{8,14},{10,8},{12,... | collective-permute-start | bytes 983048 | tf_op jit(solution)/shard_map/ppermute | solution.py:253
  8.9 0.9 collective-permute-start.1
  9.8 10.9 %collective-permute-done.t1 = f32[128,128]{1,0:T(8,128)S(1)} collective-permute-done((f32[128,128]{1,0:T(8,128)S(1)}, f32[128,128]{1,0:T(8,128)S(1)}, u32[]{:S(2)}, u32[]{:S(2)}) %collective-permute-start) | collective-permute-done | bytes 65568 | tf_op jit(solution)/shard_map/ppermute | solution.py:253
  20.7 3.1 %collective-permute-start.2 = (f32[128,128]{1,0:T(8,128)S(1)}, f32[128,128]{1,0:T(8,128)S(1)}, u32[]{:S(2)}, u32[]{:S(2)}) collective-permute-start(f32[128,128]{1,0:T(8,128)S(1)} %get-tuple-element.37), channel_id=1, source_target_pairs={{0,6},{2,0},{4,2},{6,4},{1,7},{3,1},{5,3},{7,5},{8,14},{10,8},{12,... | collective-permute-start | bytes 196616 | tf_op jit(solution)/shard_map/ppermute | solution.py:253
  23.9 1.8 %collective-permute-done.2.t3 = f32[128,128]{1,0:T(8,128)S(1)} collective-permute-done((f32[128,128]{1,0:T(8,128)S(1)}, f32[128,128]{1,0:T(8,128)S(1)}, u32[]{:S(2)}, u32[]{:S(2)}) %collective-permute-start.2) | collective-permute-done | bytes 65568 | tf_op jit(solution)/shard_map/ppermute | solution.py:253
  26.0 5.6 %collective-permute-start.4 = (f32[256,128]{1,0:T(8,128)S(1)}, f32[256,128]{1,0:T(8,128)S(1)}, u32[]{:S(2)}, u32[]{:S(2)}) collective-permute-start(f32[256,128]{1,0:T(8,128)S(1)} %get-tuple-element.39), channel_id=1, source_target_pairs={{8,16},{24,32},{40,48},{56,64},{72,80},{88,96},{104,112},{120,128}... | collective-permute-start | bytes 393224 | tf_op jit(solution)/shard_map/ppermute | solution.py:261
  31.6 2.9 %collective-permute-done.4.from_b = f32[256,128]{1,0:T(8,128)S(1)} collective-permute-done((f32[256,128]{1,0:T(8,128)S(1)}, f32[256,128]{1,0:T(8,128)S(1)}, u32[]{:S(2)}, u32[]{:S(2)}) %collective-permute-start.4) | collective-permute-done | bytes 131104 | tf_op jit(solution)/shard_map/ppermute | solution.py:261
  34.7 3.0 %collective-permute-done.8.other = f32[4,640,128]{2,1,0:T(8,128)S(1)} collective-permute-done((f32[4,640,128]{2,1,0:T(8,128)S(1)}, f32[4,640,128]{2,1,0:T(8,128)S(1)}, u32[]{:S(2)}, u32[]{:S(2)}) %collective-permute-start.8) | collective-permute-done | bytes 1310752 | tf_op jit(solution)/shard_map/ppermute | solution.py:256
  37.8 1.9 %collective-permute-start.11 = (f32[2,128,640]{2,1,0:T(8,128)S(1)}, f32[2,128,640]{2,1,0:T(8,128)S(1)}, u32[]{:S(2)}, u32[]{:S(2)}) collective-permute-start(f32[2,128,640]{2,1,0:T(8,128)S(1)} %step_edges.1), channel_id=1, source_target_pairs={{0,8},{8,0},{2,10},{10,2},{4,12},{12,4},{6,14},{14,6},{16,24},{24,... | collective-permute-start | bytes 1966088 | tf_op jit(solution)/shard_map/ppermute | solution.py:272
  39.7 2.7 %collective-permute-start.13 = (f32[2,1,128,256]{3,2,1,0:T(8,128)S(1)}, f32[2,1,128,256]{3,2,1,0:T(8,128)S(1)}, u32[]{:S(2)}, u32[]{:S(2)}) collective-permute-start(f32[2,1,128,256]{3,2,1,0:T(8,128)S(1)} %copy-done), channel_id=1, source_target_pairs={{0,4},{2,6},{4,0},{6,2},{1,5},{3,7},{5,1},{7,3},{8,12},{10,14},{12... | collective-permute-start | bytes 786440 | tf_op jit(solution)/shard_map/ppermute | solution.py:253
  42.4 0.7 margin.1.own.y0
  43.1 2.1 %collective-permute-start.9 = (f32[512,128]{1,0:T(8,128)S(1)}, f32[512,128]{1,0:T(8,128)S(1)}, u32[]{:S(2)}, u32[]{:S(2)}) collective-permute-start(f32[512,128]{1,0:T(8,128)S(1)} %margin.1.own.y0), channel_id=1, source_target_pairs={{0,8},{16,24},{32,40},{48,56},{64,72},{80,88},{96,104},{112,120},{... | collective-permute-start | bytes 786440 | tf_op jit(solution)/shard_map/ppermute | solution.py:261
  45.3 4.0 %collective-permute-start.10 = (f32[512,128]{1,0:T(8,128)S(1)}, f32[512,128]{1,0:T(8,128)S(1)}, u32[]{:S(2)}, u32[]{:S(2)}) collective-permute-start(f32[512,128]{1,0:T(8,128)S(1)} %margin.1.own.y0), channel_id=1, source_target_pairs={{8,16},{24,32},{40,48},{56,64},{72,80},{88,96},{104,112},{120,128}... | collective-permute-start | bytes 786440 | tf_op jit(solution)/shard_map/ppermute | solution.py:261
  49.3 1.9 %collective-permute-start.12 = (f32[2,1,128,256]{3,2,1,0:T(8,128)S(1)}, f32[2,1,128,256]{3,2,1,0:T(8,128)S(1)}, u32[]{:S(2)}, u32[]{:S(2)}) collective-permute-start(f32[2,1,128,256]{3,2,1,0:T(8,128)S(1)} %copy-done), channel_id=1, source_target_pairs={{0,2},{2,4},{4,6},{6,0},{1,3},{3,5},{5,7},{7,1},{8,10},{10,12},{12... | collective-permute-start | bytes 786440 | tf_op jit(solution)/shard_map/ppermute | solution.py:253
  51.2 2.0 %collective-permute-start.14 = (f32[2,1,128,256]{3,2,1,0:T(8,128)S(1)}, f32[2,1,128,256]{3,2,1,0:T(8,128)S(1)}, u32[]{:S(2)}, u32[]{:S(2)}) collective-permute-start(f32[2,1,128,256]{3,2,1,0:T(8,128)S(1)} %copy-done), channel_id=1, source_target_pairs={{0,6},{2,0},{4,2},{6,4},{1,7},{3,1},{5,3},{7,5},{8,14},{10,8},{12,... | collective-permute-start | bytes 786440 | tf_op jit(solution)/shard_map/ppermute | solution.py:253
  53.2 2.7 %collective-permute-done.9.from_a = f32[512,128]{1,0:T(8,128)S(1)} collective-permute-done((f32[512,128]{1,0:T(8,128)S(1)}, f32[512,128]{1,0:T(8,128)S(1)}, u32[]{:S(2)}, u32[]{:S(2)}) %collective-permute-start.9) | collective-permute-done | bytes 262176 | tf_op jit(solution)/shard_map/ppermute | solution.py:261
  55.9 2.6 %collective-permute-done.12.c1 = f32[2,1,128,256]{3,2,1,0:T(8,128)S(1)} collective-permute-done((f32[2,1,128,256]{3,2,1,0:T(8,128)S(1)}, f32[2,1,128,256]{3,2,1,0:T(8,128)S(1)}, u32[]{:S(2)}, u32[]{:S(2)}) %collective-permute-start.12) | collective-permute-done | bytes 262176 | tf_op jit(solution)/shard_map/ppermute | solution.py:253
  58.5 1.1 %collective-permute-done.14.c3 = f32[2,1,128,256]{3,2,1,0:T(8,128)S(1)} collective-permute-done((f32[2,1,128,256]{3,2,1,0:T(8,128)S(1)}, f32[2,1,128,256]{3,2,1,0:T(8,128)S(1)}, u32[]{:S(2)}, u32[]{:S(2)}) %collective-permute-start.14) | collective-permute-done | bytes 262176 | tf_op jit(solution)/shard_map/ppermute | solution.py:253
  62.4 1.6 %two.1 = (f32[512,128]{1,0:T(8,128)S(1)}, f32[512,128]{1,0:T(8,128)S(1)}) custom-call(s32[1]{0:T(128)} %bitcast.me, bf16[8,128,640]{2,1,0:T(8,128)(2,1)S(1)} %get-tuple-element.49.m_high, bf16[8,128,640]{2,1,0:T(8,128)(2,1)S(1)} %get-tuple-element.50.m_low, f32[512,128]{1,0:T(8,128)S(1)} %collective-permute-done.9.from_a, ...), custom_call_target="tpu_custom_call" | custom-call | flops 754974720 | bytes 4194304 | tf_op jit(solution)/shard_map/two/pallas_call | solution.py:241
  64.1 5.8 %collective-permute-start.21 = (f32[512,128]{1,0:T(8,128)S(1)}, f32[512,128]{1,0:T(8,128)S(1)}, u32[]{:S(2)}, u32[]{:S(2)}) collective-permute-start(f32[512,128]{1,0:T(8,128)S(1)} %get-tuple-element.53.own), channel_id=1, source_target_pairs={{8,16},{24,32},{40,48},{56,64},{72,80},{88,96},{104,112},{120,128}... | collective-permute-start | bytes 786440 | tf_op jit(solution)/shard_map/ppermute | solution.py:261
  70.7 2.0 %collective-permute-done.16.from_a = f32[512,128]{1,0:T(8,128)S(1)} collective-permute-done((f32[512,128]{1,0:T(8,128)S(1)}, f32[512,128]{1,0:T(8,128)S(1)}, u32[]{:S(2)}, u32[]{:S(2)}) %collective-permute-start.16) | collective-permute-done | bytes 262176 | tf_op jit(solution)/shard_map/ppermute | solution.py:261
  72.7 3.5 %collective-permute-done.21.from_b = f32[512,128]{1,0:T(8,128)S(1)} collective-permute-done((f32[512,128]{1,0:T(8,128)S(1)}, f32[512,128]{1,0:T(8,128)S(1)}, u32[]{:S(2)}, u32[]{:S(2)}) %collective-permute-start.21) | collective-permute-done | bytes 262176 | tf_op jit(solution)/shard_map/ppermute | solution.py:261
  76.2 1.6 %last.1.new = f32[4,128,128]{2,1,0:T(8,128)S(1)} custom-call(s32[1]{0:T(128)} %bitcast.me, bf16[8,128,640]{2,1,0:T(8,128)(2,1)S(1)} %get-tuple-element.49.m_high, bf16[8,128,640]{2,1,0:T(8,128)(2,1)S(1)} %get-tuple-element.50.m_low, f32[512,128]{1,0:T(8,128)S(1)} %collective-permute-done.16.from_a, f32[512,128]{1,0:T(8,128)S(1)} %collective-permute-done.21.from_b, ...), custom_call_target="tpu_custom_call" | custom-call | flops 754974720 | bytes 4718592 | tf_op jit(solution)/shard_map/last/pallas_call | solution.py:241
  78.5 21.7 %all_to_all.11 = f32[32,16,128]{2,1,0:T(8,128)S(1)} all-to-all(f32[32,16,128]{2,1,0:T(8,128)S(1)} %bitcast.4), channel_id=1, replica_groups=mesh['row'=32,'x'=4,'orb'=2] {'row'}, dimensions={0} | all-to-all | bytes 524288 | tf_op jit(solution)/shard_map/all_to_all | solution.py:341
  100.8 4.6 %collective-permute-start.23 = (f32[136,128]{1,0:T(8,128)S(1)}, f32[136,128]{1,0:T(8,128)S(1)}, u32[]{:S(2)}, u32[]{:S(2)}) collective-permute-start(f32[136,128]{1,0:T(8,128)S(1)} %get-tuple-element.64), channel_id=1, source_target_pairs={{0,4},{2,6},{4,0},{6,2},{1,5},{3,7},{5,1},{7,3},{8,12},{10,14},{12... | collective-permute-start | bytes 208904 | tf_op jit(solution)/shard_map/ppermute | solution.py:253
  105.4 0.8 collective-permute-done.22.b1
  106.3 2.2 %collective-permute-done.23.b2 = f32[136,128]{1,0:T(8,128)S(1)} collective-permute-done((f32[136,128]{1,0:T(8,128)S(1)}, f32[136,128]{1,0:T(8,128)S(1)}, u32[]{:S(2)}, u32[]{:S(2)}) %collective-permute-start.23) | collective-permute-done | bytes 69664 | tf_op jit(solution)/shard_map/ppermute | solution.py:253
  108.5 1.3 %collective-permute-done.24.b3 = f32[136,128]{1,0:T(8,128)S(1)} collective-permute-done((f32[136,128]{1,0:T(8,128)S(1)}, f32[136,128]{1,0:T(8,128)S(1)}, u32[]{:S(2)}, u32[]{:S(2)}) %collective-permute-start.24) | collective-permute-done | bytes 69664 | tf_op jit(solution)/shard_map/ppermute | solution.py:253
  109.7 0.9 finish.1
  (34 shorter events, 6.4 us)
Async XLA Ops:
  0.6 7.4 %copy-start = (f32[2,1,128,256]{3,2,1,0:T(8,128)S(1)}, f32[2,1,128,256]{3,2,1,0:T(8,128)}, u32[]{:S(2)}) copy-start(f32[2,1,128,256]{3,2,1,0:T(8,128)} %c0.1) | copy-start | bytes 786436
  2.3 32.2 %collective-permute-start.5 = (f32[640,128]{1,0:T(8,128)S(1)}, f32[640,128]{1,0:T(8,128)S(1)}, u32[]{:S(2)}, u32[]{:S(2)}) collective-permute-start(f32[640,128]{1,0:T(8,128)S(1)} %pack.1.mine), channel_id=1, source_target_pairs={{0,2},{2,4},{4,6},{6,0},{1,3},{3,5},{5,7},{7,1},{8,10},{10,12},{12... | collective-permute-start | bytes 983048 | tf_op jit(solution)/shard_map/ppermute | solution.py:253
  3.9 30.6 %collective-permute-start.6 = (f32[640,128]{1,0:T(8,128)S(1)}, f32[640,128]{1,0:T(8,128)S(1)}, u32[]{:S(2)}, u32[]{:S(2)}) collective-permute-start(f32[640,128]{1,0:T(8,128)S(1)} %pack.1.mine), channel_id=1, source_target_pairs={{0,4},{2,6},{4,0},{6,2},{1,5},{3,7},{5,1},{7,3},{8,12},{10,14},{12... | collective-permute-start | bytes 983048 | tf_op jit(solution)/shard_map/ppermute | solution.py:253
  6.6 27.9 %collective-permute-start.7 = (f32[640,128]{1,0:T(8,128)S(1)}, f32[640,128]{1,0:T(8,128)S(1)}, u32[]{:S(2)}, u32[]{:S(2)}) collective-permute-start(f32[640,128]{1,0:T(8,128)S(1)} %pack.1.mine), channel_id=1, source_target_pairs={{0,6},{2,0},{4,2},{6,4},{1,7},{3,1},{5,3},{7,5},{8,14},{10,8},{12,... | collective-permute-start | bytes 983048 | tf_op jit(solution)/shard_map/ppermute | solution.py:253
  8.2 12.5 %collective-permute-start = (f32[128,128]{1,0:T(8,128)S(1)}, f32[128,128]{1,0:T(8,128)S(1)}, u32[]{:S(2)}, u32[]{:S(2)}) collective-permute-start(f32[128,128]{1,0:T(8,128)S(1)} %get-tuple-element.35), channel_id=1, source_target_pairs={{0,2},{2,4},{4,6},{6,0},{1,3},{3,5},{5,7},{7,1},{8,10},{10,12},{12... | collective-permute-start | bytes 196616 | tf_op jit(solution)/shard_map/ppermute | solution.py:253
  8.9 15.0 %collective-permute-start.1 = (f32[128,128]{1,0:T(8,128)S(1)}, f32[128,128]{1,0:T(8,128)S(1)}, u32[]{:S(2)}, u32[]{:S(2)}) collective-permute-start(f32[128,128]{1,0:T(8,128)S(1)} %get-tuple-element.36), channel_id=1, source_target_pairs={{0,4},{2,6},{4,0},{6,2},{1,5},{3,7},{5,1},{7,3},{8,12},{10,14},{12... | collective-permute-start | bytes 196616 | tf_op jit(solution)/shard_map/ppermute | solution.py:253
  20.7 5.0 %collective-permute-start.2 = (f32[128,128]{1,0:T(8,128)S(1)}, f32[128,128]{1,0:T(8,128)S(1)}, u32[]{:S(2)}, u32[]{:S(2)}) collective-permute-start(f32[128,128]{1,0:T(8,128)S(1)} %get-tuple-element.37), channel_id=1, source_target_pairs={{0,6},{2,0},{4,2},{6,4},{1,7},{3,1},{5,3},{7,5},{8,14},{10,8},{12,... | collective-permute-start | bytes 196616 | tf_op jit(solution)/shard_map/ppermute | solution.py:253
  25.8 5.8 %collective-permute-start.3 = (f32[256,128]{1,0:T(8,128)S(1)}, f32[256,128]{1,0:T(8,128)S(1)}, u32[]{:S(2)}, u32[]{:S(2)}) collective-permute-start(f32[256,128]{1,0:T(8,128)S(1)} %get-tuple-element.38), channel_id=1, source_target_pairs={{0,8},{16,24},{32,40},{48,56},{64,72},{80,88},{96,104},{112,120},{... | collective-permute-start | bytes 393224 | tf_op jit(solution)/shard_map/ppermute | solution.py:261
  26.0 8.6 %collective-permute-start.4 = (f32[256,128]{1,0:T(8,128)S(1)}, f32[256,128]{1,0:T(8,128)S(1)}, u32[]{:S(2)}, u32[]{:S(2)}) collective-permute-start(f32[256,128]{1,0:T(8,128)S(1)} %get-tuple-element.39), channel_id=1, source_target_pairs={{8,16},{24,32},{40,48},{56,64},{72,80},{88,96},{104,112},{120,128}... | collective-permute-start | bytes 393224 | tf_op jit(solution)/shard_map/ppermute | solution.py:261
  34.6 3.1 %collective-permute-start.8 = (f32[4,640,128]{2,1,0:T(8,128)S(1)}, f32[4,640,128]{2,1,0:T(8,128)S(1)}, u32[]{:S(2)}, u32[]{:S(2)}) collective-permute-start(f32[4,640,128]{2,1,0:T(8,128)S(1)} %gather.1.mine), channel_id=1, source_target_pairs={{0,1},{1,0},{2,3},{3,2},{4,5},{5,4},{6,7},{7,6},{8,9},{9,8},{10,11... | collective-permute-start | bytes 3932168 | tf_op jit(solution)/shard_map/ppermute | solution.py:256
  37.8 21.8 %collective-permute-start.11 = (f32[2,128,640]{2,1,0:T(8,128)S(1)}, f32[2,128,640]{2,1,0:T(8,128)S(1)}, u32[]{:S(2)}, u32[]{:S(2)}) collective-permute-start(f32[2,128,640]{2,1,0:T(8,128)S(1)} %step_edges.1), channel_id=1, source_target_pairs={{0,8},{8,0},{2,10},{10,2},{4,12},{12,4},{6,14},{14,6},{16,24},{24,... | collective-permute-start | bytes 1966088 | tf_op jit(solution)/shard_map/ppermute | solution.py:272
  39.7 11.5 %collective-permute-start.13 = (f32[2,1,128,256]{3,2,1,0:T(8,128)S(1)}, f32[2,1,128,256]{3,2,1,0:T(8,128)S(1)}, u32[]{:S(2)}, u32[]{:S(2)}) collective-permute-start(f32[2,1,128,256]{3,2,1,0:T(8,128)S(1)} %copy-done), channel_id=1, source_target_pairs={{0,4},{2,6},{4,0},{6,2},{1,5},{3,7},{5,1},{7,3},{8,12},{10,14},{12... | collective-permute-start | bytes 786440 | tf_op jit(solution)/shard_map/ppermute | solution.py:253
  43.1 12.7 %collective-permute-start.9 = (f32[512,128]{1,0:T(8,128)S(1)}, f32[512,128]{1,0:T(8,128)S(1)}, u32[]{:S(2)}, u32[]{:S(2)}) collective-permute-start(f32[512,128]{1,0:T(8,128)S(1)} %margin.1.own.y0), channel_id=1, source_target_pairs={{0,8},{16,24},{32,40},{48,56},{64,72},{80,88},{96,104},{112,120},{... | collective-permute-start | bytes 786440 | tf_op jit(solution)/shard_map/ppermute | solution.py:261
  45.3 10.7 %collective-permute-start.10 = (f32[512,128]{1,0:T(8,128)S(1)}, f32[512,128]{1,0:T(8,128)S(1)}, u32[]{:S(2)}, u32[]{:S(2)}) collective-permute-start(f32[512,128]{1,0:T(8,128)S(1)} %margin.1.own.y0), channel_id=1, source_target_pairs={{8,16},{24,32},{40,48},{56,64},{72,80},{88,96},{104,112},{120,128}... | collective-permute-start | bytes 786440 | tf_op jit(solution)/shard_map/ppermute | solution.py:261
  49.3 9.2 %collective-permute-start.12 = (f32[2,1,128,256]{3,2,1,0:T(8,128)S(1)}, f32[2,1,128,256]{3,2,1,0:T(8,128)S(1)}, u32[]{:S(2)}, u32[]{:S(2)}) collective-permute-start(f32[2,1,128,256]{3,2,1,0:T(8,128)S(1)} %copy-done), channel_id=1, source_target_pairs={{0,2},{2,4},{4,6},{6,0},{1,3},{3,5},{5,7},{7,1},{8,10},{10,12},{12... | collective-permute-start | bytes 786440 | tf_op jit(solution)/shard_map/ppermute | solution.py:253
  51.2 8.4 %collective-permute-start.14 = (f32[2,1,128,256]{3,2,1,0:T(8,128)S(1)}, f32[2,1,128,256]{3,2,1,0:T(8,128)S(1)}, u32[]{:S(2)}, u32[]{:S(2)}) collective-permute-start(f32[2,1,128,256]{3,2,1,0:T(8,128)S(1)} %copy-done), channel_id=1, source_target_pairs={{0,6},{2,0},{4,2},{6,4},{1,7},{3,1},{5,3},{7,5},{8,14},{10,8},{12,... | collective-permute-start | bytes 786440 | tf_op jit(solution)/shard_map/ppermute | solution.py:253
  59.6 2.4 %collective-permute-start.15 = (f32[2,128,640]{2,1,0:T(8,128)S(1)}, f32[2,128,640]{2,1,0:T(8,128)S(1)}, u32[]{:S(2)}, u32[]{:S(2)}) collective-permute-start(f32[2,128,640]{2,1,0:T(8,128)S(1)} %collective-permute-done.11.edge), channel_id=1, source_target_pairs={{0,1},{1,0},{2,3},{3,2},{4,5},{5,4},{6,7},{7,6},{8,9},{9,8},{10,11... | collective-permute-start | bytes 1966088 | tf_op jit(solution)/shard_map/ppermute | solution.py:256
  60.2 3.8 %collective-permute-start.17 = (f32[2,1,128,256]{3,2,1,0:T(8,128)S(1)}, f32[2,1,128,256]{3,2,1,0:T(8,128)S(1)}, u32[]{:S(2)}, u32[]{:S(2)}) collective-permute-start(f32[2,1,128,256]{3,2,1,0:T(8,128)S(1)} %copy-done), channel_id=1, source_target_pairs={{0,1},{1,0},{2,3},{3,2},{4,5},{5,4},{6,7},{7,6},{8,9},{9,8},{10,11... | collective-permute-start | bytes 786440 | tf_op jit(solution)/shard_map/ppermute | solution.py:256
  60.2 9.7 %collective-permute-start.18 = (f32[2,1,128,256]{3,2,1,0:T(8,128)S(1)}, f32[2,1,128,256]{3,2,1,0:T(8,128)S(1)}, u32[]{:S(2)}, u32[]{:S(2)}) collective-permute-start(f32[2,1,128,256]{3,2,1,0:T(8,128)S(1)} %collective-permute-done.12.c1), channel_id=1, source_target_pairs={{0,1},{1,0},{2,3},{3,2},{4,5},{5,4},{6,7},{7,6},{8,9},{9,8},{10,11... | collective-permute-start | bytes 786440 | tf_op jit(solution)/shard_map/ppermute | solution.py:256
  60.8 9.2 %collective-permute-start.19 = (f32[2,1,128,256]{3,2,1,0:T(8,128)S(1)}, f32[2,1,128,256]{3,2,1,0:T(8,128)S(1)}, u32[]{:S(2)}, u32[]{:S(2)}) collective-permute-start(f32[2,1,128,256]{3,2,1,0:T(8,128)S(1)} %collective-permute-done.13.c2), channel_id=1, source_target_pairs={{0,1},{1,0},{2,3},{3,2},{4,5},{5,4},{6,7},{7,6},{8,9},{9,8},{10,11... | collective-permute-start | bytes 786440 | tf_op jit(solution)/shard_map/ppermute | solution.py:256
  60.8 9.2 %collective-permute-start.20 = (f32[2,1,128,256]{3,2,1,0:T(8,128)S(1)}, f32[2,1,128,256]{3,2,1,0:T(8,128)S(1)}, u32[]{:S(2)}, u32[]{:S(2)}) collective-permute-start(f32[2,1,128,256]{3,2,1,0:T(8,128)S(1)} %collective-permute-done.14.c3), channel_id=1, source_target_pairs={{0,1},{1,0},{2,3},{3,2},{4,5},{5,4},{6,7},{7,6},{8,9},{9,8},{10,11... | collective-permute-start | bytes 786440 | tf_op jit(solution)/shard_map/ppermute | solution.py:256
  64.0 8.7 %collective-permute-start.16 = (f32[512,128]{1,0:T(8,128)S(1)}, f32[512,128]{1,0:T(8,128)S(1)}, u32[]{:S(2)}, u32[]{:S(2)}) collective-permute-start(f32[512,128]{1,0:T(8,128)S(1)} %get-tuple-element.53.own), channel_id=1, source_target_pairs={{0,8},{16,24},{32,40},{48,56},{64,72},{80,88},{96,104},{112,120},{... | collective-permute-start | bytes 786440 | tf_op jit(solution)/shard_map/ppermute | solution.py:261
  64.1 12.1 %collective-permute-start.21 = (f32[512,128]{1,0:T(8,128)S(1)}, f32[512,128]{1,0:T(8,128)S(1)}, u32[]{:S(2)}, u32[]{:S(2)}) collective-permute-start(f32[512,128]{1,0:T(8,128)S(1)} %get-tuple-element.53.own), channel_id=1, source_target_pairs={{8,16},{24,32},{40,48},{56,64},{72,80},{88,96},{104,112},{120,128}... | collective-permute-start | bytes 786440 | tf_op jit(solution)/shard_map/ppermute | solution.py:261
  100.4 5.9 %collective-permute-start.22 = (f32[136,128]{1,0:T(8,128)S(1)}, f32[136,128]{1,0:T(8,128)S(1)}, u32[]{:S(2)}, u32[]{:S(2)}) collective-permute-start(f32[136,128]{1,0:T(8,128)S(1)} %get-tuple-element.63), channel_id=1, source_target_pairs={{0,2},{2,4},{4,6},{6,0},{1,3},{3,5},{5,7},{7,1},{8,10},{10,12},{12... | collective-permute-start | bytes 208904 | tf_op jit(solution)/shard_map/ppermute | solution.py:253
  100.8 7.6 %collective-permute-start.23 = (f32[136,128]{1,0:T(8,128)S(1)}, f32[136,128]{1,0:T(8,128)S(1)}, u32[]{:S(2)}, u32[]{:S(2)}) collective-permute-start(f32[136,128]{1,0:T(8,128)S(1)} %get-tuple-element.64), channel_id=1, source_target_pairs={{0,4},{2,6},{4,0},{6,2},{1,5},{3,7},{5,1},{7,3},{8,12},{10,14},{12... | collective-permute-start | bytes 208904 | tf_op jit(solution)/shard_map/ppermute | solution.py:253
  105.4 4.3 %collective-permute-start.24 = (f32[136,128]{1,0:T(8,128)S(1)}, f32[136,128]{1,0:T(8,128)S(1)}, u32[]{:S(2)}, u32[]{:S(2)}) collective-permute-start(f32[136,128]{1,0:T(8,128)S(1)} %get-tuple-element.65), channel_id=1, source_target_pairs={{0,6},{2,0},{4,2},{6,4},{1,7},{3,1},{5,3},{7,5},{8,14},{10,8},{12,... | collective-permute-start | bytes 208904 | tf_op jit(solution)/shard_map/ppermute | solution.py:253

commit v12 on v11

--- a/solution.py
+++ b/solution.py
@@ -56,14 +56,10 @@
     return lax.rem(lax.div(me[0], 2 * ROW), 2)
 
 
-def tile_kernel(me, coef, *refs):
-    *outs, held = refs
-    x, _ = member(me)
+def tile_kernel(coef, out):
     for q in range(ROW):
         columns = slice(q * HALF, (q + 1) * HALF)
-        held[turn_to(q, x)] = jnp.concatenate([coef[0, 0, :, columns], coef[1, 0, :, columns]], axis=1)
-    for j, out in enumerate(outs):
-        out[...] = held[j]
+        out[q] = jnp.concatenate([coef[0, 0, :, columns], coef[1, 0, :, columns]], axis=1)
 
 
 def pack_kernel(me, nbr_hbm, pat_hbm, margin_hbm, step_hbm, out, nbr, pat, margin, step, done):
@@ -106,11 +102,8 @@
         yield q, rows, slice(d * B, (d + 1) * B), source(slice(start, start + HALF))
 
 
-def edge_kernel(me, t0, t1, t2, t3, own, to_a, to_b):
-    x, _ = member(me)
+def edge_kernel(me, own, to_a, to_b):
     odd = parity(me)
-    for j, ref in enumerate((t0, t1, t2, t3)):
-        own[pl.ds(pl.multiple_of(turn_to(x, j) * B, B), B), :] = ref[...]
     for out, first in ((to_a, 2 - 2 * odd), (to_b, 2 * odd)):
         out[...] = own[pl.ds(pl.multiple_of(first * B, B), 2 * B), :]
 
@@ -272,9 +265,7 @@
         return lax.ppermute(value, ("row", "x", "orb"), pairs)
 
     slots = neighbours.shape[1]
-    tile = struct((B, B), F32)
-    tiles = call(tile_kernel, [tile] * ROW, [me, coefficients], 10**5, 8, "tiles", scratch=[pltpu.VMEM((ROW, B, B), F32)])
-    tiles = [tiles[0]] + [in_row(tiles[j], j) for j in range(1, ROW)]
+    tiles = call(tile_kernel, struct((ROW, B, B), F32), [coefficients], 10**5, 8, "tiles", scalars=0)
     hbm = pl.BlockSpec(memory_space=pltpu.HBM)
     half_blocks = pltpu.VMEM((slots, HALF, B), F32)
     packed = pl.pallas_call(
@@ -290,24 +281,28 @@
         name="pack",
         compiler_params=pltpu.CompilerParams(vmem_limit_bytes=28 * 2**20),
     )(me, *(pltpu.with_memory_space_constraint(a, pltpu.HBM) for a in (neighbours, pattern, margin, step_matrix)))
+    tiles, packed = lax.optimization_barrier((tiles, packed))
+    own = lax.all_to_all(tiles, "x", 0, 0, tiled=True).reshape(ROW * B, B)
+    own, packed = lax.optimization_barrier((own, packed))
     bands = [in_row(packed, j) for j in range(1, ROW)]
 
     state = struct((ROW * B, B), F32)
     edge = struct((2 * B, B), F32)
-    own, *edges = call(edge_kernel, [state, edge, edge], [me] + tiles, 10**5, 12, "edges")
+    edges = call(edge_kernel, [edge, edge], [me, own], 10**5, 8, "edges")
     from_a, from_b = exchange(*edges)
     from_a, from_b, *bands = lax.optimization_barrier((from_a, from_b, *bands))
     mine = call(gather_kernel, struct((ROW, 2 * BAND * HALF, B), F32), [me, packed] + bands, 10**5, 80, "gather")
     other = swap(mine)
-    step_edge = call(step_edge_kernel, struct((2, B, BAND * B), F32), [me, mine, other], 10**5, 20, "step_edges")
-    step_edge = apart(step_edge)
-
     _, held = lax.optimization_barrier((other, coefficients))
     old = [coefficients, in_row(held, 1), in_row(held, 2), None]
     y0 = call(
         margin_kernel, state, [me, own, mine, other, from_a, from_b], 10**10, 60, "margin",
         scratch=[pltpu.VMEM((ROW, B, BAND * B), F32)] + [pltpu.VMEM((2 * ROW * B, 2 * B), BF16)],
     )
+    y0, late = lax.optimization_barrier((y0, mine))
+    step_edge = call(step_edge_kernel, struct((2, B, BAND * B), F32), [me, late, other], 10**5, 20, "step_edges")
+    step_edge = apart(step_edge)
+
     arrived = exchange(y0, y0)
     _, held = lax.optimization_barrier((old[2], coefficients))
     old[3] = in_row(held, 3)

time: 111 us -> 107 us (0.964)
  blocking collectives: 21.7 us -> 32.7 us
  starting transfers between devices: 43.5 us -> 34.7 us
  waiting for transfers between devices: 35.8 us -> 28.9 us
    all_to_all x0 -> x1, blocking collectives: none -> 10.8 us  [local(): own = lax.all_to_all(tiles, 'x', 0, 0, tiled=True).reshape(ROW * B, B)]
    ppermute x12 -> x9, waiting for transfers between devices: 20.9 us -> 13 us  [in_row(): return lax.ppermute(value, 'x', [(x, (x + by) % ROW) for x in range(ROW)])]
    ppermute x12 -> x9, starting transfers between devices: 22 us -> 14.6 us  [in_row(): return lax.ppermute(value, 'x', [(x, (x + by) % ROW) for x in range(ROW)])]
  transfers between devices with their start and end apart: 25 -> 22, of which waited for: 14 -> 14; matrix products, arithmetic and copies ran while one was open for 0% -> 0% of each run, Pallas kernels for 3% -> 3%
where the time goes in v12:
time: 107 us
  starting transfers between devices  34.7 us (32%)
  blocking collectives  32.7 us (31%)
  waiting for transfers between devices  28.9 us (27%)
  Pallas kernels  8.75 us (8%)
    all_to_all x1, blocking collectives, local(): sums = lax.all_to_all(partial_value, 'row', 0, 0, tiled=True)  22 us
    ppermute x6, starting transfers between devices, swap_rows(): return lax.ppermute(value, 'row', pairs + [(j, i) for i, j in pairs])  16.9 us
    ppermute x9, starting transfers between devices, in_row(): return lax.ppermute(value, 'x', [(x, (x + by) % ROW) for x in range(ROW)])  14.6 us
    ppermute x9, waiting for transfers between devices, in_row(): return lax.ppermute(value, 'x', [(x, (x + by) % ROW) for x in range(ROW)])  13 us
    ppermute x6, waiting for transfers between devices, swap_rows(): return lax.ppermute(value, 'row', pairs + [(j, i) for i, j in pairs])  11.9 us
    all_to_all x1, blocking collectives, local(): own = lax.all_to_all(tiles, 'x', 0, 0, tiled=True).reshape(ROW * B, B)  10.8 us
    pallas_call x12, Pallas kernels, call(): pl.pallas_call(kernel, out_shape=out_shape, in_specs=[SMEM] * scalars + [...  7.1 us
    ppermute x6, waiting for transfers between devices, swap(): return lax.ppermute(value, 'orb', [(0, 1), (1, 0)])  4.02 us
  transfers between devices with their start and end apart: 22, of which 14 were waited for; matrix products, arithmetic and copies ran while one was open for 0% of the time, Pallas kernels for 3%

profile of v12, /device:TPU:32, one launch (start us, length us, event | category | flops | bytes accessed | tf_op | source)
XLA Modules:
  0.0 106.8 jit_solution(1734426815221426182)
XLA Ops:
  0.6 0.9 copy-done
  1.7 1.6 %pack.1.mine = f32[640,128]{1,0:T(8,128)S(1)} custom-call(s32[1]{0:T(128)} %bitcast.me, s32[1,16]{1,0:T(1,128)} %nbr_hbm.1, s32[1,16]{1,0:T(1,128)} %pat_hbm.1, f32[1,16,128,128]{3,2,1,0:T(8,128)} %margin_hbm.1, f32[1,16,128,128]{3,2,1,0:T(8,128)} %step_hbm.1), custom_call_target="tpu_custom_call" | custom-call | flops 1000000 | bytes 2883584 | tf_op jit(solution)/shard_map/pack/pallas_call | solution.py:271
  3.4 10.8 %all_to_all.16 = f32[4,128,128]{2,1,0:T(8,128)S(1)} all-to-all(f32[4,128,128]{2,1,0:T(8,128)S(1)} %tiles.1), channel_id=1, replica_groups=mesh['row'=32,'x'=4,'orb'=2] {'x'}, dimensions={0} | all-to-all | bytes 524288 | tf_op jit(solution)/shard_map/all_to_all | solution.py:285
  14.7 2.1 %collective-permute-start.3 = (f32[640,128]{1,0:T(8,128)S(1)}, f32[640,128]{1,0:T(8,128)S(1)}, u32[]{:S(2)}, u32[]{:S(2)}) collective-permute-start(f32[640,128]{1,0:T(8,128)S(1)} %pack.1.mine), channel_id=1, source_target_pairs={{0,4},{2,6},{4,0},{6,2},{1,5},{3,7},{5,1},{7,3},{8,12},{10,14},{12... | collective-permute-start | bytes 983048 | tf_op jit(solution)/shard_map/ppermute | solution.py:246
  16.8 0.8 collective-permute-start.4
  17.9 5.6 %collective-permute-start.1 = (f32[256,128]{1,0:T(8,128)S(1)}, f32[256,128]{1,0:T(8,128)S(1)}, u32[]{:S(2)}, u32[]{:S(2)}) collective-permute-start(f32[256,128]{1,0:T(8,128)S(1)} %get-tuple-element.40), channel_id=1, source_target_pairs={{8,16},{24,32},{40,48},{56,64},{72,80},{88,96},{104,112},{120,128}... | collective-permute-start | bytes 393224 | tf_op jit(solution)/shard_map/ppermute | solution.py:254
  23.5 2.9 %collective-permute-done.1.from_b = f32[256,128]{1,0:T(8,128)S(1)} collective-permute-done((f32[256,128]{1,0:T(8,128)S(1)}, f32[256,128]{1,0:T(8,128)S(1)}, u32[]{:S(2)}, u32[]{:S(2)}) %collective-permute-start.1) | collective-permute-done | bytes 131104 | tf_op jit(solution)/shard_map/ppermute | solution.py:254
  26.4 4.0 %collective-permute-done.2.g1 = f32[640,128]{1,0:T(8,128)S(1)} collective-permute-done((f32[640,128]{1,0:T(8,128)S(1)}, f32[640,128]{1,0:T(8,128)S(1)}, u32[]{:S(2)}, u32[]{:S(2)}) %collective-permute-start.2) | collective-permute-done | bytes 327712 | tf_op jit(solution)/shard_map/ppermute | solution.py:246
  31.3 3.0 %collective-permute-done.5.other = f32[4,640,128]{2,1,0:T(8,128)S(1)} collective-permute-done((f32[4,640,128]{2,1,0:T(8,128)S(1)}, f32[4,640,128]{2,1,0:T(8,128)S(1)}, u32[]{:S(2)}, u32[]{:S(2)}) %collective-permute-start.5) | collective-permute-done | bytes 1310752 | tf_op jit(solution)/shard_map/ppermute | solution.py:249
  34.3 0.7 margin.1.own.y0
  35.1 2.0 %collective-permute-start.8 = (f32[2,128,640]{2,1,0:T(8,128)S(1)}, f32[2,128,640]{2,1,0:T(8,128)S(1)}, u32[]{:S(2)}, u32[]{:S(2)}) collective-permute-start(f32[2,128,640]{2,1,0:T(8,128)S(1)} %step_edges.1), channel_id=1, source_target_pairs={{0,8},{8,0},{2,10},{10,2},{4,12},{12,4},{6,14},{14,6},{16,24},{24,... | collective-permute-start | bytes 1966088 | tf_op jit(solution)/shard_map/ppermute | solution.py:265
  37.2 1.2 %collective-permute-start.10 = (f32[2,1,128,256]{3,2,1,0:T(8,128)S(1)}, f32[2,1,128,256]{3,2,1,0:T(8,128)S(1)}, u32[]{:S(2)}, u32[]{:S(2)}) collective-permute-start(f32[2,1,128,256]{3,2,1,0:T(8,128)S(1)} %copy-done.1), channel_id=1, source_target_pairs={{0,4},{2,6},{4,0},{6,2},{1,5},{3,7},{5,1},{7,3},{8,12},{10,14},{12... | collective-permute-start | bytes 786440 | tf_op jit(solution)/shard_map/ppermute | solution.py:246
  38.3 1.9 %collective-permute-start.6 = (f32[512,128]{1,0:T(8,128)S(1)}, f32[512,128]{1,0:T(8,128)S(1)}, u32[]{:S(2)}, u32[]{:S(2)}) collective-permute-start(f32[512,128]{1,0:T(8,128)S(1)} %margin.1.own.y0), channel_id=1, source_target_pairs={{0,8},{16,24},{32,40},{48,56},{64,72},{80,88},{96,104},{112,120},{... | collective-permute-start | bytes 786440 | tf_op jit(solution)/shard_map/ppermute | solution.py:254
  40.3 3.8 %collective-permute-start.7 = (f32[512,128]{1,0:T(8,128)S(1)}, f32[512,128]{1,0:T(8,128)S(1)}, u32[]{:S(2)}, u32[]{:S(2)}) collective-permute-start(f32[512,128]{1,0:T(8,128)S(1)} %margin.1.own.y0), channel_id=1, source_target_pairs={{8,16},{24,32},{40,48},{56,64},{72,80},{88,96},{104,112},{120,128}... | collective-permute-start | bytes 786440 | tf_op jit(solution)/shard_map/ppermute | solution.py:254
  44.1 2.4 %collective-permute-start.9 = (f32[2,1,128,256]{3,2,1,0:T(8,128)S(1)}, f32[2,1,128,256]{3,2,1,0:T(8,128)S(1)}, u32[]{:S(2)}, u32[]{:S(2)}) collective-permute-start(f32[2,1,128,256]{3,2,1,0:T(8,128)S(1)} %copy-done.1), channel_id=1, source_target_pairs={{0,2},{2,4},{4,6},{6,0},{1,3},{3,5},{5,7},{7,1},{8,10},{10,12},{12... | collective-permute-start | bytes 786440 | tf_op jit(solution)/shard_map/ppermute | solution.py:246
  46.5 0.8 collective-permute-done.10.c2
  47.3 2.5 %collective-permute-start.11 = (f32[2,1,128,256]{3,2,1,0:T(8,128)S(1)}, f32[2,1,128,256]{3,2,1,0:T(8,128)S(1)}, u32[]{:S(2)}, u32[]{:S(2)}) collective-permute-start(f32[2,1,128,256]{3,2,1,0:T(8,128)S(1)} %copy-done.1), channel_id=1, source_target_pairs={{0,6},{2,0},{4,2},{6,4},{1,7},{3,1},{5,3},{7,5},{8,14},{10,8},{12,... | collective-permute-start | bytes 786440 | tf_op jit(solution)/shard_map/ppermute | solution.py:246
  49.8 3.4 %collective-permute-done.6.from_a = f32[512,128]{1,0:T(8,128)S(1)} collective-permute-done((f32[512,128]{1,0:T(8,128)S(1)}, f32[512,128]{1,0:T(8,128)S(1)}, u32[]{:S(2)}, u32[]{:S(2)}) %collective-permute-start.6) | collective-permute-done | bytes 262176 | tf_op jit(solution)/shard_map/ppermute | solution.py:254
  53.5 3.0 %collective-permute-done.11.c3 = f32[2,1,128,256]{3,2,1,0:T(8,128)S(1)} collective-permute-done((f32[2,1,128,256]{3,2,1,0:T(8,128)S(1)}, f32[2,1,128,256]{3,2,1,0:T(8,128)S(1)}, u32[]{:S(2)}, u32[]{:S(2)}) %collective-permute-start.11) | collective-permute-done | bytes 262176 | tf_op jit(solution)/shard_map/ppermute | solution.py:246
  57.5 1.0 collective-permute-done.12.edge_other
  59.0 1.6 %two.1 = (f32[512,128]{1,0:T(8,128)S(1)}, f32[512,128]{1,0:T(8,128)S(1)}) custom-call(s32[1]{0:T(128)} %bitcast.me, bf16[8,128,640]{2,1,0:T(8,128)(2,1)S(1)} %get-tuple-element.51.m_high, bf16[8,128,640]{2,1,0:T(8,128)(2,1)S(1)} %get-tuple-element.52.m_low, f32[512,128]{1,0:T(8,128)S(1)} %collective-permute-done.6.from_a, ...), custom_call_target="tpu_custom_call" | custom-call | flops 754974720 | bytes 4194304 | tf_op jit(solution)/shard_map/two/pallas_call | solution.py:234
  60.7 5.2 %collective-permute-start.18 = (f32[512,128]{1,0:T(8,128)S(1)}, f32[512,128]{1,0:T(8,128)S(1)}, u32[]{:S(2)}, u32[]{:S(2)}) collective-permute-start(f32[512,128]{1,0:T(8,128)S(1)} %get-tuple-element.55.own), channel_id=1, source_target_pairs={{8,16},{24,32},{40,48},{56,64},{72,80},{88,96},{104,112},{120,128}... | collective-permute-start | bytes 786440 | tf_op jit(solution)/shard_map/ppermute | solution.py:254
  66.0 0.7 old_parts.1
  66.7 2.3 %collective-permute-done.13.from_a = f32[512,128]{1,0:T(8,128)S(1)} collective-permute-done((f32[512,128]{1,0:T(8,128)S(1)}, f32[512,128]{1,0:T(8,128)S(1)}, u32[]{:S(2)}, u32[]{:S(2)}) %collective-permute-start.13) | collective-permute-done | bytes 262176 | tf_op jit(solution)/shard_map/ppermute | solution.py:254
  69.0 3.2 %collective-permute-done.18.from_b = f32[512,128]{1,0:T(8,128)S(1)} collective-permute-done((f32[512,128]{1,0:T(8,128)S(1)}, f32[512,128]{1,0:T(8,128)S(1)}, u32[]{:S(2)}, u32[]{:S(2)}) %collective-permute-start.18) | collective-permute-done | bytes 262176 | tf_op jit(solution)/shard_map/ppermute | solution.py:254
  72.2 1.6 %last.1.new = f32[4,128,128]{2,1,0:T(8,128)S(1)} custom-call(s32[1]{0:T(128)} %bitcast.me, bf16[8,128,640]{2,1,0:T(8,128)(2,1)S(1)} %get-tuple-element.51.m_high, bf16[8,128,640]{2,1,0:T(8,128)(2,1)S(1)} %get-tuple-element.52.m_low, f32[512,128]{1,0:T(8,128)S(1)} %collective-permute-done.13.from_a, f32[512,128]{1,0:T(8,128)S(1)} %collective-permute-done.18.from_b, ...), custom_call_target="tpu_custom_call" | custom-call | flops 754974720 | bytes 4718592 | tf_op jit(solution)/shard_map/last/pallas_call | solution.py:234
  74.6 22.0 %all_to_all.17 = f32[32,16,128]{2,1,0:T(8,128)S(1)} all-to-all(f32[32,16,128]{2,1,0:T(8,128)S(1)} %bitcast.7), channel_id=1, replica_groups=mesh['row'=32,'x'=4,'orb'=2] {'row'}, dimensions={0} | all-to-all | bytes 524288 | tf_op jit(solution)/shard_map/all_to_all | solution.py:336
  96.9 4.8 %collective-permute-start.20 = (f32[136,128]{1,0:T(8,128)S(1)}, f32[136,128]{1,0:T(8,128)S(1)}, u32[]{:S(2)}, u32[]{:S(2)}) collective-permute-start(f32[136,128]{1,0:T(8,128)S(1)} %get-tuple-element.66), channel_id=1, source_target_pairs={{0,4},{2,6},{4,0},{6,2},{1,5},{3,7},{5,1},{7,3},{8,12},{10,14},{12... | collective-permute-start | bytes 208904 | tf_op jit(solution)/shard_map/ppermute | solution.py:246
  101.7 0.8 collective-permute-done.19.b1
  102.5 2.2 %collective-permute-done.20.b2 = f32[136,128]{1,0:T(8,128)S(1)} collective-permute-done((f32[136,128]{1,0:T(8,128)S(1)}, f32[136,128]{1,0:T(8,128)S(1)}, u32[]{:S(2)}, u32[]{:S(2)}) %collective-permute-start.20) | collective-permute-done | bytes 69664 | tf_op jit(solution)/shard_map/ppermute | solution.py:246
  104.7 1.3 %collective-permute-done.21.b3 = f32[136,128]{1,0:T(8,128)S(1)} collective-permute-done((f32[136,128]{1,0:T(8,128)S(1)}, f32[136,128]{1,0:T(8,128)S(1)}, u32[]{:S(2)}, u32[]{:S(2)}) %collective-permute-start.21) | collective-permute-done | bytes 69664 | tf_op jit(solution)/shard_map/ppermute | solution.py:246
  106.0 0.9 finish.1
  (31 shorter events, 4.8 us)
Async XLA Ops:
  0.6 1.0 copy-start
  14.2 16.3 %collective-permute-start.2 = (f32[640,128]{1,0:T(8,128)S(1)}, f32[640,128]{1,0:T(8,128)S(1)}, u32[]{:S(2)}, u32[]{:S(2)}) collective-permute-start(f32[640,128]{1,0:T(8,128)S(1)} %pack.1.mine), channel_id=1, source_target_pairs={{0,2},{2,4},{4,6},{6,0},{1,3},{3,5},{5,7},{7,1},{8,10},{10,12},{12... | collective-permute-start | bytes 983048 | tf_op jit(solution)/shard_map/ppermute | solution.py:246
  14.7 15.7 %collective-permute-start.3 = (f32[640,128]{1,0:T(8,128)S(1)}, f32[640,128]{1,0:T(8,128)S(1)}, u32[]{:S(2)}, u32[]{:S(2)}) collective-permute-start(f32[640,128]{1,0:T(8,128)S(1)} %pack.1.mine), channel_id=1, source_target_pairs={{0,4},{2,6},{4,0},{6,2},{1,5},{3,7},{5,1},{7,3},{8,12},{10,14},{12... | collective-permute-start | bytes 983048 | tf_op jit(solution)/shard_map/ppermute | solution.py:246
  16.8 14.3 %collective-permute-start.4 = (f32[640,128]{1,0:T(8,128)S(1)}, f32[640,128]{1,0:T(8,128)S(1)}, u32[]{:S(2)}, u32[]{:S(2)}) collective-permute-start(f32[640,128]{1,0:T(8,128)S(1)} %pack.1.mine), channel_id=1, source_target_pairs={{0,6},{2,0},{4,2},{6,4},{1,7},{3,1},{5,3},{7,5},{8,14},{10,8},{12,... | collective-permute-start | bytes 983048 | tf_op jit(solution)/shard_map/ppermute | solution.py:246
  17.6 5.8 %collective-permute-start = (f32[256,128]{1,0:T(8,128)S(1)}, f32[256,128]{1,0:T(8,128)S(1)}, u32[]{:S(2)}, u32[]{:S(2)}) collective-permute-start(f32[256,128]{1,0:T(8,128)S(1)} %get-tuple-element.39), channel_id=1, source_target_pairs={{0,8},{16,24},{32,40},{48,56},{64,72},{80,88},{96,104},{112,120},{... | collective-permute-start | bytes 393224 | tf_op jit(solution)/shard_map/ppermute | solution.py:254
  17.9 8.5 %collective-permute-start.1 = (f32[256,128]{1,0:T(8,128)S(1)}, f32[256,128]{1,0:T(8,128)S(1)}, u32[]{:S(2)}, u32[]{:S(2)}) collective-permute-start(f32[256,128]{1,0:T(8,128)S(1)} %get-tuple-element.40), channel_id=1, source_target_pairs={{8,16},{24,32},{40,48},{56,64},{72,80},{88,96},{104,112},{120,128}... | collective-permute-start | bytes 393224 | tf_op jit(solution)/shard_map/ppermute | solution.py:254
  31.2 3.1 %collective-permute-start.5 = (f32[4,640,128]{2,1,0:T(8,128)S(1)}, f32[4,640,128]{2,1,0:T(8,128)S(1)}, u32[]{:S(2)}, u32[]{:S(2)}) collective-permute-start(f32[4,640,128]{2,1,0:T(8,128)S(1)} %gather.1.mine), channel_id=1, source_target_pairs={{0,1},{1,0},{2,3},{3,2},{4,5},{5,4},{6,7},{7,6},{8,9},{9,8},{10,11... | collective-permute-start | bytes 3932168 | tf_op jit(solution)/shard_map/ppermute | solution.py:249
  35.0 2.1 %copy-start.1 = (f32[2,1,128,256]{3,2,1,0:T(8,128)S(1)}, f32[2,1,128,256]{3,2,1,0:T(8,128)}, u32[]{:S(2)}) copy-start(f32[2,1,128,256]{3,2,1,0:T(8,128)} %c0.1) | copy-start | bytes 786436
  35.1 21.3 %collective-permute-start.8 = (f32[2,128,640]{2,1,0:T(8,128)S(1)}, f32[2,128,640]{2,1,0:T(8,128)S(1)}, u32[]{:S(2)}, u32[]{:S(2)}) collective-permute-start(f32[2,128,640]{2,1,0:T(8,128)S(1)} %step_edges.1), channel_id=1, source_target_pairs={{0,8},{8,0},{2,10},{10,2},{4,12},{12,4},{6,14},{14,6},{16,24},{24,... | collective-permute-start | bytes 1966088 | tf_op jit(solution)/shard_map/ppermute | solution.py:265
  37.2 10.1 %collective-permute-start.10 = (f32[2,1,128,256]{3,2,1,0:T(8,128)S(1)}, f32[2,1,128,256]{3,2,1,0:T(8,128)S(1)}, u32[]{:S(2)}, u32[]{:S(2)}) collective-permute-start(f32[2,1,128,256]{3,2,1,0:T(8,128)S(1)} %copy-done.1), channel_id=1, source_target_pairs={{0,4},{2,6},{4,0},{6,2},{1,5},{3,7},{5,1},{7,3},{8,12},{10,14},{12... | collective-permute-start | bytes 786440 | tf_op jit(solution)/shard_map/ppermute | solution.py:246
  38.3 14.9 %collective-permute-start.6 = (f32[512,128]{1,0:T(8,128)S(1)}, f32[512,128]{1,0:T(8,128)S(1)}, u32[]{:S(2)}, u32[]{:S(2)}) collective-permute-start(f32[512,128]{1,0:T(8,128)S(1)} %margin.1.own.y0), channel_id=1, source_target_pairs={{0,8},{16,24},{32,40},{48,56},{64,72},{80,88},{96,104},{112,120},{... | collective-permute-start | bytes 786440 | tf_op jit(solution)/shard_map/ppermute | solution.py:254
  40.3 13.0 %collective-permute-start.7 = (f32[512,128]{1,0:T(8,128)S(1)}, f32[512,128]{1,0:T(8,128)S(1)}, u32[]{:S(2)}, u32[]{:S(2)}) collective-permute-start(f32[512,128]{1,0:T(8,128)S(1)} %margin.1.own.y0), channel_id=1, source_target_pairs={{8,16},{24,32},{40,48},{56,64},{72,80},{88,96},{104,112},{120,128}... | collective-permute-start | bytes 786440 | tf_op jit(solution)/shard_map/ppermute | solution.py:254
  44.1 9.4 %collective-permute-start.9 = (f32[2,1,128,256]{3,2,1,0:T(8,128)S(1)}, f32[2,1,128,256]{3,2,1,0:T(8,128)S(1)}, u32[]{:S(2)}, u32[]{:S(2)}) collective-permute-start(f32[2,1,128,256]{3,2,1,0:T(8,128)S(1)} %copy-done.1), channel_id=1, source_target_pairs={{0,2},{2,4},{4,6},{6,0},{1,3},{3,5},{5,7},{7,1},{8,10},{10,12},{12... | collective-permute-start | bytes 786440 | tf_op jit(solution)/shard_map/ppermute | solution.py:246
  47.3 9.1 %collective-permute-start.11 = (f32[2,1,128,256]{3,2,1,0:T(8,128)S(1)}, f32[2,1,128,256]{3,2,1,0:T(8,128)S(1)}, u32[]{:S(2)}, u32[]{:S(2)}) collective-permute-start(f32[2,1,128,256]{3,2,1,0:T(8,128)S(1)} %copy-done.1), channel_id=1, source_target_pairs={{0,6},{2,0},{4,2},{6,4},{1,7},{3,1},{5,3},{7,5},{8,14},{10,8},{12,... | collective-permute-start | bytes 786440 | tf_op jit(solution)/shard_map/ppermute | solution.py:246
  56.4 2.1 %collective-permute-start.12 = (f32[2,128,640]{2,1,0:T(8,128)S(1)}, f32[2,128,640]{2,1,0:T(8,128)S(1)}, u32[]{:S(2)}, u32[]{:S(2)}) collective-permute-start(f32[2,128,640]{2,1,0:T(8,128)S(1)} %collective-permute-done.8.edge), channel_id=1, source_target_pairs={{0,1},{1,0},{2,3},{3,2},{4,5},{5,4},{6,7},{7,6},{8,9},{9,8},{10,11... | collective-permute-start | bytes 1966088 | tf_op jit(solution)/shard_map/ppermute | solution.py:249
  56.5 4.1 %collective-permute-start.14 = (f32[2,1,128,256]{3,2,1,0:T(8,128)S(1)}, f32[2,1,128,256]{3,2,1,0:T(8,128)S(1)}, u32[]{:S(2)}, u32[]{:S(2)}) collective-permute-start(f32[2,1,128,256]{3,2,1,0:T(8,128)S(1)} %copy-done.1), channel_id=1, source_target_pairs={{0,1},{1,0},{2,3},{3,2},{4,5},{5,4},{6,7},{7,6},{8,9},{9,8},{10,11... | collective-permute-start | bytes 786440 | tf_op jit(solution)/shard_map/ppermute | solution.py:249
  56.9 9.0 %collective-permute-start.15 = (f32[2,1,128,256]{3,2,1,0:T(8,128)S(1)}, f32[2,1,128,256]{3,2,1,0:T(8,128)S(1)}, u32[]{:S(2)}, u32[]{:S(2)}) collective-permute-start(f32[2,1,128,256]{3,2,1,0:T(8,128)S(1)} %collective-permute-done.9.c1), channel_id=1, source_target_pairs={{0,1},{1,0},{2,3},{3,2},{4,5},{5,4},{6,7},{7,6},{8,9},{9,8},{10,11... | collective-permute-start | bytes 786440 | tf_op jit(solution)/shard_map/ppermute | solution.py:249
  57.0 8.9 %collective-permute-start.16 = (f32[2,1,128,256]{3,2,1,0:T(8,128)S(1)}, f32[2,1,128,256]{3,2,1,0:T(8,128)S(1)}, u32[]{:S(2)}, u32[]{:S(2)}) collective-permute-start(f32[2,1,128,256]{3,2,1,0:T(8,128)S(1)} %collective-permute-done.10.c2), channel_id=1, source_target_pairs={{0,1},{1,0},{2,3},{3,2},{4,5},{5,4},{6,7},{7,6},{8,9},{9,8},{10,11... | collective-permute-start | bytes 786440 | tf_op jit(solution)/shard_map/ppermute | solution.py:249
  57.5 8.5 %collective-permute-start.17 = (f32[2,1,128,256]{3,2,1,0:T(8,128)S(1)}, f32[2,1,128,256]{3,2,1,0:T(8,128)S(1)}, u32[]{:S(2)}, u32[]{:S(2)}) collective-permute-start(f32[2,1,128,256]{3,2,1,0:T(8,128)S(1)} %collective-permute-done.11.c3), channel_id=1, source_target_pairs={{0,1},{1,0},{2,3},{3,2},{4,5},{5,4},{6,7},{7,6},{8,9},{9,8},{10,11... | collective-permute-start | bytes 786440 | tf_op jit(solution)/shard_map/ppermute | solution.py:249
  60.6 8.4 %collective-permute-start.13 = (f32[512,128]{1,0:T(8,128)S(1)}, f32[512,128]{1,0:T(8,128)S(1)}, u32[]{:S(2)}, u32[]{:S(2)}) collective-permute-start(f32[512,128]{1,0:T(8,128)S(1)} %get-tuple-element.55.own), channel_id=1, source_target_pairs={{0,8},{16,24},{32,40},{48,56},{64,72},{80,88},{96,104},{112,120},{... | collective-permute-start | bytes 786440 | tf_op jit(solution)/shard_map/ppermute | solution.py:254
  60.7 11.6 %collective-permute-start.18 = (f32[512,128]{1,0:T(8,128)S(1)}, f32[512,128]{1,0:T(8,128)S(1)}, u32[]{:S(2)}, u32[]{:S(2)}) collective-permute-start(f32[512,128]{1,0:T(8,128)S(1)} %get-tuple-element.55.own), channel_id=1, source_target_pairs={{8,16},{24,32},{40,48},{56,64},{72,80},{88,96},{104,112},{120,128}... | collective-permute-start | bytes 786440 | tf_op jit(solution)/shard_map/ppermute | solution.py:254
  96.6 5.9 %collective-permute-start.19 = (f32[136,128]{1,0:T(8,128)S(1)}, f32[136,128]{1,0:T(8,128)S(1)}, u32[]{:S(2)}, u32[]{:S(2)}) collective-permute-start(f32[136,128]{1,0:T(8,128)S(1)} %get-tuple-element.65), channel_id=1, source_target_pairs={{0,2},{2,4},{4,6},{6,0},{1,3},{3,5},{5,7},{7,1},{8,10},{10,12},{12... | collective-permute-start | bytes 208904 | tf_op jit(solution)/shard_map/ppermute | solution.py:246
  96.9 7.8 %collective-permute-start.20 = (f32[136,128]{1,0:T(8,128)S(1)}, f32[136,128]{1,0:T(8,128)S(1)}, u32[]{:S(2)}, u32[]{:S(2)}) collective-permute-start(f32[136,128]{1,0:T(8,128)S(1)} %get-tuple-element.66), channel_id=1, source_target_pairs={{0,4},{2,6},{4,0},{6,2},{1,5},{3,7},{5,1},{7,3},{8,12},{10,14},{12... | collective-permute-start | bytes 208904 | tf_op jit(solution)/shard_map/ppermute | solution.py:246
  101.7 4.3 %collective-permute-start.21 = (f32[136,128]{1,0:T(8,128)S(1)}, f32[136,128]{1,0:T(8,128)S(1)}, u32[]{:S(2)}, u32[]{:S(2)}) collective-permute-start(f32[136,128]{1,0:T(8,128)S(1)} %get-tuple-element.67), channel_id=1, source_target_pairs={{0,6},{2,0},{4,2},{6,4},{1,7},{3,1},{5,3},{7,5},{8,14},{10,8},{12,... | collective-permute-start | bytes 208904 | tf_op jit(solution)/shard_map/ppermute | solution.py:246

commit v13 on v10

--- a/solution.py
+++ b/solution.py
@@ -304,6 +304,7 @@
             10**6, 80, "step_parts",
         )
     )
+    step[0], *old = lax.optimization_barrier((step[0], *old))
     scratch = [pltpu.VMEM((3 * ROW * B, 2 * B), BF16), pltpu.VMEM((2 * ROW * B, 2 * B), BF16)]
     y1, y2 = call(
         functools.partial(two_kernel, 1), [state, state], [me] + step + arrived + [y0], 3 * ROW * step_flops, 64,

time: 104 us -> 104 us (level)
  blocking collectives: 47.2 us -> 45.4 us
  starting transfers between devices: 29.5 us -> 31 us
    ppermute x6, starting transfers between devices: 7.77 us -> 9.6 us  [in_row(): return lax.ppermute(value, 'x', [(x, (x + by) % ROW) for x in range(ROW)])]
    all_to_all x1, blocking collectives: 22.4 us -> 20.6 us  [local(): sums = lax.all_to_all(partial_value, 'row', 0, 0, tiled=True)]
    ppermute x6, waiting for transfers between devices: 5.75 us -> 4.62 us  [in_row(): return lax.ppermute(value, 'x', [(x, (x + by) % ROW) for x in range(ROW)])]
    ppermute x6, waiting for transfers between devices: 0.99 us -> 2.1 us  [swap(): return lax.ppermute(value, 'orb', [(0, 1), (1, 0)])]
  transfers between devices with their start and end apart: 19 -> 19, of which waited for: 10 -> 9; matrix products, arithmetic and copies ran while one was open for 0% -> 0% of each run, Pallas kernels for 3% -> 3%
where the time goes in v13:
time: 104 us; the launch traced here: 103 us
  blocking collectives  45.4 us (44%)
  starting transfers between devices  31 us (30%)
  waiting for transfers between devices  17 us (16%)
  Pallas kernels  8.75 us (8%)
    all_to_all x1, blocking collectives, local(): mine = lax.all_to_all(packed, 'x', 0, 0, tiled=True)  24.8 us
    all_to_all x1, blocking collectives, local(): sums = lax.all_to_all(partial_value, 'row', 0, 0, tiled=True)  20.6 us
    ppermute x6, starting transfers between devices, swap_rows(): return lax.ppermute(value, 'row', pairs + [(j, i) for i, j in pairs])  18.3 us
    ppermute x6, waiting for transfers between devices, swap_rows(): return lax.ppermute(value, 'row', pairs + [(j, i) for i, j in pairs])  10.3 us
    ppermute x6, starting transfers between devices, in_row(): return lax.ppermute(value, 'x', [(x, (x + by) % ROW) for x in range(ROW)])  9.6 us
    pallas_call x10, Pallas kernels, call(): pl.pallas_call(kernel, out_shape=out_shape, in_specs=[SMEM] * scalars + [...  6.85 us
    ppermute x6, waiting for transfers between devices, in_row(): return lax.ppermute(value, 'x', [(x, (x + by) % ROW) for x in range(ROW)])  4.62 us
    ppermute x6, waiting for transfers between devices, swap(): return lax.ppermute(value, 'orb', [(0, 1), (1, 0)])  2.1 us
  transfers between devices with their start and end apart: 19, of which 9 were waited for; matrix products, arithmetic and copies ran while one was open for 0% of the time, Pallas kernels for 3%

profile of v13, /device:TPU:32, one launch (start us, length us, event | category | flops | bytes accessed | tf_op | source)
XLA Modules:
  0.0 103.1 jit_solution(15284452843962386735)
XLA Ops:
  0.6 1.9 %pack.1 = f32[4,768,128]{2,1,0:T(8,128)S(1)} custom-call(s32[1]{0:T(128)} %bitcast.me, s32[1,16]{1,0:T(1,128)} %nbr_hbm.1, s32[1,16]{1,0:T(1,128)} %pat_hbm.1, f32[2,1,128,256]{3,2,1,0:T(8,128)} %c0, f32[1,16,128,128]{3,2,1,0:T(8,128)} %margin_hbm.1, f32[1,16,128,128]{3,2,1,0:T(8,128)} %step_hbm.1), custom_call_target="tpu_custom_call" | custom-call | flops 1000000 | bytes 2883584 | tf_op jit(solution)/shard_map/pack/pallas_call | solution.py:266
  2.5 24.8 %all_to_all.16.mine = f32[4,768,128]{2,1,0:T(8,128)S(1)} all-to-all(f32[4,768,128]{2,1,0:T(8,128)S(1)} %pack.1), channel_id=1, replica_groups=mesh['row'=32,'x'=4,'orb'=2] {'x'}, dimensions={0} | all-to-all | bytes 3145728 | tf_op jit(solution)/shard_map/all_to_all | solution.py:279
  27.7 5.6 %collective-permute-start.2 = (f32[256,128]{1,0:T(8,128)S(1)}, f32[256,128]{1,0:T(8,128)S(1)}, u32[]{:S(2)}, u32[]{:S(2)}) collective-permute-start(f32[256,128]{1,0:T(8,128)S(1)} %get-tuple-element.36), channel_id=1, source_target_pairs={{8,16},{24,32},{40,48},{56,64},{72,80},{88,96},{104,112},{120,128}... | collective-permute-start | bytes 393224 | tf_op jit(solution)/shard_map/ppermute | solution.py:250
  33.3 0.9 collective-permute-start.7
  34.2 1.2 %collective-permute-start.6 = (f32[2,1,128,256]{3,2,1,0:T(8,128)S(1)}, f32[2,1,128,256]{3,2,1,0:T(8,128)S(1)}, u32[]{:S(2)}, u32[]{:S(2)}) collective-permute-start(f32[2,1,128,256]{3,2,1,0:T(8,128)S(1)} %copy-done), channel_id=1, source_target_pairs={{0,2},{2,4},{4,6},{6,0},{1,3},{3,5},{5,7},{7,1},{8,10},{10,12},{12... | collective-permute-start | bytes 786440 | tf_op jit(solution)/shard_map/ppermute | solution.py:242
  35.5 1.9 %collective-permute-start.5 = (f32[2,128,640]{2,1,0:T(8,128)S(1)}, f32[2,128,640]{2,1,0:T(8,128)S(1)}, u32[]{:S(2)}, u32[]{:S(2)}) collective-permute-start(f32[2,128,640]{2,1,0:T(8,128)S(1)} %step_edges.1), channel_id=1, source_target_pairs={{0,8},{8,0},{2,10},{10,2},{4,12},{12,4},{6,14},{14,6},{16,24},{24,... | collective-permute-start | bytes 1966088 | tf_op jit(solution)/shard_map/ppermute | solution.py:261
  37.4 0.8 margin.1.own.y0
  38.2 6.0 %collective-permute-start.4 = (f32[512,128]{1,0:T(8,128)S(1)}, f32[512,128]{1,0:T(8,128)S(1)}, u32[]{:S(2)}, u32[]{:S(2)}) collective-permute-start(f32[512,128]{1,0:T(8,128)S(1)} %margin.1.own.y0), channel_id=1, source_target_pairs={{8,16},{24,32},{40,48},{56,64},{72,80},{88,96},{104,112},{120,128}... | collective-permute-start | bytes 786440 | tf_op jit(solution)/shard_map/ppermute | solution.py:250
  44.3 2.1 %collective-permute-start.8 = (f32[2,1,128,256]{3,2,1,0:T(8,128)S(1)}, f32[2,1,128,256]{3,2,1,0:T(8,128)S(1)}, u32[]{:S(2)}, u32[]{:S(2)}) collective-permute-start(f32[2,1,128,256]{3,2,1,0:T(8,128)S(1)} %copy-done), channel_id=1, source_target_pairs={{0,6},{2,0},{4,2},{6,4},{1,7},{3,1},{5,3},{7,5},{8,14},{10,8},{12,... | collective-permute-start | bytes 786440 | tf_op jit(solution)/shard_map/ppermute | solution.py:242
  46.5 2.2 %collective-permute-done.6.c1 = f32[2,1,128,256]{3,2,1,0:T(8,128)S(1)} collective-permute-done((f32[2,1,128,256]{3,2,1,0:T(8,128)S(1)}, f32[2,1,128,256]{3,2,1,0:T(8,128)S(1)}, u32[]{:S(2)}, u32[]{:S(2)}) %collective-permute-start.6) | collective-permute-done | bytes 262176 | tf_op jit(solution)/shard_map/ppermute | solution.py:242
  48.6 2.8 %collective-permute-done.4.from_b = f32[512,128]{1,0:T(8,128)S(1)} collective-permute-done((f32[512,128]{1,0:T(8,128)S(1)}, f32[512,128]{1,0:T(8,128)S(1)}, u32[]{:S(2)}, u32[]{:S(2)}) %collective-permute-start.4) | collective-permute-done | bytes 262176 | tf_op jit(solution)/shard_map/ppermute | solution.py:250
  51.4 2.1 %collective-permute-done.3.from_a = f32[512,128]{1,0:T(8,128)S(1)} collective-permute-done((f32[512,128]{1,0:T(8,128)S(1)}, f32[512,128]{1,0:T(8,128)S(1)}, u32[]{:S(2)}, u32[]{:S(2)}) %collective-permute-start.3) | collective-permute-done | bytes 262176 | tf_op jit(solution)/shard_map/ppermute | solution.py:250
  53.6 2.1 %collective-permute-done.9.edge_other = f32[2,128,640]{2,1,0:T(8,128)S(1)} collective-permute-done((f32[2,128,640]{2,1,0:T(8,128)S(1)}, f32[2,128,640]{2,1,0:T(8,128)S(1)}, u32[]{:S(2)}, u32[]{:S(2)}) %collective-permute-start.9) | collective-permute-done | bytes 655392 | tf_op jit(solution)/shard_map/ppermute | solution.py:245
  55.7 0.4 step_parts.1
  56.1 0.2 collective-permute-start.11
  56.4 0.4 collective-permute-start.12
  56.9 0.4 collective-permute-start.14
  57.2 1.6 %two.1 = (f32[512,128]{1,0:T(8,128)S(1)}, f32[512,128]{1,0:T(8,128)S(1)}) custom-call(s32[1]{0:T(128)} %bitcast.me, bf16[8,128,640]{2,1,0:T(8,128)(2,1)S(1)} %get-tuple-element.44.m_high, bf16[8,128,640]{2,1,0:T(8,128)(2,1)S(1)} %get-tuple-element.45.m_low, f32[512,128]{1,0:T(8,128)S(1)} %collective-permute-done.3.from_a, ...), custom_call_target="tpu_custom_call" | custom-call | flops 754974720 | bytes 4194304 | tf_op jit(solution)/shard_map/two/pallas_call | solution.py:230
  58.9 6.2 %collective-permute-start.15 = (f32[512,128]{1,0:T(8,128)S(1)}, f32[512,128]{1,0:T(8,128)S(1)}, u32[]{:S(2)}, u32[]{:S(2)}) collective-permute-start(f32[512,128]{1,0:T(8,128)S(1)} %get-tuple-element.48.own), channel_id=1, source_target_pairs={{8,16},{24,32},{40,48},{56,64},{72,80},{88,96},{104,112},{120,128}... | collective-permute-start | bytes 786440 | tf_op jit(solution)/shard_map/ppermute | solution.py:250
  65.2 0.7 old_parts.1
  65.9 1.3 %collective-permute-done.10.from_a = f32[512,128]{1,0:T(8,128)S(1)} collective-permute-done((f32[512,128]{1,0:T(8,128)S(1)}, f32[512,128]{1,0:T(8,128)S(1)}, u32[]{:S(2)}, u32[]{:S(2)}) %collective-permute-start.10) | collective-permute-done | bytes 262176 | tf_op jit(solution)/shard_map/ppermute | solution.py:250
  67.2 4.0 %collective-permute-done.15.from_b = f32[512,128]{1,0:T(8,128)S(1)} collective-permute-done((f32[512,128]{1,0:T(8,128)S(1)}, f32[512,128]{1,0:T(8,128)S(1)}, u32[]{:S(2)}, u32[]{:S(2)}) %collective-permute-start.15) | collective-permute-done | bytes 262176 | tf_op jit(solution)/shard_map/ppermute | solution.py:250
  71.3 1.6 %last.1.new = f32[4,128,128]{2,1,0:T(8,128)S(1)} custom-call(s32[1]{0:T(128)} %bitcast.me, bf16[8,128,640]{2,1,0:T(8,128)(2,1)S(1)} %get-tuple-element.44.m_high, bf16[8,128,640]{2,1,0:T(8,128)(2,1)S(1)} %get-tuple-element.45.m_low, f32[512,128]{1,0:T(8,128)S(1)} %collective-permute-done.10.from_a, f32[512,128]{1,0:T(8,128)S(1)} %collective-permute-done.15.from_b, ...), custom_call_target="tpu_custom_call" | custom-call | flops 754974720 | bytes 4718592 | tf_op jit(solution)/shard_map/last/pallas_call | solution.py:230
  72.9 0.7 project.1
  73.6 20.6 %all_to_all.17 = f32[32,16,128]{2,1,0:T(8,128)S(1)} all-to-all(f32[32,16,128]{2,1,0:T(8,128)S(1)} %bitcast.4), channel_id=1, replica_groups=mesh['row'=32,'x'=4,'orb'=2] {'row'}, dimensions={0} | all-to-all | bytes 524288 | tf_op jit(solution)/shard_map/all_to_all | solution.py:327
  94.3 1.5 %collective-permute-start.16 = (f32[136,128]{1,0:T(8,128)S(1)}, f32[136,128]{1,0:T(8,128)S(1)}, u32[]{:S(2)}, u32[]{:S(2)}) collective-permute-start(f32[136,128]{1,0:T(8,128)S(1)} %get-tuple-element.59), channel_id=1, source_target_pairs={{0,2},{2,4},{4,6},{6,0},{1,3},{3,5},{5,7},{7,1},{8,10},{10,12},{12... | collective-permute-start | bytes 208904 | tf_op jit(solution)/shard_map/ppermute | solution.py:242
  95.8 2.0 %collective-permute-start.17 = (f32[136,128]{1,0:T(8,128)S(1)}, f32[136,128]{1,0:T(8,128)S(1)}, u32[]{:S(2)}, u32[]{:S(2)}) collective-permute-start(f32[136,128]{1,0:T(8,128)S(1)} %get-tuple-element.60), channel_id=1, source_target_pairs={{0,4},{2,6},{4,0},{6,2},{1,5},{3,7},{5,1},{7,3},{8,12},{10,14},{12... | collective-permute-start | bytes 208904 | tf_op jit(solution)/shard_map/ppermute | solution.py:242
  97.9 1.8 %collective-permute-start.18 = (f32[136,128]{1,0:T(8,128)S(1)}, f32[136,128]{1,0:T(8,128)S(1)}, u32[]{:S(2)}, u32[]{:S(2)}) collective-permute-start(f32[136,128]{1,0:T(8,128)S(1)} %get-tuple-element.61), channel_id=1, source_target_pairs={{0,6},{2,0},{4,2},{6,4},{1,7},{3,1},{5,3},{7,5},{8,14},{10,8},{12,... | collective-permute-start | bytes 208904 | tf_op jit(solution)/shard_map/ppermute | solution.py:242
  99.7 0.2 collective-permute-done.16.b1
  99.9 1.7 %collective-permute-done.17.b2 = f32[136,128]{1,0:T(8,128)S(1)} collective-permute-done((f32[136,128]{1,0:T(8,128)S(1)}, f32[136,128]{1,0:T(8,128)S(1)}, u32[]{:S(2)}, u32[]{:S(2)}) %collective-permute-start.17) | collective-permute-done | bytes 69664 | tf_op jit(solution)/shard_map/ppermute | solution.py:242
  101.7 0.5 collective-permute-done.18.b3
  102.2 0.9 finish.1
  (21 shorter events, 0.8 us)
Async XLA Ops:
  27.3 6.0 %copy-start = (f32[2,1,128,256]{3,2,1,0:T(8,128)S(1)}, f32[2,1,128,256]{3,2,1,0:T(8,128)}, u32[]{:S(2)}) copy-start(f32[2,1,128,256]{3,2,1,0:T(8,128)} %c0) | copy-start | bytes 786436
  27.4 5.9 %collective-permute-start = (f32[4,768,128]{2,1,0:T(8,128)S(1)}, f32[4,768,128]{2,1,0:T(8,128)S(1)}, u32[]{:S(2)}, u32[]{:S(2)}) collective-permute-start(f32[4,768,128]{2,1,0:T(8,128)S(1)} %all_to_all.16.mine), channel_id=1, source_target_pairs={{0,1},{1,0},{2,3},{3,2},{4,5},{5,4},{6,7},{7,6},{8,9},{9,8},{10,11... | collective-permute-start | bytes 4718600 | tf_op jit(solution)/shard_map/ppermute | solution.py:245
  27.5 9.9 %collective-permute-start.1 = (f32[256,128]{1,0:T(8,128)S(1)}, f32[256,128]{1,0:T(8,128)S(1)}, u32[]{:S(2)}, u32[]{:S(2)}) collective-permute-start(f32[256,128]{1,0:T(8,128)S(1)} %get-tuple-element.35), channel_id=1, source_target_pairs={{0,8},{16,24},{32,40},{48,56},{64,72},{80,88},{96,104},{112,120},{... | collective-permute-start | bytes 393224 | tf_op jit(solution)/shard_map/ppermute | solution.py:250
  27.7 9.8 %collective-permute-start.2 = (f32[256,128]{1,0:T(8,128)S(1)}, f32[256,128]{1,0:T(8,128)S(1)}, u32[]{:S(2)}, u32[]{:S(2)}) collective-permute-start(f32[256,128]{1,0:T(8,128)S(1)} %get-tuple-element.36), channel_id=1, source_target_pairs={{8,16},{24,32},{40,48},{56,64},{72,80},{88,96},{104,112},{120,128}... | collective-permute-start | bytes 393224 | tf_op jit(solution)/shard_map/ppermute | solution.py:250
  33.3 11.0 %collective-permute-start.7 = (f32[2,1,128,256]{3,2,1,0:T(8,128)S(1)}, f32[2,1,128,256]{3,2,1,0:T(8,128)S(1)}, u32[]{:S(2)}, u32[]{:S(2)}) collective-permute-start(f32[2,1,128,256]{3,2,1,0:T(8,128)S(1)} %copy-done), channel_id=1, source_target_pairs={{0,4},{2,6},{4,0},{6,2},{1,5},{3,7},{5,1},{7,3},{8,12},{10,14},{12... | collective-permute-start | bytes 786440 | tf_op jit(solution)/shard_map/ppermute | solution.py:242
  34.2 14.4 %collective-permute-start.6 = (f32[2,1,128,256]{3,2,1,0:T(8,128)S(1)}, f32[2,1,128,256]{3,2,1,0:T(8,128)S(1)}, u32[]{:S(2)}, u32[]{:S(2)}) collective-permute-start(f32[2,1,128,256]{3,2,1,0:T(8,128)S(1)} %copy-done), channel_id=1, source_target_pairs={{0,2},{2,4},{4,6},{6,0},{1,3},{3,5},{5,7},{7,1},{8,10},{10,12},{12... | collective-permute-start | bytes 786440 | tf_op jit(solution)/shard_map/ppermute | solution.py:242
  35.5 18.1 %collective-permute-start.5 = (f32[2,128,640]{2,1,0:T(8,128)S(1)}, f32[2,128,640]{2,1,0:T(8,128)S(1)}, u32[]{:S(2)}, u32[]{:S(2)}) collective-permute-start(f32[2,128,640]{2,1,0:T(8,128)S(1)} %step_edges.1), channel_id=1, source_target_pairs={{0,8},{8,0},{2,10},{10,2},{4,12},{12,4},{6,14},{14,6},{16,24},{24,... | collective-permute-start | bytes 1966088 | tf_op jit(solution)/shard_map/ppermute | solution.py:261
  38.2 13.3 %collective-permute-start.4 = (f32[512,128]{1,0:T(8,128)S(1)}, f32[512,128]{1,0:T(8,128)S(1)}, u32[]{:S(2)}, u32[]{:S(2)}) collective-permute-start(f32[512,128]{1,0:T(8,128)S(1)} %margin.1.own.y0), channel_id=1, source_target_pairs={{8,16},{24,32},{40,48},{56,64},{72,80},{88,96},{104,112},{120,128}... | collective-permute-start | bytes 786440 | tf_op jit(solution)/shard_map/ppermute | solution.py:250
  44.2 9.3 %collective-permute-start.3 = (f32[512,128]{1,0:T(8,128)S(1)}, f32[512,128]{1,0:T(8,128)S(1)}, u32[]{:S(2)}, u32[]{:S(2)}) collective-permute-start(f32[512,128]{1,0:T(8,128)S(1)} %margin.1.own.y0), channel_id=1, source_target_pairs={{0,8},{16,24},{32,40},{48,56},{64,72},{80,88},{96,104},{112,120},{... | collective-permute-start | bytes 786440 | tf_op jit(solution)/shard_map/ppermute | solution.py:250
  44.3 9.2 %collective-permute-start.8 = (f32[2,1,128,256]{3,2,1,0:T(8,128)S(1)}, f32[2,1,128,256]{3,2,1,0:T(8,128)S(1)}, u32[]{:S(2)}, u32[]{:S(2)}) collective-permute-start(f32[2,1,128,256]{3,2,1,0:T(8,128)S(1)} %copy-done), channel_id=1, source_target_pairs={{0,6},{2,0},{4,2},{6,4},{1,7},{3,1},{5,3},{7,5},{8,14},{10,8},{12,... | collective-permute-start | bytes 786440 | tf_op jit(solution)/shard_map/ppermute | solution.py:242
  53.6 2.1 %collective-permute-start.9 = (f32[2,128,640]{2,1,0:T(8,128)S(1)}, f32[2,128,640]{2,1,0:T(8,128)S(1)}, u32[]{:S(2)}, u32[]{:S(2)}) collective-permute-start(f32[2,128,640]{2,1,0:T(8,128)S(1)} %collective-permute-done.5.edge), channel_id=1, source_target_pairs={{0,1},{1,0},{2,3},{3,2},{4,5},{5,4},{6,7},{7,6},{8,9},{9,8},{10,11... | collective-permute-start | bytes 1966088 | tf_op jit(solution)/shard_map/ppermute | solution.py:245
  56.1 2.8 %collective-permute-start.11 = (f32[2,1,128,256]{3,2,1,0:T(8,128)S(1)}, f32[2,1,128,256]{3,2,1,0:T(8,128)S(1)}, u32[]{:S(2)}, u32[]{:S(2)}) collective-permute-start(f32[2,1,128,256]{3,2,1,0:T(8,128)S(1)} %copy-done), channel_id=1, source_target_pairs={{0,1},{1,0},{2,3},{3,2},{4,5},{5,4},{6,7},{7,6},{8,9},{9,8},{10,11... | collective-permute-start | bytes 786440 | tf_op jit(solution)/shard_map/ppermute | solution.py:245
  56.4 8.8 %collective-permute-start.12 = (f32[2,1,128,256]{3,2,1,0:T(8,128)S(1)}, f32[2,1,128,256]{3,2,1,0:T(8,128)S(1)}, u32[]{:S(2)}, u32[]{:S(2)}) collective-permute-start(f32[2,1,128,256]{3,2,1,0:T(8,128)S(1)} %collective-permute-done.6.c1), channel_id=1, source_target_pairs={{0,1},{1,0},{2,3},{3,2},{4,5},{5,4},{6,7},{7,6},{8,9},{9,8},{10,11... | collective-permute-start | bytes 786440 | tf_op jit(solution)/shard_map/ppermute | solution.py:245
  56.7 8.4 %collective-permute-start.13 = (f32[2,1,128,256]{3,2,1,0:T(8,128)S(1)}, f32[2,1,128,256]{3,2,1,0:T(8,128)S(1)}, u32[]{:S(2)}, u32[]{:S(2)}) collective-permute-start(f32[2,1,128,256]{3,2,1,0:T(8,128)S(1)} %collective-permute-done.7.c2), channel_id=1, source_target_pairs={{0,1},{1,0},{2,3},{3,2},{4,5},{5,4},{6,7},{7,6},{8,9},{9,8},{10,11... | collective-permute-start | bytes 786440 | tf_op jit(solution)/shard_map/ppermute | solution.py:245
  56.9 8.3 %collective-permute-start.14 = (f32[2,1,128,256]{3,2,1,0:T(8,128)S(1)}, f32[2,1,128,256]{3,2,1,0:T(8,128)S(1)}, u32[]{:S(2)}, u32[]{:S(2)}) collective-permute-start(f32[2,1,128,256]{3,2,1,0:T(8,128)S(1)} %collective-permute-done.8.c3), channel_id=1, source_target_pairs={{0,1},{1,0},{2,3},{3,2},{4,5},{5,4},{6,7},{7,6},{8,9},{9,8},{10,11... | collective-permute-start | bytes 786440 | tf_op jit(solution)/shard_map/ppermute | solution.py:245
  58.8 8.4 %collective-permute-start.10 = (f32[512,128]{1,0:T(8,128)S(1)}, f32[512,128]{1,0:T(8,128)S(1)}, u32[]{:S(2)}, u32[]{:S(2)}) collective-permute-start(f32[512,128]{1,0:T(8,128)S(1)} %get-tuple-element.48.own), channel_id=1, source_target_pairs={{0,8},{16,24},{32,40},{48,56},{64,72},{80,88},{96,104},{112,120},{... | collective-permute-start | bytes 786440 | tf_op jit(solution)/shard_map/ppermute | solution.py:250
  58.9 12.3 %collective-permute-start.15 = (f32[512,128]{1,0:T(8,128)S(1)}, f32[512,128]{1,0:T(8,128)S(1)}, u32[]{:S(2)}, u32[]{:S(2)}) collective-permute-start(f32[512,128]{1,0:T(8,128)S(1)} %get-tuple-element.48.own), channel_id=1, source_target_pairs={{8,16},{24,32},{40,48},{56,64},{72,80},{88,96},{104,112},{120,128}... | collective-permute-start | bytes 786440 | tf_op jit(solution)/shard_map/ppermute | solution.py:250
  94.3 5.6 %collective-permute-start.16 = (f32[136,128]{1,0:T(8,128)S(1)}, f32[136,128]{1,0:T(8,128)S(1)}, u32[]{:S(2)}, u32[]{:S(2)}) collective-permute-start(f32[136,128]{1,0:T(8,128)S(1)} %get-tuple-element.59), channel_id=1, source_target_pairs={{0,2},{2,4},{4,6},{6,0},{1,3},{3,5},{5,7},{7,1},{8,10},{10,12},{12... | collective-permute-start | bytes 208904 | tf_op jit(solution)/shard_map/ppermute | solution.py:242
  95.8 5.8 %collective-permute-start.17 = (f32[136,128]{1,0:T(8,128)S(1)}, f32[136,128]{1,0:T(8,128)S(1)}, u32[]{:S(2)}, u32[]{:S(2)}) collective-permute-start(f32[136,128]{1,0:T(8,128)S(1)} %get-tuple-element.60), channel_id=1, source_target_pairs={{0,4},{2,6},{4,0},{6,2},{1,5},{3,7},{5,1},{7,3},{8,12},{10,14},{12... | collective-permute-start | bytes 208904 | tf_op jit(solution)/shard_map/ppermute | solution.py:242
  97.9 4.3 %collective-permute-start.18 = (f32[136,128]{1,0:T(8,128)S(1)}, f32[136,128]{1,0:T(8,128)S(1)}, u32[]{:S(2)}, u32[]{:S(2)}) collective-permute-start(f32[136,128]{1,0:T(8,128)S(1)} %get-tuple-element.61), channel_id=1, source_target_pairs={{0,6},{2,0},{4,2},{6,4},{1,7},{3,1},{5,3},{7,5},{8,14},{10,8},{12,... | collective-permute-start | bytes 208904 | tf_op jit(solution)/shard_map/ppermute | solution.py:242

commit v14 on v10

--- a/solution.py
+++ b/solution.py
@@ -282,7 +282,7 @@
     edge = struct((2 * B, B), F32)
     edges = call(edge_kernel, [edge, edge], [me, mine], 10**5, 28, "edges")
     *edges, held = lax.optimization_barrier((*edges, mine))
-    other = swap(held)
+    other, first_across = lax.optimization_barrier((swap(held), swap(coefficients)))
     from_a, from_b = exchange(*edges)
     step_edge = call(step_edge_kernel, struct((2, B, BAND * B), F32), [me, mine, other], 10**5, 20, "step_edges")
     step_edge = apart(step_edge)
@@ -312,7 +312,7 @@
     arrived = exchange(y2, y2)
     old_type = struct((2 * width, 2 * ROW * B), BF16)
     old_high, old_low = call(
-        old_kernel, [old_type, old_type], [me] + old + [swap(o) for o in old], 10**6, 64, "old_parts"
+        old_kernel, [old_type, old_type], [me] + old + [first_across] + [swap(o) for o in old[1:]], 10**6, 64, "old_parts"
     )
     arrived[0], old_high = lax.optimization_barrier((arrived[0], old_high))
     new = call(

time: 104 us -> 105 us (level)
  no operation moved by 1% of the time
where the time goes in v14:
time: 105 us; the launch traced here: 104 us
  blocking collectives  47.9 us (46%)
  starting transfers between devices  28.6 us (27%)
  waiting for transfers between devices  17.4 us (17%)
  Pallas kernels  8.77 us (8%)
    all_to_all x1, blocking collectives, local(): mine = lax.all_to_all(packed, 'x', 0, 0, tiled=True)  24.8 us
    all_to_all x1, blocking collectives, local(): sums = lax.all_to_all(partial_value, 'row', 0, 0, tiled=True)  23.1 us
    ppermute x6, starting transfers between devices, swap_rows(): return lax.ppermute(value, 'row', pairs + [(j, i) for i, j in pairs])  17.8 us
    ppermute x6, waiting for transfers between devices, swap_rows(): return lax.ppermute(value, 'row', pairs + [(j, i) for i, j in pairs])  10.4 us
    ppermute x6, starting transfers between devices, in_row(): return lax.ppermute(value, 'x', [(x, (x + by) % ROW) for x in range(ROW)])  7.78 us
    pallas_call x10, Pallas kernels, call(): pl.pallas_call(kernel, out_shape=out_shape, in_specs=[SMEM] * scalars + [...  6.87 us
    ppermute x6, waiting for transfers between devices, in_row(): return lax.ppermute(value, 'x', [(x, (x + by) % ROW) for x in range(ROW)])  5.91 us
  transfers between devices with their start and end apart: 19, of which 10 were waited for; matrix products, arithmetic and copies ran while one was open for 0% of the time, Pallas kernels for 3%

profile of v14, /device:TPU:32, one launch (start us, length us, event | category | flops | bytes accessed | tf_op | source)
XLA Modules:
  0.0 104.3 jit_solution(17421654637259989441)
XLA Ops:
  0.6 1.9 %pack.1 = f32[4,768,128]{2,1,0:T(8,128)S(1)} custom-call(s32[1]{0:T(128)} %bitcast.me, s32[1,16]{1,0:T(1,128)} %nbr_hbm.1, s32[1,16]{1,0:T(1,128)} %pat_hbm.1, f32[2,1,128,256]{3,2,1,0:T(8,128)} %c0.1, f32[1,16,128,128]{3,2,1,0:T(8,128)} %margin_hbm.1, f32[1,16,128,128]{3,2,1,0:T(8,128)} %step_hbm.1), custom_call_target="tpu_custom_call" | custom-call | flops 1000000 | bytes 2883584 | tf_op jit(solution)/shard_map/pack/pallas_call | solution.py:266
  2.5 24.8 %all_to_all.16.mine = f32[4,768,128]{2,1,0:T(8,128)S(1)} all-to-all(f32[4,768,128]{2,1,0:T(8,128)S(1)} %pack.1), channel_id=1, replica_groups=mesh['row'=32,'x'=4,'orb'=2] {'x'}, dimensions={0} | all-to-all | bytes 3145728 | tf_op jit(solution)/shard_map/all_to_all | solution.py:279
  27.5 0.8 copy-done
  28.4 5.6 %collective-permute-start.3 = (f32[256,128]{1,0:T(8,128)S(1)}, f32[256,128]{1,0:T(8,128)S(1)}, u32[]{:S(2)}, u32[]{:S(2)}) collective-permute-start(f32[256,128]{1,0:T(8,128)S(1)} %get-tuple-element.34), channel_id=1, source_target_pairs={{8,16},{24,32},{40,48},{56,64},{72,80},{88,96},{104,112},{120,128}... | collective-permute-start | bytes 393224 | tf_op jit(solution)/shard_map/ppermute | solution.py:250
  34.1 1.9 %collective-permute-start.6 = (f32[2,128,640]{2,1,0:T(8,128)S(1)}, f32[2,128,640]{2,1,0:T(8,128)S(1)}, u32[]{:S(2)}, u32[]{:S(2)}) collective-permute-start(f32[2,128,640]{2,1,0:T(8,128)S(1)} %step_edges.1), channel_id=1, source_target_pairs={{0,8},{8,0},{2,10},{10,2},{4,12},{12,4},{6,14},{14,6},{16,24},{24,... | collective-permute-start | bytes 1966088 | tf_op jit(solution)/shard_map/ppermute | solution.py:261
  36.1 0.9 collective-permute-start.8
  37.0 0.9 collective-permute-done.3.from_b
  37.9 0.7 margin.1.own.y0
  38.7 1.2 %collective-permute-start.4 = (f32[512,128]{1,0:T(8,128)S(1)}, f32[512,128]{1,0:T(8,128)S(1)}, u32[]{:S(2)}, u32[]{:S(2)}) collective-permute-start(f32[512,128]{1,0:T(8,128)S(1)} %margin.1.own.y0), channel_id=1, source_target_pairs={{0,8},{16,24},{32,40},{48,56},{64,72},{80,88},{96,104},{112,120},{... | collective-permute-start | bytes 786440 | tf_op jit(solution)/shard_map/ppermute | solution.py:250
  39.8 5.0 %collective-permute-start.5 = (f32[512,128]{1,0:T(8,128)S(1)}, f32[512,128]{1,0:T(8,128)S(1)}, u32[]{:S(2)}, u32[]{:S(2)}) collective-permute-start(f32[512,128]{1,0:T(8,128)S(1)} %margin.1.own.y0), channel_id=1, source_target_pairs={{8,16},{24,32},{40,48},{56,64},{72,80},{88,96},{104,112},{120,128}... | collective-permute-start | bytes 786440 | tf_op jit(solution)/shard_map/ppermute | solution.py:250
  44.8 0.6 collective-permute-start.7
  45.8 2.3 %collective-permute-start.9 = (f32[2,1,128,256]{3,2,1,0:T(8,128)S(1)}, f32[2,1,128,256]{3,2,1,0:T(8,128)S(1)}, u32[]{:S(2)}, u32[]{:S(2)}) collective-permute-start(f32[2,1,128,256]{3,2,1,0:T(8,128)S(1)} %copy-done), channel_id=1, source_target_pairs={{0,6},{2,0},{4,2},{6,4},{1,7},{3,1},{5,3},{7,5},{8,14},{10,8},{12,... | collective-permute-start | bytes 786440 | tf_op jit(solution)/shard_map/ppermute | solution.py:242
  48.1 4.1 %collective-permute-done.4.from_a = f32[512,128]{1,0:T(8,128)S(1)} collective-permute-done((f32[512,128]{1,0:T(8,128)S(1)}, f32[512,128]{1,0:T(8,128)S(1)}, u32[]{:S(2)}, u32[]{:S(2)}) %collective-permute-start.4) | collective-permute-done | bytes 262176 | tf_op jit(solution)/shard_map/ppermute | solution.py:250
  52.2 1.2 %collective-permute-done.7.c1 = f32[2,1,128,256]{3,2,1,0:T(8,128)S(1)} collective-permute-done((f32[2,1,128,256]{3,2,1,0:T(8,128)S(1)}, f32[2,1,128,256]{3,2,1,0:T(8,128)S(1)}, u32[]{:S(2)}, u32[]{:S(2)}) %collective-permute-start.7) | collective-permute-done | bytes 262176 | tf_op jit(solution)/shard_map/ppermute | solution.py:242
  53.5 0.5 collective-permute-start.12
  54.5 1.1 %collective-permute-done.10.edge_other = f32[2,128,640]{2,1,0:T(8,128)S(1)} collective-permute-done((f32[2,128,640]{2,1,0:T(8,128)S(1)}, f32[2,128,640]{2,1,0:T(8,128)S(1)}, u32[]{:S(2)}, u32[]{:S(2)}) %collective-permute-start.10) | collective-permute-done | bytes 655392 | tf_op jit(solution)/shard_map/ppermute | solution.py:245
  55.6 0.4 step_parts.1
  56.0 1.6 %two.1 = (f32[512,128]{1,0:T(8,128)S(1)}, f32[512,128]{1,0:T(8,128)S(1)}) custom-call(s32[1]{0:T(128)} %bitcast.me, bf16[8,128,640]{2,1,0:T(8,128)(2,1)S(1)} %get-tuple-element.38.m_high, bf16[8,128,640]{2,1,0:T(8,128)(2,1)S(1)} %get-tuple-element.39.m_low, f32[512,128]{1,0:T(8,128)S(1)} %collective-permute-done.4.from_a, ...), custom_call_target="tpu_custom_call" | custom-call | flops 754974720 | bytes 4194304 | tf_op jit(solution)/shard_map/two/pallas_call | solution.py:230
  57.6 0.6 collective-permute-start.11
  58.2 5.3 %collective-permute-start.15 = (f32[512,128]{1,0:T(8,128)S(1)}, f32[512,128]{1,0:T(8,128)S(1)}, u32[]{:S(2)}, u32[]{:S(2)}) collective-permute-start(f32[512,128]{1,0:T(8,128)S(1)} %get-tuple-element.42.own), channel_id=1, source_target_pairs={{8,16},{24,32},{40,48},{56,64},{72,80},{88,96},{104,112},{120,128}... | collective-permute-start | bytes 786440 | tf_op jit(solution)/shard_map/ppermute | solution.py:250
  63.6 0.7 old_parts.1
  64.3 1.7 %collective-permute-done.11.from_a = f32[512,128]{1,0:T(8,128)S(1)} collective-permute-done((f32[512,128]{1,0:T(8,128)S(1)}, f32[512,128]{1,0:T(8,128)S(1)}, u32[]{:S(2)}, u32[]{:S(2)}) %collective-permute-start.11) | collective-permute-done | bytes 262176 | tf_op jit(solution)/shard_map/ppermute | solution.py:250
  66.0 3.6 %collective-permute-done.15.from_b = f32[512,128]{1,0:T(8,128)S(1)} collective-permute-done((f32[512,128]{1,0:T(8,128)S(1)}, f32[512,128]{1,0:T(8,128)S(1)}, u32[]{:S(2)}, u32[]{:S(2)}) %collective-permute-start.15) | collective-permute-done | bytes 262176 | tf_op jit(solution)/shard_map/ppermute | solution.py:250
  69.7 1.6 %last.1.new = f32[4,128,128]{2,1,0:T(8,128)S(1)} custom-call(s32[1]{0:T(128)} %bitcast.me, bf16[8,128,640]{2,1,0:T(8,128)(2,1)S(1)} %get-tuple-element.38.m_high, bf16[8,128,640]{2,1,0:T(8,128)(2,1)S(1)} %get-tuple-element.39.m_low, f32[512,128]{1,0:T(8,128)S(1)} %collective-permute-done.11.from_a, f32[512,128]{1,0:T(8,128)S(1)} %collective-permute-done.15.from_b, ...), custom_call_target="tpu_custom_call" | custom-call | flops 754974720 | bytes 4718592 | tf_op jit(solution)/shard_map/last/pallas_call | solution.py:230
  71.3 0.7 project.1
  72.0 23.1 %all_to_all.17 = f32[32,16,128]{2,1,0:T(8,128)S(1)} all-to-all(f32[32,16,128]{2,1,0:T(8,128)S(1)} %bitcast.4), channel_id=1, replica_groups=mesh['row'=32,'x'=4,'orb'=2] {'row'}, dimensions={0} | all-to-all | bytes 524288 | tf_op jit(solution)/shard_map/all_to_all | solution.py:326
  95.2 0.7 collective-permute-start.16
  95.9 3.3 %collective-permute-start.17 = (f32[136,128]{1,0:T(8,128)S(1)}, f32[136,128]{1,0:T(8,128)S(1)}, u32[]{:S(2)}, u32[]{:S(2)}) collective-permute-start(f32[136,128]{1,0:T(8,128)S(1)} %get-tuple-element.54), channel_id=1, source_target_pairs={{0,4},{2,6},{4,0},{6,2},{1,5},{3,7},{5,1},{7,3},{8,12},{10,14},{12... | collective-permute-start | bytes 208904 | tf_op jit(solution)/shard_map/ppermute | solution.py:242
  99.1 1.7 %collective-permute-done.16.b1 = f32[136,128]{1,0:T(8,128)S(1)} collective-permute-done((f32[136,128]{1,0:T(8,128)S(1)}, f32[136,128]{1,0:T(8,128)S(1)}, u32[]{:S(2)}, u32[]{:S(2)}) %collective-permute-start.16) | collective-permute-done | bytes 69664 | tf_op jit(solution)/shard_map/ppermute | solution.py:242
  100.8 1.3 %collective-permute-done.17.b2 = f32[136,128]{1,0:T(8,128)S(1)} collective-permute-done((f32[136,128]{1,0:T(8,128)S(1)}, f32[136,128]{1,0:T(8,128)S(1)}, u32[]{:S(2)}, u32[]{:S(2)}) %collective-permute-start.17) | collective-permute-done | bytes 69664 | tf_op jit(solution)/shard_map/ppermute | solution.py:242
  102.2 1.3 %collective-permute-done.18.b3 = f32[136,128]{1,0:T(8,128)S(1)} collective-permute-done((f32[136,128]{1,0:T(8,128)S(1)}, f32[136,128]{1,0:T(8,128)S(1)}, u32[]{:S(2)}, u32[]{:S(2)}) %collective-permute-start.18) | collective-permute-done | bytes 69664 | tf_op jit(solution)/shard_map/ppermute | solution.py:242
  103.4 0.9 finish.1
  (21 shorter events, 1.3 us)
Async XLA Ops:
  27.3 1.0 copy-start
  27.4 6.7 %collective-permute-start = (f32[4,768,128]{2,1,0:T(8,128)S(1)}, f32[4,768,128]{2,1,0:T(8,128)S(1)}, u32[]{:S(2)}, u32[]{:S(2)}) collective-permute-start(f32[4,768,128]{2,1,0:T(8,128)S(1)} %all_to_all.16.mine), channel_id=1, source_target_pairs={{0,1},{1,0},{2,3},{3,2},{4,5},{5,4},{6,7},{7,6},{8,9},{9,8},{10,11... | collective-permute-start | bytes 4718600 | tf_op jit(solution)/shard_map/ppermute | solution.py:245
  28.3 5.7 %collective-permute-start.1 = (f32[2,1,128,256]{3,2,1,0:T(8,128)S(1)}, f32[2,1,128,256]{3,2,1,0:T(8,128)S(1)}, u32[]{:S(2)}, u32[]{:S(2)}) collective-permute-start(f32[2,1,128,256]{3,2,1,0:T(8,128)S(1)} %copy-done), channel_id=1, source_target_pairs={{0,1},{1,0},{2,3},{3,2},{4,5},{5,4},{6,7},{7,6},{8,9},{9,8},{10,11... | collective-permute-start | bytes 786440 | tf_op jit(solution)/shard_map/ppermute | solution.py:245
  28.3 8.7 %collective-permute-start.2 = (f32[256,128]{1,0:T(8,128)S(1)}, f32[256,128]{1,0:T(8,128)S(1)}, u32[]{:S(2)}, u32[]{:S(2)}) collective-permute-start(f32[256,128]{1,0:T(8,128)S(1)} %get-tuple-element.33), channel_id=1, source_target_pairs={{0,8},{16,24},{32,40},{48,56},{64,72},{80,88},{96,104},{112,120},{... | collective-permute-start | bytes 393224 | tf_op jit(solution)/shard_map/ppermute | solution.py:250
  28.4 9.5 %collective-permute-start.3 = (f32[256,128]{1,0:T(8,128)S(1)}, f32[256,128]{1,0:T(8,128)S(1)}, u32[]{:S(2)}, u32[]{:S(2)}) collective-permute-start(f32[256,128]{1,0:T(8,128)S(1)} %get-tuple-element.34), channel_id=1, source_target_pairs={{8,16},{24,32},{40,48},{56,64},{72,80},{88,96},{104,112},{120,128}... | collective-permute-start | bytes 393224 | tf_op jit(solution)/shard_map/ppermute | solution.py:250
  34.1 19.3 %collective-permute-start.6 = (f32[2,128,640]{2,1,0:T(8,128)S(1)}, f32[2,128,640]{2,1,0:T(8,128)S(1)}, u32[]{:S(2)}, u32[]{:S(2)}) collective-permute-start(f32[2,128,640]{2,1,0:T(8,128)S(1)} %step_edges.1), channel_id=1, source_target_pairs={{0,8},{8,0},{2,10},{10,2},{4,12},{12,4},{6,14},{14,6},{16,24},{24,... | collective-permute-start | bytes 1966088 | tf_op jit(solution)/shard_map/ppermute | solution.py:261
  36.1 9.7 %collective-permute-start.8 = (f32[2,1,128,256]{3,2,1,0:T(8,128)S(1)}, f32[2,1,128,256]{3,2,1,0:T(8,128)S(1)}, u32[]{:S(2)}, u32[]{:S(2)}) collective-permute-start(f32[2,1,128,256]{3,2,1,0:T(8,128)S(1)} %copy-done), channel_id=1, source_target_pairs={{0,4},{2,6},{4,0},{6,2},{1,5},{3,7},{5,1},{7,3},{8,12},{10,14},{12... | collective-permute-start | bytes 786440 | tf_op jit(solution)/shard_map/ppermute | solution.py:242
  38.7 13.6 %collective-permute-start.4 = (f32[512,128]{1,0:T(8,128)S(1)}, f32[512,128]{1,0:T(8,128)S(1)}, u32[]{:S(2)}, u32[]{:S(2)}) collective-permute-start(f32[512,128]{1,0:T(8,128)S(1)} %margin.1.own.y0), channel_id=1, source_target_pairs={{0,8},{16,24},{32,40},{48,56},{64,72},{80,88},{96,104},{112,120},{... | collective-permute-start | bytes 786440 | tf_op jit(solution)/shard_map/ppermute | solution.py:250
  39.8 12.4 %collective-permute-start.5 = (f32[512,128]{1,0:T(8,128)S(1)}, f32[512,128]{1,0:T(8,128)S(1)}, u32[]{:S(2)}, u32[]{:S(2)}) collective-permute-start(f32[512,128]{1,0:T(8,128)S(1)} %margin.1.own.y0), channel_id=1, source_target_pairs={{8,16},{24,32},{40,48},{56,64},{72,80},{88,96},{104,112},{120,128}... | collective-permute-start | bytes 786440 | tf_op jit(solution)/shard_map/ppermute | solution.py:250
  44.8 8.7 %collective-permute-start.7 = (f32[2,1,128,256]{3,2,1,0:T(8,128)S(1)}, f32[2,1,128,256]{3,2,1,0:T(8,128)S(1)}, u32[]{:S(2)}, u32[]{:S(2)}) collective-permute-start(f32[2,1,128,256]{3,2,1,0:T(8,128)S(1)} %copy-done), channel_id=1, source_target_pairs={{0,2},{2,4},{4,6},{6,0},{1,3},{3,5},{5,7},{7,1},{8,10},{10,12},{12... | collective-permute-start | bytes 786440 | tf_op jit(solution)/shard_map/ppermute | solution.py:242
  45.8 7.7 %collective-permute-start.9 = (f32[2,1,128,256]{3,2,1,0:T(8,128)S(1)}, f32[2,1,128,256]{3,2,1,0:T(8,128)S(1)}, u32[]{:S(2)}, u32[]{:S(2)}) collective-permute-start(f32[2,1,128,256]{3,2,1,0:T(8,128)S(1)} %copy-done), channel_id=1, source_target_pairs={{0,6},{2,0},{4,2},{6,4},{1,7},{3,1},{5,3},{7,5},{8,14},{10,8},{12,... | collective-permute-start | bytes 786440 | tf_op jit(solution)/shard_map/ppermute | solution.py:242
  53.5 2.1 %collective-permute-start.10 = (f32[2,128,640]{2,1,0:T(8,128)S(1)}, f32[2,128,640]{2,1,0:T(8,128)S(1)}, u32[]{:S(2)}, u32[]{:S(2)}) collective-permute-start(f32[2,128,640]{2,1,0:T(8,128)S(1)} %collective-permute-done.6.edge), channel_id=1, source_target_pairs={{0,1},{1,0},{2,3},{3,2},{4,5},{5,4},{6,7},{7,6},{8,9},{9,8},{10,11... | collective-permute-start | bytes 1966088 | tf_op jit(solution)/shard_map/ppermute | solution.py:245
  53.5 10.1 %collective-permute-start.12 = (f32[2,1,128,256]{3,2,1,0:T(8,128)S(1)}, f32[2,1,128,256]{3,2,1,0:T(8,128)S(1)}, u32[]{:S(2)}, u32[]{:S(2)}) collective-permute-start(f32[2,1,128,256]{3,2,1,0:T(8,128)S(1)} %collective-permute-done.7.c1), channel_id=1, source_target_pairs={{0,1},{1,0},{2,3},{3,2},{4,5},{5,4},{6,7},{7,6},{8,9},{9,8},{10,11... | collective-permute-start | bytes 786440 | tf_op jit(solution)/shard_map/ppermute | solution.py:245
  54.0 9.6 %collective-permute-start.13 = (f32[2,1,128,256]{3,2,1,0:T(8,128)S(1)}, f32[2,1,128,256]{3,2,1,0:T(8,128)S(1)}, u32[]{:S(2)}, u32[]{:S(2)}) collective-permute-start(f32[2,1,128,256]{3,2,1,0:T(8,128)S(1)} %collective-permute-done.8.c2), channel_id=1, source_target_pairs={{0,1},{1,0},{2,3},{3,2},{4,5},{5,4},{6,7},{7,6},{8,9},{9,8},{10,11... | collective-permute-start | bytes 786440 | tf_op jit(solution)/shard_map/ppermute | solution.py:245
  54.1 9.5 %collective-permute-start.14 = (f32[2,1,128,256]{3,2,1,0:T(8,128)S(1)}, f32[2,1,128,256]{3,2,1,0:T(8,128)S(1)}, u32[]{:S(2)}, u32[]{:S(2)}) collective-permute-start(f32[2,1,128,256]{3,2,1,0:T(8,128)S(1)} %collective-permute-done.9.c3), channel_id=1, source_target_pairs={{0,1},{1,0},{2,3},{3,2},{4,5},{5,4},{6,7},{7,6},{8,9},{9,8},{10,11... | collective-permute-start | bytes 786440 | tf_op jit(solution)/shard_map/ppermute | solution.py:245
  57.6 8.4 %collective-permute-start.11 = (f32[512,128]{1,0:T(8,128)S(1)}, f32[512,128]{1,0:T(8,128)S(1)}, u32[]{:S(2)}, u32[]{:S(2)}) collective-permute-start(f32[512,128]{1,0:T(8,128)S(1)} %get-tuple-element.42.own), channel_id=1, source_target_pairs={{0,8},{16,24},{32,40},{48,56},{64,72},{80,88},{96,104},{112,120},{... | collective-permute-start | bytes 786440 | tf_op jit(solution)/shard_map/ppermute | solution.py:250
  58.2 11.5 %collective-permute-start.15 = (f32[512,128]{1,0:T(8,128)S(1)}, f32[512,128]{1,0:T(8,128)S(1)}, u32[]{:S(2)}, u32[]{:S(2)}) collective-permute-start(f32[512,128]{1,0:T(8,128)S(1)} %get-tuple-element.42.own), channel_id=1, source_target_pairs={{8,16},{24,32},{40,48},{56,64},{72,80},{88,96},{104,112},{120,128}... | collective-permute-start | bytes 786440 | tf_op jit(solution)/shard_map/ppermute | solution.py:250
  95.2 5.6 %collective-permute-start.16 = (f32[136,128]{1,0:T(8,128)S(1)}, f32[136,128]{1,0:T(8,128)S(1)}, u32[]{:S(2)}, u32[]{:S(2)}) collective-permute-start(f32[136,128]{1,0:T(8,128)S(1)} %get-tuple-element.53), channel_id=1, source_target_pairs={{0,2},{2,4},{4,6},{6,0},{1,3},{3,5},{5,7},{7,1},{8,10},{10,12},{12... | collective-permute-start | bytes 208904 | tf_op jit(solution)/shard_map/ppermute | solution.py:242
  95.9 6.3 %collective-permute-start.17 = (f32[136,128]{1,0:T(8,128)S(1)}, f32[136,128]{1,0:T(8,128)S(1)}, u32[]{:S(2)}, u32[]{:S(2)}) collective-permute-start(f32[136,128]{1,0:T(8,128)S(1)} %get-tuple-element.54), channel_id=1, source_target_pairs={{0,4},{2,6},{4,0},{6,2},{1,5},{3,7},{5,1},{7,3},{8,12},{10,14},{12... | collective-permute-start | bytes 208904 | tf_op jit(solution)/shard_map/ppermute | solution.py:242
  99.1 4.3 %collective-permute-start.18 = (f32[136,128]{1,0:T(8,128)S(1)}, f32[136,128]{1,0:T(8,128)S(1)}, u32[]{:S(2)}, u32[]{:S(2)}) collective-permute-start(f32[136,128]{1,0:T(8,128)S(1)} %get-tuple-element.55), channel_id=1, source_target_pairs={{0,6},{2,0},{4,2},{6,4},{1,7},{3,1},{5,3},{7,5},{8,14},{10,8},{12,... | collective-permute-start | bytes 208904 | tf_op jit(solution)/shard_map/ppermute | solution.py:242
